TPU v7x, 32 devices: a whole 2x2x4 slice. The times are simulated.
32 devices in a mesh: dp: 2 (over x), node: 4 (over z), local: 4 (over y, core).
Axes of the slice: x: 2, y: 2, z: 4, core: 2. Of those that a mesh axis runs over, the one named last changes fastest.
Arguments:
- tokens: bfloat16 [6144, 2048], P(('dp', 'node', 'local')), may hold values from -6 to 6
- cotangent: bfloat16 [6144, 2048], P(('dp', 'node', 'local')), may hold values from -6 to 6
- expert_of: int32 [6144, 1], P(('dp', 'node', 'local')), may hold values from 0 to 3; in each aligned block of 192 rows (0 to 191, 192 to 383, ...) at most 60 rows name the same one
- w1_codes: bfloat16 [4, 2048, 512], P('local', 'node'), may hold values from -4 to 4
- w1_scales: bfloat16 [4, 64, 512], P('local', 'node'), may hold values from 0.010986328 to 0.044921875
Outputs:
- grad_w2: bfloat16 [4, 2048, 512], P('local', 'node')
Inputs may be any that keep to these rules, and one draw needn't show every extreme that they name: `expert_of`: within the rows of one device (aligned blocks of 192 rows) no expert is named by more than 60 rows, a bound that some block reaches.
All inputs are finite; a program needn't handle non-finite values.
Results may differ from a plain program's by a relative error of at most 0.018.
Values may be sent and summed in bfloat16 or wider, within the bound.
No kernel may reach another device: no remote copies, remote signals or barrier semaphores. Data moves between devices by JAX's collectives and lax.ppermute only.
A program may use at most 64 MiB of HBM per device.

v0:
```python
import functools
import jax
import jax.numpy as jnp
from jax import lax
from jax.experimental import pallas as pl
from jax.experimental.pallas import tpu as pltpu
from jax.sharding import PartitionSpec as P

QB = 32
CHUNKS = 2
F32 = jnp.float32
BF16 = jnp.bfloat16


def mate(i, k, size):
    return i ^ k if size & (size - 1) == 0 else (i + k) % size


def traced_mate(i, k, size):
    return lax.bitwise_xor(i, jnp.int32(k)) if size & (size - 1) == 0 else lax.rem(i + k, size)


def traced_origin(i, k, size):
    if size & (size - 1) == 0:
        return lax.bitwise_xor(i, jnp.int32(k))
    return lax.rem(i + (size - k), size)


def call(body, outs, scalars, args, scratch=(), flops=0, space=pltpu.VMEM):
    moved = sum(a.size * a.dtype.itemsize for a in args)
    moved += sum(o.size * o.dtype.itemsize for o in outs)
    room = 2 * moved + (8 << 20)
    return pl.pallas_call(
        body,
        out_shape=outs,
        in_specs=[pl.BlockSpec(memory_space=pltpu.SMEM)]
        + [pl.BlockSpec(memory_space=space)] * len(args),
        out_specs=[pl.BlockSpec(memory_space=pltpu.VMEM)] * len(outs),
        scratch_shapes=list(scratch),
        compiler_params=pltpu.CompilerParams(vmem_limit_bytes=min(room, 60 << 20)),
        cost_estimate=pl.CostEstimate(flops=flops, bytes_accessed=moved, transcendentals=0),
    )(scalars, *args)


def fence_body(pos, out):
    for i in range(pos.shape[0]):
        out[i] = pos[i]


def fence(pos):
    spec = pl.BlockSpec(memory_space=pltpu.SMEM)
    kind = jax.ShapeDtypeStruct(pos.shape, pos.dtype)
    return pl.pallas_call(fence_body, out_shape=kind, in_specs=[spec], out_specs=spec)(pos)


def shape(rows, cols, dtype):
    return jax.ShapeDtypeStruct((rows, cols), dtype)


def dequant_body(pos, codes, scales, *refs):
    outs, (raw, steps, wide, sems) = refs[:-4], refs[-4:]
    mine, ff = raw.shape
    at = pl.multiple_of(pos[0] * mine, 16)
    first = pltpu.make_async_copy(codes.at[pl.ds(at, mine), :], raw, sems.at[0])
    second = pltpu.make_async_copy(scales, steps, sems.at[1])
    first.start()
    second.start()
    second.wait()
    wide[...] = steps[...].astype(F32)
    used = max(1, mine // QB)
    begin = lax.div(pos[0] * mine, jnp.int32(QB))
    if used % 8 == 0:
        begin = pl.multiple_of(begin, 8)
    factors = wide[pl.ds(begin, used), :]
    first.wait()
    blocks = raw[...].astype(F32).reshape(used, mine // used, ff)
    kept = (blocks * factors[:, None, :]).astype(BF16).reshape(mine, ff)
    width = ff // len(outs)
    for i, out in enumerate(outs):
        out[...] = kept[:, i * width : (i + 1) * width]


def route_body(dims, cap, blocks, pos, ids, rows_x, rows_dy, *outs):
    copies, _, locals_ = dims
    count = rows_x.shape[0]
    high = max(16, locals_)
    if locals_ & (locals_ - 1) == 0:
        relative = lax.bitwise_xor(ids[...], pos[2])
    else:
        relative = lax.rem(ids[...] - pos[2] + locals_, locals_)
    onehot = relative == lax.broadcasted_iota(jnp.int32, (high, count), 0)
    first = lax.broadcasted_iota(jnp.int32, (count, count), 0)
    second = lax.broadcasted_iota(jnp.int32, (count, count), 1)
    earlier = (first < second).astype(F32).astype(BF16)
    ranks = jnp.dot(onehot.astype(F32).astype(BF16), earlier, preferred_element_type=F32)
    rank = jnp.sum(jnp.where(onehot, ranks, 0.0), axis=0, keepdims=True).astype(jnp.int32)
    slot = relative * cap + rank
    places = lax.broadcasted_iota(jnp.int32, (locals_ * cap, count), 0)
    pick = (slot == places).astype(F32).astype(BF16)
    width = rows_x.shape[1] // (copies * blocks)
    for half, rows in enumerate((rows_x, rows_dy)):
        for j in range(copies):
            which = traced_mate(pos[0], j, copies)
            for b in range(blocks):
                at = pl.multiple_of((b * copies + which) * width, 128)
                got = jnp.dot(pick, rows[:, pl.ds(at, width)], preferred_element_type=F32)
                got = got.astype(BF16)
                for k in range(locals_):
                    out = outs[(half * copies + j) * locals_ + k]
                    out[:, b * width : (b + 1) * width] = got[k * cap : (k + 1) * cap]


def join_body(dims, pos, *refs):
    copies, _, locals_ = dims
    pieces, out = refs[:-1], refs[-1]
    cap = pieces[0].shape[0]
    for j in range(copies):
        base = traced_origin(pos[0], j, copies) * (locals_ * cap)
        for k in range(locals_):
            at = pl.multiple_of(base + k * cap, 16)
            out[pl.ds(at, cap), :] = pieces[j * locals_ + k][...]


def turn_body(dims, pos, *refs):
    pieces, out, held = refs[:-2], refs[-2], refs[-1]
    join_body(dims, pos, *pieces, held)
    out[...] = jnp.transpose(held[...])


def up_body(dims, pos, rows, *refs):
    _, nodes, _ = dims
    weights, (kept, sent), held = refs[:nodes], refs[nodes : nodes + 2], refs[-1]
    mine = weights[0].shape[0]
    for s in range(nodes):
        at = pl.multiple_of(lax.rem(pos[1] + (nodes - s), nodes) * mine, 16)
        held[pl.ds(at, mine), :] = weights[s][...]
    pre = jnp.dot(rows[...], held[...], preferred_element_type=F32)
    kept[...] = pre
    sent[...] = pre.astype(BF16)


def down_body(dims, factor, pos, turned, kept, *refs):
    _, nodes, _ = dims
    got, outs, act = refs[: -nodes - 1], refs[-nodes - 1 : -1], refs[-1]
    pre = kept[...]
    for part in got:
        pre = pre + part[...].astype(F32)
    act[...] = (pre * jax.nn.sigmoid(pre)).astype(BF16)
    mine = outs[0].shape[0]
    for s in reversed(range(nodes)):
        at = pl.multiple_of(lax.rem(pos[1] + s, nodes) * mine, 16)
        term = jnp.dot(turned[pl.ds(at, mine), :], act[...], preferred_element_type=F32)
        outs[s][...] = (term * factor).astype(outs[s].dtype)


def sum_body(pos, own, *refs):
    total = own[...]
    for part in refs[:-1]:
        total = total + part[...].astype(F32)
    refs[-1][...] = total.astype(BF16)


def lay_body(dims, chunks, pos, *refs):
    copies = dims[0]
    parts, out = refs[:-1], refs[-1]
    mine, width = parts[0].shape
    for j in range(copies):
        at = pl.multiple_of(traced_origin(pos[0], j, copies) * mine, 16)
        for i in range(chunks):
            out[pl.ds(at, mine), i * width : (i + 1) * width] = parts[i * copies + j][...]


def on_device(tokens, cotangent, expert_of, w1_codes, w1_scales):
    copies, nodes, locals_ = (lax.axis_size(a) for a in ("dp", "node", "local"))
    dims = (copies, nodes, locals_)
    count, features = tokens.shape
    capacity = 5 * count // (4 * locals_)
    cap = -(-capacity // 16) * 16
    shard, hidden = w1_codes.shape[1:]
    mine = shard // copies
    part = features // copies
    width = hidden // CHUNKS
    everyone = copies * locals_ * cap
    pos = jnp.stack([lax.axis_index(a) for a in ("dp", "node", "local")]).astype(jnp.int32)

    weights = call(
        dequant_body,
        [shape(mine, width, BF16)] * CHUNKS,
        pos,
        [w1_codes[0], w1_scales[0]],
        [
            pltpu.VMEM((mine, hidden), BF16),
            pltpu.VMEM((shard // QB, hidden), BF16),
            pltpu.VMEM((shard // QB, hidden), F32),
            pltpu.SemaphoreType.DMA((2,)),
        ],
        space=pltpu.HBM,
    )
    order = [s for s in (2, 1, 3) if s < nodes] + list(range(4, nodes))
    held = []
    for chunk in weights:
        got = {0: chunk}
        for s in order:
            got[s] = lax.ppermute(chunk, "node", [(a, (a + s) % nodes) for a in range(nodes)])
        held.append([got[s] for s in range(nodes)])

    blocks = nodes
    if mine % 128:
        blocks = 1
        tokens, cotangent = (
            a.reshape(count, nodes, copies, mine).swapaxes(1, 2).reshape(count, features)
            for a in (tokens, cotangent)
        )

    pieces = call(
        functools.partial(route_body, dims, cap, blocks),
        [shape(cap, part, BF16)] * (2 * copies * locals_),
        pos,
        [expert_of.reshape(1, count), tokens, cotangent],
        flops=4 * locals_ * cap * count * features,
    )

    def exchange(pieces):
        moved = list(pieces)
        for k in reversed(range(locals_)):
            for j in reversed(range(copies)):
                if j or k:
                    pairs = [
                        (a * locals_ + b, mate(a, j, copies) * locals_ + mate(b, k, locals_))
                        for a in range(copies)
                        for b in range(locals_)
                    ]
                    at = j * locals_ + k
                    moved[at] = lax.ppermute(pieces[at], ("dp", "local"), pairs)
        return moved

    got_x = exchange(pieces[: copies * locals_])
    got_dy = exchange(pieces[copies * locals_ :])
    late = fence(pos)
    (rows_x,) = call(functools.partial(join_body, dims), [shape(everyone, part, BF16)], late, got_x)
    (turned,) = call(
        functools.partial(turn_body, dims),
        [shape(part, everyone, BF16)],
        pos,
        got_dy,
        [pltpu.VMEM((everyone, part), BF16)],
    )
    factor = float(count * copies * nodes) ** (-0.5)
    finished = []
    for i in range(CHUNKS):
        kept, sent = call(
            functools.partial(up_body, dims),
            [shape(everyone, width, F32), shape(everyone, width, BF16)],
            pos,
            [rows_x] + held[i],
            [pltpu.VMEM((part, width), BF16)],
            flops=2 * everyone * part * width,
        )
        if copies == 2:
            others = [lax.ppermute(sent, "dp", [(0, 1), (1, 0)])]
        else:
            kept, others = lax.psum(kept, "dp"), []
        terms = call(
            functools.partial(down_body, dims, factor),
            [shape(mine, width, F32)] + [shape(mine, width, BF16)] * (nodes - 1),
            pos,
            [turned, kept] + others,
            [pltpu.VMEM((everyone, width), BF16)],
            flops=2 * everyone * part * width,
        )
        arrived = []
        for s in order:
            pairs = [(a, (a + s) % nodes) for a in range(nodes)]
            arrived.append(lax.ppermute(terms[s], "node", pairs))
        (summed,) = call(sum_body, [shape(mine, width, BF16)], pos, [terms[0]] + arrived)
        finished.append(summed)
        for j in range(1, copies):
            pairs = [(a, mate(a, j, copies)) for a in range(copies)]
            finished.append(lax.ppermute(summed, "dp", pairs))
    (result,) = call(
        functools.partial(lay_body, dims, CHUNKS), [shape(shard, hidden, BF16)], pos, finished
    )
    return result[None]


def solution(mesh):
    rows = P(("dp", "node", "local"), None)
    weights = P("local", "node", None)
    return jax.shard_map(
        on_device,
        mesh=mesh,
        in_specs=(rows, rows, rows, weights, weights),
        out_specs=weights,
        check_vma=False,
    )
```

profile of v0, /device:TPU:0, one launch (start us, length us, event | category | flops | bytes accessed | tf_op | source)
XLA Modules:
  0.0 97.5 jit_solution(4164310145640511665)
XLA Ops:
  0.1 0.7 copy-done.6
  0.8 1.1 %copy-done = bf16[192,2048]{1,0:T(8,128)(2,1)S(1)} copy-done((bf16[192,2048]{1,0:T(8,128)(2,1)S(1)}, bf16[192,2048]{1,0:T(8,128)(2,1)}, u32[]{:S(2)}) %copy-start) | copy-done | bytes 786456
  1.9 1.1 %copy-done.1 = bf16[192,2048]{1,0:T(8,128)(2,1)S(1)} copy-done((bf16[192,2048]{1,0:T(8,128)(2,1)S(1)}, bf16[192,2048]{1,0:T(8,128)(2,1)}, u32[]{:S(2)}) %copy-start.1) | copy-done | bytes 786456
  3.0 1.4 %shard_map.55 = (bf16[64,1024]{1,0:T(8,128)(2,1)S(1)}, bf16[64,1024]{1,0:T(8,128)(2,1)S(1)}, bf16[64,1024]{1,0:T(8,128)(2,1)S(1)}, bf16[64,1024]{1,0:T(8,128)(2,...) custom-call(s32[3]{0:T(128)S(1)} %pad_add_fusion.pos, ...), custom_call_target="tpu_custom_call" | custom-call | flops 402653184 | bytes 3670784 | tf_op jit(solution)/shard_map/pallas_call | solution.py:33
  5.0 2.6 %collective-permute-start.8 = (bf16[64,1024]{1,0:T(8,128)(2,1)S(1)}, bf16[64,1024]{1,0:T(8,128)(2,1)S(1)}, u32[]{:S(2)}, u32[]{:S(2)}) collective-permute-start(bf16[64,1024]{1,0:T(8,128)(2,1)S(1)} %get-tuple-element.45), channel_id=1, source_target_pairs={{0,2},{1,3},{2,0},{3,1},{16,18},{17,19},{18,16},{19,17},{4,6},{5,7... | collective-permute-start | bytes 393224 | tf_op jit(solution)/shard_map/ppermute | solution.py:234
  7.6 1.7 %collective-permute-start.10 = (bf16[64,1024]{1,0:T(8,128)(2,1)S(1)}, bf16[64,1024]{1,0:T(8,128)(2,1)S(1)}, u32[]{:S(2)}, u32[]{:S(2)}) collective-permute-start(bf16[64,1024]{1,0:T(8,128)(2,1)S(1)} %get-tuple-element.47), channel_id=1, source_target_pairs={{0,16},{1,17},{2,18},{3,19},{16,0},{17,1},{18,2},{19,3},{4,20},{5,... | collective-permute-start | bytes 393224 | tf_op jit(solution)/shard_map/ppermute | solution.py:234
  9.3 2.7 %collective-permute-start.12 = (bf16[64,1024]{1,0:T(8,128)(2,1)S(1)}, bf16[64,1024]{1,0:T(8,128)(2,1)S(1)}, u32[]{:S(2)}, u32[]{:S(2)}) collective-permute-start(bf16[64,1024]{1,0:T(8,128)(2,1)S(1)} %get-tuple-element.49), channel_id=1, source_target_pairs={{0,18},{1,19},{2,16},{3,17},{16,2},{17,3},{18,0},{19,1},{4,22},{5,... | collective-permute-start | bytes 393224 | tf_op jit(solution)/shard_map/ppermute | solution.py:234
  12.0 1.5 %collective-permute-start.13 = (bf16[64,1024]{1,0:T(8,128)(2,1)S(1)}, bf16[64,1024]{1,0:T(8,128)(2,1)S(1)}, u32[]{:S(2)}, u32[]{:S(2)}) collective-permute-start(bf16[64,1024]{1,0:T(8,128)(2,1)S(1)} %get-tuple-element.50), channel_id=1, source_target_pairs={{0,19},{1,18},{2,17},{3,16},{16,3},{17,2},{18,1},{19,0},{4,23},{5,... | collective-permute-start | bytes 393224 | tf_op jit(solution)/shard_map/ppermute | solution.py:234
  13.5 0.7 shard_map.59
  14.2 1.6 %collective-permute-start.14 = (bf16[256,256]{1,0:T(8,128)(2,1)S(1)}, bf16[256,256]{1,0:T(8,128)(2,1)S(1)}, u32[]{:S(2)}, u32[]{:S(2)}) collective-permute-start(bf16[256,256]{1,0:T(8,128)(2,1)S(1)} %get-tuple-element.51.refs_0_), channel_id=1, source_target_pairs={{0,4},{4,8},{8,12},{12,0},{1,5},{5,9},{9,13},{13,1},{2,6},{6,10},{... | collective-permute-start | bytes 393224 | tf_op jit(solution)/shard_map/ppermute | solution.py:204
  15.8 2.6 %collective-permute-start.15 = (bf16[256,256]{1,0:T(8,128)(2,1)S(1)}, bf16[256,256]{1,0:T(8,128)(2,1)S(1)}, u32[]{:S(2)}, u32[]{:S(2)}) collective-permute-start(bf16[256,256]{1,0:T(8,128)(2,1)S(1)} %get-tuple-element.51.refs_0_), channel_id=1, source_target_pairs={{0,8},{4,12},{8,0},{12,4},{1,9},{5,13},{9,1},{13,5},{2,10},{6,14},... | collective-permute-start | bytes 393224 | tf_op jit(solution)/shard_map/ppermute | solution.py:204
  18.4 1.3 %collective-permute-start.16 = (bf16[256,256]{1,0:T(8,128)(2,1)S(1)}, bf16[256,256]{1,0:T(8,128)(2,1)S(1)}, u32[]{:S(2)}, u32[]{:S(2)}) collective-permute-start(bf16[256,256]{1,0:T(8,128)(2,1)S(1)} %get-tuple-element.51.refs_0_), channel_id=1, source_target_pairs={{0,12},{4,0},{8,4},{12,8},{1,13},{5,1},{9,5},{13,9},{2,14},{6,2},{... | collective-permute-start | bytes 393224 | tf_op jit(solution)/shard_map/ppermute | solution.py:204
  19.8 1.0 %collective-permute-done.12.refs_6_ = bf16[64,1024]{1,0:T(8,128)(2,1)S(1)} collective-permute-done((bf16[64,1024]{1,0:T(8,128)(2,1)S(1)}, bf16[64,1024]{1,0:T(8,128)(2,1)S(1)}, u32[]{:S(2)}, u32[]{:S(2)}) %collective-permute-start.12) | collective-permute-done | bytes 131104 | tf_op jit(solution)/shard_map/ppermute | solution.py:234
  20.8 1.6 %collective-permute-start.22 = (bf16[256,256]{1,0:T(8,128)(2,1)S(1)}, bf16[256,256]{1,0:T(8,128)(2,1)S(1)}, u32[]{:S(2)}, u32[]{:S(2)}) collective-permute-start(bf16[256,256]{1,0:T(8,128)(2,1)S(1)} %get-tuple-element.58.refs_0_), channel_id=1, source_target_pairs={{0,4},{4,8},{8,12},{12,0},{1,5},{5,9},{9,13},{13,1},{2,6},{6,10},{... | collective-permute-start | bytes 393224 | tf_op jit(solution)/shard_map/ppermute | solution.py:204
  22.4 2.6 %collective-permute-start.23 = (bf16[256,256]{1,0:T(8,128)(2,1)S(1)}, bf16[256,256]{1,0:T(8,128)(2,1)S(1)}, u32[]{:S(2)}, u32[]{:S(2)}) collective-permute-start(bf16[256,256]{1,0:T(8,128)(2,1)S(1)} %get-tuple-element.58.refs_0_), channel_id=1, source_target_pairs={{0,8},{4,12},{8,0},{12,4},{1,9},{5,13},{9,1},{13,5},{2,10},{6,14},... | collective-permute-start | bytes 393224 | tf_op jit(solution)/shard_map/ppermute | solution.py:204
  25.0 1.3 %collective-permute-start.24 = (bf16[256,256]{1,0:T(8,128)(2,1)S(1)}, bf16[256,256]{1,0:T(8,128)(2,1)S(1)}, u32[]{:S(2)}, u32[]{:S(2)}) collective-permute-start(bf16[256,256]{1,0:T(8,128)(2,1)S(1)} %get-tuple-element.58.refs_0_), channel_id=1, source_target_pairs={{0,12},{4,0},{8,4},{12,8},{1,13},{5,1},{9,5},{13,9},{2,14},{6,2},{... | collective-permute-start | bytes 393224 | tf_op jit(solution)/shard_map/ppermute | solution.py:204
  26.3 1.2 %shard_map.57.pos = s32[3]{0:T(128)} custom-call(s32[3]{0:T(128)} %copy-done.3), custom_call_target="tpu_custom_call" | custom-call | tf_op jit(solution)/shard_map/pallas_call | solution.py:53
  27.5 0.6 copy-done.7
  28.1 0.6 shard_map.58.rows
  29.6 0.9 collective-permute-done.22.refs_1_
  30.4 1.1 %collective-permute-start.2 = (bf16[64,1024]{1,0:T(8,128)(2,1)S(1)}, bf16[64,1024]{1,0:T(8,128)(2,1)S(1)}, u32[]{:S(2)}, u32[]{:S(2)}) collective-permute-start(bf16[64,1024]{1,0:T(8,128)(2,1)S(1)} %get-tuple-element.38), channel_id=1, source_target_pairs={{0,3},{1,2},{2,1},{3,0},{16,19},{17,18},{18,17},{19,16},{4,7},{5,6... | collective-permute-start | bytes 393224 | tf_op jit(solution)/shard_map/ppermute | solution.py:234
  31.6 7.7 %collective-permute-done.23.refs_2_ = bf16[256,256]{1,0:T(8,128)(2,1)S(1)} collective-permute-done((bf16[256,256]{1,0:T(8,128)(2,1)S(1)}, bf16[256,256]{1,0:T(8,128)(2,1)S(1)}, u32[]{:S(2)}, u32[]{:S(2)}) %collective-permute-start.23) | collective-permute-done | bytes 131104 | tf_op jit(solution)/shard_map/ppermute | solution.py:204
  39.3 1.2 %collective-permute-start.3 = (bf16[64,1024]{1,0:T(8,128)(2,1)S(1)}, bf16[64,1024]{1,0:T(8,128)(2,1)S(1)}, u32[]{:S(2)}, u32[]{:S(2)}) collective-permute-start(bf16[64,1024]{1,0:T(8,128)(2,1)S(1)} %get-tuple-element.39), channel_id=1, source_target_pairs={{0,16},{1,17},{2,18},{3,19},{16,0},{17,1},{18,2},{19,3},{4,20},{5,... | collective-permute-start | bytes 393224 | tf_op jit(solution)/shard_map/ppermute | solution.py:234
  40.5 1.0 %shard_map.60 = (f32[512,256]{1,0:T(8,128)S(1)}, bf16[512,256]{1,0:T(8,128)(2,1)S(1)}) custom-call(s32[3]{0:T(128)S(1)} %copy-done.4, bf16[512,1024]{1,0:T(8,128)(2,1)S(1)} %shard_map.58.rows, bf16[256,256]{1,0:T(8,128)(2,1)S(1)} %get-tuple-element.51.refs_0_, bf16[256,256]{1,0:T(8,128)(2,1)S(1)} %collective-permute-done.14.refs_1_, ...), custom_call_target="tpu_custom_call" | custom-call | flops 268435456 | bytes 2359296 | tf_op jit(solution)/shard_map/pallas_call | solution.py:33
  41.5 0.9 collective-permute-start.17
  42.4 1.0 %shard_map.63 = (f32[512,256]{1,0:T(8,128)S(1)}, bf16[512,256]{1,0:T(8,128)(2,1)S(1)}) custom-call(s32[3]{0:T(128)S(1)} %copy-done.4, bf16[512,1024]{1,0:T(8,128)(2,1)S(1)} %shard_map.58.rows, bf16[256,256]{1,0:T(8,128)(2,1)S(1)} %get-tuple-element.58.refs_0_, bf16[256,256]{1,0:T(8,128)(2,1)S(1)} %collective-permute-done.22.refs_1_, ...), custom_call_target="tpu_custom_call" | custom-call | flops 268435456 | bytes 2359296 | tf_op jit(solution)/shard_map/pallas_call | solution.py:33
  43.8 2.0 %collective-permute-start.5 = (bf16[64,1024]{1,0:T(8,128)(2,1)S(1)}, bf16[64,1024]{1,0:T(8,128)(2,1)S(1)}, u32[]{:S(2)}, u32[]{:S(2)}) collective-permute-start(bf16[64,1024]{1,0:T(8,128)(2,1)S(1)} %get-tuple-element.41), channel_id=1, source_target_pairs={{0,18},{1,19},{2,16},{3,17},{16,2},{17,3},{18,0},{19,1},{4,22},{5,... | collective-permute-start | bytes 393224 | tf_op jit(solution)/shard_map/ppermute | solution.py:234
  45.7 1.0 %collective-permute-start.25 = (bf16[512,256]{1,0:T(8,128)(2,1)S(1)}, bf16[512,256]{1,0:T(8,128)(2,1)S(1)}, u32[]{:S(2)}, u32[]{:S(2)}) collective-permute-start(bf16[512,256]{1,0:T(8,128)(2,1)S(1)} %get-tuple-element.60), channel_id=1, source_target_pairs={{0,16},{16,0},{1,17},{17,1},{2,18},{18,2},{3,19},{19,3},{4,20},{20... | collective-permute-start | bytes 786440 | tf_op jit(solution)/shard_map/ppermute | solution.py:260
  46.7 0.9 collective-permute-start.6
  47.6 5.2 %collective-permute-done.4.refs_5_ = bf16[64,1024]{1,0:T(8,128)(2,1)S(1)} collective-permute-done((bf16[64,1024]{1,0:T(8,128)(2,1)S(1)}, bf16[64,1024]{1,0:T(8,128)(2,1)S(1)}, u32[]{:S(2)}, u32[]{:S(2)}) %collective-permute-start.4) | collective-permute-done | bytes 131104 | tf_op jit(solution)/shard_map/ppermute | solution.py:234
  52.8 4.5 %collective-permute-done.5.refs_6_ = bf16[64,1024]{1,0:T(8,128)(2,1)S(1)} collective-permute-done((bf16[64,1024]{1,0:T(8,128)(2,1)S(1)}, bf16[64,1024]{1,0:T(8,128)(2,1)S(1)}, u32[]{:S(2)}, u32[]{:S(2)}) %collective-permute-start.5) | collective-permute-done | bytes 131104 | tf_op jit(solution)/shard_map/ppermute | solution.py:234
  57.3 6.9 %collective-permute-done.6.refs_7_ = bf16[64,1024]{1,0:T(8,128)(2,1)S(1)} collective-permute-done((bf16[64,1024]{1,0:T(8,128)(2,1)S(1)}, bf16[64,1024]{1,0:T(8,128)(2,1)S(1)}, u32[]{:S(2)}, u32[]{:S(2)}) %collective-permute-start.6) | collective-permute-done | bytes 131104 | tf_op jit(solution)/shard_map/ppermute | solution.py:234
  64.3 0.9 shard_map.56.turned
  65.2 1.0 %shard_map.61 = (f32[256,256]{1,0:T(8,128)S(1)}, bf16[256,256]{1,0:T(8,128)(2,1)S(1)}, bf16[256,256]{1,0:T(8,128)(2,1)S(1)}, bf16[256,256]{1,0:T(8,128)(2,1)S(1)}) custom-call(s32[3]{0:T(128)S(1)} %copy-done.4, bf16[1024,512]{1,0:T(8,128)(2,1)S(1)} %shard_map.56.turned, f32[512,256]{1,0:T(8,128)S(1)} %get-tuple-element.52.kept, ...), custom_call_target="tpu_custom_call" | custom-call | flops 268435456 | bytes 2490368 | tf_op jit(solution)/shard_map/pallas_call | solution.py:33
  66.2 1.8 %collective-permute-start.18 = (bf16[256,256]{1,0:T(8,128)(2,1)S(1)}, bf16[256,256]{1,0:T(8,128)(2,1)S(1)}, u32[]{:S(2)}, u32[]{:S(2)}) collective-permute-start(bf16[256,256]{1,0:T(8,128)(2,1)S(1)} %get-tuple-element.55), channel_id=1, source_target_pairs={{0,8},{4,12},{8,0},{12,4},{1,9},{5,13},{9,1},{13,5},{2,10},{6,14},... | collective-permute-start | bytes 393224 | tf_op jit(solution)/shard_map/ppermute | solution.py:274
  68.0 2.8 %collective-permute-start.19 = (bf16[256,256]{1,0:T(8,128)(2,1)S(1)}, bf16[256,256]{1,0:T(8,128)(2,1)S(1)}, u32[]{:S(2)}, u32[]{:S(2)}) collective-permute-start(bf16[256,256]{1,0:T(8,128)(2,1)S(1)} %get-tuple-element.56), channel_id=1, source_target_pairs={{0,4},{4,8},{8,12},{12,0},{1,5},{5,9},{9,13},{13,1},{2,6},{6,10},{... | collective-permute-start | bytes 393224 | tf_op jit(solution)/shard_map/ppermute | solution.py:274
  70.9 1.0 %collective-permute-start.20 = (bf16[256,256]{1,0:T(8,128)(2,1)S(1)}, bf16[256,256]{1,0:T(8,128)(2,1)S(1)}, u32[]{:S(2)}, u32[]{:S(2)}) collective-permute-start(bf16[256,256]{1,0:T(8,128)(2,1)S(1)} %get-tuple-element.57), channel_id=1, source_target_pairs={{0,12},{4,0},{8,4},{12,8},{1,13},{5,1},{9,5},{13,9},{2,14},{6,2},{... | collective-permute-start | bytes 393224 | tf_op jit(solution)/shard_map/ppermute | solution.py:274
  71.9 1.0 %shard_map.64 = (f32[256,256]{1,0:T(8,128)S(1)}, bf16[256,256]{1,0:T(8,128)(2,1)S(1)}, bf16[256,256]{1,0:T(8,128)(2,1)S(1)}, bf16[256,256]{1,0:T(8,128)(2,1)S(1)}) custom-call(s32[3]{0:T(128)S(1)} %copy-done.4, bf16[1024,512]{1,0:T(8,128)(2,1)S(1)} %shard_map.56.turned, f32[512,256]{1,0:T(8,128)S(1)} %get-tuple-element.59.kept, ...), custom_call_target="tpu_custom_call" | custom-call | flops 268435456 | bytes 2490368 | tf_op jit(solution)/shard_map/pallas_call | solution.py:33
  73.4 0.6 collective-permute-start.27
  74.0 5.2 %collective-permute-done.18.refs_0_ = bf16[256,256]{1,0:T(8,128)(2,1)S(1)} collective-permute-done((bf16[256,256]{1,0:T(8,128)(2,1)S(1)}, bf16[256,256]{1,0:T(8,128)(2,1)S(1)}, u32[]{:S(2)}, u32[]{:S(2)}) %collective-permute-start.18) | collective-permute-done | bytes 131104 | tf_op jit(solution)/shard_map/ppermute | solution.py:274
  79.2 1.3 %collective-permute-done.20.refs_2_ = bf16[256,256]{1,0:T(8,128)(2,1)S(1)} collective-permute-done((bf16[256,256]{1,0:T(8,128)(2,1)S(1)}, bf16[256,256]{1,0:T(8,128)(2,1)S(1)}, u32[]{:S(2)}, u32[]{:S(2)}) %collective-permute-start.20) | collective-permute-done | bytes 131104 | tf_op jit(solution)/shard_map/ppermute | solution.py:274
  80.5 0.6 shard_map.62.refs_0_
  81.1 1.8 %collective-permute-start.21 = (bf16[256,256]{1,0:T(8,128)(2,1)S(1)}, bf16[256,256]{1,0:T(8,128)(2,1)S(1)}, u32[]{:S(2)}, u32[]{:S(2)}) collective-permute-start(bf16[256,256]{1,0:T(8,128)(2,1)S(1)} %shard_map.62.refs_0_), channel_id=1, source_target_pairs={{0,16},{16,0},{1,17},{17,1},{2,18},{18,2},{3,19},{19,3},{4,20},{20... | collective-permute-start | bytes 393224 | tf_op jit(solution)/shard_map/ppermute | solution.py:279
  82.9 7.6 %collective-permute-done.26.refs_0_ = bf16[256,256]{1,0:T(8,128)(2,1)S(1)} collective-permute-done((bf16[256,256]{1,0:T(8,128)(2,1)S(1)}, bf16[256,256]{1,0:T(8,128)(2,1)S(1)}, u32[]{:S(2)}, u32[]{:S(2)}) %collective-permute-start.26) | collective-permute-done | bytes 131104 | tf_op jit(solution)/shard_map/ppermute | solution.py:274
  90.5 0.6 shard_map.65.refs_2_
  91.1 1.3 %collective-permute-start.29 = (bf16[256,256]{1,0:T(8,128)(2,1)S(1)}, bf16[256,256]{1,0:T(8,128)(2,1)S(1)}, u32[]{:S(2)}, u32[]{:S(2)}) collective-permute-start(bf16[256,256]{1,0:T(8,128)(2,1)S(1)} %shard_map.65.refs_2_), channel_id=1, source_target_pairs={{0,16},{16,0},{1,17},{17,1},{2,18},{18,2},{3,19},{19,3},{4,20},{20... | collective-permute-start | bytes 393224 | tf_op jit(solution)/shard_map/ppermute | solution.py:279
  92.4 3.7 %collective-permute-done.29.refs_3_ = bf16[256,256]{1,0:T(8,128)(2,1)S(1)} collective-permute-done((bf16[256,256]{1,0:T(8,128)(2,1)S(1)}, bf16[256,256]{1,0:T(8,128)(2,1)S(1)}, u32[]{:S(2)}, u32[]{:S(2)}) %collective-permute-start.29) | collective-permute-done | bytes 131104 | tf_op jit(solution)/shard_map/ppermute | solution.py:279
  96.1 1.4 %shard_map.66 = bf16[512,512]{1,0:T(8,128)(2,1)} custom-call(s32[3]{0:T(128)S(1)} %copy-done.4, bf16[256,256]{1,0:T(8,128)(2,1)S(1)} %shard_map.62.refs_0_, bf16[256,256]{1,0:T(8,128)(2,1)S(1)} %collective-permute-done.21.refs_1_, bf16[256,256]{1,0:T(8,128)(2,1)S(1)} %shard_map.65.refs_2_, bf16[256,256]{1,0:T(8,128)(2,1)S(1)} %collective-permute-done.29.refs_3_), custom_call_target="tpu_custom_call" | custom-call | bytes 1048576 | tf_op jit(solution)/shard_map/pallas_call | solution.py:33
  (41 shorter events, 2.4 us)
Async XLA Ops:
  0.1 13.4 %copy-start.3 = (s32[3]{0:T(128)}, s32[3]{0:T(128)S(1)}, u32[]{:S(2)}) copy-start(s32[3]{0:T(128)S(1)} %pad_add_fusion.pos) | copy-start | bytes 40
  0.1 0.7 copy-start.6
  0.8 1.1 %copy-start = (bf16[192,2048]{1,0:T(8,128)(2,1)S(1)}, bf16[192,2048]{1,0:T(8,128)(2,1)}, u32[]{:S(2)}) copy-start(bf16[192,2048]{1,0:T(8,128)(2,1)} %rows_x.1) | copy-start | bytes 2359300
  1.9 1.1 %copy-start.1 = (bf16[192,2048]{1,0:T(8,128)(2,1)S(1)}, bf16[192,2048]{1,0:T(8,128)(2,1)}, u32[]{:S(2)}) copy-start(bf16[192,2048]{1,0:T(8,128)(2,1)} %rows_dy.1) | copy-start | bytes 2359300
  3.0 10.5 %copy-start.2 = (bf16[1,512,512]{2,1,0:T(8,128)(2,1)S(1)}, bf16[1,512,512]{2,1,0:T(8,128)(2,1)}, u32[]{:S(2)}) copy-start(bf16[1,512,512]{2,1,0:T(8,128)(2,1)} %param.8) | copy-start | bytes 1572868
  4.4 9.1 %copy-start.5 = (bf16[1,16,512]{2,1,0:T(8,128)(2,1)S(1)}, bf16[1,16,512]{2,1,0:T(8,128)(2,1)}, u32[]{:S(2)}) copy-start(bf16[1,16,512]{2,1,0:T(8,128)(2,1)} %param.9) | copy-start | bytes 49156
  4.4 4.9 %collective-permute-start.7 = (bf16[64,1024]{1,0:T(8,128)(2,1)S(1)}, bf16[64,1024]{1,0:T(8,128)(2,1)S(1)}, u32[]{:S(2)}, u32[]{:S(2)}) collective-permute-start(bf16[64,1024]{1,0:T(8,128)(2,1)S(1)} %get-tuple-element.44), channel_id=1, source_target_pairs={{0,1},{1,0},{2,3},{3,2},{16,17},{17,16},{18,19},{19,18},{4,5},{5,4... | collective-permute-start | bytes 393224 | tf_op jit(solution)/shard_map/ppermute | solution.py:234
  5.0 7.0 %collective-permute-start.8 = (bf16[64,1024]{1,0:T(8,128)(2,1)S(1)}, bf16[64,1024]{1,0:T(8,128)(2,1)S(1)}, u32[]{:S(2)}, u32[]{:S(2)}) collective-permute-start(bf16[64,1024]{1,0:T(8,128)(2,1)S(1)} %get-tuple-element.45), channel_id=1, source_target_pairs={{0,2},{1,3},{2,0},{3,1},{16,18},{17,19},{18,16},{19,17},{4,6},{5,7... | collective-permute-start | bytes 393224 | tf_op jit(solution)/shard_map/ppermute | solution.py:234
  7.6 6.6 %collective-permute-start.9 = (bf16[64,1024]{1,0:T(8,128)(2,1)S(1)}, bf16[64,1024]{1,0:T(8,128)(2,1)S(1)}, u32[]{:S(2)}, u32[]{:S(2)}) collective-permute-start(bf16[64,1024]{1,0:T(8,128)(2,1)S(1)} %get-tuple-element.46), channel_id=1, source_target_pairs={{0,3},{1,2},{2,1},{3,0},{16,19},{17,18},{18,17},{19,16},{4,7},{5,6... | collective-permute-start | bytes 393224 | tf_op jit(solution)/shard_map/ppermute | solution.py:234
  7.6 8.2 %collective-permute-start.10 = (bf16[64,1024]{1,0:T(8,128)(2,1)S(1)}, bf16[64,1024]{1,0:T(8,128)(2,1)S(1)}, u32[]{:S(2)}, u32[]{:S(2)}) collective-permute-start(bf16[64,1024]{1,0:T(8,128)(2,1)S(1)} %get-tuple-element.47), channel_id=1, source_target_pairs={{0,16},{1,17},{2,18},{3,19},{16,0},{17,1},{18,2},{19,3},{4,20},{5,... | collective-permute-start | bytes 393224 | tf_op jit(solution)/shard_map/ppermute | solution.py:234
  9.3 9.1 %collective-permute-start.11 = (bf16[64,1024]{1,0:T(8,128)(2,1)S(1)}, bf16[64,1024]{1,0:T(8,128)(2,1)S(1)}, u32[]{:S(2)}, u32[]{:S(2)}) collective-permute-start(bf16[64,1024]{1,0:T(8,128)(2,1)S(1)} %get-tuple-element.48), channel_id=1, source_target_pairs={{0,17},{1,16},{2,19},{3,18},{16,1},{17,0},{18,3},{19,2},{4,21},{5,... | collective-permute-start | bytes 393224 | tf_op jit(solution)/shard_map/ppermute | solution.py:234
  9.3 11.4 %collective-permute-start.12 = (bf16[64,1024]{1,0:T(8,128)(2,1)S(1)}, bf16[64,1024]{1,0:T(8,128)(2,1)S(1)}, u32[]{:S(2)}, u32[]{:S(2)}) collective-permute-start(bf16[64,1024]{1,0:T(8,128)(2,1)S(1)} %get-tuple-element.49), channel_id=1, source_target_pairs={{0,18},{1,19},{2,16},{3,17},{16,2},{17,3},{18,0},{19,1},{4,22},{5,... | collective-permute-start | bytes 393224 | tf_op jit(solution)/shard_map/ppermute | solution.py:234
  12.0 10.4 %collective-permute-start.13 = (bf16[64,1024]{1,0:T(8,128)(2,1)S(1)}, bf16[64,1024]{1,0:T(8,128)(2,1)S(1)}, u32[]{:S(2)}, u32[]{:S(2)}) collective-permute-start(bf16[64,1024]{1,0:T(8,128)(2,1)S(1)} %get-tuple-element.50), channel_id=1, source_target_pairs={{0,19},{1,18},{2,17},{3,16},{16,3},{17,2},{18,1},{19,0},{4,23},{5,... | collective-permute-start | bytes 393224 | tf_op jit(solution)/shard_map/ppermute | solution.py:234
  14.2 10.7 %collective-permute-start.14 = (bf16[256,256]{1,0:T(8,128)(2,1)S(1)}, bf16[256,256]{1,0:T(8,128)(2,1)S(1)}, u32[]{:S(2)}, u32[]{:S(2)}) collective-permute-start(bf16[256,256]{1,0:T(8,128)(2,1)S(1)} %get-tuple-element.51.refs_0_), channel_id=1, source_target_pairs={{0,4},{4,8},{8,12},{12,0},{1,5},{5,9},{9,13},{13,1},{2,6},{6,10},{... | collective-permute-start | bytes 393224 | tf_op jit(solution)/shard_map/ppermute | solution.py:204
  15.8 12.9 %collective-permute-start.15 = (bf16[256,256]{1,0:T(8,128)(2,1)S(1)}, bf16[256,256]{1,0:T(8,128)(2,1)S(1)}, u32[]{:S(2)}, u32[]{:S(2)}) collective-permute-start(bf16[256,256]{1,0:T(8,128)(2,1)S(1)} %get-tuple-element.51.refs_0_), channel_id=1, source_target_pairs={{0,8},{4,12},{8,0},{12,4},{1,9},{5,13},{9,1},{13,5},{2,10},{6,14},... | collective-permute-start | bytes 393224 | tf_op jit(solution)/shard_map/ppermute | solution.py:204
  18.4 10.6 %collective-permute-start.16 = (bf16[256,256]{1,0:T(8,128)(2,1)S(1)}, bf16[256,256]{1,0:T(8,128)(2,1)S(1)}, u32[]{:S(2)}, u32[]{:S(2)}) collective-permute-start(bf16[256,256]{1,0:T(8,128)(2,1)S(1)} %get-tuple-element.51.refs_0_), channel_id=1, source_target_pairs={{0,12},{4,0},{8,4},{12,8},{1,13},{5,1},{9,5},{13,9},{2,14},{6,2},{... | collective-permute-start | bytes 393224 | tf_op jit(solution)/shard_map/ppermute | solution.py:204
  20.8 9.6 %collective-permute-start.22 = (bf16[256,256]{1,0:T(8,128)(2,1)S(1)}, bf16[256,256]{1,0:T(8,128)(2,1)S(1)}, u32[]{:S(2)}, u32[]{:S(2)}) collective-permute-start(bf16[256,256]{1,0:T(8,128)(2,1)S(1)} %get-tuple-element.58.refs_0_), channel_id=1, source_target_pairs={{0,4},{4,8},{8,12},{12,0},{1,5},{5,9},{9,13},{13,1},{2,6},{6,10},{... | collective-permute-start | bytes 393224 | tf_op jit(solution)/shard_map/ppermute | solution.py:204
  22.4 16.9 %collective-permute-start.23 = (bf16[256,256]{1,0:T(8,128)(2,1)S(1)}, bf16[256,256]{1,0:T(8,128)(2,1)S(1)}, u32[]{:S(2)}, u32[]{:S(2)}) collective-permute-start(bf16[256,256]{1,0:T(8,128)(2,1)S(1)} %get-tuple-element.58.refs_0_), channel_id=1, source_target_pairs={{0,8},{4,12},{8,0},{12,4},{1,9},{5,13},{9,1},{13,5},{2,10},{6,14},... | collective-permute-start | bytes 393224 | tf_op jit(solution)/shard_map/ppermute | solution.py:204
  25.0 16.5 %collective-permute-start.24 = (bf16[256,256]{1,0:T(8,128)(2,1)S(1)}, bf16[256,256]{1,0:T(8,128)(2,1)S(1)}, u32[]{:S(2)}, u32[]{:S(2)}) collective-permute-start(bf16[256,256]{1,0:T(8,128)(2,1)S(1)} %get-tuple-element.58.refs_0_), channel_id=1, source_target_pairs={{0,12},{4,0},{8,4},{12,8},{1,13},{5,1},{9,5},{13,9},{2,14},{6,2},{... | collective-permute-start | bytes 393224 | tf_op jit(solution)/shard_map/ppermute | solution.py:204
  27.5 0.6 copy-start.7
  28.8 14.6 %collective-permute-start = (bf16[64,1024]{1,0:T(8,128)(2,1)S(1)}, bf16[64,1024]{1,0:T(8,128)(2,1)S(1)}, u32[]{:S(2)}, u32[]{:S(2)}) collective-permute-start(bf16[64,1024]{1,0:T(8,128)(2,1)S(1)} %get-tuple-element.36), channel_id=1, source_target_pairs={{0,1},{1,0},{2,3},{3,2},{16,17},{17,16},{18,19},{19,18},{4,5},{5,4... | collective-permute-start | bytes 393224 | tf_op jit(solution)/shard_map/ppermute | solution.py:234
  29.0 14.8 %collective-permute-start.1 = (bf16[64,1024]{1,0:T(8,128)(2,1)S(1)}, bf16[64,1024]{1,0:T(8,128)(2,1)S(1)}, u32[]{:S(2)}, u32[]{:S(2)}) collective-permute-start(bf16[64,1024]{1,0:T(8,128)(2,1)S(1)} %get-tuple-element.37), channel_id=1, source_target_pairs={{0,2},{1,3},{2,0},{3,1},{16,18},{17,19},{18,16},{19,17},{4,6},{5,7... | collective-permute-start | bytes 393224 | tf_op jit(solution)/shard_map/ppermute | solution.py:234
  30.4 10.0 %copy-start.4 = (s32[3]{0:T(128)S(1)}, s32[3]{0:T(128)}, u32[]{:S(2)}) copy-start(s32[3]{0:T(128)} %copy-done.3) | copy-start | bytes 40
  30.4 15.3 %collective-permute-start.2 = (bf16[64,1024]{1,0:T(8,128)(2,1)S(1)}, bf16[64,1024]{1,0:T(8,128)(2,1)S(1)}, u32[]{:S(2)}, u32[]{:S(2)}) collective-permute-start(bf16[64,1024]{1,0:T(8,128)(2,1)S(1)} %get-tuple-element.38), channel_id=1, source_target_pairs={{0,3},{1,2},{2,1},{3,0},{16,19},{17,18},{18,17},{19,16},{4,7},{5,6... | collective-permute-start | bytes 393224 | tf_op jit(solution)/shard_map/ppermute | solution.py:234
  39.3 7.5 %collective-permute-start.3 = (bf16[64,1024]{1,0:T(8,128)(2,1)S(1)}, bf16[64,1024]{1,0:T(8,128)(2,1)S(1)}, u32[]{:S(2)}, u32[]{:S(2)}) collective-permute-start(bf16[64,1024]{1,0:T(8,128)(2,1)S(1)} %get-tuple-element.39), channel_id=1, source_target_pairs={{0,16},{1,17},{2,18},{3,19},{16,0},{17,1},{18,2},{19,3},{4,20},{5,... | collective-permute-start | bytes 393224 | tf_op jit(solution)/shard_map/ppermute | solution.py:234
  41.5 23.7 %collective-permute-start.17 = (bf16[512,256]{1,0:T(8,128)(2,1)S(1)}, bf16[512,256]{1,0:T(8,128)(2,1)S(1)}, u32[]{:S(2)}, u32[]{:S(2)}) collective-permute-start(bf16[512,256]{1,0:T(8,128)(2,1)S(1)} %get-tuple-element.53), channel_id=1, source_target_pairs={{0,16},{16,0},{1,17},{17,1},{2,18},{18,2},{3,19},{19,3},{4,20},{20... | collective-permute-start | bytes 786440 | tf_op jit(solution)/shard_map/ppermute | solution.py:260
  43.4 9.4 %collective-permute-start.4 = (bf16[64,1024]{1,0:T(8,128)(2,1)S(1)}, bf16[64,1024]{1,0:T(8,128)(2,1)S(1)}, u32[]{:S(2)}, u32[]{:S(2)}) collective-permute-start(bf16[64,1024]{1,0:T(8,128)(2,1)S(1)} %get-tuple-element.40), channel_id=1, source_target_pairs={{0,17},{1,16},{2,19},{3,18},{16,1},{17,0},{18,3},{19,2},{4,21},{5,... | collective-permute-start | bytes 393224 | tf_op jit(solution)/shard_map/ppermute | solution.py:234
  43.8 13.6 %collective-permute-start.5 = (bf16[64,1024]{1,0:T(8,128)(2,1)S(1)}, bf16[64,1024]{1,0:T(8,128)(2,1)S(1)}, u32[]{:S(2)}, u32[]{:S(2)}) collective-permute-start(bf16[64,1024]{1,0:T(8,128)(2,1)S(1)} %get-tuple-element.41), channel_id=1, source_target_pairs={{0,18},{1,19},{2,16},{3,17},{16,2},{17,3},{18,0},{19,1},{4,22},{5,... | collective-permute-start | bytes 393224 | tf_op jit(solution)/shard_map/ppermute | solution.py:234
  45.7 26.1 %collective-permute-start.25 = (bf16[512,256]{1,0:T(8,128)(2,1)S(1)}, bf16[512,256]{1,0:T(8,128)(2,1)S(1)}, u32[]{:S(2)}, u32[]{:S(2)}) collective-permute-start(bf16[512,256]{1,0:T(8,128)(2,1)S(1)} %get-tuple-element.60), channel_id=1, source_target_pairs={{0,16},{16,0},{1,17},{17,1},{2,18},{18,2},{3,19},{19,3},{4,20},{20... | collective-permute-start | bytes 786440 | tf_op jit(solution)/shard_map/ppermute | solution.py:260
  46.7 17.5 %collective-permute-start.6 = (bf16[64,1024]{1,0:T(8,128)(2,1)S(1)}, bf16[64,1024]{1,0:T(8,128)(2,1)S(1)}, u32[]{:S(2)}, u32[]{:S(2)}) collective-permute-start(bf16[64,1024]{1,0:T(8,128)(2,1)S(1)} %get-tuple-element.42), channel_id=1, source_target_pairs={{0,19},{1,18},{2,17},{3,16},{16,3},{17,2},{18,1},{19,0},{4,23},{5,... | collective-permute-start | bytes 393224 | tf_op jit(solution)/shard_map/ppermute | solution.py:234
  66.2 13.0 %collective-permute-start.18 = (bf16[256,256]{1,0:T(8,128)(2,1)S(1)}, bf16[256,256]{1,0:T(8,128)(2,1)S(1)}, u32[]{:S(2)}, u32[]{:S(2)}) collective-permute-start(bf16[256,256]{1,0:T(8,128)(2,1)S(1)} %get-tuple-element.55), channel_id=1, source_target_pairs={{0,8},{4,12},{8,0},{12,4},{1,9},{5,13},{9,1},{13,5},{2,10},{6,14},... | collective-permute-start | bytes 393224 | tf_op jit(solution)/shard_map/ppermute | solution.py:274
  68.0 11.2 %collective-permute-start.19 = (bf16[256,256]{1,0:T(8,128)(2,1)S(1)}, bf16[256,256]{1,0:T(8,128)(2,1)S(1)}, u32[]{:S(2)}, u32[]{:S(2)}) collective-permute-start(bf16[256,256]{1,0:T(8,128)(2,1)S(1)} %get-tuple-element.56), channel_id=1, source_target_pairs={{0,4},{4,8},{8,12},{12,0},{1,5},{5,9},{9,13},{13,1},{2,6},{6,10},{... | collective-permute-start | bytes 393224 | tf_op jit(solution)/shard_map/ppermute | solution.py:274
  70.9 9.6 %collective-permute-start.20 = (bf16[256,256]{1,0:T(8,128)(2,1)S(1)}, bf16[256,256]{1,0:T(8,128)(2,1)S(1)}, u32[]{:S(2)}, u32[]{:S(2)}) collective-permute-start(bf16[256,256]{1,0:T(8,128)(2,1)S(1)} %get-tuple-element.57), channel_id=1, source_target_pairs={{0,12},{4,0},{8,4},{12,8},{1,13},{5,1},{9,5},{13,9},{2,14},{6,2},{... | collective-permute-start | bytes 393224 | tf_op jit(solution)/shard_map/ppermute | solution.py:274
  72.9 17.6 %collective-permute-start.26 = (bf16[256,256]{1,0:T(8,128)(2,1)S(1)}, bf16[256,256]{1,0:T(8,128)(2,1)S(1)}, u32[]{:S(2)}, u32[]{:S(2)}) collective-permute-start(bf16[256,256]{1,0:T(8,128)(2,1)S(1)} %get-tuple-element.62), channel_id=1, source_target_pairs={{0,8},{4,12},{8,0},{12,4},{1,9},{5,13},{9,1},{13,5},{2,10},{6,14},... | collective-permute-start | bytes 393224 | tf_op jit(solution)/shard_map/ppermute | solution.py:274
  73.4 17.1 %collective-permute-start.27 = (bf16[256,256]{1,0:T(8,128)(2,1)S(1)}, bf16[256,256]{1,0:T(8,128)(2,1)S(1)}, u32[]{:S(2)}, u32[]{:S(2)}) collective-permute-start(bf16[256,256]{1,0:T(8,128)(2,1)S(1)} %get-tuple-element.63), channel_id=1, source_target_pairs={{0,4},{4,8},{8,12},{12,0},{1,5},{5,9},{9,13},{13,1},{2,6},{6,10},{... | collective-permute-start | bytes 393224 | tf_op jit(solution)/shard_map/ppermute | solution.py:274
  79.2 11.2 %collective-permute-start.28 = (bf16[256,256]{1,0:T(8,128)(2,1)S(1)}, bf16[256,256]{1,0:T(8,128)(2,1)S(1)}, u32[]{:S(2)}, u32[]{:S(2)}) collective-permute-start(bf16[256,256]{1,0:T(8,128)(2,1)S(1)} %get-tuple-element.64), channel_id=1, source_target_pairs={{0,12},{4,0},{8,4},{12,8},{1,13},{5,1},{9,5},{13,9},{2,14},{6,2},{... | collective-permute-start | bytes 393224 | tf_op jit(solution)/shard_map/ppermute | solution.py:274
  81.1 11.3 %collective-permute-start.21 = (bf16[256,256]{1,0:T(8,128)(2,1)S(1)}, bf16[256,256]{1,0:T(8,128)(2,1)S(1)}, u32[]{:S(2)}, u32[]{:S(2)}) collective-permute-start(bf16[256,256]{1,0:T(8,128)(2,1)S(1)} %shard_map.62.refs_0_), channel_id=1, source_target_pairs={{0,16},{16,0},{1,17},{17,1},{2,18},{18,2},{3,19},{19,3},{4,20},{20... | collective-permute-start | bytes 393224 | tf_op jit(solution)/shard_map/ppermute | solution.py:279
  91.1 5.0 %collective-permute-start.29 = (bf16[256,256]{1,0:T(8,128)(2,1)S(1)}, bf16[256,256]{1,0:T(8,128)(2,1)S(1)}, u32[]{:S(2)}, u32[]{:S(2)}) collective-permute-start(bf16[256,256]{1,0:T(8,128)(2,1)S(1)} %shard_map.65.refs_2_), channel_id=1, source_target_pairs={{0,16},{16,0},{1,17},{17,1},{2,18},{18,2},{3,19},{19,3},{4,20},{20... | collective-permute-start | bytes 393224 | tf_op jit(solution)/shard_map/ppermute | solution.py:279
where the time goes:
time: 98.4 us; the launch traced here: 97.5 us
  waiting for transfers between devices  44 us (45%)
  starting transfers between devices  38.3 us (39%)
  Pallas kernels  11.4 us (12%)
  local copies, waits for them, and re-layouts  3.59 us (4%)
    ppermute x14, waiting for transfers between devices, exchange(): moved[at] = lax.ppermute(pieces[at], ('dp', 'local'), pairs)  17.7 us
    ppermute x14, starting transfers between devices, exchange(): moved[at] = lax.ppermute(pieces[at], ('dp', 'local'), pairs)  15.4 us
    ppermute x6, waiting for transfers between devices, on_device(): arrived.append(lax.ppermute(terms[s], 'node', pairs))  14 us
    ppermute x6, starting transfers between devices, on_device(): lax.ppermute(chunk, 'node', [(a, (a + s) % nodes) for a in range(nodes)])  11.1 us
    pallas_call x11, Pallas kernels, call(): pl.pallas_call(body, out_shape=outs, in_specs=[pl.BlockSpec(memory_space=...  10.2 us
    ppermute x6, waiting for transfers between devices, on_device(): lax.ppermute(chunk, 'node', [(a, (a + s) % nodes) for a in range(nodes)])  8.55 us
    ppermute x6, starting transfers between devices, on_device(): arrived.append(lax.ppermute(terms[s], 'node', pairs))  6.8 us
    ppermute x2, waiting for transfers between devices, on_device(): finished.append(lax.ppermute(summed, 'dp', pairs))  3.69 us
  transfers between devices with their start and end apart: 30, of which 10 were waited for; matrix products, arithmetic and copies ran while one was open for 0% of the time, Pallas kernels for 9%

commit v1 on v0

--- a/solution.py
+++ b/solution.py
@@ -42,15 +42,13 @@
     )(scalars, *args)
 
 
-def fence_body(pos, out):
-    for i in range(pos.shape[0]):
-        out[i] = pos[i]
-
-
-def fence(pos):
-    spec = pl.BlockSpec(memory_space=pltpu.SMEM)
-    kind = jax.ShapeDtypeStruct(pos.shape, pos.dtype)
-    return pl.pallas_call(fence_body, out_shape=kind, in_specs=[spec], out_specs=spec)(pos)
+def partition(values):
+    return values[0], values[1], values[2:]
+
+
+def slots_of(copies, pairs):
+    slots = [(j, k) for k in reversed(range(pairs)) for j in reversed(range(copies))]
+    return [slot for slot in slots if slot != (0, 0)]
 
 
 def shape(rows, cols, dtype):
@@ -80,50 +78,80 @@
         out[...] = kept[:, i * width : (i + 1) * width]
 
 
-def route_body(dims, cap, blocks, pos, ids, rows_x, rows_dy, *outs):
-    copies, _, locals_ = dims
-    count = rows_x.shape[0]
-    high = max(16, locals_)
-    if locals_ & (locals_ - 1) == 0:
-        relative = lax.bitwise_xor(ids[...], pos[2])
-    else:
-        relative = lax.rem(ids[...] - pos[2] + locals_, locals_)
-    onehot = relative == lax.broadcasted_iota(jnp.int32, (high, count), 0)
+def select_body(dims, stride, pos, ids, ids_pair, *picks):
+    _, _, locals_ = dims
+    pairs = locals_ // 2
+    count = ids.shape[1]
+    high = max(16, pairs)
     first = lax.broadcasted_iota(jnp.int32, (count, count), 0)
     second = lax.broadcasted_iota(jnp.int32, (count, count), 1)
     earlier = (first < second).astype(F32).astype(BF16)
-    ranks = jnp.dot(onehot.astype(F32).astype(BF16), earlier, preferred_element_type=F32)
-    rank = jnp.sum(jnp.where(onehot, ranks, 0.0), axis=0, keepdims=True).astype(jnp.int32)
-    slot = relative * cap + rank
-    places = lax.broadcasted_iota(jnp.int32, (locals_ * cap, count), 0)
-    pick = (slot == places).astype(F32).astype(BF16)
-    width = rows_x.shape[1] // (copies * blocks)
-    for half, rows in enumerate((rows_x, rows_dy)):
-        for j in range(copies):
-            which = traced_mate(pos[0], j, copies)
-            for b in range(blocks):
-                at = pl.multiple_of((b * copies + which) * width, 128)
-                got = jnp.dot(pick, rows[:, pl.ds(at, width)], preferred_element_type=F32)
-                got = got.astype(BF16)
-                for k in range(locals_):
-                    out = outs[(half * copies + j) * locals_ + k]
-                    out[:, b * width : (b + 1) * width] = got[k * cap : (k + 1) * cap]
-
-
-def join_body(dims, pos, *refs):
+    places = lax.broadcasted_iota(jnp.int32, (pairs * stride, count), 0)
+    owner = lax.shift_right_logical(pos[2], 1)
+    held = jnp.zeros((high, 1), F32)
+    for chosen, pick in zip((ids[...], ids_pair[...]), picks):
+        group = lax.shift_right_logical(chosen, 1)
+        if pairs & (pairs - 1) == 0:
+            relative = lax.bitwise_xor(group, owner)
+        else:
+            relative = lax.rem(group - owner + pairs, pairs)
+        mine = lax.bitwise_and(chosen, 1) == lax.bitwise_and(pos[2], 1)
+        relative = jnp.where(mine, relative, high)
+        onehot = relative == lax.broadcasted_iota(jnp.int32, (high, count), 0)
+        marks = onehot.astype(F32)
+        ranks = held + jnp.dot(marks.astype(BF16), earlier, preferred_element_type=F32)
+        rank = jnp.sum(jnp.where(onehot, ranks, 0.0), axis=0, keepdims=True)
+        slot = jnp.where(mine, relative * stride + rank.astype(jnp.int32), -1)
+        pick[...] = (slot == places).astype(F32).astype(BF16)
+        held = held + jnp.sum(marks, axis=1, keepdims=True)
+
+
+def place_rows(dims, stride, blocks, pos, picks, sources, outs):
     copies, _, locals_ = dims
+    pairs = locals_ // 2
+    rows = outs[0].shape[0]
+    width = sources[0].shape[1] // (copies * blocks)
+    for j in reversed(range(copies)):
+        which = traced_mate(pos[0], j, copies)
+        for b in range(blocks):
+            at = pl.multiple_of((b * copies + which) * width, 128)
+            got = sum(
+                jnp.dot(pick[...], source[:, pl.ds(at, width)], preferred_element_type=F32)
+                for pick, source in zip(picks, sources)
+            ).astype(BF16)
+            for k in range(pairs):
+                out = outs[j * pairs + k]
+                out[:, b * width : (b + 1) * width] = got[k * stride : k * stride + rows]
+
+
+def first_body(dims, stride, blocks, pos, ids, ids_pair, rows, rows_pair, *outs):
+    select_body(dims, stride, pos, ids, ids_pair, *outs[:2])
+    place_rows(dims, stride, blocks, pos, outs[:2], (rows, rows_pair), outs[2:])
+
+
+def later_body(dims, stride, blocks, pos, pick, pick_pair, rows, rows_pair, *outs):
+    place_rows(dims, stride, blocks, pos, (pick, pick_pair), (rows, rows_pair), outs)
+
+
+def join_body(dims, stride, pos, *refs):
+    copies, _, locals_ = dims
+    pairs = locals_ // 2
     pieces, out = refs[:-1], refs[-1]
-    cap = pieces[0].shape[0]
+    rows, width = pieces[0].shape
     for j in range(copies):
-        base = traced_origin(pos[0], j, copies) * (locals_ * cap)
-        for k in range(locals_):
-            at = pl.multiple_of(base + k * cap, 16)
-            out[pl.ds(at, cap), :] = pieces[j * locals_ + k][...]
-
-
-def turn_body(dims, pos, *refs):
+        base = traced_origin(pos[0], j, copies) * (pairs * stride)
+        for k in range(pairs):
+            at = pl.multiple_of(base + k * stride, 16)
+            block = pieces[j * pairs + k][...]
+            if rows < stride:
+                blank = jnp.zeros((stride - rows, width), block.dtype)
+                block = jnp.concatenate([block, blank], axis=0)
+            out[pl.ds(at, stride), :] = block
+
+
+def turn_body(dims, stride, pos, *refs):
     pieces, out, held = refs[:-2], refs[-2], refs[-1]
-    join_body(dims, pos, *pieces, held)
+    join_body(dims, stride, pos, *pieces, held)
     out[...] = jnp.transpose(held[...])
 
 
@@ -175,13 +203,28 @@
     dims = (copies, nodes, locals_)
     count, features = tokens.shape
     capacity = 5 * count // (4 * locals_)
-    cap = -(-capacity // 16) * 16
+    pairs = locals_ // 2
+    sent_rows = -(-2 * capacity // 8) * 8
+    stride = -(-sent_rows // 16) * 16
     shard, hidden = w1_codes.shape[1:]
     mine = shard // copies
     part = features // copies
     width = hidden // CHUNKS
-    everyone = copies * locals_ * cap
+    everyone = copies * pairs * stride
     pos = jnp.stack([lax.axis_index(a) for a in ("dp", "node", "local")]).astype(jnp.int32)
+
+    blocks = nodes
+    if mine % 128:
+        blocks = 1
+        tokens, cotangent = (
+            a.reshape(count, nodes, copies, mine).swapaxes(1, 2).reshape(count, features)
+            for a in (tokens, cotangent)
+        )
+    chosen = expert_of.reshape(1, count)
+    swap = [(i, i ^ 1) for i in range(locals_)]
+    chosen_pair = lax.ppermute(chosen, "local", swap)
+    tokens_pair = lax.ppermute(tokens, "local", swap)
+    cotangent_pair = lax.ppermute(cotangent, "local", swap)
 
     weights = call(
         dequant_body,
@@ -204,42 +247,44 @@
             got[s] = lax.ppermute(chunk, "node", [(a, (a + s) % nodes) for a in range(nodes)])
         held.append([got[s] for s in range(nodes)])
 
-    blocks = nodes
-    if mine % 128:
-        blocks = 1
-        tokens, cotangent = (
-            a.reshape(count, nodes, copies, mine).swapaxes(1, 2).reshape(count, features)
-            for a in (tokens, cotangent)
+    flops = 4 * pairs * stride * count * features
+    sent = [shape(sent_rows, part, BF16)] * (copies * pairs)
+    *picks, pieces_x = partition(
+        call(
+            functools.partial(first_body, dims, stride, blocks),
+            [shape(pairs * stride, count, BF16)] * 2 + sent,
+            pos,
+            [chosen, chosen_pair, tokens, tokens_pair],
+            flops=flops,
         )
-
-    pieces = call(
-        functools.partial(route_body, dims, cap, blocks),
-        [shape(cap, part, BF16)] * (2 * copies * locals_),
+    )
+    pieces_y = call(
+        functools.partial(later_body, dims, stride, blocks),
+        sent,
         pos,
-        [expert_of.reshape(1, count), tokens, cotangent],
-        flops=4 * locals_ * cap * count * features,
+        [*picks, cotangent, cotangent_pair],
+        flops=flops,
     )
 
     def exchange(pieces):
         moved = list(pieces)
-        for k in reversed(range(locals_)):
-            for j in reversed(range(copies)):
-                if j or k:
-                    pairs = [
-                        (a * locals_ + b, mate(a, j, copies) * locals_ + mate(b, k, locals_))
-                        for a in range(copies)
-                        for b in range(locals_)
-                    ]
-                    at = j * locals_ + k
-                    moved[at] = lax.ppermute(pieces[at], ("dp", "local"), pairs)
+        for j, k in slots_of(copies, pairs):
+            links = [
+                (a * locals_ + b, mate(a, j, copies) * locals_ + 2 * mate(b // 2, k, pairs) + b % 2)
+                for a in range(copies)
+                for b in range(locals_)
+            ]
+            at = j * pairs + k
+            moved[at] = lax.ppermute(pieces[at], ("dp", "local"), links)
         return moved
 
-    got_x = exchange(pieces[: copies * locals_])
-    got_dy = exchange(pieces[copies * locals_ :])
-    late = fence(pos)
-    (rows_x,) = call(functools.partial(join_body, dims), [shape(everyone, part, BF16)], late, got_x)
+    got_x = exchange(pieces_x)
+    got_dy = exchange(pieces_y)
+    (rows_x,) = call(
+        functools.partial(join_body, dims, stride), [shape(everyone, part, BF16)], pos, got_x
+    )
     (turned,) = call(
-        functools.partial(turn_body, dims),
+        functools.partial(turn_body, dims, stride),
         [shape(part, everyone, BF16)],
         pos,
         got_dy,

time: 98.4 us -> 79.7 us (0.81)
  waiting for transfers between devices: 44 us -> 33.3 us
  starting transfers between devices: 38.3 us -> 33.3 us
  local copies, waits for them, and re-layouts: 3.59 us -> 1.27 us
    ppermute x6, waiting for transfers between devices: 14 us -> 6.3 us  [on_device(): arrived.append(lax.ppermute(terms[s], 'node', pairs))]
    ppermute x14 -> x9, starting transfers between devices: 15.4 us -> 9.08 us  [the longest x6 8.04 us: exchange(): moved[at] = lax.ppermute(pieces[at], ('dp', 'local'), links)]
    ppermute x14 -> x9, waiting for transfers between devices: 17.7 us -> 12.3 us  [the longest x6 9.79 us: exchange(): moved[at] = lax.ppermute(pieces[at], ('dp', 'local'), links)]
    ppermute x6, waiting for transfers between devices: 8.55 us -> 11.2 us  [on_device(): lax.ppermute(chunk, 'node', [(a, (a + s) % nodes) for a in range(nodes)])]
    unnamed x16 -> x10, local copies, waits for them, and re-layouts: 3.59 us -> 1.27 us
    pallas_call x11 -> x12, Pallas kernels: 10.2 us -> 11.5 us  [call(): pl.pallas_call(body, out_shape=outs, in_specs=[pl.BlockSpec(memory_space=...]
    pallas_call x1 -> x0, Pallas kernels: 1.18 us -> none  [fence(): pl.pallas_call(fence_body, out_shape=kind, in_specs=[spec], out_specs=spec)]
    ppermute x6, starting transfers between devices: 6.8 us -> 7.9 us  [on_device(): arrived.append(lax.ppermute(terms[s], 'node', pairs))]
  transfers between devices with their start and end apart: 30 -> 25, of which waited for: 10 -> 10; matrix products, arithmetic and copies ran while one was open for 0% -> 0% of each run, Pallas kernels for 9% -> 13%
where the time goes in v1:
time: 79.7 us; the launch traced here: 79.6 us
  starting transfers between devices  33.3 us (42%)
  waiting for transfers between devices  33.3 us (42%)
  Pallas kernels  11.5 us (14%)
  local copies, waits for them, and re-layouts  1.27 us (2%)
    pallas_call x12, Pallas kernels, call(): pl.pallas_call(body, out_shape=outs, in_specs=[pl.BlockSpec(memory_space=...  11.5 us
    ppermute x6, waiting for transfers between devices, on_device(): lax.ppermute(chunk, 'node', [(a, (a + s) % nodes) for a in range(nodes)])  11.2 us
    ppermute x6, starting transfers between devices, on_device(): lax.ppermute(chunk, 'node', [(a, (a + s) % nodes) for a in range(nodes)])  10.8 us
    ppermute x6, waiting for transfers between devices, exchange(): moved[at] = lax.ppermute(pieces[at], ('dp', 'local'), links)  9.79 us
    ppermute x6, starting transfers between devices, exchange(): moved[at] = lax.ppermute(pieces[at], ('dp', 'local'), links)  8.04 us
    ppermute x6, starting transfers between devices, on_device(): arrived.append(lax.ppermute(terms[s], 'node', pairs))  7.9 us
    ppermute x6, waiting for transfers between devices, on_device(): arrived.append(lax.ppermute(terms[s], 'node', pairs))  6.3 us
    ppermute x2, waiting for transfers between devices, on_device(): finished.append(lax.ppermute(summed, 'dp', pairs))  3.48 us
  transfers between devices with their start and end apart: 25, of which 10 were waited for; matrix products, arithmetic and copies ran while one was open for 0% of the time, Pallas kernels for 13%

profile of v1, /device:TPU:0, one launch (start us, length us, event | category | flops | bytes accessed | tf_op | source)
XLA Modules:
  0.0 79.6 jit_solution(249324958465331823)
XLA Ops:
  0.0 0.5 collective-permute-start.1
  0.5 0.1 collective-permute-start.2
  0.6 0.1 copy-done.4
  0.7 0.5 collective-permute-start
  1.2 0.1 pad_add_fusion.pos
  1.2 2.5 %collective-permute-done.ids_pair = s32[1,192]{1,0:T(1,128)S(1)} collective-permute-done((s32[1,192]{1,0:T(1,128)S(1)}, s32[1,192]{1,0:T(1,128)S(1)}, u32[]{:S(2)}, u32[]{:S(2)}) %collective-permute-start) | collective-permute-done | bytes 800 | tf_op jit(solution)/shard_map/ppermute | solution.py:225
  3.8 1.1 %copy-done = bf16[192,2048]{1,0:T(8,128)(2,1)S(1)} copy-done((bf16[192,2048]{1,0:T(8,128)(2,1)S(1)}, bf16[192,2048]{1,0:T(8,128)(2,1)}, u32[]{:S(2)}) %copy-start) | copy-done | bytes 786456
  4.9 1.4 %shard_map.55 = (bf16[256,192]{1,0:T(8,128)(2,1)S(1)}, bf16[256,192]{1,0:T(8,128)(2,1)S(1)}, bf16[120,1024]{1,0:T(8,128)(2,1)S(1)}, bf16[120,1024]{1,0:T(8,128)(...) custom-call(s32[3]{0:T(128)S(1)} %pad_add_fusion.pos, s32[1,192]{1,0:T(1,128)S(1)} %bitcast.10, ...), custom_call_target="tpu_custom_call" | custom-call | flops 402653184 | bytes 2754048 | tf_op jit(solution)/shard_map/pallas_call | solution.py:33
  6.3 2.9 %collective-permute-start.6 = (bf16[120,1024]{1,0:T(8,128)(2,1)S(1)}, bf16[120,1024]{1,0:T(8,128)(2,1)S(1)}, u32[]{:S(2)}, u32[]{:S(2)}) collective-permute-start(bf16[120,1024]{1,0:T(8,128)(2,1)S(1)} %get-tuple-element.36), channel_id=1, source_target_pairs={{0,2},{1,3},{2,0},{3,1},{16,18},{17,19},{18,16},{19,17},{4,6},{5,7... | collective-permute-start | bytes 737288 | tf_op jit(solution)/shard_map/ppermute | solution.py:278
  9.3 1.5 %collective-permute-start.7 = (bf16[120,1024]{1,0:T(8,128)(2,1)S(1)}, bf16[120,1024]{1,0:T(8,128)(2,1)S(1)}, u32[]{:S(2)}, u32[]{:S(2)}) collective-permute-start(bf16[120,1024]{1,0:T(8,128)(2,1)S(1)} %get-tuple-element.37), channel_id=1, source_target_pairs={{0,16},{1,17},{2,18},{3,19},{16,0},{17,1},{18,2},{19,3},{4,20},{5,... | collective-permute-start | bytes 737288 | tf_op jit(solution)/shard_map/ppermute | solution.py:278
  10.8 0.0 collective-permute-start.8
  10.8 0.7 shard_map.59
  11.5 4.1 %collective-permute-start.19 = (bf16[256,256]{1,0:T(8,128)(2,1)S(1)}, bf16[256,256]{1,0:T(8,128)(2,1)S(1)}, u32[]{:S(2)}, u32[]{:S(2)}) collective-permute-start(bf16[256,256]{1,0:T(8,128)(2,1)S(1)} %get-tuple-element.46.refs_0_), channel_id=1, source_target_pairs={{0,12},{4,0},{8,4},{12,8},{1,13},{5,1},{9,5},{13,9},{2,14},{6,2},{... | collective-permute-start | bytes 393224 | tf_op jit(solution)/shard_map/ppermute | solution.py:247
  15.6 2.5 %collective-permute-done.19.refs_3_ = bf16[256,256]{1,0:T(8,128)(2,1)S(1)} collective-permute-done((bf16[256,256]{1,0:T(8,128)(2,1)S(1)}, bf16[256,256]{1,0:T(8,128)(2,1)S(1)}, u32[]{:S(2)}, u32[]{:S(2)}) %collective-permute-start.19) | collective-permute-done | bytes 131104 | tf_op jit(solution)/shard_map/ppermute | solution.py:247
  18.1 1.4 %collective-permute-start.18 = (bf16[256,256]{1,0:T(8,128)(2,1)S(1)}, bf16[256,256]{1,0:T(8,128)(2,1)S(1)}, u32[]{:S(2)}, u32[]{:S(2)}) collective-permute-start(bf16[256,256]{1,0:T(8,128)(2,1)S(1)} %get-tuple-element.46.refs_0_), channel_id=1, source_target_pairs={{0,8},{4,12},{8,0},{12,4},{1,9},{5,13},{9,1},{13,5},{2,10},{6,14},... | collective-permute-start | bytes 393224 | tf_op jit(solution)/shard_map/ppermute | solution.py:247
  19.5 3.4 %collective-permute-start.17 = (bf16[256,256]{1,0:T(8,128)(2,1)S(1)}, bf16[256,256]{1,0:T(8,128)(2,1)S(1)}, u32[]{:S(2)}, u32[]{:S(2)}) collective-permute-start(bf16[256,256]{1,0:T(8,128)(2,1)S(1)} %get-tuple-element.46.refs_0_), channel_id=1, source_target_pairs={{0,4},{4,8},{8,12},{12,0},{1,5},{5,9},{9,13},{13,1},{2,6},{6,10},{... | collective-permute-start | bytes 393224 | tf_op jit(solution)/shard_map/ppermute | solution.py:247
  22.9 0.5 collective-permute-start.11
  23.4 1.4 %collective-permute-start.10 = (bf16[256,256]{1,0:T(8,128)(2,1)S(1)}, bf16[256,256]{1,0:T(8,128)(2,1)S(1)}, u32[]{:S(2)}, u32[]{:S(2)}) collective-permute-start(bf16[256,256]{1,0:T(8,128)(2,1)S(1)} %get-tuple-element.39.refs_0_), channel_id=1, source_target_pairs={{0,8},{4,12},{8,0},{12,4},{1,9},{5,13},{9,1},{13,5},{2,10},{6,14},... | collective-permute-start | bytes 393224 | tf_op jit(solution)/shard_map/ppermute | solution.py:247
  24.8 0.6 shard_map.58.rows
  25.4 8.7 %collective-permute-done.18.refs_2_ = bf16[256,256]{1,0:T(8,128)(2,1)S(1)} collective-permute-done((bf16[256,256]{1,0:T(8,128)(2,1)S(1)}, bf16[256,256]{1,0:T(8,128)(2,1)S(1)}, u32[]{:S(2)}, u32[]{:S(2)}) %collective-permute-start.18) | collective-permute-done | bytes 131104 | tf_op jit(solution)/shard_map/ppermute | solution.py:247
  34.1 1.0 %shard_map.63 = (f32[512,256]{1,0:T(8,128)S(1)}, bf16[512,256]{1,0:T(8,128)(2,1)S(1)}) custom-call(s32[3]{0:T(128)S(1)} %pad_add_fusion.pos, bf16[512,1024]{1,0:T(8,128)(2,1)S(1)} %shard_map.58.rows, bf16[256,256]{1,0:T(8,128)(2,1)S(1)} %get-tuple-element.46.refs_0_, bf16[256,256]{1,0:T(8,128)(2,1)S(1)} %collective-permute-done.17.refs_1_, ...), custom_call_target="tpu_custom_call" | custom-call | flops 268435456 | bytes 2359296 | tf_op jit(solution)/shard_map/pallas_call | solution.py:33
  35.1 1.6 %collective-permute-start.20 = (bf16[512,256]{1,0:T(8,128)(2,1)S(1)}, bf16[512,256]{1,0:T(8,128)(2,1)S(1)}, u32[]{:S(2)}, u32[]{:S(2)}) collective-permute-start(bf16[512,256]{1,0:T(8,128)(2,1)S(1)} %get-tuple-element.48), channel_id=1, source_target_pairs={{0,16},{16,0},{1,17},{17,1},{2,18},{18,2},{3,19},{19,3},{4,20},{20... | collective-permute-start | bytes 786440 | tf_op jit(solution)/shard_map/ppermute | solution.py:305
  36.7 1.3 %shard_map.56 = (bf16[120,1024]{1,0:T(8,128)(2,1)S(1)}, bf16[120,1024]{1,0:T(8,128)(2,1)S(1)}, bf16[120,1024]{1,0:T(8,128)(2,1)S(1)}, bf16[120,1024]{1,0:T(8,128)(2,1)S(1)}) custom-call(s32[3]{0:T(128)S(1)} %pad_add_fusion.pos, bf16[256,192]{1,0:T(8,128)(2,1)S(1)} %get-tuple-element.29.pick, bf16[256,192]{1,0:T(8,128)(2,1)S(1)} %get-tuple-element.30.pick_pair, ...), custom_call_target="tpu_custom_call" | custom-call | flops 402653184 | bytes 2752512 | tf_op jit(solution)/shard_map/pallas_call | solution.py:33
  38.0 1.6 %collective-permute-start.3 = (bf16[120,1024]{1,0:T(8,128)(2,1)S(1)}, bf16[120,1024]{1,0:T(8,128)(2,1)S(1)}, u32[]{:S(2)}, u32[]{:S(2)}) collective-permute-start(bf16[120,1024]{1,0:T(8,128)(2,1)S(1)} %get-tuple-element.32), channel_id=1, source_target_pairs={{0,2},{1,3},{2,0},{3,1},{16,18},{17,19},{18,16},{19,17},{4,6},{5,7... | collective-permute-start | bytes 737288 | tf_op jit(solution)/shard_map/ppermute | solution.py:278
  39.5 0.5 collective-permute-start.4
  40.1 1.4 %collective-permute-start.5 = (bf16[120,1024]{1,0:T(8,128)(2,1)S(1)}, bf16[120,1024]{1,0:T(8,128)(2,1)S(1)}, u32[]{:S(2)}, u32[]{:S(2)}) collective-permute-start(bf16[120,1024]{1,0:T(8,128)(2,1)S(1)} %get-tuple-element.34), channel_id=1, source_target_pairs={{0,18},{1,19},{2,16},{3,17},{16,2},{17,3},{18,0},{19,1},{4,22},{5,... | collective-permute-start | bytes 737288 | tf_op jit(solution)/shard_map/ppermute | solution.py:278
  41.5 1.0 %shard_map.60 = (f32[512,256]{1,0:T(8,128)S(1)}, bf16[512,256]{1,0:T(8,128)(2,1)S(1)}) custom-call(s32[3]{0:T(128)S(1)} %pad_add_fusion.pos, bf16[512,1024]{1,0:T(8,128)(2,1)S(1)} %shard_map.58.rows, bf16[256,256]{1,0:T(8,128)(2,1)S(1)} %get-tuple-element.39.refs_0_, bf16[256,256]{1,0:T(8,128)(2,1)S(1)} %collective-permute-done.9.refs_1_, ...), custom_call_target="tpu_custom_call" | custom-call | flops 268435456 | bytes 2359296 | tf_op jit(solution)/shard_map/pallas_call | solution.py:33
  42.5 0.9 %collective-permute-start.12 = (bf16[512,256]{1,0:T(8,128)(2,1)S(1)}, bf16[512,256]{1,0:T(8,128)(2,1)S(1)}, u32[]{:S(2)}, u32[]{:S(2)}) collective-permute-start(bf16[512,256]{1,0:T(8,128)(2,1)S(1)} %get-tuple-element.41), channel_id=1, source_target_pairs={{0,16},{16,0},{1,17},{17,1},{2,18},{18,2},{3,19},{19,3},{4,20},{20... | collective-permute-start | bytes 786440 | tf_op jit(solution)/shard_map/ppermute | solution.py:305
  43.4 2.7 %collective-permute-done.3.refs_1_ = bf16[120,1024]{1,0:T(8,128)(2,1)S(1)} collective-permute-done((bf16[120,1024]{1,0:T(8,128)(2,1)S(1)}, bf16[120,1024]{1,0:T(8,128)(2,1)S(1)}, u32[]{:S(2)}, u32[]{:S(2)}) %collective-permute-start.3) | collective-permute-done | bytes 245792 | tf_op jit(solution)/shard_map/ppermute | solution.py:278
  46.2 2.2 %collective-permute-done.4.refs_2_ = bf16[120,1024]{1,0:T(8,128)(2,1)S(1)} collective-permute-done((bf16[120,1024]{1,0:T(8,128)(2,1)S(1)}, bf16[120,1024]{1,0:T(8,128)(2,1)S(1)}, u32[]{:S(2)}, u32[]{:S(2)}) %collective-permute-start.4) | collective-permute-done | bytes 245792 | tf_op jit(solution)/shard_map/ppermute | solution.py:278
  48.4 4.8 %collective-permute-done.5.refs_3_ = bf16[120,1024]{1,0:T(8,128)(2,1)S(1)} collective-permute-done((bf16[120,1024]{1,0:T(8,128)(2,1)S(1)}, bf16[120,1024]{1,0:T(8,128)(2,1)S(1)}, u32[]{:S(2)}, u32[]{:S(2)}) %collective-permute-start.5) | collective-permute-done | bytes 245792 | tf_op jit(solution)/shard_map/ppermute | solution.py:278
  53.2 0.9 %shard_map.57.turned = bf16[1024,512]{1,0:T(8,128)(2,1)S(1)} custom-call(s32[3]{0:T(128)S(1)} %pad_add_fusion.pos, bf16[120,1024]{1,0:T(8,128)(2,1)S(1)} %get-tuple-element.31.refs_0_, bf16[120,1024]{1,0:T(8,128)(2,1)S(1)} %collective-permute-done.3.refs_1_, bf16[120,1024]{1,0:T(8,128)(2,1)S(1)} %collective-permute-done.4.refs_2_, ...), custom_call_target="tpu_custom_call" | custom-call | bytes 2031616 | tf_op jit(solution)/shard_map/pallas_call | solution.py:33
  54.2 1.0 %shard_map.64 = (f32[256,256]{1,0:T(8,128)S(1)}, bf16[256,256]{1,0:T(8,128)(2,1)S(1)}, bf16[256,256]{1,0:T(8,128)(2,1)S(1)}, bf16[256,256]{1,0:T(8,128)(2,1)S(1)}) custom-call(s32[3]{0:T(128)S(1)} %pad_add_fusion.pos, bf16[1024,512]{1,0:T(8,128)(2,1)S(1)} %shard_map.57.turned, f32[512,256]{1,0:T(8,128)S(1)} %get-tuple-element.47.kept, ...), custom_call_target="tpu_custom_call" | custom-call | flops 268435456 | bytes 2490368 | tf_op jit(solution)/shard_map/pallas_call | solution.py:33
  55.2 2.7 %collective-permute-start.21 = (bf16[256,256]{1,0:T(8,128)(2,1)S(1)}, bf16[256,256]{1,0:T(8,128)(2,1)S(1)}, u32[]{:S(2)}, u32[]{:S(2)}) collective-permute-start(bf16[256,256]{1,0:T(8,128)(2,1)S(1)} %get-tuple-element.50), channel_id=1, source_target_pairs={{0,8},{4,12},{8,0},{12,4},{1,9},{5,13},{9,1},{13,5},{2,10},{6,14},... | collective-permute-start | bytes 393224 | tf_op jit(solution)/shard_map/ppermute | solution.py:319
  57.9 3.8 %collective-permute-start.23 = (bf16[256,256]{1,0:T(8,128)(2,1)S(1)}, bf16[256,256]{1,0:T(8,128)(2,1)S(1)}, u32[]{:S(2)}, u32[]{:S(2)}) collective-permute-start(bf16[256,256]{1,0:T(8,128)(2,1)S(1)} %get-tuple-element.52), channel_id=1, source_target_pairs={{0,12},{4,0},{8,4},{12,8},{1,13},{5,1},{9,5},{13,9},{2,14},{6,2},{... | collective-permute-start | bytes 393224 | tf_op jit(solution)/shard_map/ppermute | solution.py:319
  61.7 1.0 %shard_map.61 = (f32[256,256]{1,0:T(8,128)S(1)}, bf16[256,256]{1,0:T(8,128)(2,1)S(1)}, bf16[256,256]{1,0:T(8,128)(2,1)S(1)}, bf16[256,256]{1,0:T(8,128)(2,1)S(1)}) custom-call(s32[3]{0:T(128)S(1)} %pad_add_fusion.pos, bf16[1024,512]{1,0:T(8,128)(2,1)S(1)} %shard_map.57.turned, f32[512,256]{1,0:T(8,128)S(1)} %get-tuple-element.40.kept, ...), custom_call_target="tpu_custom_call" | custom-call | flops 268435456 | bytes 2490368 | tf_op jit(solution)/shard_map/pallas_call | solution.py:33
  62.7 0.1 collective-permute-start.13
  62.8 0.6 collective-permute-start.14
  63.4 2.6 %collective-permute-done.21.refs_0_ = bf16[256,256]{1,0:T(8,128)(2,1)S(1)} collective-permute-done((bf16[256,256]{1,0:T(8,128)(2,1)S(1)}, bf16[256,256]{1,0:T(8,128)(2,1)S(1)}, u32[]{:S(2)}, u32[]{:S(2)}) %collective-permute-start.21) | collective-permute-done | bytes 131104 | tf_op jit(solution)/shard_map/ppermute | solution.py:319
  66.0 0.7 collective-permute-start.15
  66.7 0.6 shard_map.65.refs_2_
  67.3 1.6 %collective-permute-start.24 = (bf16[256,256]{1,0:T(8,128)(2,1)S(1)}, bf16[256,256]{1,0:T(8,128)(2,1)S(1)}, u32[]{:S(2)}, u32[]{:S(2)}) collective-permute-start(bf16[256,256]{1,0:T(8,128)(2,1)S(1)} %shard_map.65.refs_2_), channel_id=1, source_target_pairs={{0,16},{16,0},{1,17},{17,1},{2,18},{18,2},{3,19},{19,3},{4,20},{20... | collective-permute-start | bytes 393224 | tf_op jit(solution)/shard_map/ppermute | solution.py:324
  68.9 3.1 %collective-permute-done.13.refs_0_ = bf16[256,256]{1,0:T(8,128)(2,1)S(1)} collective-permute-done((bf16[256,256]{1,0:T(8,128)(2,1)S(1)}, bf16[256,256]{1,0:T(8,128)(2,1)S(1)}, u32[]{:S(2)}, u32[]{:S(2)}) %collective-permute-start.13) | collective-permute-done | bytes 131104 | tf_op jit(solution)/shard_map/ppermute | solution.py:319
  71.9 0.6 collective-permute-done.15.refs_2_
  72.6 0.6 shard_map.62.refs_0_
  73.2 1.6 %collective-permute-start.16 = (bf16[256,256]{1,0:T(8,128)(2,1)S(1)}, bf16[256,256]{1,0:T(8,128)(2,1)S(1)}, u32[]{:S(2)}, u32[]{:S(2)}) collective-permute-start(bf16[256,256]{1,0:T(8,128)(2,1)S(1)} %shard_map.62.refs_0_), channel_id=1, source_target_pairs={{0,16},{16,0},{1,17},{17,1},{2,18},{18,2},{3,19},{19,3},{4,20},{20... | collective-permute-start | bytes 393224 | tf_op jit(solution)/shard_map/ppermute | solution.py:324
  74.7 3.5 %collective-permute-done.16.refs_1_ = bf16[256,256]{1,0:T(8,128)(2,1)S(1)} collective-permute-done((bf16[256,256]{1,0:T(8,128)(2,1)S(1)}, bf16[256,256]{1,0:T(8,128)(2,1)S(1)}, u32[]{:S(2)}, u32[]{:S(2)}) %collective-permute-start.16) | collective-permute-done | bytes 131104 | tf_op jit(solution)/shard_map/ppermute | solution.py:324
  78.2 1.4 %shard_map.66 = bf16[512,512]{1,0:T(8,128)(2,1)} custom-call(s32[3]{0:T(128)S(1)} %pad_add_fusion.pos, bf16[256,256]{1,0:T(8,128)(2,1)S(1)} %shard_map.62.refs_0_, bf16[256,256]{1,0:T(8,128)(2,1)S(1)} %collective-permute-done.16.refs_1_, bf16[256,256]{1,0:T(8,128)(2,1)S(1)} %shard_map.65.refs_2_, bf16[256,256]{1,0:T(8,128)(2,1)S(1)} %collective-permute-done.24.refs_3_), custom_call_target="tpu_custom_call" | custom-call | bytes 1048576 | tf_op jit(solution)/shard_map/pallas_call | solution.py:33
  (25 shorter events, 0.1 us)
Async XLA Ops:
  0.0 0.7 copy-start.4
  0.0 3.7 %collective-permute-start.1 = (bf16[192,2048]{1,0:T(8,128)(2,1)}, bf16[192,2048]{1,0:T(8,128)(2,1)S(1)}, u32[]{:S(2)}, u32[]{:S(2)}) collective-permute-start(bf16[192,2048]{1,0:T(8,128)(2,1)} %rows.2), channel_id=1, source_target_pairs={{0,1},{1,0},{2,3},{3,2},{4,5},{5,4},{6,7},{7,6},{8,9},{9,8},{10,11... | collective-permute-start | bytes 2359304 | tf_op jit(solution)/shard_map/ppermute | solution.py:226
  0.5 36.2 %collective-permute-start.2 = (bf16[192,2048]{1,0:T(8,128)(2,1)}, bf16[192,2048]{1,0:T(8,128)(2,1)S(1)}, u32[]{:S(2)}, u32[]{:S(2)}) collective-permute-start(bf16[192,2048]{1,0:T(8,128)(2,1)} %rows.3), channel_id=1, source_target_pairs={{0,1},{1,0},{2,3},{3,2},{4,5},{5,4},{6,7},{7,6},{8,9},{9,8},{10,11... | collective-permute-start | bytes 2359304 | tf_op jit(solution)/shard_map/ppermute | solution.py:227
  0.7 3.1 %collective-permute-start = (s32[1,192]{1,0:T(1,128)S(1)}, s32[1,192]{1,0:T(1,128)S(1)}, u32[]{:S(2)}, u32[]{:S(2)}) collective-permute-start(s32[1,192]{1,0:T(1,128)S(1)} %bitcast.9), channel_id=1, source_target_pairs={{0,1},{1,0},{2,3},{3,2},{4,5},{5,4},{6,7},{7,6},{8,9},{9,8},{10,11... | collective-permute-start | bytes 2312 | tf_op jit(solution)/shard_map/ppermute | solution.py:225
  3.7 1.1 %copy-start = (bf16[192,2048]{1,0:T(8,128)(2,1)S(1)}, bf16[192,2048]{1,0:T(8,128)(2,1)}, u32[]{:S(2)}) copy-start(bf16[192,2048]{1,0:T(8,128)(2,1)} %rows.2) | copy-start | bytes 2359300
  4.9 5.9 %copy-start.2 = (bf16[1,512,512]{2,1,0:T(8,128)(2,1)S(1)}, bf16[1,512,512]{2,1,0:T(8,128)(2,1)}, u32[]{:S(2)}) copy-start(bf16[1,512,512]{2,1,0:T(8,128)(2,1)} %param.8) | copy-start | bytes 1572868
  4.9 5.9 %copy-start.3 = (bf16[1,16,512]{2,1,0:T(8,128)(2,1)S(1)}, bf16[1,16,512]{2,1,0:T(8,128)(2,1)}, u32[]{:S(2)}) copy-start(bf16[1,16,512]{2,1,0:T(8,128)(2,1)} %param.9) | copy-start | bytes 49156
  6.3 13.2 %collective-permute-start.6 = (bf16[120,1024]{1,0:T(8,128)(2,1)S(1)}, bf16[120,1024]{1,0:T(8,128)(2,1)S(1)}, u32[]{:S(2)}, u32[]{:S(2)}) collective-permute-start(bf16[120,1024]{1,0:T(8,128)(2,1)S(1)} %get-tuple-element.36), channel_id=1, source_target_pairs={{0,2},{1,3},{2,0},{3,1},{16,18},{17,19},{18,16},{19,17},{4,6},{5,7... | collective-permute-start | bytes 737288 | tf_op jit(solution)/shard_map/ppermute | solution.py:278
  9.3 13.6 %collective-permute-start.7 = (bf16[120,1024]{1,0:T(8,128)(2,1)S(1)}, bf16[120,1024]{1,0:T(8,128)(2,1)S(1)}, u32[]{:S(2)}, u32[]{:S(2)}) collective-permute-start(bf16[120,1024]{1,0:T(8,128)(2,1)S(1)} %get-tuple-element.37), channel_id=1, source_target_pairs={{0,16},{1,17},{2,18},{3,19},{16,0},{17,1},{18,2},{19,3},{4,20},{5,... | collective-permute-start | bytes 737288 | tf_op jit(solution)/shard_map/ppermute | solution.py:278
  10.8 12.6 %collective-permute-start.8 = (bf16[120,1024]{1,0:T(8,128)(2,1)S(1)}, bf16[120,1024]{1,0:T(8,128)(2,1)S(1)}, u32[]{:S(2)}, u32[]{:S(2)}) collective-permute-start(bf16[120,1024]{1,0:T(8,128)(2,1)S(1)} %get-tuple-element.38), channel_id=1, source_target_pairs={{0,18},{1,19},{2,16},{3,17},{16,2},{17,3},{18,0},{19,1},{4,22},{5,... | collective-permute-start | bytes 737288 | tf_op jit(solution)/shard_map/ppermute | solution.py:278
  11.5 6.6 %collective-permute-start.19 = (bf16[256,256]{1,0:T(8,128)(2,1)S(1)}, bf16[256,256]{1,0:T(8,128)(2,1)S(1)}, u32[]{:S(2)}, u32[]{:S(2)}) collective-permute-start(bf16[256,256]{1,0:T(8,128)(2,1)S(1)} %get-tuple-element.46.refs_0_), channel_id=1, source_target_pairs={{0,12},{4,0},{8,4},{12,8},{1,13},{5,1},{9,5},{13,9},{2,14},{6,2},{... | collective-permute-start | bytes 393224 | tf_op jit(solution)/shard_map/ppermute | solution.py:247
  18.1 16.0 %collective-permute-start.18 = (bf16[256,256]{1,0:T(8,128)(2,1)S(1)}, bf16[256,256]{1,0:T(8,128)(2,1)S(1)}, u32[]{:S(2)}, u32[]{:S(2)}) collective-permute-start(bf16[256,256]{1,0:T(8,128)(2,1)S(1)} %get-tuple-element.46.refs_0_), channel_id=1, source_target_pairs={{0,8},{4,12},{8,0},{12,4},{1,9},{5,13},{9,1},{13,5},{2,10},{6,14},... | collective-permute-start | bytes 393224 | tf_op jit(solution)/shard_map/ppermute | solution.py:247
  19.5 14.5 %collective-permute-start.17 = (bf16[256,256]{1,0:T(8,128)(2,1)S(1)}, bf16[256,256]{1,0:T(8,128)(2,1)S(1)}, u32[]{:S(2)}, u32[]{:S(2)}) collective-permute-start(bf16[256,256]{1,0:T(8,128)(2,1)S(1)} %get-tuple-element.46.refs_0_), channel_id=1, source_target_pairs={{0,4},{4,8},{8,12},{12,0},{1,5},{5,9},{9,13},{13,1},{2,6},{6,10},{... | collective-permute-start | bytes 393224 | tf_op jit(solution)/shard_map/ppermute | solution.py:247
  22.9 16.6 %collective-permute-start.11 = (bf16[256,256]{1,0:T(8,128)(2,1)S(1)}, bf16[256,256]{1,0:T(8,128)(2,1)S(1)}, u32[]{:S(2)}, u32[]{:S(2)}) collective-permute-start(bf16[256,256]{1,0:T(8,128)(2,1)S(1)} %get-tuple-element.39.refs_0_), channel_id=1, source_target_pairs={{0,12},{4,0},{8,4},{12,8},{1,13},{5,1},{9,5},{13,9},{2,14},{6,2},{... | collective-permute-start | bytes 393224 | tf_op jit(solution)/shard_map/ppermute | solution.py:247
  23.4 16.7 %collective-permute-start.10 = (bf16[256,256]{1,0:T(8,128)(2,1)S(1)}, bf16[256,256]{1,0:T(8,128)(2,1)S(1)}, u32[]{:S(2)}, u32[]{:S(2)}) collective-permute-start(bf16[256,256]{1,0:T(8,128)(2,1)S(1)} %get-tuple-element.39.refs_0_), channel_id=1, source_target_pairs={{0,8},{4,12},{8,0},{12,4},{1,9},{5,13},{9,1},{13,5},{2,10},{6,14},... | collective-permute-start | bytes 393224 | tf_op jit(solution)/shard_map/ppermute | solution.py:247
  25.4 11.3 %copy-start.1 = (bf16[192,2048]{1,0:T(8,128)(2,1)S(1)}, bf16[192,2048]{1,0:T(8,128)(2,1)}, u32[]{:S(2)}) copy-start(bf16[192,2048]{1,0:T(8,128)(2,1)} %rows.3) | copy-start | bytes 2359300
  34.1 7.4 %collective-permute-start.9 = (bf16[256,256]{1,0:T(8,128)(2,1)S(1)}, bf16[256,256]{1,0:T(8,128)(2,1)S(1)}, u32[]{:S(2)}, u32[]{:S(2)}) collective-permute-start(bf16[256,256]{1,0:T(8,128)(2,1)S(1)} %get-tuple-element.39.refs_0_), channel_id=1, source_target_pairs={{0,4},{4,8},{8,12},{12,0},{1,5},{5,9},{9,13},{13,1},{2,6},{6,10},{... | collective-permute-start | bytes 393224 | tf_op jit(solution)/shard_map/ppermute | solution.py:247
  35.1 19.0 %collective-permute-start.20 = (bf16[512,256]{1,0:T(8,128)(2,1)S(1)}, bf16[512,256]{1,0:T(8,128)(2,1)S(1)}, u32[]{:S(2)}, u32[]{:S(2)}) collective-permute-start(bf16[512,256]{1,0:T(8,128)(2,1)S(1)} %get-tuple-element.48), channel_id=1, source_target_pairs={{0,16},{16,0},{1,17},{17,1},{2,18},{18,2},{3,19},{19,3},{4,20},{20... | collective-permute-start | bytes 786440 | tf_op jit(solution)/shard_map/ppermute | solution.py:305
  38.0 8.2 %collective-permute-start.3 = (bf16[120,1024]{1,0:T(8,128)(2,1)S(1)}, bf16[120,1024]{1,0:T(8,128)(2,1)S(1)}, u32[]{:S(2)}, u32[]{:S(2)}) collective-permute-start(bf16[120,1024]{1,0:T(8,128)(2,1)S(1)} %get-tuple-element.32), channel_id=1, source_target_pairs={{0,2},{1,3},{2,0},{3,1},{16,18},{17,19},{18,16},{19,17},{4,6},{5,7... | collective-permute-start | bytes 737288 | tf_op jit(solution)/shard_map/ppermute | solution.py:278
  39.5 8.8 %collective-permute-start.4 = (bf16[120,1024]{1,0:T(8,128)(2,1)S(1)}, bf16[120,1024]{1,0:T(8,128)(2,1)S(1)}, u32[]{:S(2)}, u32[]{:S(2)}) collective-permute-start(bf16[120,1024]{1,0:T(8,128)(2,1)S(1)} %get-tuple-element.33), channel_id=1, source_target_pairs={{0,16},{1,17},{2,18},{3,19},{16,0},{17,1},{18,2},{19,3},{4,20},{5,... | collective-permute-start | bytes 737288 | tf_op jit(solution)/shard_map/ppermute | solution.py:278
  40.1 13.1 %collective-permute-start.5 = (bf16[120,1024]{1,0:T(8,128)(2,1)S(1)}, bf16[120,1024]{1,0:T(8,128)(2,1)S(1)}, u32[]{:S(2)}, u32[]{:S(2)}) collective-permute-start(bf16[120,1024]{1,0:T(8,128)(2,1)S(1)} %get-tuple-element.34), channel_id=1, source_target_pairs={{0,18},{1,19},{2,16},{3,17},{16,2},{17,3},{18,0},{19,1},{4,22},{5,... | collective-permute-start | bytes 737288 | tf_op jit(solution)/shard_map/ppermute | solution.py:278
  42.5 19.2 %collective-permute-start.12 = (bf16[512,256]{1,0:T(8,128)(2,1)S(1)}, bf16[512,256]{1,0:T(8,128)(2,1)S(1)}, u32[]{:S(2)}, u32[]{:S(2)}) collective-permute-start(bf16[512,256]{1,0:T(8,128)(2,1)S(1)} %get-tuple-element.41), channel_id=1, source_target_pairs={{0,16},{16,0},{1,17},{17,1},{2,18},{18,2},{3,19},{19,3},{4,20},{20... | collective-permute-start | bytes 786440 | tf_op jit(solution)/shard_map/ppermute | solution.py:305
  55.2 10.8 %collective-permute-start.21 = (bf16[256,256]{1,0:T(8,128)(2,1)S(1)}, bf16[256,256]{1,0:T(8,128)(2,1)S(1)}, u32[]{:S(2)}, u32[]{:S(2)}) collective-permute-start(bf16[256,256]{1,0:T(8,128)(2,1)S(1)} %get-tuple-element.50), channel_id=1, source_target_pairs={{0,8},{4,12},{8,0},{12,4},{1,9},{5,13},{9,1},{13,5},{2,10},{6,14},... | collective-permute-start | bytes 393224 | tf_op jit(solution)/shard_map/ppermute | solution.py:319
  57.9 8.8 %collective-permute-start.22 = (bf16[256,256]{1,0:T(8,128)(2,1)S(1)}, bf16[256,256]{1,0:T(8,128)(2,1)S(1)}, u32[]{:S(2)}, u32[]{:S(2)}) collective-permute-start(bf16[256,256]{1,0:T(8,128)(2,1)S(1)} %get-tuple-element.51), channel_id=1, source_target_pairs={{0,4},{4,8},{8,12},{12,0},{1,5},{5,9},{9,13},{13,1},{2,6},{6,10},{... | collective-permute-start | bytes 393224 | tf_op jit(solution)/shard_map/ppermute | solution.py:319
  57.9 8.8 %collective-permute-start.23 = (bf16[256,256]{1,0:T(8,128)(2,1)S(1)}, bf16[256,256]{1,0:T(8,128)(2,1)S(1)}, u32[]{:S(2)}, u32[]{:S(2)}) collective-permute-start(bf16[256,256]{1,0:T(8,128)(2,1)S(1)} %get-tuple-element.52), channel_id=1, source_target_pairs={{0,12},{4,0},{8,4},{12,8},{1,13},{5,1},{9,5},{13,9},{2,14},{6,2},{... | collective-permute-start | bytes 393224 | tf_op jit(solution)/shard_map/ppermute | solution.py:319
  62.7 9.2 %collective-permute-start.13 = (bf16[256,256]{1,0:T(8,128)(2,1)S(1)}, bf16[256,256]{1,0:T(8,128)(2,1)S(1)}, u32[]{:S(2)}, u32[]{:S(2)}) collective-permute-start(bf16[256,256]{1,0:T(8,128)(2,1)S(1)} %get-tuple-element.43), channel_id=1, source_target_pairs={{0,8},{4,12},{8,0},{12,4},{1,9},{5,13},{9,1},{13,5},{2,10},{6,14},... | collective-permute-start | bytes 393224 | tf_op jit(solution)/shard_map/ppermute | solution.py:319
  62.8 9.1 %collective-permute-start.14 = (bf16[256,256]{1,0:T(8,128)(2,1)S(1)}, bf16[256,256]{1,0:T(8,128)(2,1)S(1)}, u32[]{:S(2)}, u32[]{:S(2)}) collective-permute-start(bf16[256,256]{1,0:T(8,128)(2,1)S(1)} %get-tuple-element.44), channel_id=1, source_target_pairs={{0,4},{4,8},{8,12},{12,0},{1,5},{5,9},{9,13},{13,1},{2,6},{6,10},{... | collective-permute-start | bytes 393224 | tf_op jit(solution)/shard_map/ppermute | solution.py:319
  66.0 6.6 %collective-permute-start.15 = (bf16[256,256]{1,0:T(8,128)(2,1)S(1)}, bf16[256,256]{1,0:T(8,128)(2,1)S(1)}, u32[]{:S(2)}, u32[]{:S(2)}) collective-permute-start(bf16[256,256]{1,0:T(8,128)(2,1)S(1)} %get-tuple-element.45), channel_id=1, source_target_pairs={{0,12},{4,0},{8,4},{12,8},{1,13},{5,1},{9,5},{13,9},{2,14},{6,2},{... | collective-permute-start | bytes 393224 | tf_op jit(solution)/shard_map/ppermute | solution.py:319
  67.3 7.4 %collective-permute-start.24 = (bf16[256,256]{1,0:T(8,128)(2,1)S(1)}, bf16[256,256]{1,0:T(8,128)(2,1)S(1)}, u32[]{:S(2)}, u32[]{:S(2)}) collective-permute-start(bf16[256,256]{1,0:T(8,128)(2,1)S(1)} %shard_map.65.refs_2_), channel_id=1, source_target_pairs={{0,16},{16,0},{1,17},{17,1},{2,18},{18,2},{3,19},{19,3},{4,20},{20... | collective-permute-start | bytes 393224 | tf_op jit(solution)/shard_map/ppermute | solution.py:324
  73.2 5.0 %collective-permute-start.16 = (bf16[256,256]{1,0:T(8,128)(2,1)S(1)}, bf16[256,256]{1,0:T(8,128)(2,1)S(1)}, u32[]{:S(2)}, u32[]{:S(2)}) collective-permute-start(bf16[256,256]{1,0:T(8,128)(2,1)S(1)} %shard_map.62.refs_0_), channel_id=1, source_target_pairs={{0,16},{16,0},{1,17},{17,1},{2,18},{18,2},{3,19},{19,3},{4,20},{20... | collective-permute-start | bytes 393224 | tf_op jit(solution)/shard_map/ppermute | solution.py:324

commit v2 on v1

--- a/solution.py
+++ b/solution.py
@@ -26,7 +26,7 @@
     return lax.rem(i + (size - k), size)
 
 
-def call(body, outs, scalars, args, scratch=(), flops=0, space=pltpu.VMEM):
+def call(body, outs, scalars, args, scratch=(), flops=0, space=pltpu.VMEM, target=pltpu.VMEM):
     moved = sum(a.size * a.dtype.itemsize for a in args)
     moved += sum(o.size * o.dtype.itemsize for o in outs)
     room = 2 * moved + (8 << 20)
@@ -35,7 +35,7 @@
         out_shape=outs,
         in_specs=[pl.BlockSpec(memory_space=pltpu.SMEM)]
         + [pl.BlockSpec(memory_space=space)] * len(args),
-        out_specs=[pl.BlockSpec(memory_space=pltpu.VMEM)] * len(outs),
+        out_specs=[pl.BlockSpec(memory_space=target)] * len(outs),
         scratch_shapes=list(scratch),
         compiler_params=pltpu.CompilerParams(vmem_limit_bytes=min(room, 60 << 20)),
         cost_estimate=pl.CostEstimate(flops=flops, bytes_accessed=moved, transcendentals=0),
@@ -44,6 +44,10 @@
 
 def partition(values):
     return values[0], values[1], values[2:]
+
+
+def node_order(nodes):
+    return [s for s in (2, 3, 1) if s < nodes] + list(range(4, nodes))
 
 
 def slots_of(copies, pairs):
@@ -160,7 +164,7 @@
     weights, (kept, sent), held = refs[:nodes], refs[nodes : nodes + 2], refs[-1]
     mine = weights[0].shape[0]
     for s in range(nodes):
-        at = pl.multiple_of(lax.rem(pos[1] + (nodes - s), nodes) * mine, 16)
+        at = pl.multiple_of(traced_origin(pos[1], s, nodes) * mine, 16)
         held[pl.ds(at, mine), :] = weights[s][...]
     pre = jnp.dot(rows[...], held[...], preferred_element_type=F32)
     kept[...] = pre
@@ -176,7 +180,7 @@
     act[...] = (pre * jax.nn.sigmoid(pre)).astype(BF16)
     mine = outs[0].shape[0]
     for s in reversed(range(nodes)):
-        at = pl.multiple_of(lax.rem(pos[1] + s, nodes) * mine, 16)
+        at = pl.multiple_of(traced_mate(pos[1], s, nodes) * mine, 16)
         term = jnp.dot(turned[pl.ds(at, mine), :], act[...], preferred_element_type=F32)
         outs[s][...] = (term * factor).astype(outs[s].dtype)
 
@@ -190,12 +194,18 @@
 
 def lay_body(dims, chunks, pos, *refs):
     copies = dims[0]
-    parts, out = refs[:-1], refs[-1]
+    parts, out, sems = refs[:-2], refs[-2], refs[-1]
     mine, width = parts[0].shape
+    moves = []
     for j in range(copies):
         at = pl.multiple_of(traced_origin(pos[0], j, copies) * mine, 16)
         for i in range(chunks):
-            out[pl.ds(at, mine), i * width : (i + 1) * width] = parts[i * copies + j][...]
+            spot = out.at[pl.ds(at, mine), pl.ds(i * width, width)]
+            moves.append(pltpu.make_async_copy(parts[i * copies + j], spot, sems.at[i * copies + j]))
+    for move in moves:
+        move.start()
+    for move in moves:
+        move.wait()
 
 
 def on_device(tokens, cotangent, expert_of, w1_codes, w1_scales):
@@ -239,12 +249,12 @@
         ],
         space=pltpu.HBM,
     )
-    order = [s for s in (2, 1, 3) if s < nodes] + list(range(4, nodes))
+    order = node_order(nodes)
     held = []
     for chunk in weights:
         got = {0: chunk}
         for s in order:
-            got[s] = lax.ppermute(chunk, "node", [(a, (a + s) % nodes) for a in range(nodes)])
+            got[s] = lax.ppermute(chunk, "node", [(a, mate(a, s, nodes)) for a in range(nodes)])
         held.append([got[s] for s in range(nodes)])
 
     flops = 4 * pairs * stride * count * features
@@ -315,15 +325,20 @@
         )
         arrived = []
         for s in order:
-            pairs = [(a, (a + s) % nodes) for a in range(nodes)]
-            arrived.append(lax.ppermute(terms[s], "node", pairs))
+            links = [(a, mate(a, s, nodes)) for a in range(nodes)]
+            arrived.append(lax.ppermute(terms[s], "node", links))
         (summed,) = call(sum_body, [shape(mine, width, BF16)], pos, [terms[0]] + arrived)
         finished.append(summed)
         for j in range(1, copies):
-            pairs = [(a, mate(a, j, copies)) for a in range(copies)]
-            finished.append(lax.ppermute(summed, "dp", pairs))
+            links = [(a, mate(a, j, copies)) for a in range(copies)]
+            finished.append(lax.ppermute(summed, "dp", links))
     (result,) = call(
-        functools.partial(lay_body, dims, CHUNKS), [shape(shard, hidden, BF16)], pos, finished
+        functools.partial(lay_body, dims, CHUNKS),
+        [shape(shard, hidden, BF16)],
+        pos,
+        finished,
+        [pltpu.SemaphoreType.DMA((CHUNKS * copies,))],
+        target=pltpu.HBM,
     )
     return result[None]
 

time: 79.7 us -> 78.4 us (0.984)
  waiting for transfers between devices: 33.3 us -> 30.7 us
  starting transfers between devices: 33.3 us -> 34.5 us
    ppermute x14, waiting for transfers between devices: 21 us -> 19.1 us  [the longest x6 9.24 us: on_device(): lax.ppermute(chunk, 'node', [(a, mate(a, s, nodes)) for a in range(nodes)])]
    ppermute x6, starting transfers between devices: 8.04 us -> 9.01 us  [exchange(): moved[at] = lax.ppermute(pieces[at], ('dp', 'local'), links)]
where the time goes in v2:
time: 78.4 us; the launch traced here: 78.2 us
  starting transfers between devices  34.5 us (44%)
  waiting for transfers between devices  30.7 us (39%)
  Pallas kernels  11.5 us (15%)
  local copies, waits for them, and re-layouts  1.27 us (2%)
    pallas_call x12, Pallas kernels, call(): pl.pallas_call(body, out_shape=outs, in_specs=[pl.BlockSpec(memory_space=...  11.5 us
    ppermute x6, starting transfers between devices, on_device(): lax.ppermute(chunk, 'node', [(a, mate(a, s, nodes)) for a in range(nodes)])  11.3 us
    ppermute x6, waiting for transfers between devices, on_device(): lax.ppermute(chunk, 'node', [(a, mate(a, s, nodes)) for a in range(nodes)])  9.24 us
    ppermute x6, waiting for transfers between devices, exchange(): moved[at] = lax.ppermute(pieces[at], ('dp', 'local'), links)  9.11 us
    ppermute x6, starting transfers between devices, exchange(): moved[at] = lax.ppermute(pieces[at], ('dp', 'local'), links)  9.01 us
    ppermute x6, starting transfers between devices, on_device(): arrived.append(lax.ppermute(terms[s], 'node', links))  8.16 us
    ppermute x6, waiting for transfers between devices, on_device(): arrived.append(lax.ppermute(terms[s], 'node', links))  6.36 us
    ppermute x2, waiting for transfers between devices, on_device(): finished.append(lax.ppermute(summed, 'dp', links))  3.47 us
  transfers between devices with their start and end apart: 25, of which 10 were waited for; matrix products, arithmetic and copies ran while one was open for 0% of the time, Pallas kernels for 13%

profile of v2, /device:TPU:0, one launch (start us, length us, event | category | flops | bytes accessed | tf_op | source)
XLA Modules:
  0.0 78.2 jit_solution(11239132960154506651)
XLA Ops:
  0.0 0.5 collective-permute-start.1
  0.5 0.1 collective-permute-start.2
  0.6 0.1 copy-done.4
  0.7 0.5 collective-permute-start
  1.2 0.1 pad_add_fusion.pos
  1.2 2.5 %collective-permute-done.ids_pair = s32[1,192]{1,0:T(1,128)S(1)} collective-permute-done((s32[1,192]{1,0:T(1,128)S(1)}, s32[1,192]{1,0:T(1,128)S(1)}, u32[]{:S(2)}, u32[]{:S(2)}) %collective-permute-start) | collective-permute-done | bytes 800 | tf_op jit(solution)/shard_map/ppermute | solution.py:235
  3.8 1.1 %copy-done = bf16[192,2048]{1,0:T(8,128)(2,1)S(1)} copy-done((bf16[192,2048]{1,0:T(8,128)(2,1)S(1)}, bf16[192,2048]{1,0:T(8,128)(2,1)}, u32[]{:S(2)}) %copy-start) | copy-done | bytes 786456
  4.9 1.4 %shard_map.55 = (bf16[256,192]{1,0:T(8,128)(2,1)S(1)}, bf16[256,192]{1,0:T(8,128)(2,1)S(1)}, bf16[120,1024]{1,0:T(8,128)(2,1)S(1)}, bf16[120,1024]{1,0:T(8,128)(...) custom-call(s32[3]{0:T(128)S(1)} %pad_add_fusion.pos, s32[1,192]{1,0:T(1,128)S(1)} %bitcast.10, ...), custom_call_target="tpu_custom_call" | custom-call | flops 402653184 | bytes 2754048 | tf_op jit(solution)/shard_map/pallas_call | solution.py:33
  6.3 2.9 %collective-permute-start.6 = (bf16[120,1024]{1,0:T(8,128)(2,1)S(1)}, bf16[120,1024]{1,0:T(8,128)(2,1)S(1)}, u32[]{:S(2)}, u32[]{:S(2)}) collective-permute-start(bf16[120,1024]{1,0:T(8,128)(2,1)S(1)} %get-tuple-element.36), channel_id=1, source_target_pairs={{0,2},{1,3},{2,0},{3,1},{16,18},{17,19},{18,16},{19,17},{4,6},{5,7... | collective-permute-start | bytes 737288 | tf_op jit(solution)/shard_map/ppermute | solution.py:288
  9.3 1.5 %collective-permute-start.7 = (bf16[120,1024]{1,0:T(8,128)(2,1)S(1)}, bf16[120,1024]{1,0:T(8,128)(2,1)S(1)}, u32[]{:S(2)}, u32[]{:S(2)}) collective-permute-start(bf16[120,1024]{1,0:T(8,128)(2,1)S(1)} %get-tuple-element.37), channel_id=1, source_target_pairs={{0,16},{1,17},{2,18},{3,19},{16,0},{17,1},{18,2},{19,3},{4,20},{5,... | collective-permute-start | bytes 737288 | tf_op jit(solution)/shard_map/ppermute | solution.py:288
  10.8 0.0 collective-permute-start.8
  10.8 0.7 shard_map.59
  11.5 4.1 %collective-permute-start.19 = (bf16[256,256]{1,0:T(8,128)(2,1)S(1)}, bf16[256,256]{1,0:T(8,128)(2,1)S(1)}, u32[]{:S(2)}, u32[]{:S(2)}) collective-permute-start(bf16[256,256]{1,0:T(8,128)(2,1)S(1)} %get-tuple-element.46.refs_0_), channel_id=1, source_target_pairs={{0,12},{4,8},{8,4},{12,0},{1,13},{5,9},{9,5},{13,1},{2,14},{6,10},... | collective-permute-start | bytes 393224 | tf_op jit(solution)/shard_map/ppermute | solution.py:257
  15.6 3.1 %collective-permute-done.19.refs_3_ = bf16[256,256]{1,0:T(8,128)(2,1)S(1)} collective-permute-done((bf16[256,256]{1,0:T(8,128)(2,1)S(1)}, bf16[256,256]{1,0:T(8,128)(2,1)S(1)}, u32[]{:S(2)}, u32[]{:S(2)}) %collective-permute-start.19) | collective-permute-done | bytes 131104 | tf_op jit(solution)/shard_map/ppermute | solution.py:257
  18.7 3.7 %collective-permute-start.18 = (bf16[256,256]{1,0:T(8,128)(2,1)S(1)}, bf16[256,256]{1,0:T(8,128)(2,1)S(1)}, u32[]{:S(2)}, u32[]{:S(2)}) collective-permute-start(bf16[256,256]{1,0:T(8,128)(2,1)S(1)} %get-tuple-element.46.refs_0_), channel_id=1, source_target_pairs={{0,8},{4,12},{8,0},{12,4},{1,9},{5,13},{9,1},{13,5},{2,10},{6,14},... | collective-permute-start | bytes 393224 | tf_op jit(solution)/shard_map/ppermute | solution.py:257
  22.4 0.6 collective-permute-start.17
  22.9 0.9 %collective-permute-start.11 = (bf16[256,256]{1,0:T(8,128)(2,1)S(1)}, bf16[256,256]{1,0:T(8,128)(2,1)S(1)}, u32[]{:S(2)}, u32[]{:S(2)}) collective-permute-start(bf16[256,256]{1,0:T(8,128)(2,1)S(1)} %get-tuple-element.39.refs_0_), channel_id=1, source_target_pairs={{0,12},{4,8},{8,4},{12,0},{1,13},{5,9},{9,5},{13,1},{2,14},{6,10},... | collective-permute-start | bytes 393224 | tf_op jit(solution)/shard_map/ppermute | solution.py:257
  23.8 2.0 %collective-permute-start.10 = (bf16[256,256]{1,0:T(8,128)(2,1)S(1)}, bf16[256,256]{1,0:T(8,128)(2,1)S(1)}, u32[]{:S(2)}, u32[]{:S(2)}) collective-permute-start(bf16[256,256]{1,0:T(8,128)(2,1)S(1)} %get-tuple-element.39.refs_0_), channel_id=1, source_target_pairs={{0,8},{4,12},{8,0},{12,4},{1,9},{5,13},{9,1},{13,5},{2,10},{6,14},... | collective-permute-start | bytes 393224 | tf_op jit(solution)/shard_map/ppermute | solution.py:257
  25.9 0.6 shard_map.58.rows
  26.5 0.0 copy-start.1
  26.5 6.2 %collective-permute-done.18.refs_2_ = bf16[256,256]{1,0:T(8,128)(2,1)S(1)} collective-permute-done((bf16[256,256]{1,0:T(8,128)(2,1)S(1)}, bf16[256,256]{1,0:T(8,128)(2,1)S(1)}, u32[]{:S(2)}, u32[]{:S(2)}) %collective-permute-start.18) | collective-permute-done | bytes 131104 | tf_op jit(solution)/shard_map/ppermute | solution.py:257
  32.7 1.0 %shard_map.63 = (f32[512,256]{1,0:T(8,128)S(1)}, bf16[512,256]{1,0:T(8,128)(2,1)S(1)}) custom-call(s32[3]{0:T(128)S(1)} %pad_add_fusion.pos, bf16[512,1024]{1,0:T(8,128)(2,1)S(1)} %shard_map.58.rows, bf16[256,256]{1,0:T(8,128)(2,1)S(1)} %get-tuple-element.46.refs_0_, bf16[256,256]{1,0:T(8,128)(2,1)S(1)} %collective-permute-done.17.refs_1_, ...), custom_call_target="tpu_custom_call" | custom-call | flops 268435456 | bytes 2359296 | tf_op jit(solution)/shard_map/pallas_call | solution.py:33
  33.7 1.6 %collective-permute-start.20 = (bf16[512,256]{1,0:T(8,128)(2,1)S(1)}, bf16[512,256]{1,0:T(8,128)(2,1)S(1)}, u32[]{:S(2)}, u32[]{:S(2)}) collective-permute-start(bf16[512,256]{1,0:T(8,128)(2,1)S(1)} %get-tuple-element.48), channel_id=1, source_target_pairs={{0,16},{16,0},{1,17},{17,1},{2,18},{18,2},{3,19},{19,3},{4,20},{20... | collective-permute-start | bytes 786440 | tf_op jit(solution)/shard_map/ppermute | solution.py:315
  35.3 1.3 %shard_map.56 = (bf16[120,1024]{1,0:T(8,128)(2,1)S(1)}, bf16[120,1024]{1,0:T(8,128)(2,1)S(1)}, bf16[120,1024]{1,0:T(8,128)(2,1)S(1)}, bf16[120,1024]{1,0:T(8,128)(2,1)S(1)}) custom-call(s32[3]{0:T(128)S(1)} %pad_add_fusion.pos, bf16[256,192]{1,0:T(8,128)(2,1)S(1)} %get-tuple-element.29.pick, bf16[256,192]{1,0:T(8,128)(2,1)S(1)} %get-tuple-element.30.pick_pair, ...), custom_call_target="tpu_custom_call" | custom-call | flops 402653184 | bytes 2752512 | tf_op jit(solution)/shard_map/pallas_call | solution.py:33
  36.5 1.6 %collective-permute-start.3 = (bf16[120,1024]{1,0:T(8,128)(2,1)S(1)}, bf16[120,1024]{1,0:T(8,128)(2,1)S(1)}, u32[]{:S(2)}, u32[]{:S(2)}) collective-permute-start(bf16[120,1024]{1,0:T(8,128)(2,1)S(1)} %get-tuple-element.32), channel_id=1, source_target_pairs={{0,2},{1,3},{2,0},{3,1},{16,18},{17,19},{18,16},{19,17},{4,6},{5,7... | collective-permute-start | bytes 737288 | tf_op jit(solution)/shard_map/ppermute | solution.py:288
  38.1 0.5 collective-permute-start.4
  38.7 2.4 %collective-permute-start.5 = (bf16[120,1024]{1,0:T(8,128)(2,1)S(1)}, bf16[120,1024]{1,0:T(8,128)(2,1)S(1)}, u32[]{:S(2)}, u32[]{:S(2)}) collective-permute-start(bf16[120,1024]{1,0:T(8,128)(2,1)S(1)} %get-tuple-element.34), channel_id=1, source_target_pairs={{0,18},{1,19},{2,16},{3,17},{16,2},{17,3},{18,0},{19,1},{4,22},{5,... | collective-permute-start | bytes 737288 | tf_op jit(solution)/shard_map/ppermute | solution.py:288
  41.1 1.0 %shard_map.60 = (f32[512,256]{1,0:T(8,128)S(1)}, bf16[512,256]{1,0:T(8,128)(2,1)S(1)}) custom-call(s32[3]{0:T(128)S(1)} %pad_add_fusion.pos, bf16[512,1024]{1,0:T(8,128)(2,1)S(1)} %shard_map.58.rows, bf16[256,256]{1,0:T(8,128)(2,1)S(1)} %get-tuple-element.39.refs_0_, bf16[256,256]{1,0:T(8,128)(2,1)S(1)} %collective-permute-done.9.refs_1_, ...), custom_call_target="tpu_custom_call" | custom-call | flops 268435456 | bytes 2359296 | tf_op jit(solution)/shard_map/pallas_call | solution.py:33
  42.1 0.6 collective-permute-start.12
  42.7 2.4 %collective-permute-done.3.refs_1_ = bf16[120,1024]{1,0:T(8,128)(2,1)S(1)} collective-permute-done((bf16[120,1024]{1,0:T(8,128)(2,1)S(1)}, bf16[120,1024]{1,0:T(8,128)(2,1)S(1)}, u32[]{:S(2)}, u32[]{:S(2)}) %collective-permute-start.3) | collective-permute-done | bytes 245792 | tf_op jit(solution)/shard_map/ppermute | solution.py:288
  45.1 1.8 %collective-permute-done.4.refs_2_ = bf16[120,1024]{1,0:T(8,128)(2,1)S(1)} collective-permute-done((bf16[120,1024]{1,0:T(8,128)(2,1)S(1)}, bf16[120,1024]{1,0:T(8,128)(2,1)S(1)}, u32[]{:S(2)}, u32[]{:S(2)}) %collective-permute-start.4) | collective-permute-done | bytes 245792 | tf_op jit(solution)/shard_map/ppermute | solution.py:288
  47.0 4.8 %collective-permute-done.5.refs_3_ = bf16[120,1024]{1,0:T(8,128)(2,1)S(1)} collective-permute-done((bf16[120,1024]{1,0:T(8,128)(2,1)S(1)}, bf16[120,1024]{1,0:T(8,128)(2,1)S(1)}, u32[]{:S(2)}, u32[]{:S(2)}) %collective-permute-start.5) | collective-permute-done | bytes 245792 | tf_op jit(solution)/shard_map/ppermute | solution.py:288
  51.8 0.9 %shard_map.57.turned = bf16[1024,512]{1,0:T(8,128)(2,1)S(1)} custom-call(s32[3]{0:T(128)S(1)} %pad_add_fusion.pos, bf16[120,1024]{1,0:T(8,128)(2,1)S(1)} %get-tuple-element.31.refs_0_, bf16[120,1024]{1,0:T(8,128)(2,1)S(1)} %collective-permute-done.3.refs_1_, bf16[120,1024]{1,0:T(8,128)(2,1)S(1)} %collective-permute-done.4.refs_2_, ...), custom_call_target="tpu_custom_call" | custom-call | bytes 2031616 | tf_op jit(solution)/shard_map/pallas_call | solution.py:33
  52.7 1.0 %shard_map.64 = (f32[256,256]{1,0:T(8,128)S(1)}, bf16[256,256]{1,0:T(8,128)(2,1)S(1)}, bf16[256,256]{1,0:T(8,128)(2,1)S(1)}, bf16[256,256]{1,0:T(8,128)(2,1)S(1)}) custom-call(s32[3]{0:T(128)S(1)} %pad_add_fusion.pos, bf16[1024,512]{1,0:T(8,128)(2,1)S(1)} %shard_map.57.turned, f32[512,256]{1,0:T(8,128)S(1)} %get-tuple-element.47.kept, ...), custom_call_target="tpu_custom_call" | custom-call | flops 268435456 | bytes 2490368 | tf_op jit(solution)/shard_map/pallas_call | solution.py:33
  53.8 2.1 %collective-permute-start.21 = (bf16[256,256]{1,0:T(8,128)(2,1)S(1)}, bf16[256,256]{1,0:T(8,128)(2,1)S(1)}, u32[]{:S(2)}, u32[]{:S(2)}) collective-permute-start(bf16[256,256]{1,0:T(8,128)(2,1)S(1)} %get-tuple-element.50), channel_id=1, source_target_pairs={{0,8},{4,12},{8,0},{12,4},{1,9},{5,13},{9,1},{13,5},{2,10},{6,14},... | collective-permute-start | bytes 393224 | tf_op jit(solution)/shard_map/ppermute | solution.py:329
  55.9 1.6 %collective-permute-start.22 = (bf16[256,256]{1,0:T(8,128)(2,1)S(1)}, bf16[256,256]{1,0:T(8,128)(2,1)S(1)}, u32[]{:S(2)}, u32[]{:S(2)}) collective-permute-start(bf16[256,256]{1,0:T(8,128)(2,1)S(1)} %get-tuple-element.51), channel_id=1, source_target_pairs={{0,12},{4,8},{8,4},{12,0},{1,13},{5,9},{9,5},{13,1},{2,14},{6,10},... | collective-permute-start | bytes 393224 | tf_op jit(solution)/shard_map/ppermute | solution.py:329
  57.5 1.0 %shard_map.61 = (f32[256,256]{1,0:T(8,128)S(1)}, bf16[256,256]{1,0:T(8,128)(2,1)S(1)}, bf16[256,256]{1,0:T(8,128)(2,1)S(1)}, bf16[256,256]{1,0:T(8,128)(2,1)S(1)}) custom-call(s32[3]{0:T(128)S(1)} %pad_add_fusion.pos, bf16[1024,512]{1,0:T(8,128)(2,1)S(1)} %shard_map.57.turned, f32[512,256]{1,0:T(8,128)S(1)} %get-tuple-element.40.kept, ...), custom_call_target="tpu_custom_call" | custom-call | flops 268435456 | bytes 2490368 | tf_op jit(solution)/shard_map/pallas_call | solution.py:33
  58.5 2.9 %collective-permute-start.13 = (bf16[256,256]{1,0:T(8,128)(2,1)S(1)}, bf16[256,256]{1,0:T(8,128)(2,1)S(1)}, u32[]{:S(2)}, u32[]{:S(2)}) collective-permute-start(bf16[256,256]{1,0:T(8,128)(2,1)S(1)} %get-tuple-element.43), channel_id=1, source_target_pairs={{0,8},{4,12},{8,0},{12,4},{1,9},{5,13},{9,1},{13,5},{2,10},{6,14},... | collective-permute-start | bytes 393224 | tf_op jit(solution)/shard_map/ppermute | solution.py:329
  61.3 1.6 %collective-permute-start.14 = (bf16[256,256]{1,0:T(8,128)(2,1)S(1)}, bf16[256,256]{1,0:T(8,128)(2,1)S(1)}, u32[]{:S(2)}, u32[]{:S(2)}) collective-permute-start(bf16[256,256]{1,0:T(8,128)(2,1)S(1)} %get-tuple-element.44), channel_id=1, source_target_pairs={{0,12},{4,8},{8,4},{12,0},{1,13},{5,9},{9,5},{13,1},{2,14},{6,10},... | collective-permute-start | bytes 393224 | tf_op jit(solution)/shard_map/ppermute | solution.py:329
  62.9 1.1 %collective-permute-done.21.refs_0_ = bf16[256,256]{1,0:T(8,128)(2,1)S(1)} collective-permute-done((bf16[256,256]{1,0:T(8,128)(2,1)S(1)}, bf16[256,256]{1,0:T(8,128)(2,1)S(1)}, u32[]{:S(2)}, u32[]{:S(2)}) %collective-permute-start.21) | collective-permute-done | bytes 131104 | tf_op jit(solution)/shard_map/ppermute | solution.py:329
  64.0 1.5 %collective-permute-done.23.refs_2_ = bf16[256,256]{1,0:T(8,128)(2,1)S(1)} collective-permute-done((bf16[256,256]{1,0:T(8,128)(2,1)S(1)}, bf16[256,256]{1,0:T(8,128)(2,1)S(1)}, u32[]{:S(2)}, u32[]{:S(2)}) %collective-permute-start.23) | collective-permute-done | bytes 131104 | tf_op jit(solution)/shard_map/ppermute | solution.py:329
  65.5 0.6 shard_map.65.refs_2_
  66.1 1.3 %collective-permute-start.24 = (bf16[256,256]{1,0:T(8,128)(2,1)S(1)}, bf16[256,256]{1,0:T(8,128)(2,1)S(1)}, u32[]{:S(2)}, u32[]{:S(2)}) collective-permute-start(bf16[256,256]{1,0:T(8,128)(2,1)S(1)} %shard_map.65.refs_2_), channel_id=1, source_target_pairs={{0,16},{16,0},{1,17},{17,1},{2,18},{18,2},{3,19},{19,3},{4,20},{20... | collective-permute-start | bytes 393224 | tf_op jit(solution)/shard_map/ppermute | solution.py:334
  67.4 3.8 %collective-permute-done.13.refs_0_ = bf16[256,256]{1,0:T(8,128)(2,1)S(1)} collective-permute-done((bf16[256,256]{1,0:T(8,128)(2,1)S(1)}, bf16[256,256]{1,0:T(8,128)(2,1)S(1)}, u32[]{:S(2)}, u32[]{:S(2)}) %collective-permute-start.13) | collective-permute-done | bytes 131104 | tf_op jit(solution)/shard_map/ppermute | solution.py:329
  71.2 0.6 shard_map.62.refs_0_
  71.8 1.6 %collective-permute-start.16 = (bf16[256,256]{1,0:T(8,128)(2,1)S(1)}, bf16[256,256]{1,0:T(8,128)(2,1)S(1)}, u32[]{:S(2)}, u32[]{:S(2)}) collective-permute-start(bf16[256,256]{1,0:T(8,128)(2,1)S(1)} %shard_map.62.refs_0_), channel_id=1, source_target_pairs={{0,16},{16,0},{1,17},{17,1},{2,18},{18,2},{3,19},{19,3},{4,20},{20... | collective-permute-start | bytes 393224 | tf_op jit(solution)/shard_map/ppermute | solution.py:334
  73.4 3.5 %collective-permute-done.16.refs_1_ = bf16[256,256]{1,0:T(8,128)(2,1)S(1)} collective-permute-done((bf16[256,256]{1,0:T(8,128)(2,1)S(1)}, bf16[256,256]{1,0:T(8,128)(2,1)S(1)}, u32[]{:S(2)}, u32[]{:S(2)}) %collective-permute-start.16) | collective-permute-done | bytes 131104 | tf_op jit(solution)/shard_map/ppermute | solution.py:334
  76.8 1.4 %shard_map.66 = bf16[512,512]{1,0:T(8,128)(2,1)} custom-call(s32[3]{0:T(128)S(1)} %pad_add_fusion.pos, bf16[256,256]{1,0:T(8,128)(2,1)S(1)} %shard_map.62.refs_0_, bf16[256,256]{1,0:T(8,128)(2,1)S(1)} %collective-permute-done.16.refs_1_, bf16[256,256]{1,0:T(8,128)(2,1)S(1)} %shard_map.65.refs_2_, bf16[256,256]{1,0:T(8,128)(2,1)S(1)} %collective-permute-done.24.refs_3_), custom_call_target="tpu_custom_call" | custom-call | bytes 1048576 | tf_op jit(solution)/shard_map/pallas_call | solution.py:33
  (25 shorter events, 0.1 us)
Async XLA Ops:
  0.0 0.7 copy-start.4
  0.0 3.7 %collective-permute-start.1 = (bf16[192,2048]{1,0:T(8,128)(2,1)}, bf16[192,2048]{1,0:T(8,128)(2,1)S(1)}, u32[]{:S(2)}, u32[]{:S(2)}) collective-permute-start(bf16[192,2048]{1,0:T(8,128)(2,1)} %rows.2), channel_id=1, source_target_pairs={{0,1},{1,0},{2,3},{3,2},{4,5},{5,4},{6,7},{7,6},{8,9},{9,8},{10,11... | collective-permute-start | bytes 2359304 | tf_op jit(solution)/shard_map/ppermute | solution.py:236
  0.5 34.8 %collective-permute-start.2 = (bf16[192,2048]{1,0:T(8,128)(2,1)}, bf16[192,2048]{1,0:T(8,128)(2,1)S(1)}, u32[]{:S(2)}, u32[]{:S(2)}) collective-permute-start(bf16[192,2048]{1,0:T(8,128)(2,1)} %rows.3), channel_id=1, source_target_pairs={{0,1},{1,0},{2,3},{3,2},{4,5},{5,4},{6,7},{7,6},{8,9},{9,8},{10,11... | collective-permute-start | bytes 2359304 | tf_op jit(solution)/shard_map/ppermute | solution.py:237
  0.7 3.1 %collective-permute-start = (s32[1,192]{1,0:T(1,128)S(1)}, s32[1,192]{1,0:T(1,128)S(1)}, u32[]{:S(2)}, u32[]{:S(2)}) collective-permute-start(s32[1,192]{1,0:T(1,128)S(1)} %bitcast.9), channel_id=1, source_target_pairs={{0,1},{1,0},{2,3},{3,2},{4,5},{5,4},{6,7},{7,6},{8,9},{9,8},{10,11... | collective-permute-start | bytes 2312 | tf_op jit(solution)/shard_map/ppermute | solution.py:235
  3.7 1.1 %copy-start = (bf16[192,2048]{1,0:T(8,128)(2,1)S(1)}, bf16[192,2048]{1,0:T(8,128)(2,1)}, u32[]{:S(2)}) copy-start(bf16[192,2048]{1,0:T(8,128)(2,1)} %rows.2) | copy-start | bytes 2359300
  4.9 5.9 %copy-start.2 = (bf16[1,512,512]{2,1,0:T(8,128)(2,1)S(1)}, bf16[1,512,512]{2,1,0:T(8,128)(2,1)}, u32[]{:S(2)}) copy-start(bf16[1,512,512]{2,1,0:T(8,128)(2,1)} %param.8) | copy-start | bytes 1572868
  4.9 5.9 %copy-start.3 = (bf16[1,16,512]{2,1,0:T(8,128)(2,1)S(1)}, bf16[1,16,512]{2,1,0:T(8,128)(2,1)}, u32[]{:S(2)}) copy-start(bf16[1,16,512]{2,1,0:T(8,128)(2,1)} %param.9) | copy-start | bytes 49156
  6.3 16.0 %collective-permute-start.6 = (bf16[120,1024]{1,0:T(8,128)(2,1)S(1)}, bf16[120,1024]{1,0:T(8,128)(2,1)S(1)}, u32[]{:S(2)}, u32[]{:S(2)}) collective-permute-start(bf16[120,1024]{1,0:T(8,128)(2,1)S(1)} %get-tuple-element.36), channel_id=1, source_target_pairs={{0,2},{1,3},{2,0},{3,1},{16,18},{17,19},{18,16},{19,17},{4,6},{5,7... | collective-permute-start | bytes 737288 | tf_op jit(solution)/shard_map/ppermute | solution.py:288
  9.3 13.7 %collective-permute-start.7 = (bf16[120,1024]{1,0:T(8,128)(2,1)S(1)}, bf16[120,1024]{1,0:T(8,128)(2,1)S(1)}, u32[]{:S(2)}, u32[]{:S(2)}) collective-permute-start(bf16[120,1024]{1,0:T(8,128)(2,1)S(1)} %get-tuple-element.37), channel_id=1, source_target_pairs={{0,16},{1,17},{2,18},{3,19},{16,0},{17,1},{18,2},{19,3},{4,20},{5,... | collective-permute-start | bytes 737288 | tf_op jit(solution)/shard_map/ppermute | solution.py:288
  10.8 13.1 %collective-permute-start.8 = (bf16[120,1024]{1,0:T(8,128)(2,1)S(1)}, bf16[120,1024]{1,0:T(8,128)(2,1)S(1)}, u32[]{:S(2)}, u32[]{:S(2)}) collective-permute-start(bf16[120,1024]{1,0:T(8,128)(2,1)S(1)} %get-tuple-element.38), channel_id=1, source_target_pairs={{0,18},{1,19},{2,16},{3,17},{16,2},{17,3},{18,0},{19,1},{4,22},{5,... | collective-permute-start | bytes 737288 | tf_op jit(solution)/shard_map/ppermute | solution.py:288
  11.5 7.2 %collective-permute-start.19 = (bf16[256,256]{1,0:T(8,128)(2,1)S(1)}, bf16[256,256]{1,0:T(8,128)(2,1)S(1)}, u32[]{:S(2)}, u32[]{:S(2)}) collective-permute-start(bf16[256,256]{1,0:T(8,128)(2,1)S(1)} %get-tuple-element.46.refs_0_), channel_id=1, source_target_pairs={{0,12},{4,8},{8,4},{12,0},{1,13},{5,9},{9,5},{13,1},{2,14},{6,10},... | collective-permute-start | bytes 393224 | tf_op jit(solution)/shard_map/ppermute | solution.py:257
  18.7 14.0 %collective-permute-start.18 = (bf16[256,256]{1,0:T(8,128)(2,1)S(1)}, bf16[256,256]{1,0:T(8,128)(2,1)S(1)}, u32[]{:S(2)}, u32[]{:S(2)}) collective-permute-start(bf16[256,256]{1,0:T(8,128)(2,1)S(1)} %get-tuple-element.46.refs_0_), channel_id=1, source_target_pairs={{0,8},{4,12},{8,0},{12,4},{1,9},{5,13},{9,1},{13,5},{2,10},{6,14},... | collective-permute-start | bytes 393224 | tf_op jit(solution)/shard_map/ppermute | solution.py:257
  22.4 10.3 %collective-permute-start.17 = (bf16[256,256]{1,0:T(8,128)(2,1)S(1)}, bf16[256,256]{1,0:T(8,128)(2,1)S(1)}, u32[]{:S(2)}, u32[]{:S(2)}) collective-permute-start(bf16[256,256]{1,0:T(8,128)(2,1)S(1)} %get-tuple-element.46.refs_0_), channel_id=1, source_target_pairs={{0,4},{4,0},{8,12},{12,8},{1,5},{5,1},{9,13},{13,9},{2,6},{6,2},{1... | collective-permute-start | bytes 393224 | tf_op jit(solution)/shard_map/ppermute | solution.py:257
  22.9 15.2 %collective-permute-start.11 = (bf16[256,256]{1,0:T(8,128)(2,1)S(1)}, bf16[256,256]{1,0:T(8,128)(2,1)S(1)}, u32[]{:S(2)}, u32[]{:S(2)}) collective-permute-start(bf16[256,256]{1,0:T(8,128)(2,1)S(1)} %get-tuple-element.39.refs_0_), channel_id=1, source_target_pairs={{0,12},{4,8},{8,4},{12,0},{1,13},{5,9},{9,5},{13,1},{2,14},{6,10},... | collective-permute-start | bytes 393224 | tf_op jit(solution)/shard_map/ppermute | solution.py:257
  23.8 14.8 %collective-permute-start.10 = (bf16[256,256]{1,0:T(8,128)(2,1)S(1)}, bf16[256,256]{1,0:T(8,128)(2,1)S(1)}, u32[]{:S(2)}, u32[]{:S(2)}) collective-permute-start(bf16[256,256]{1,0:T(8,128)(2,1)S(1)} %get-tuple-element.39.refs_0_), channel_id=1, source_target_pairs={{0,8},{4,12},{8,0},{12,4},{1,9},{5,13},{9,1},{13,5},{2,10},{6,14},... | collective-permute-start | bytes 393224 | tf_op jit(solution)/shard_map/ppermute | solution.py:257
  26.5 8.8 %copy-start.1 = (bf16[192,2048]{1,0:T(8,128)(2,1)S(1)}, bf16[192,2048]{1,0:T(8,128)(2,1)}, u32[]{:S(2)}) copy-start(bf16[192,2048]{1,0:T(8,128)(2,1)} %rows.3) | copy-start | bytes 2359300
  32.7 8.4 %collective-permute-start.9 = (bf16[256,256]{1,0:T(8,128)(2,1)S(1)}, bf16[256,256]{1,0:T(8,128)(2,1)S(1)}, u32[]{:S(2)}, u32[]{:S(2)}) collective-permute-start(bf16[256,256]{1,0:T(8,128)(2,1)S(1)} %get-tuple-element.39.refs_0_), channel_id=1, source_target_pairs={{0,4},{4,0},{8,12},{12,8},{1,5},{5,1},{9,13},{13,9},{2,6},{6,2},{1... | collective-permute-start | bytes 393224 | tf_op jit(solution)/shard_map/ppermute | solution.py:257
  33.7 19.0 %collective-permute-start.20 = (bf16[512,256]{1,0:T(8,128)(2,1)S(1)}, bf16[512,256]{1,0:T(8,128)(2,1)S(1)}, u32[]{:S(2)}, u32[]{:S(2)}) collective-permute-start(bf16[512,256]{1,0:T(8,128)(2,1)S(1)} %get-tuple-element.48), channel_id=1, source_target_pairs={{0,16},{16,0},{1,17},{17,1},{2,18},{18,2},{3,19},{19,3},{4,20},{20... | collective-permute-start | bytes 786440 | tf_op jit(solution)/shard_map/ppermute | solution.py:315
  36.5 8.6 %collective-permute-start.3 = (bf16[120,1024]{1,0:T(8,128)(2,1)S(1)}, bf16[120,1024]{1,0:T(8,128)(2,1)S(1)}, u32[]{:S(2)}, u32[]{:S(2)}) collective-permute-start(bf16[120,1024]{1,0:T(8,128)(2,1)S(1)} %get-tuple-element.32), channel_id=1, source_target_pairs={{0,2},{1,3},{2,0},{3,1},{16,18},{17,19},{18,16},{19,17},{4,6},{5,7... | collective-permute-start | bytes 737288 | tf_op jit(solution)/shard_map/ppermute | solution.py:288
  38.1 8.8 %collective-permute-start.4 = (bf16[120,1024]{1,0:T(8,128)(2,1)S(1)}, bf16[120,1024]{1,0:T(8,128)(2,1)S(1)}, u32[]{:S(2)}, u32[]{:S(2)}) collective-permute-start(bf16[120,1024]{1,0:T(8,128)(2,1)S(1)} %get-tuple-element.33), channel_id=1, source_target_pairs={{0,16},{1,17},{2,18},{3,19},{16,0},{17,1},{18,2},{19,3},{4,20},{5,... | collective-permute-start | bytes 737288 | tf_op jit(solution)/shard_map/ppermute | solution.py:288
  38.7 13.1 %collective-permute-start.5 = (bf16[120,1024]{1,0:T(8,128)(2,1)S(1)}, bf16[120,1024]{1,0:T(8,128)(2,1)S(1)}, u32[]{:S(2)}, u32[]{:S(2)}) collective-permute-start(bf16[120,1024]{1,0:T(8,128)(2,1)S(1)} %get-tuple-element.34), channel_id=1, source_target_pairs={{0,18},{1,19},{2,16},{3,17},{16,2},{17,3},{18,0},{19,1},{4,22},{5,... | collective-permute-start | bytes 737288 | tf_op jit(solution)/shard_map/ppermute | solution.py:288
  42.1 15.4 %collective-permute-start.12 = (bf16[512,256]{1,0:T(8,128)(2,1)S(1)}, bf16[512,256]{1,0:T(8,128)(2,1)S(1)}, u32[]{:S(2)}, u32[]{:S(2)}) collective-permute-start(bf16[512,256]{1,0:T(8,128)(2,1)S(1)} %get-tuple-element.41), channel_id=1, source_target_pairs={{0,16},{16,0},{1,17},{17,1},{2,18},{18,2},{3,19},{19,3},{4,20},{20... | collective-permute-start | bytes 786440 | tf_op jit(solution)/shard_map/ppermute | solution.py:315
  53.8 10.2 %collective-permute-start.21 = (bf16[256,256]{1,0:T(8,128)(2,1)S(1)}, bf16[256,256]{1,0:T(8,128)(2,1)S(1)}, u32[]{:S(2)}, u32[]{:S(2)}) collective-permute-start(bf16[256,256]{1,0:T(8,128)(2,1)S(1)} %get-tuple-element.50), channel_id=1, source_target_pairs={{0,8},{4,12},{8,0},{12,4},{1,9},{5,13},{9,1},{13,5},{2,10},{6,14},... | collective-permute-start | bytes 393224 | tf_op jit(solution)/shard_map/ppermute | solution.py:329
  55.9 8.1 %collective-permute-start.22 = (bf16[256,256]{1,0:T(8,128)(2,1)S(1)}, bf16[256,256]{1,0:T(8,128)(2,1)S(1)}, u32[]{:S(2)}, u32[]{:S(2)}) collective-permute-start(bf16[256,256]{1,0:T(8,128)(2,1)S(1)} %get-tuple-element.51), channel_id=1, source_target_pairs={{0,12},{4,8},{8,4},{12,0},{1,13},{5,9},{9,5},{13,1},{2,14},{6,10},... | collective-permute-start | bytes 393224 | tf_op jit(solution)/shard_map/ppermute | solution.py:329
  57.5 8.1 %collective-permute-start.23 = (bf16[256,256]{1,0:T(8,128)(2,1)S(1)}, bf16[256,256]{1,0:T(8,128)(2,1)S(1)}, u32[]{:S(2)}, u32[]{:S(2)}) collective-permute-start(bf16[256,256]{1,0:T(8,128)(2,1)S(1)} %get-tuple-element.52), channel_id=1, source_target_pairs={{0,4},{4,0},{8,12},{12,8},{1,5},{5,1},{9,13},{13,9},{2,6},{6,2},{1... | collective-permute-start | bytes 393224 | tf_op jit(solution)/shard_map/ppermute | solution.py:329
  58.5 12.7 %collective-permute-start.13 = (bf16[256,256]{1,0:T(8,128)(2,1)S(1)}, bf16[256,256]{1,0:T(8,128)(2,1)S(1)}, u32[]{:S(2)}, u32[]{:S(2)}) collective-permute-start(bf16[256,256]{1,0:T(8,128)(2,1)S(1)} %get-tuple-element.43), channel_id=1, source_target_pairs={{0,8},{4,12},{8,0},{12,4},{1,9},{5,13},{9,1},{13,5},{2,10},{6,14},... | collective-permute-start | bytes 393224 | tf_op jit(solution)/shard_map/ppermute | solution.py:329
  61.3 9.9 %collective-permute-start.14 = (bf16[256,256]{1,0:T(8,128)(2,1)S(1)}, bf16[256,256]{1,0:T(8,128)(2,1)S(1)}, u32[]{:S(2)}, u32[]{:S(2)}) collective-permute-start(bf16[256,256]{1,0:T(8,128)(2,1)S(1)} %get-tuple-element.44), channel_id=1, source_target_pairs={{0,12},{4,8},{8,4},{12,0},{1,13},{5,9},{9,5},{13,1},{2,14},{6,10},... | collective-permute-start | bytes 393224 | tf_op jit(solution)/shard_map/ppermute | solution.py:329
  64.0 7.2 %collective-permute-start.15 = (bf16[256,256]{1,0:T(8,128)(2,1)S(1)}, bf16[256,256]{1,0:T(8,128)(2,1)S(1)}, u32[]{:S(2)}, u32[]{:S(2)}) collective-permute-start(bf16[256,256]{1,0:T(8,128)(2,1)S(1)} %get-tuple-element.45), channel_id=1, source_target_pairs={{0,4},{4,0},{8,12},{12,8},{1,5},{5,1},{9,13},{13,9},{2,6},{6,2},{1... | collective-permute-start | bytes 393224 | tf_op jit(solution)/shard_map/ppermute | solution.py:329
  66.1 7.2 %collective-permute-start.24 = (bf16[256,256]{1,0:T(8,128)(2,1)S(1)}, bf16[256,256]{1,0:T(8,128)(2,1)S(1)}, u32[]{:S(2)}, u32[]{:S(2)}) collective-permute-start(bf16[256,256]{1,0:T(8,128)(2,1)S(1)} %shard_map.65.refs_2_), channel_id=1, source_target_pairs={{0,16},{16,0},{1,17},{17,1},{2,18},{18,2},{3,19},{19,3},{4,20},{20... | collective-permute-start | bytes 393224 | tf_op jit(solution)/shard_map/ppermute | solution.py:334
  71.8 5.0 %collective-permute-start.16 = (bf16[256,256]{1,0:T(8,128)(2,1)S(1)}, bf16[256,256]{1,0:T(8,128)(2,1)S(1)}, u32[]{:S(2)}, u32[]{:S(2)}) collective-permute-start(bf16[256,256]{1,0:T(8,128)(2,1)S(1)} %shard_map.62.refs_0_), channel_id=1, source_target_pairs={{0,16},{16,0},{1,17},{17,1},{2,18},{18,2},{3,19},{19,3},{4,20},{20... | collective-permute-start | bytes 393224 | tf_op jit(solution)/shard_map/ppermute | solution.py:334

commit v3 on v2

--- a/solution.py
+++ b/solution.py
@@ -7,7 +7,7 @@
 from jax.sharding import PartitionSpec as P
 
 QB = 32
-CHUNKS = 2
+SPLITS = ((1, 1), (2,))
 F32 = jnp.float32
 BF16 = jnp.bfloat16
 
@@ -29,21 +29,18 @@
 def call(body, outs, scalars, args, scratch=(), flops=0, space=pltpu.VMEM, target=pltpu.VMEM):
     moved = sum(a.size * a.dtype.itemsize for a in args)
     moved += sum(o.size * o.dtype.itemsize for o in outs)
+    spaces = space if isinstance(space, list) else [space] * len(args)
     room = 2 * moved + (8 << 20)
     return pl.pallas_call(
         body,
         out_shape=outs,
         in_specs=[pl.BlockSpec(memory_space=pltpu.SMEM)]
-        + [pl.BlockSpec(memory_space=space)] * len(args),
+        + [pl.BlockSpec(memory_space=kind) for kind in spaces],
         out_specs=[pl.BlockSpec(memory_space=target)] * len(outs),
         scratch_shapes=list(scratch),
         compiler_params=pltpu.CompilerParams(vmem_limit_bytes=min(room, 60 << 20)),
         cost_estimate=pl.CostEstimate(flops=flops, bytes_accessed=moved, transcendentals=0),
     )(scalars, *args)
-
-
-def partition(values):
-    return values[0], values[1], values[2:]
 
 
 def node_order(nodes):
@@ -128,12 +125,15 @@
                 out[:, b * width : (b + 1) * width] = got[k * stride : k * stride + rows]
 
 
-def first_body(dims, stride, blocks, pos, ids, ids_pair, rows, rows_pair, *outs):
-    select_body(dims, stride, pos, ids, ids_pair, *outs[:2])
-    place_rows(dims, stride, blocks, pos, outs[:2], (rows, rows_pair), outs[2:])
-
-
-def later_body(dims, stride, blocks, pos, pick, pick_pair, rows, rows_pair, *outs):
+def choose_body(dims, stride, pos, ids, ids_pair, rows, *refs):
+    picks, near, sem = refs[:2], refs[2], refs[3]
+    move = pltpu.make_async_copy(rows, near, sem)
+    move.start()
+    select_body(dims, stride, pos, ids, ids_pair, *picks)
+    move.wait()
+
+
+def route_body(dims, stride, blocks, pos, pick, pick_pair, rows, rows_pair, *outs):
     place_rows(dims, stride, blocks, pos, (pick, pick_pair), (rows, rows_pair), outs)
 
 
@@ -161,14 +161,18 @@
 
 def up_body(dims, pos, rows, *refs):
     _, nodes, _ = dims
-    weights, (kept, sent), held = refs[:nodes], refs[nodes : nodes + 2], refs[-1]
+    weights, outs, held = refs[:nodes], refs[nodes:-1], refs[-1]
     mine = weights[0].shape[0]
     for s in range(nodes):
         at = pl.multiple_of(traced_origin(pos[1], s, nodes) * mine, 16)
         held[pl.ds(at, mine), :] = weights[s][...]
-    pre = jnp.dot(rows[...], held[...], preferred_element_type=F32)
-    kept[...] = pre
-    sent[...] = pre.astype(BF16)
+    begin = 0
+    for kept, sent in zip(outs[::2], outs[1::2]):
+        end = begin + kept.shape[1]
+        pre = jnp.dot(rows[...], held[:, begin:end], preferred_element_type=F32)
+        kept[...] = pre
+        sent[...] = pre.astype(BF16)
+        begin = end
 
 
 def down_body(dims, factor, pos, turned, kept, *refs):
@@ -192,16 +196,18 @@
     refs[-1][...] = total.astype(BF16)
 
 
-def lay_body(dims, chunks, pos, *refs):
+def lay_body(dims, pos, *refs):
     copies = dims[0]
     parts, out, sems = refs[:-2], refs[-2], refs[-1]
-    mine, width = parts[0].shape
     moves = []
-    for j in range(copies):
-        at = pl.multiple_of(traced_origin(pos[0], j, copies) * mine, 16)
-        for i in range(chunks):
-            spot = out.at[pl.ds(at, mine), pl.ds(i * width, width)]
+    begin = 0
+    for i in range(len(parts) // copies):
+        mine, width = parts[i * copies].shape
+        for j in range(copies):
+            at = pl.multiple_of(traced_origin(pos[0], j, copies) * mine, 16)
+            spot = out.at[pl.ds(at, mine), pl.ds(begin, width)]
             moves.append(pltpu.make_async_copy(parts[i * copies + j], spot, sems.at[i * copies + j]))
+        begin += width
     for move in moves:
         move.start()
     for move in moves:
@@ -219,7 +225,7 @@
     shard, hidden = w1_codes.shape[1:]
     mine = shard // copies
     part = features // copies
-    width = hidden // CHUNKS
+    width = hidden // len(SPLITS)
     everyone = copies * pairs * stride
     pos = jnp.stack([lax.axis_index(a) for a in ("dp", "node", "local")]).astype(jnp.int32)
 
@@ -232,15 +238,15 @@
         )
     chosen = expert_of.reshape(1, count)
     swap = [(i, i ^ 1) for i in range(locals_)]
+    tokens_pair = lax.ppermute(tokens, "local", swap)
     chosen_pair = lax.ppermute(chosen, "local", swap)
-    tokens_pair = lax.ppermute(tokens, "local", swap)
     cotangent_pair = lax.ppermute(cotangent, "local", swap)
 
     weights = call(
         dequant_body,
-        [shape(mine, width, BF16)] * CHUNKS,
+        [shape(mine, width, BF16)] * len(SPLITS),
         pos,
-        [w1_codes[0], w1_scales[0]],
+        [pltpu.with_memory_space_constraint(a[0], pltpu.HBM) for a in (w1_codes, w1_scales)],
         [
             pltpu.VMEM((mine, hidden), BF16),
             pltpu.VMEM((shard // QB, hidden), BF16),
@@ -257,24 +263,26 @@
             got[s] = lax.ppermute(chunk, "node", [(a, mate(a, s, nodes)) for a in range(nodes)])
         held.append([got[s] for s in range(nodes)])
 
-    flops = 4 * pairs * stride * count * features
-    sent = [shape(sent_rows, part, BF16)] * (copies * pairs)
-    *picks, pieces_x = partition(
-        call(
-            functools.partial(first_body, dims, stride, blocks),
-            [shape(pairs * stride, count, BF16)] * 2 + sent,
+    *picks, tokens = call(
+        functools.partial(choose_body, dims, stride),
+        [shape(pairs * stride, count, BF16)] * 2 + [shape(count, features, BF16)],
+        pos,
+        [chosen, chosen_pair, pltpu.with_memory_space_constraint(tokens, pltpu.HBM)],
+        [pltpu.SemaphoreType.DMA],
+        space=[pltpu.VMEM, pltpu.VMEM, pltpu.HBM],
+    )
+
+    def route(rows, rows_pair):
+        return call(
+            functools.partial(route_body, dims, stride, blocks),
+            [shape(sent_rows, part, BF16)] * (copies * pairs),
             pos,
-            [chosen, chosen_pair, tokens, tokens_pair],
-            flops=flops,
+            [*picks, rows, rows_pair],
+            flops=4 * pairs * stride * count * features,
         )
-    )
-    pieces_y = call(
-        functools.partial(later_body, dims, stride, blocks),
-        sent,
-        pos,
-        [*picks, cotangent, cotangent_pair],
-        flops=flops,
-    )
+
+    pieces_x = route(tokens, tokens_pair)
+    pieces_y = route(cotangent, cotangent_pair)
 
     def exchange(pieces):
         moved = list(pieces)
@@ -301,43 +309,47 @@
         [pltpu.VMEM((everyone, part), BF16)],
     )
     factor = float(count * copies * nodes) ** (-0.5)
-    finished = []
-    for i in range(CHUNKS):
-        kept, sent = call(
+    groups = []
+    for i, split in enumerate(SPLITS):
+        widths = [width * share // sum(split) for share in split]
+        parts = call(
             functools.partial(up_body, dims),
-            [shape(everyone, width, F32), shape(everyone, width, BF16)],
+            [shape(everyone, w, kind) for w in widths for kind in (F32, BF16)],
             pos,
             [rows_x] + held[i],
             [pltpu.VMEM((part, width), BF16)],
             flops=2 * everyone * part * width,
         )
+        groups += list(zip(widths, parts[::2], parts[1::2]))
+    finished = []
+    for wide, kept, sent in groups:
         if copies == 2:
             others = [lax.ppermute(sent, "dp", [(0, 1), (1, 0)])]
         else:
             kept, others = lax.psum(kept, "dp"), []
         terms = call(
             functools.partial(down_body, dims, factor),
-            [shape(mine, width, F32)] + [shape(mine, width, BF16)] * (nodes - 1),
+            [shape(mine, wide, F32)] + [shape(mine, wide, BF16)] * (nodes - 1),
             pos,
             [turned, kept] + others,
-            [pltpu.VMEM((everyone, width), BF16)],
-            flops=2 * everyone * part * width,
+            [pltpu.VMEM((everyone, wide), BF16)],
+            flops=2 * everyone * part * wide,
         )
         arrived = []
         for s in order:
             links = [(a, mate(a, s, nodes)) for a in range(nodes)]
             arrived.append(lax.ppermute(terms[s], "node", links))
-        (summed,) = call(sum_body, [shape(mine, width, BF16)], pos, [terms[0]] + arrived)
+        (summed,) = call(sum_body, [shape(mine, wide, BF16)], pos, [terms[0]] + arrived)
         finished.append(summed)
         for j in range(1, copies):
             links = [(a, mate(a, j, copies)) for a in range(copies)]
             finished.append(lax.ppermute(summed, "dp", links))
     (result,) = call(
-        functools.partial(lay_body, dims, CHUNKS),
+        functools.partial(lay_body, dims),
         [shape(shard, hidden, BF16)],
         pos,
         finished,
-        [pltpu.SemaphoreType.DMA((CHUNKS * copies,))],
+        [pltpu.SemaphoreType.DMA((len(finished),))],
         target=pltpu.HBM,
     )
     return result[None]

time: 78.4 us -> 82.7 us (1.055)
  starting transfers between devices: 34.5 us -> 42.8 us
  waiting for transfers between devices: 30.7 us -> 23.6 us
  Pallas kernels: 11.5 us -> 15.8 us
  local copies, waits for them, and re-layouts: 1.27 us -> 0.13 us
    ppermute x6 -> x9, starting transfers between devices: 8.16 us -> 13.8 us  [on_device(): arrived.append(lax.ppermute(terms[s], 'node', links))]
    pallas_call x12 -> x15, Pallas kernels: 11.5 us -> 15.8 us  [call(): pl.pallas_call(body, out_shape=outs, in_specs=[pl.BlockSpec(memory_space=...]
    ppermute x6, waiting for transfers between devices: 9.24 us -> 5.26 us  [on_device(): lax.ppermute(chunk, 'node', [(a, mate(a, s, nodes)) for a in range(nodes)])]
    ppermute x6, waiting for transfers between devices: 9.11 us -> 7.47 us  [exchange(): moved[at] = lax.ppermute(pieces[at], ('dp', 'local'), links)]
    ppermute x2 -> x3, starting transfers between devices: 2.15 us -> 3.65 us  [on_device(): others = [lax.ppermute(sent, 'dp', [(0, 1), (1, 0)])]]
    ppermute x6, starting transfers between devices: 11.3 us -> 12.5 us  [on_device(): lax.ppermute(chunk, 'node', [(a, mate(a, s, nodes)) for a in range(nodes)])]
    unnamed x10 -> x4, local copies, waits for them, and re-layouts: 1.27 us -> 0.13 us
    ppermute x6, starting transfers between devices: 9.01 us -> 8.09 us  [exchange(): moved[at] = lax.ppermute(pieces[at], ('dp', 'local'), links)]
  transfers between devices with their start and end apart: 25 -> 30, of which waited for: 10 -> 10; matrix products, arithmetic and copies ran while one was open for 0% -> 0% of each run, Pallas kernels for 13% -> 17%
where the time goes in v3:
time: 82.7 us; the launch traced here: 82.5 us
  starting transfers between devices  42.8 us (52%)
  waiting for transfers between devices  23.6 us (29%)
  Pallas kernels  15.8 us (19%)
    pallas_call x15, Pallas kernels, call(): pl.pallas_call(body, out_shape=outs, in_specs=[pl.BlockSpec(memory_space=...  15.8 us
    ppermute x9, starting transfers between devices, on_device(): arrived.append(lax.ppermute(terms[s], 'node', links))  13.8 us
    ppermute x6, starting transfers between devices, on_device(): lax.ppermute(chunk, 'node', [(a, mate(a, s, nodes)) for a in range(nodes)])  12.5 us
    ppermute x6, starting transfers between devices, exchange(): moved[at] = lax.ppermute(pieces[at], ('dp', 'local'), links)  8.09 us
    ppermute x6, waiting for transfers between devices, exchange(): moved[at] = lax.ppermute(pieces[at], ('dp', 'local'), links)  7.47 us
    ppermute x9, waiting for transfers between devices, on_device(): arrived.append(lax.ppermute(terms[s], 'node', links))  5.55 us
    ppermute x6, waiting for transfers between devices, on_device(): lax.ppermute(chunk, 'node', [(a, mate(a, s, nodes)) for a in range(nodes)])  5.26 us
    ppermute x3, starting transfers between devices, on_device(): finished.append(lax.ppermute(summed, 'dp', links))  3.72 us
  transfers between devices with their start and end apart: 30, of which 10 were waited for; matrix products, arithmetic and copies ran while one was open for 0% of the time, Pallas kernels for 17%

profile of v3, /device:TPU:0, one launch (start us, length us, event | category | flops | bytes accessed | tf_op | source)
XLA Modules:
  0.0 82.5 jit_solution(10498501652577989083)
XLA Ops:
  0.0 0.5 collective-permute-start.5
  0.7 0.5 collective-permute-start
  1.2 2.5 %collective-permute-done.ids_pair = s32[1,192]{1,0:T(1,128)S(1)} collective-permute-done((s32[1,192]{1,0:T(1,128)S(1)}, s32[1,192]{1,0:T(1,128)S(1)}, u32[]{:S(2)}, u32[]{:S(2)}) %collective-permute-start) | collective-permute-done | bytes 800 | tf_op jit(solution)/shard_map/ppermute | solution.py:242
  3.7 1.7 %shard_map.55 = (bf16[256,192]{1,0:T(8,128)(2,1)S(1)}, bf16[256,192]{1,0:T(8,128)(2,1)S(1)}, bf16[192,2048]{1,0:T(8,128)(2,1)S(1)}) custom-call(s32[3]{0:T(128)S(1)} %pad_add_fusion.pos, s32[1,192]{1,0:T(1,128)S(1)} %bitcast.8, s32[1,192]{1,0:T(1,128)S(1)} %collective-permute-done.ids_pair, bf16[192,2048]{1,0:T(8,128)(2,1)} %rows.2), custom_call_target="tpu_custom_call" | custom-call | bytes 1771008 | tf_op jit(solution)/shard_map/pallas_call | solution.py:34
  5.5 1.3 %shard_map.58 = (bf16[120,1024]{1,0:T(8,128)(2,1)S(1)}, bf16[120,1024]{1,0:T(8,128)(2,1)S(1)}, bf16[120,1024]{1,0:T(8,128)(2,1)S(1)}, bf16[120,1024]{1,0:T(8,128)(2,1)S(1)}) custom-call(s32[3]{0:T(128)S(1)} %pad_add_fusion.pos, bf16[256,192]{1,0:T(8,128)(2,1)S(1)} %get-tuple-element.36.pick, bf16[256,192]{1,0:T(8,128)(2,1)S(1)} %get-tuple-element.37.pick_pair, ...), custom_call_target="tpu_custom_call" | custom-call | flops 402653184 | bytes 2752512 | tf_op jit(solution)/shard_map/pallas_call | solution.py:34
  6.7 2.9 %collective-permute-start.6 = (bf16[120,1024]{1,0:T(8,128)(2,1)S(1)}, bf16[120,1024]{1,0:T(8,128)(2,1)S(1)}, u32[]{:S(2)}, u32[]{:S(2)}) collective-permute-start(bf16[120,1024]{1,0:T(8,128)(2,1)S(1)} %get-tuple-element.44), channel_id=1, source_target_pairs={{0,2},{1,3},{2,0},{3,1},{16,18},{17,19},{18,16},{19,17},{4,6},{5,7... | collective-permute-start | bytes 737288 | tf_op jit(solution)/shard_map/ppermute | solution.py:296
  9.7 1.5 %collective-permute-start.7 = (bf16[120,1024]{1,0:T(8,128)(2,1)S(1)}, bf16[120,1024]{1,0:T(8,128)(2,1)S(1)}, u32[]{:S(2)}, u32[]{:S(2)}) collective-permute-start(bf16[120,1024]{1,0:T(8,128)(2,1)S(1)} %get-tuple-element.45), channel_id=1, source_target_pairs={{0,16},{1,17},{2,18},{3,19},{16,0},{17,1},{18,2},{19,3},{4,20},{5,... | collective-permute-start | bytes 737288 | tf_op jit(solution)/shard_map/ppermute | solution.py:296
  11.2 1.6 %shard_map.60 = (bf16[256,256]{1,0:T(8,128)(2,1)S(1)}, bf16[256,256]{1,0:T(8,128)(2,1)S(1)}) custom-call(s32[3]{0:T(128)S(1)} %pad_add_fusion.pos, bf16[512,512]{1,0:T(8,128)(2,1)} %bitcast.9, bf16[16,512]{1,0:T(8,128)(2,1)} %bitcast.10), custom_call_target="tpu_custom_call" | custom-call | bytes 802816 | tf_op jit(solution)/shard_map/pallas_call | solution.py:34
  12.8 2.1 %collective-permute-start.22 = (bf16[256,256]{1,0:T(8,128)(2,1)S(1)}, bf16[256,256]{1,0:T(8,128)(2,1)S(1)}, u32[]{:S(2)}, u32[]{:S(2)}) collective-permute-start(bf16[256,256]{1,0:T(8,128)(2,1)S(1)} %get-tuple-element.60.refs_0_), channel_id=1, source_target_pairs={{0,4},{4,0},{8,12},{12,8},{1,5},{5,1},{9,13},{13,9},{2,6},{6,2},{1... | collective-permute-start | bytes 393224 | tf_op jit(solution)/shard_map/ppermute | solution.py:263
  14.9 2.6 %collective-permute-start.23 = (bf16[256,256]{1,0:T(8,128)(2,1)S(1)}, bf16[256,256]{1,0:T(8,128)(2,1)S(1)}, u32[]{:S(2)}, u32[]{:S(2)}) collective-permute-start(bf16[256,256]{1,0:T(8,128)(2,1)S(1)} %get-tuple-element.60.refs_0_), channel_id=1, source_target_pairs={{0,8},{4,12},{8,0},{12,4},{1,9},{5,13},{9,1},{13,5},{2,10},{6,14},... | collective-permute-start | bytes 393224 | tf_op jit(solution)/shard_map/ppermute | solution.py:263
  17.5 2.3 %collective-permute-start.24 = (bf16[256,256]{1,0:T(8,128)(2,1)S(1)}, bf16[256,256]{1,0:T(8,128)(2,1)S(1)}, u32[]{:S(2)}, u32[]{:S(2)}) collective-permute-start(bf16[256,256]{1,0:T(8,128)(2,1)S(1)} %get-tuple-element.60.refs_0_), channel_id=1, source_target_pairs={{0,12},{4,8},{8,4},{12,0},{1,13},{5,9},{9,5},{13,1},{2,14},{6,10},... | collective-permute-start | bytes 393224 | tf_op jit(solution)/shard_map/ppermute | solution.py:263
  20.1 2.4 %collective-permute-done.8.refs_3_ = bf16[120,1024]{1,0:T(8,128)(2,1)S(1)} collective-permute-done((bf16[120,1024]{1,0:T(8,128)(2,1)S(1)}, bf16[120,1024]{1,0:T(8,128)(2,1)S(1)}, u32[]{:S(2)}, u32[]{:S(2)}) %collective-permute-start.8) | collective-permute-done | bytes 245792 | tf_op jit(solution)/shard_map/ppermute | solution.py:296
  22.5 2.7 %collective-permute-start.10 = (bf16[256,256]{1,0:T(8,128)(2,1)S(1)}, bf16[256,256]{1,0:T(8,128)(2,1)S(1)}, u32[]{:S(2)}, u32[]{:S(2)}) collective-permute-start(bf16[256,256]{1,0:T(8,128)(2,1)S(1)} %get-tuple-element.47.refs_0_), channel_id=1, source_target_pairs={{0,8},{4,12},{8,0},{12,4},{1,9},{5,13},{9,1},{13,5},{2,10},{6,14},... | collective-permute-start | bytes 393224 | tf_op jit(solution)/shard_map/ppermute | solution.py:263
  25.2 1.3 %shard_map.56 = (bf16[120,1024]{1,0:T(8,128)(2,1)S(1)}, bf16[120,1024]{1,0:T(8,128)(2,1)S(1)}, bf16[120,1024]{1,0:T(8,128)(2,1)S(1)}, bf16[120,1024]{1,0:T(8,128)(2,1)S(1)}) custom-call(s32[3]{0:T(128)S(1)} %pad_add_fusion.pos, bf16[256,192]{1,0:T(8,128)(2,1)S(1)} %get-tuple-element.36.pick, bf16[256,192]{1,0:T(8,128)(2,1)S(1)} %get-tuple-element.37.pick_pair, ...), custom_call_target="tpu_custom_call" | custom-call | flops 402653184 | bytes 2752512 | tf_op jit(solution)/shard_map/pallas_call | solution.py:34
  26.5 0.6 shard_map.59.rows
  27.1 1.6 %collective-permute-start.2 = (bf16[120,1024]{1,0:T(8,128)(2,1)S(1)}, bf16[120,1024]{1,0:T(8,128)(2,1)S(1)}, u32[]{:S(2)}, u32[]{:S(2)}) collective-permute-start(bf16[120,1024]{1,0:T(8,128)(2,1)S(1)} %get-tuple-element.39), channel_id=1, source_target_pairs={{0,2},{1,3},{2,0},{3,1},{16,18},{17,19},{18,16},{19,17},{4,6},{5,7... | collective-permute-start | bytes 737288 | tf_op jit(solution)/shard_map/ppermute | solution.py:296
  28.7 1.0 %shard_map.66 = (f32[512,256]{1,0:T(8,128)S(1)}, bf16[512,256]{1,0:T(8,128)(2,1)S(1)}) custom-call(s32[3]{0:T(128)S(1)} %pad_add_fusion.pos, bf16[512,1024]{1,0:T(8,128)(2,1)S(1)} %shard_map.59.rows, bf16[256,256]{1,0:T(8,128)(2,1)S(1)} %get-tuple-element.60.refs_0_, bf16[256,256]{1,0:T(8,128)(2,1)S(1)} %collective-permute-done.22.refs_1_, ...), custom_call_target="tpu_custom_call" | custom-call | flops 268435456 | bytes 2359296 | tf_op jit(solution)/shard_map/pallas_call | solution.py:34
  29.7 1.6 %collective-permute-start.25 = (bf16[512,256]{1,0:T(8,128)(2,1)S(1)}, bf16[512,256]{1,0:T(8,128)(2,1)S(1)}, u32[]{:S(2)}, u32[]{:S(2)}) collective-permute-start(bf16[512,256]{1,0:T(8,128)(2,1)S(1)} %get-tuple-element.62), channel_id=1, source_target_pairs={{0,16},{16,0},{1,17},{17,1},{2,18},{18,2},{3,19},{19,3},{4,20},{20... | collective-permute-start | bytes 786440 | tf_op jit(solution)/shard_map/ppermute | solution.py:327
  31.3 0.5 collective-permute-start.3
  31.8 1.5 %collective-permute-start.4 = (bf16[120,1024]{1,0:T(8,128)(2,1)S(1)}, bf16[120,1024]{1,0:T(8,128)(2,1)S(1)}, u32[]{:S(2)}, u32[]{:S(2)}) collective-permute-start(bf16[120,1024]{1,0:T(8,128)(2,1)S(1)} %get-tuple-element.41), channel_id=1, source_target_pairs={{0,18},{1,19},{2,16},{3,17},{16,2},{17,3},{18,0},{19,1},{4,22},{5,... | collective-permute-start | bytes 737288 | tf_op jit(solution)/shard_map/ppermute | solution.py:296
  33.3 1.0 %collective-permute-done.10.refs_2_ = bf16[256,256]{1,0:T(8,128)(2,1)S(1)} collective-permute-done((bf16[256,256]{1,0:T(8,128)(2,1)S(1)}, bf16[256,256]{1,0:T(8,128)(2,1)S(1)}, u32[]{:S(2)}, u32[]{:S(2)}) %collective-permute-start.10) | collective-permute-done | bytes 131104 | tf_op jit(solution)/shard_map/ppermute | solution.py:263
  34.3 2.5 %collective-permute-start.11 = (bf16[256,256]{1,0:T(8,128)(2,1)S(1)}, bf16[256,256]{1,0:T(8,128)(2,1)S(1)}, u32[]{:S(2)}, u32[]{:S(2)}) collective-permute-start(bf16[256,256]{1,0:T(8,128)(2,1)S(1)} %get-tuple-element.47.refs_0_), channel_id=1, source_target_pairs={{0,12},{4,8},{8,4},{12,0},{1,13},{5,9},{9,5},{13,1},{2,14},{6,10},... | collective-permute-start | bytes 393224 | tf_op jit(solution)/shard_map/ppermute | solution.py:263
  36.7 4.3 %collective-permute-done.11.refs_3_ = bf16[256,256]{1,0:T(8,128)(2,1)S(1)} collective-permute-done((bf16[256,256]{1,0:T(8,128)(2,1)S(1)}, bf16[256,256]{1,0:T(8,128)(2,1)S(1)}, u32[]{:S(2)}, u32[]{:S(2)}) %collective-permute-start.11) | collective-permute-done | bytes 131104 | tf_op jit(solution)/shard_map/ppermute | solution.py:263
  41.0 1.3 %shard_map.61 = (f32[512,128]{1,0:T(8,128)S(1)}, bf16[512,128]{1,0:T(8,128)(2,1)S(1)}, f32[512,128]{1,0:T(8,128)S(1)}, bf16[512,128]{1,0:T(8,128)(2,1)S(1)}) custom-call(s32[3]{0:T(128)S(1)} %pad_add_fusion.pos, bf16[512,1024]{1,0:T(8,128)(2,1)S(1)} %shard_map.59.rows, bf16[256,256]{1,0:T(8,128)(2,1)S(1)} %get-tuple-element.47.refs_0_, ...), custom_call_target="tpu_custom_call" | custom-call | flops 268435456 | bytes 2359296 | tf_op jit(solution)/shard_map/pallas_call | solution.py:34
  42.3 1.6 %collective-permute-start.12 = (bf16[512,128]{1,0:T(8,128)(2,1)S(1)}, bf16[512,128]{1,0:T(8,128)(2,1)S(1)}, u32[]{:S(2)}, u32[]{:S(2)}) collective-permute-start(bf16[512,128]{1,0:T(8,128)(2,1)S(1)} %get-tuple-element.49), channel_id=1, source_target_pairs={{0,16},{16,0},{1,17},{17,1},{2,18},{18,2},{3,19},{19,3},{4,20},{20... | collective-permute-start | bytes 393224 | tf_op jit(solution)/shard_map/ppermute | solution.py:327
  43.9 0.5 collective-permute-start.17
  44.4 5.1 %collective-permute-done.4.refs_3_ = bf16[120,1024]{1,0:T(8,128)(2,1)S(1)} collective-permute-done((bf16[120,1024]{1,0:T(8,128)(2,1)S(1)}, bf16[120,1024]{1,0:T(8,128)(2,1)S(1)}, u32[]{:S(2)}, u32[]{:S(2)}) %collective-permute-start.4) | collective-permute-done | bytes 245792 | tf_op jit(solution)/shard_map/ppermute | solution.py:296
  49.5 0.9 %shard_map.57.turned = bf16[1024,512]{1,0:T(8,128)(2,1)S(1)} custom-call(s32[3]{0:T(128)S(1)} %pad_add_fusion.pos, bf16[120,1024]{1,0:T(8,128)(2,1)S(1)} %get-tuple-element.38.refs_0_, bf16[120,1024]{1,0:T(8,128)(2,1)S(1)} %collective-permute-done.2.refs_1_, bf16[120,1024]{1,0:T(8,128)(2,1)S(1)} %collective-permute-done.3.refs_2_, ...), custom_call_target="tpu_custom_call" | custom-call | bytes 2031616 | tf_op jit(solution)/shard_map/pallas_call | solution.py:34
  50.4 1.0 %shard_map.67 = (f32[256,256]{1,0:T(8,128)S(1)}, bf16[256,256]{1,0:T(8,128)(2,1)S(1)}, bf16[256,256]{1,0:T(8,128)(2,1)S(1)}, bf16[256,256]{1,0:T(8,128)(2,1)S(1)}) custom-call(s32[3]{0:T(128)S(1)} %pad_add_fusion.pos, bf16[1024,512]{1,0:T(8,128)(2,1)S(1)} %shard_map.57.turned, f32[512,256]{1,0:T(8,128)S(1)} %get-tuple-element.61.kept, ...), custom_call_target="tpu_custom_call" | custom-call | flops 268435456 | bytes 2490368 | tf_op jit(solution)/shard_map/pallas_call | solution.py:34
  51.5 3.7 %collective-permute-start.26 = (bf16[256,256]{1,0:T(8,128)(2,1)S(1)}, bf16[256,256]{1,0:T(8,128)(2,1)S(1)}, u32[]{:S(2)}, u32[]{:S(2)}) collective-permute-start(bf16[256,256]{1,0:T(8,128)(2,1)S(1)} %get-tuple-element.64), channel_id=1, source_target_pairs={{0,8},{4,12},{8,0},{12,4},{1,9},{5,13},{9,1},{13,5},{2,10},{6,14},... | collective-permute-start | bytes 393224 | tf_op jit(solution)/shard_map/ppermute | solution.py:341
  55.1 1.3 %collective-permute-start.27 = (bf16[256,256]{1,0:T(8,128)(2,1)S(1)}, bf16[256,256]{1,0:T(8,128)(2,1)S(1)}, u32[]{:S(2)}, u32[]{:S(2)}) collective-permute-start(bf16[256,256]{1,0:T(8,128)(2,1)S(1)} %get-tuple-element.65), channel_id=1, source_target_pairs={{0,12},{4,8},{8,4},{12,0},{1,13},{5,9},{9,5},{13,1},{2,14},{6,10},... | collective-permute-start | bytes 393224 | tf_op jit(solution)/shard_map/ppermute | solution.py:341
  56.4 1.0 %shard_map.62 = (f32[256,128]{1,0:T(8,128)S(1)}, bf16[256,128]{1,0:T(8,128)(2,1)S(1)}, bf16[256,128]{1,0:T(8,128)(2,1)S(1)}, bf16[256,128]{1,0:T(8,128)(2,1)S(1)}) custom-call(s32[3]{0:T(128)S(1)} %pad_add_fusion.pos, bf16[1024,512]{1,0:T(8,128)(2,1)S(1)} %shard_map.57.turned, f32[512,128]{1,0:T(8,128)S(1)} %get-tuple-element.48.kept, ...), custom_call_target="tpu_custom_call" | custom-call | flops 134217728 | bytes 1769472 | tf_op jit(solution)/shard_map/pallas_call | solution.py:34
  57.5 3.2 %collective-permute-start.13 = (bf16[256,128]{1,0:T(8,128)(2,1)S(1)}, bf16[256,128]{1,0:T(8,128)(2,1)S(1)}, u32[]{:S(2)}, u32[]{:S(2)}) collective-permute-start(bf16[256,128]{1,0:T(8,128)(2,1)S(1)} %get-tuple-element.51), channel_id=1, source_target_pairs={{0,8},{4,12},{8,0},{12,4},{1,9},{5,13},{9,1},{13,5},{2,10},{6,14},... | collective-permute-start | bytes 196616 | tf_op jit(solution)/shard_map/ppermute | solution.py:341
  60.6 1.3 %collective-permute-start.14 = (bf16[256,128]{1,0:T(8,128)(2,1)S(1)}, bf16[256,128]{1,0:T(8,128)(2,1)S(1)}, u32[]{:S(2)}, u32[]{:S(2)}) collective-permute-start(bf16[256,128]{1,0:T(8,128)(2,1)S(1)} %get-tuple-element.52), channel_id=1, source_target_pairs={{0,12},{4,8},{8,4},{12,0},{1,13},{5,9},{9,5},{13,1},{2,14},{6,10},... | collective-permute-start | bytes 196616 | tf_op jit(solution)/shard_map/ppermute | solution.py:341
  61.9 1.0 %shard_map.64 = (f32[256,128]{1,0:T(8,128)S(1)}, bf16[256,128]{1,0:T(8,128)(2,1)S(1)}, bf16[256,128]{1,0:T(8,128)(2,1)S(1)}, bf16[256,128]{1,0:T(8,128)(2,1)S(1)}) custom-call(s32[3]{0:T(128)S(1)} %pad_add_fusion.pos, bf16[1024,512]{1,0:T(8,128)(2,1)S(1)} %shard_map.57.turned, f32[512,128]{1,0:T(8,128)S(1)} %get-tuple-element.54.kept, ...), custom_call_target="tpu_custom_call" | custom-call | flops 134217728 | bytes 1769472 | tf_op jit(solution)/shard_map/pallas_call | solution.py:34
  62.9 4.6 %collective-permute-done.13.refs_0_ = bf16[256,128]{1,0:T(8,128)(2,1)S(1)} collective-permute-done((bf16[256,128]{1,0:T(8,128)(2,1)S(1)}, bf16[256,128]{1,0:T(8,128)(2,1)S(1)}, u32[]{:S(2)}, u32[]{:S(2)}) %collective-permute-start.13) | collective-permute-done | bytes 65568 | tf_op jit(solution)/shard_map/ppermute | solution.py:341
  67.6 1.7 %collective-permute-start.18 = (bf16[256,128]{1,0:T(8,128)(2,1)S(1)}, bf16[256,128]{1,0:T(8,128)(2,1)S(1)}, u32[]{:S(2)}, u32[]{:S(2)}) collective-permute-start(bf16[256,128]{1,0:T(8,128)(2,1)S(1)} %get-tuple-element.57), channel_id=1, source_target_pairs={{0,8},{4,12},{8,0},{12,4},{1,9},{5,13},{9,1},{13,5},{2,10},{6,14},... | collective-permute-start | bytes 196616 | tf_op jit(solution)/shard_map/ppermute | solution.py:341
  69.3 2.6 %collective-permute-start.19 = (bf16[256,128]{1,0:T(8,128)(2,1)S(1)}, bf16[256,128]{1,0:T(8,128)(2,1)S(1)}, u32[]{:S(2)}, u32[]{:S(2)}) collective-permute-start(bf16[256,128]{1,0:T(8,128)(2,1)S(1)} %get-tuple-element.58), channel_id=1, source_target_pairs={{0,12},{4,8},{8,4},{12,0},{1,13},{5,9},{9,5},{13,1},{2,14},{6,10},... | collective-permute-start | bytes 196616 | tf_op jit(solution)/shard_map/ppermute | solution.py:341
  72.0 0.6 shard_map.68.refs_4_
  72.6 1.6 %collective-permute-start.29 = (bf16[256,256]{1,0:T(8,128)(2,1)S(1)}, bf16[256,256]{1,0:T(8,128)(2,1)S(1)}, u32[]{:S(2)}, u32[]{:S(2)}) collective-permute-start(bf16[256,256]{1,0:T(8,128)(2,1)S(1)} %shard_map.68.refs_4_), channel_id=1, source_target_pairs={{0,16},{16,0},{1,17},{17,1},{2,18},{18,2},{3,19},{19,3},{4,20},{20... | collective-permute-start | bytes 393224 | tf_op jit(solution)/shard_map/ppermute | solution.py:346
  74.2 0.6 shard_map.63.refs_0_
  74.7 0.6 collective-permute-start.16
  75.4 0.8 %collective-permute-done.20.refs_2_ = bf16[256,128]{1,0:T(8,128)(2,1)S(1)} collective-permute-done((bf16[256,128]{1,0:T(8,128)(2,1)S(1)}, bf16[256,128]{1,0:T(8,128)(2,1)S(1)}, u32[]{:S(2)}, u32[]{:S(2)}) %collective-permute-start.20) | collective-permute-done | bytes 65568 | tf_op jit(solution)/shard_map/ppermute | solution.py:341
  76.2 0.6 shard_map.65.refs_2_
  76.8 1.6 %collective-permute-start.21 = (bf16[256,128]{1,0:T(8,128)(2,1)S(1)}, bf16[256,128]{1,0:T(8,128)(2,1)S(1)}, u32[]{:S(2)}, u32[]{:S(2)}) collective-permute-start(bf16[256,128]{1,0:T(8,128)(2,1)S(1)} %shard_map.65.refs_2_), channel_id=1, source_target_pairs={{0,16},{16,0},{1,17},{17,1},{2,18},{18,2},{3,19},{19,3},{4,20},{20... | collective-permute-start | bytes 196616 | tf_op jit(solution)/shard_map/ppermute | solution.py:346
  78.4 0.7 collective-permute-done.16.refs_1_
  79.1 2.1 %collective-permute-done.21.refs_3_ = bf16[256,128]{1,0:T(8,128)(2,1)S(1)} collective-permute-done((bf16[256,128]{1,0:T(8,128)(2,1)S(1)}, bf16[256,128]{1,0:T(8,128)(2,1)S(1)}, u32[]{:S(2)}, u32[]{:S(2)}) %collective-permute-start.21) | collective-permute-done | bytes 65568 | tf_op jit(solution)/shard_map/ppermute | solution.py:346
  81.1 1.4 %shard_map.69 = bf16[512,512]{1,0:T(8,128)(2,1)} custom-call(s32[3]{0:T(128)S(1)} %pad_add_fusion.pos, bf16[256,128]{1,0:T(8,128)(2,1)S(1)} %shard_map.63.refs_0_, bf16[256,128]{1,0:T(8,128)(2,1)S(1)} %collective-permute-done.16.refs_1_, bf16[256,128]{1,0:T(8,128)(2,1)S(1)} %shard_map.65.refs_2_, bf16[256,128]{1,0:T(8,128)(2,1)S(1)} %collective-permute-done.21.refs_3_, ...), custom_call_target="tpu_custom_call" | custom-call | bytes 1048576 | tf_op jit(solution)/shard_map/pallas_call | solution.py:34
  (32 shorter events, 0.8 us)
Async XLA Ops:
  0.0 0.7 copy-start.1
  0.0 5.4 %collective-permute-start.5 = (bf16[192,2048]{1,0:T(8,128)(2,1)}, bf16[192,2048]{1,0:T(8,128)(2,1)S(1)}, u32[]{:S(2)}, u32[]{:S(2)}) collective-permute-start(bf16[192,2048]{1,0:T(8,128)(2,1)} %rows.2), channel_id=1, source_target_pairs={{0,1},{1,0},{2,3},{3,2},{4,5},{5,4},{6,7},{7,6},{8,9},{9,8},{10,11... | collective-permute-start | bytes 2359304 | tf_op jit(solution)/shard_map/ppermute | solution.py:241
  0.5 14.4 %collective-permute-start.1 = (bf16[192,2048]{1,0:T(8,128)(2,1)}, bf16[192,2048]{1,0:T(8,128)(2,1)S(1)}, u32[]{:S(2)}, u32[]{:S(2)}) collective-permute-start(bf16[192,2048]{1,0:T(8,128)(2,1)} %rows.3), channel_id=1, source_target_pairs={{0,1},{1,0},{2,3},{3,2},{4,5},{5,4},{6,7},{7,6},{8,9},{9,8},{10,11... | collective-permute-start | bytes 2359304 | tf_op jit(solution)/shard_map/ppermute | solution.py:243
  0.7 3.1 %collective-permute-start = (s32[1,192]{1,0:T(1,128)S(1)}, s32[1,192]{1,0:T(1,128)S(1)}, u32[]{:S(2)}, u32[]{:S(2)}) collective-permute-start(s32[1,192]{1,0:T(1,128)S(1)} %bitcast.7), channel_id=1, source_target_pairs={{0,1},{1,0},{2,3},{3,2},{4,5},{5,4},{6,7},{7,6},{8,9},{9,8},{10,11... | collective-permute-start | bytes 2312 | tf_op jit(solution)/shard_map/ppermute | solution.py:242
  5.4 19.7 %copy-start = (bf16[192,2048]{1,0:T(8,128)(2,1)S(1)}, bf16[192,2048]{1,0:T(8,128)(2,1)}, u32[]{:S(2)}) copy-start(bf16[192,2048]{1,0:T(8,128)(2,1)} %rows.3) | copy-start | bytes 2359300
  6.7 10.7 %collective-permute-start.6 = (bf16[120,1024]{1,0:T(8,128)(2,1)S(1)}, bf16[120,1024]{1,0:T(8,128)(2,1)S(1)}, u32[]{:S(2)}, u32[]{:S(2)}) collective-permute-start(bf16[120,1024]{1,0:T(8,128)(2,1)S(1)} %get-tuple-element.44), channel_id=1, source_target_pairs={{0,2},{1,3},{2,0},{3,1},{16,18},{17,19},{18,16},{19,17},{4,6},{5,7... | collective-permute-start | bytes 737288 | tf_op jit(solution)/shard_map/ppermute | solution.py:296
  9.7 10.1 %collective-permute-start.7 = (bf16[120,1024]{1,0:T(8,128)(2,1)S(1)}, bf16[120,1024]{1,0:T(8,128)(2,1)S(1)}, u32[]{:S(2)}, u32[]{:S(2)}) collective-permute-start(bf16[120,1024]{1,0:T(8,128)(2,1)S(1)} %get-tuple-element.45), channel_id=1, source_target_pairs={{0,16},{1,17},{2,18},{3,19},{16,0},{17,1},{18,2},{19,3},{4,20},{5,... | collective-permute-start | bytes 737288 | tf_op jit(solution)/shard_map/ppermute | solution.py:296
  11.2 11.3 %collective-permute-start.8 = (bf16[120,1024]{1,0:T(8,128)(2,1)S(1)}, bf16[120,1024]{1,0:T(8,128)(2,1)S(1)}, u32[]{:S(2)}, u32[]{:S(2)}) collective-permute-start(bf16[120,1024]{1,0:T(8,128)(2,1)S(1)} %get-tuple-element.46), channel_id=1, source_target_pairs={{0,18},{1,19},{2,16},{3,17},{16,2},{17,3},{18,0},{19,1},{4,22},{5,... | collective-permute-start | bytes 737288 | tf_op jit(solution)/shard_map/ppermute | solution.py:296
  12.8 14.3 %collective-permute-start.22 = (bf16[256,256]{1,0:T(8,128)(2,1)S(1)}, bf16[256,256]{1,0:T(8,128)(2,1)S(1)}, u32[]{:S(2)}, u32[]{:S(2)}) collective-permute-start(bf16[256,256]{1,0:T(8,128)(2,1)S(1)} %get-tuple-element.60.refs_0_), channel_id=1, source_target_pairs={{0,4},{4,0},{8,12},{12,8},{1,5},{5,1},{9,13},{13,9},{2,6},{6,2},{1... | collective-permute-start | bytes 393224 | tf_op jit(solution)/shard_map/ppermute | solution.py:263
  14.9 13.8 %collective-permute-start.23 = (bf16[256,256]{1,0:T(8,128)(2,1)S(1)}, bf16[256,256]{1,0:T(8,128)(2,1)S(1)}, u32[]{:S(2)}, u32[]{:S(2)}) collective-permute-start(bf16[256,256]{1,0:T(8,128)(2,1)S(1)} %get-tuple-element.60.refs_0_), channel_id=1, source_target_pairs={{0,8},{4,12},{8,0},{12,4},{1,9},{5,13},{9,1},{13,5},{2,10},{6,14},... | collective-permute-start | bytes 393224 | tf_op jit(solution)/shard_map/ppermute | solution.py:263
  17.5 11.2 %collective-permute-start.24 = (bf16[256,256]{1,0:T(8,128)(2,1)S(1)}, bf16[256,256]{1,0:T(8,128)(2,1)S(1)}, u32[]{:S(2)}, u32[]{:S(2)}) collective-permute-start(bf16[256,256]{1,0:T(8,128)(2,1)S(1)} %get-tuple-element.60.refs_0_), channel_id=1, source_target_pairs={{0,12},{4,8},{8,4},{12,0},{1,13},{5,9},{9,5},{13,1},{2,14},{6,10},... | collective-permute-start | bytes 393224 | tf_op jit(solution)/shard_map/ppermute | solution.py:263
  19.8 12.1 %collective-permute-start.9 = (bf16[256,256]{1,0:T(8,128)(2,1)S(1)}, bf16[256,256]{1,0:T(8,128)(2,1)S(1)}, u32[]{:S(2)}, u32[]{:S(2)}) collective-permute-start(bf16[256,256]{1,0:T(8,128)(2,1)S(1)} %get-tuple-element.47.refs_0_), channel_id=1, source_target_pairs={{0,4},{4,0},{8,12},{12,8},{1,5},{5,1},{9,13},{13,9},{2,6},{6,2},{1... | collective-permute-start | bytes 393224 | tf_op jit(solution)/shard_map/ppermute | solution.py:263
  22.5 11.8 %collective-permute-start.10 = (bf16[256,256]{1,0:T(8,128)(2,1)S(1)}, bf16[256,256]{1,0:T(8,128)(2,1)S(1)}, u32[]{:S(2)}, u32[]{:S(2)}) collective-permute-start(bf16[256,256]{1,0:T(8,128)(2,1)S(1)} %get-tuple-element.47.refs_0_), channel_id=1, source_target_pairs={{0,8},{4,12},{8,0},{12,4},{1,9},{5,13},{9,1},{13,5},{2,10},{6,14},... | collective-permute-start | bytes 393224 | tf_op jit(solution)/shard_map/ppermute | solution.py:263
  27.1 16.8 %collective-permute-start.2 = (bf16[120,1024]{1,0:T(8,128)(2,1)S(1)}, bf16[120,1024]{1,0:T(8,128)(2,1)S(1)}, u32[]{:S(2)}, u32[]{:S(2)}) collective-permute-start(bf16[120,1024]{1,0:T(8,128)(2,1)S(1)} %get-tuple-element.39), channel_id=1, source_target_pairs={{0,2},{1,3},{2,0},{3,1},{16,18},{17,19},{18,16},{19,17},{4,6},{5,7... | collective-permute-start | bytes 737288 | tf_op jit(solution)/shard_map/ppermute | solution.py:296
  29.7 20.7 %collective-permute-start.25 = (bf16[512,256]{1,0:T(8,128)(2,1)S(1)}, bf16[512,256]{1,0:T(8,128)(2,1)S(1)}, u32[]{:S(2)}, u32[]{:S(2)}) collective-permute-start(bf16[512,256]{1,0:T(8,128)(2,1)S(1)} %get-tuple-element.62), channel_id=1, source_target_pairs={{0,16},{16,0},{1,17},{17,1},{2,18},{18,2},{3,19},{19,3},{4,20},{20... | collective-permute-start | bytes 786440 | tf_op jit(solution)/shard_map/ppermute | solution.py:327
  31.3 13.1 %collective-permute-start.3 = (bf16[120,1024]{1,0:T(8,128)(2,1)S(1)}, bf16[120,1024]{1,0:T(8,128)(2,1)S(1)}, u32[]{:S(2)}, u32[]{:S(2)}) collective-permute-start(bf16[120,1024]{1,0:T(8,128)(2,1)S(1)} %get-tuple-element.40), channel_id=1, source_target_pairs={{0,16},{1,17},{2,18},{3,19},{16,0},{17,1},{18,2},{19,3},{4,20},{5,... | collective-permute-start | bytes 737288 | tf_op jit(solution)/shard_map/ppermute | solution.py:296
  31.8 17.7 %collective-permute-start.4 = (bf16[120,1024]{1,0:T(8,128)(2,1)S(1)}, bf16[120,1024]{1,0:T(8,128)(2,1)S(1)}, u32[]{:S(2)}, u32[]{:S(2)}) collective-permute-start(bf16[120,1024]{1,0:T(8,128)(2,1)S(1)} %get-tuple-element.41), channel_id=1, source_target_pairs={{0,18},{1,19},{2,16},{3,17},{16,2},{17,3},{18,0},{19,1},{4,22},{5,... | collective-permute-start | bytes 737288 | tf_op jit(solution)/shard_map/ppermute | solution.py:296
  34.3 6.8 %collective-permute-start.11 = (bf16[256,256]{1,0:T(8,128)(2,1)S(1)}, bf16[256,256]{1,0:T(8,128)(2,1)S(1)}, u32[]{:S(2)}, u32[]{:S(2)}) collective-permute-start(bf16[256,256]{1,0:T(8,128)(2,1)S(1)} %get-tuple-element.47.refs_0_), channel_id=1, source_target_pairs={{0,12},{4,8},{8,4},{12,0},{1,13},{5,9},{9,5},{13,1},{2,14},{6,10},... | collective-permute-start | bytes 393224 | tf_op jit(solution)/shard_map/ppermute | solution.py:263
  42.3 14.1 %collective-permute-start.12 = (bf16[512,128]{1,0:T(8,128)(2,1)S(1)}, bf16[512,128]{1,0:T(8,128)(2,1)S(1)}, u32[]{:S(2)}, u32[]{:S(2)}) collective-permute-start(bf16[512,128]{1,0:T(8,128)(2,1)S(1)} %get-tuple-element.49), channel_id=1, source_target_pairs={{0,16},{16,0},{1,17},{17,1},{2,18},{18,2},{3,19},{19,3},{4,20},{20... | collective-permute-start | bytes 393224 | tf_op jit(solution)/shard_map/ppermute | solution.py:327
  43.9 16.8 %collective-permute-start.17 = (bf16[512,128]{1,0:T(8,128)(2,1)S(1)}, bf16[512,128]{1,0:T(8,128)(2,1)S(1)}, u32[]{:S(2)}, u32[]{:S(2)}) collective-permute-start(bf16[512,128]{1,0:T(8,128)(2,1)S(1)} %get-tuple-element.55), channel_id=1, source_target_pairs={{0,16},{16,0},{1,17},{17,1},{2,18},{18,2},{3,19},{19,3},{4,20},{20... | collective-permute-start | bytes 393224 | tf_op jit(solution)/shard_map/ppermute | solution.py:327
  51.5 16.1 %collective-permute-start.26 = (bf16[256,256]{1,0:T(8,128)(2,1)S(1)}, bf16[256,256]{1,0:T(8,128)(2,1)S(1)}, u32[]{:S(2)}, u32[]{:S(2)}) collective-permute-start(bf16[256,256]{1,0:T(8,128)(2,1)S(1)} %get-tuple-element.64), channel_id=1, source_target_pairs={{0,8},{4,12},{8,0},{12,4},{1,9},{5,13},{9,1},{13,5},{2,10},{6,14},... | collective-permute-start | bytes 393224 | tf_op jit(solution)/shard_map/ppermute | solution.py:341
  55.1 14.2 %collective-permute-start.27 = (bf16[256,256]{1,0:T(8,128)(2,1)S(1)}, bf16[256,256]{1,0:T(8,128)(2,1)S(1)}, u32[]{:S(2)}, u32[]{:S(2)}) collective-permute-start(bf16[256,256]{1,0:T(8,128)(2,1)S(1)} %get-tuple-element.65), channel_id=1, source_target_pairs={{0,12},{4,8},{8,4},{12,0},{1,13},{5,9},{9,5},{13,1},{2,14},{6,10},... | collective-permute-start | bytes 393224 | tf_op jit(solution)/shard_map/ppermute | solution.py:341
  56.4 15.6 %collective-permute-start.28 = (bf16[256,256]{1,0:T(8,128)(2,1)S(1)}, bf16[256,256]{1,0:T(8,128)(2,1)S(1)}, u32[]{:S(2)}, u32[]{:S(2)}) collective-permute-start(bf16[256,256]{1,0:T(8,128)(2,1)S(1)} %get-tuple-element.66), channel_id=1, source_target_pairs={{0,4},{4,0},{8,12},{12,8},{1,5},{5,1},{9,13},{13,9},{2,6},{6,2},{1... | collective-permute-start | bytes 393224 | tf_op jit(solution)/shard_map/ppermute | solution.py:341
  57.5 10.1 %collective-permute-start.13 = (bf16[256,128]{1,0:T(8,128)(2,1)S(1)}, bf16[256,128]{1,0:T(8,128)(2,1)S(1)}, u32[]{:S(2)}, u32[]{:S(2)}) collective-permute-start(bf16[256,128]{1,0:T(8,128)(2,1)S(1)} %get-tuple-element.51), channel_id=1, source_target_pairs={{0,8},{4,12},{8,0},{12,4},{1,9},{5,13},{9,1},{13,5},{2,10},{6,14},... | collective-permute-start | bytes 196616 | tf_op jit(solution)/shard_map/ppermute | solution.py:341
  60.6 11.9 %collective-permute-start.14 = (bf16[256,128]{1,0:T(8,128)(2,1)S(1)}, bf16[256,128]{1,0:T(8,128)(2,1)S(1)}, u32[]{:S(2)}, u32[]{:S(2)}) collective-permute-start(bf16[256,128]{1,0:T(8,128)(2,1)S(1)} %get-tuple-element.52), channel_id=1, source_target_pairs={{0,12},{4,8},{8,4},{12,0},{1,13},{5,9},{9,5},{13,1},{2,14},{6,10},... | collective-permute-start | bytes 196616 | tf_op jit(solution)/shard_map/ppermute | solution.py:341
  67.6 6.6 %collective-permute-start.15 = (bf16[256,128]{1,0:T(8,128)(2,1)S(1)}, bf16[256,128]{1,0:T(8,128)(2,1)S(1)}, u32[]{:S(2)}, u32[]{:S(2)}) collective-permute-start(bf16[256,128]{1,0:T(8,128)(2,1)S(1)} %get-tuple-element.53), channel_id=1, source_target_pairs={{0,4},{4,0},{8,12},{12,8},{1,5},{5,1},{9,13},{13,9},{2,6},{6,2},{1... | collective-permute-start | bytes 196616 | tf_op jit(solution)/shard_map/ppermute | solution.py:341
  67.6 7.8 %collective-permute-start.18 = (bf16[256,128]{1,0:T(8,128)(2,1)S(1)}, bf16[256,128]{1,0:T(8,128)(2,1)S(1)}, u32[]{:S(2)}, u32[]{:S(2)}) collective-permute-start(bf16[256,128]{1,0:T(8,128)(2,1)S(1)} %get-tuple-element.57), channel_id=1, source_target_pairs={{0,8},{4,12},{8,0},{12,4},{1,9},{5,13},{9,1},{13,5},{2,10},{6,14},... | collective-permute-start | bytes 196616 | tf_op jit(solution)/shard_map/ppermute | solution.py:341
  69.3 6.1 %collective-permute-start.19 = (bf16[256,128]{1,0:T(8,128)(2,1)S(1)}, bf16[256,128]{1,0:T(8,128)(2,1)S(1)}, u32[]{:S(2)}, u32[]{:S(2)}) collective-permute-start(bf16[256,128]{1,0:T(8,128)(2,1)S(1)} %get-tuple-element.58), channel_id=1, source_target_pairs={{0,12},{4,8},{8,4},{12,0},{1,13},{5,9},{9,5},{13,1},{2,14},{6,10},... | collective-permute-start | bytes 196616 | tf_op jit(solution)/shard_map/ppermute | solution.py:341
  72.0 4.3 %collective-permute-start.20 = (bf16[256,128]{1,0:T(8,128)(2,1)S(1)}, bf16[256,128]{1,0:T(8,128)(2,1)S(1)}, u32[]{:S(2)}, u32[]{:S(2)}) collective-permute-start(bf16[256,128]{1,0:T(8,128)(2,1)S(1)} %get-tuple-element.59), channel_id=1, source_target_pairs={{0,4},{4,0},{8,12},{12,8},{1,5},{5,1},{9,13},{13,9},{2,6},{6,2},{1... | collective-permute-start | bytes 196616 | tf_op jit(solution)/shard_map/ppermute | solution.py:341
  72.6 8.6 %collective-permute-start.29 = (bf16[256,256]{1,0:T(8,128)(2,1)S(1)}, bf16[256,256]{1,0:T(8,128)(2,1)S(1)}, u32[]{:S(2)}, u32[]{:S(2)}) collective-permute-start(bf16[256,256]{1,0:T(8,128)(2,1)S(1)} %shard_map.68.refs_4_), channel_id=1, source_target_pairs={{0,16},{16,0},{1,17},{17,1},{2,18},{18,2},{3,19},{19,3},{4,20},{20... | collective-permute-start | bytes 393224 | tf_op jit(solution)/shard_map/ppermute | solution.py:346
  74.7 4.3 %collective-permute-start.16 = (bf16[256,128]{1,0:T(8,128)(2,1)S(1)}, bf16[256,128]{1,0:T(8,128)(2,1)S(1)}, u32[]{:S(2)}, u32[]{:S(2)}) collective-permute-start(bf16[256,128]{1,0:T(8,128)(2,1)S(1)} %shard_map.63.refs_0_), channel_id=1, source_target_pairs={{0,16},{16,0},{1,17},{17,1},{2,18},{18,2},{3,19},{19,3},{4,20},{20... | collective-permute-start | bytes 196616 | tf_op jit(solution)/shard_map/ppermute | solution.py:346
  76.8 4.3 %collective-permute-start.21 = (bf16[256,128]{1,0:T(8,128)(2,1)S(1)}, bf16[256,128]{1,0:T(8,128)(2,1)S(1)}, u32[]{:S(2)}, u32[]{:S(2)}) collective-permute-start(bf16[256,128]{1,0:T(8,128)(2,1)S(1)} %shard_map.65.refs_2_), channel_id=1, source_target_pairs={{0,16},{16,0},{1,17},{17,1},{2,18},{18,2},{3,19},{19,3},{4,20},{20... | collective-permute-start | bytes 196616 | tf_op jit(solution)/shard_map/ppermute | solution.py:346

commit v4 on v3

--- a/solution.py
+++ b/solution.py
@@ -7,7 +7,7 @@
 from jax.sharding import PartitionSpec as P
 
 QB = 32
-SPLITS = ((1, 1), (2,))
+SPLITS = ((1, 2), (1,))
 F32 = jnp.float32
 BF16 = jnp.bfloat16
 
@@ -26,7 +26,7 @@
     return lax.rem(i + (size - k), size)
 
 
-def call(body, outs, scalars, args, scratch=(), flops=0, space=pltpu.VMEM, target=pltpu.VMEM):
+def call(body, outs, scalars, args, scratch=(), flops=0, space=pltpu.VMEM, target=pltpu.VMEM, aliases=None):
     moved = sum(a.size * a.dtype.itemsize for a in args)
     moved += sum(o.size * o.dtype.itemsize for o in outs)
     spaces = space if isinstance(space, list) else [space] * len(args)
@@ -38,13 +38,14 @@
         + [pl.BlockSpec(memory_space=kind) for kind in spaces],
         out_specs=[pl.BlockSpec(memory_space=target)] * len(outs),
         scratch_shapes=list(scratch),
+        input_output_aliases=aliases or {},
         compiler_params=pltpu.CompilerParams(vmem_limit_bytes=min(room, 60 << 20)),
         cost_estimate=pl.CostEstimate(flops=flops, bytes_accessed=moved, transcendentals=0),
     )(scalars, *args)
 
 
 def node_order(nodes):
-    return [s for s in (2, 3, 1) if s < nodes] + list(range(4, nodes))
+    return [s for s in (3, 1, 2) if s < nodes] + list(range(4, nodes))
 
 
 def slots_of(copies, pairs):
@@ -74,9 +75,11 @@
     first.wait()
     blocks = raw[...].astype(F32).reshape(used, mine // used, ff)
     kept = (blocks * factors[:, None, :]).astype(BF16).reshape(mine, ff)
-    width = ff // len(outs)
-    for i, out in enumerate(outs):
-        out[...] = kept[:, i * width : (i + 1) * width]
+    begin = 0
+    for out in outs:
+        end = begin + out.shape[1]
+        out[...] = kept[:, begin:end]
+        begin = end
 
 
 def select_body(dims, stride, pos, ids, ids_pair, *picks):
@@ -196,18 +199,15 @@
     refs[-1][...] = total.astype(BF16)
 
 
-def lay_body(dims, pos, *refs):
+def lay_body(dims, spots, pos, *refs):
     copies = dims[0]
-    parts, out, sems = refs[:-2], refs[-2], refs[-1]
+    parts, out, sems = refs[: len(spots)], refs[-2], refs[-1]
     moves = []
-    begin = 0
-    for i in range(len(parts) // copies):
-        mine, width = parts[i * copies].shape
-        for j in range(copies):
-            at = pl.multiple_of(traced_origin(pos[0], j, copies) * mine, 16)
-            spot = out.at[pl.ds(at, mine), pl.ds(begin, width)]
-            moves.append(pltpu.make_async_copy(parts[i * copies + j], spot, sems.at[i * copies + j]))
-        begin += width
+    for i, (part, (j, begin)) in enumerate(zip(parts, spots)):
+        mine, width = part.shape
+        at = pl.multiple_of(traced_origin(pos[0], j, copies) * mine, 16)
+        spot = out.at[pl.ds(at, mine), pl.ds(begin, width)]
+        moves.append(pltpu.make_async_copy(part, spot, sems.at[i]))
     for move in moves:
         move.start()
     for move in moves:
@@ -225,7 +225,8 @@
     shard, hidden = w1_codes.shape[1:]
     mine = shard // copies
     part = features // copies
-    width = hidden // len(SPLITS)
+    unit = hidden // sum(sum(split) for split in SPLITS)
+    gathered = [unit * sum(split) for split in SPLITS]
     everyone = copies * pairs * stride
     pos = jnp.stack([lax.axis_index(a) for a in ("dp", "node", "local")]).astype(jnp.int32)
 
@@ -244,7 +245,7 @@
 
     weights = call(
         dequant_body,
-        [shape(mine, width, BF16)] * len(SPLITS),
+        [shape(mine, w, BF16) for w in gathered],
         pos,
         [pltpu.with_memory_space_constraint(a[0], pltpu.HBM) for a in (w1_codes, w1_scales)],
         [
@@ -311,14 +312,14 @@
     factor = float(count * copies * nodes) ** (-0.5)
     groups = []
     for i, split in enumerate(SPLITS):
-        widths = [width * share // sum(split) for share in split]
+        widths = [unit * share for share in split]
         parts = call(
             functools.partial(up_body, dims),
             [shape(everyone, w, kind) for w in widths for kind in (F32, BF16)],
             pos,
             [rows_x] + held[i],
-            [pltpu.VMEM((part, width), BF16)],
-            flops=2 * everyone * part * width,
+            [pltpu.VMEM((part, gathered[i]), BF16)],
+            flops=2 * everyone * part * gathered[i],
         )
         groups += list(zip(widths, parts[::2], parts[1::2]))
     finished = []
@@ -344,13 +345,30 @@
         for j in range(1, copies):
             links = [(a, mate(a, j, copies)) for a in range(copies)]
             finished.append(lax.ppermute(summed, "dp", links))
+    spots = []
+    begin = 0
+    for wide, _, _ in groups:
+        spots += [(j, begin) for j in range(copies)]
+        begin += wide
+    early = len(finished) - copies + 1
+    last = copies - 1
     (result,) = call(
-        functools.partial(lay_body, dims),
+        functools.partial(lay_body, dims, spots[:early]),
         [shape(shard, hidden, BF16)],
         pos,
-        finished,
-        [pltpu.SemaphoreType.DMA((len(finished),))],
+        finished[:early],
+        [pltpu.SemaphoreType.DMA((early,))],
         target=pltpu.HBM,
+    )
+    (result,) = call(
+        functools.partial(lay_body, dims, spots[early:]),
+        [shape(shard, hidden, BF16)],
+        pos,
+        finished[early:] + [result],
+        [pltpu.SemaphoreType.DMA((last,))],
+        space=[pltpu.VMEM] * last + [pltpu.HBM],
+        target=pltpu.HBM,
+        aliases={last + 1: 0},
     )
     return result[None]
 

time: 82.7 us -> 87.7 us (1.060)
  starting transfers between devices: 42.8 us -> 44.9 us
  waiting for transfers between devices: 23.6 us -> 25.2 us
  Pallas kernels: 15.8 us -> 17 us
    ppermute x6, waiting for transfers between devices: 5.26 us -> 17.6 us  [on_device(): lax.ppermute(chunk, 'node', [(a, mate(a, s, nodes)) for a in range(nodes)])]
    ppermute x6, waiting for transfers between devices: 7.47 us -> 0.02 us  [exchange(): moved[at] = lax.ppermute(pieces[at], ('dp', 'local'), links)]
    ppermute x9, waiting for transfers between devices: 5.55 us -> 2.4 us  [on_device(): arrived.append(lax.ppermute(terms[s], 'node', links))]
    ppermute x6, starting transfers between devices: 12.5 us -> 14 us  [on_device(): lax.ppermute(chunk, 'node', [(a, mate(a, s, nodes)) for a in range(nodes)])]
    pallas_call x15 -> x16, Pallas kernels: 15.8 us -> 17 us  [call(): pl.pallas_call(body, out_shape=outs, in_specs=[pl.BlockSpec(memory_space=...]
    ppermute x9, starting transfers between devices: 13.8 us -> 12.8 us  [on_device(): arrived.append(lax.ppermute(terms[s], 'node', links))]
    ppermute x6, starting transfers between devices: 8.09 us -> 9.04 us  [exchange(): moved[at] = lax.ppermute(pieces[at], ('dp', 'local'), links)]
  transfers between devices with their start and end apart: 30 -> 30, of which waited for: 10 -> 7; matrix products, arithmetic and copies ran while one was open for 0% -> 0% of each run, Pallas kernels for 17% -> 18%
where the time goes in v4:
time: 87.7 us; the launch traced here: 87.5 us
  starting transfers between devices  44.9 us (51%)
  waiting for transfers between devices  25.2 us (29%)
  Pallas kernels  17 us (19%)
    ppermute x6, waiting for transfers between devices, on_device(): lax.ppermute(chunk, 'node', [(a, mate(a, s, nodes)) for a in range(nodes)])  17.6 us
    pallas_call x16, Pallas kernels, call(): pl.pallas_call(body, out_shape=outs, in_specs=[pl.BlockSpec(memory_space=...  17 us
    ppermute x6, starting transfers between devices, on_device(): lax.ppermute(chunk, 'node', [(a, mate(a, s, nodes)) for a in range(nodes)])  14 us
    ppermute x9, starting transfers between devices, on_device(): arrived.append(lax.ppermute(terms[s], 'node', links))  12.8 us
    ppermute x6, starting transfers between devices, exchange(): moved[at] = lax.ppermute(pieces[at], ('dp', 'local'), links)  9.04 us
    ppermute x3, starting transfers between devices, on_device(): finished.append(lax.ppermute(summed, 'dp', links))  4.4 us
    ppermute x3, starting transfers between devices, on_device(): others = [lax.ppermute(sent, 'dp', [(0, 1), (1, 0)])]  3.65 us
    ppermute x3, waiting for transfers between devices, on_device(): finished.append(lax.ppermute(summed, 'dp', links))  2.65 us
  transfers between devices with their start and end apart: 30, of which 7 were waited for; matrix products, arithmetic and copies ran while one was open for 0% of the time, Pallas kernels for 18%

profile of v4, /device:TPU:0, one launch (start us, length us, event | category | flops | bytes accessed | tf_op | source)
XLA Modules:
  0.0 87.5 jit_solution(3673916250979394455)
XLA Ops:
  0.0 0.5 collective-permute-start.5
  0.7 0.5 collective-permute-start
  1.2 2.5 %collective-permute-done.ids_pair = s32[1,192]{1,0:T(1,128)S(1)} collective-permute-done((s32[1,192]{1,0:T(1,128)S(1)}, s32[1,192]{1,0:T(1,128)S(1)}, u32[]{:S(2)}, u32[]{:S(2)}) %collective-permute-start) | collective-permute-done | bytes 800 | tf_op jit(solution)/shard_map/ppermute | solution.py:243
  3.7 1.7 %shard_map.55 = (bf16[256,192]{1,0:T(8,128)(2,1)S(1)}, bf16[256,192]{1,0:T(8,128)(2,1)S(1)}, bf16[192,2048]{1,0:T(8,128)(2,1)S(1)}) custom-call(s32[3]{0:T(128)S(1)} %pad_add_fusion.pos, s32[1,192]{1,0:T(1,128)S(1)} %bitcast.8, s32[1,192]{1,0:T(1,128)S(1)} %collective-permute-done.ids_pair, bf16[192,2048]{1,0:T(8,128)(2,1)} %rows.2), custom_call_target="tpu_custom_call" | custom-call | bytes 1771008 | tf_op jit(solution)/shard_map/pallas_call | solution.py:34
  5.5 1.3 %shard_map.58 = (bf16[120,1024]{1,0:T(8,128)(2,1)S(1)}, bf16[120,1024]{1,0:T(8,128)(2,1)S(1)}, bf16[120,1024]{1,0:T(8,128)(2,1)S(1)}, bf16[120,1024]{1,0:T(8,128)(2,1)S(1)}) custom-call(s32[3]{0:T(128)S(1)} %pad_add_fusion.pos, bf16[256,192]{1,0:T(8,128)(2,1)S(1)} %get-tuple-element.36.pick, bf16[256,192]{1,0:T(8,128)(2,1)S(1)} %get-tuple-element.37.pick_pair, ...), custom_call_target="tpu_custom_call" | custom-call | flops 402653184 | bytes 2752512 | tf_op jit(solution)/shard_map/pallas_call | solution.py:34
  6.7 2.9 %collective-permute-start.6 = (bf16[120,1024]{1,0:T(8,128)(2,1)S(1)}, bf16[120,1024]{1,0:T(8,128)(2,1)S(1)}, u32[]{:S(2)}, u32[]{:S(2)}) collective-permute-start(bf16[120,1024]{1,0:T(8,128)(2,1)S(1)} %get-tuple-element.44), channel_id=1, source_target_pairs={{0,2},{1,3},{2,0},{3,1},{16,18},{17,19},{18,16},{19,17},{4,6},{5,7... | collective-permute-start | bytes 737288 | tf_op jit(solution)/shard_map/ppermute | solution.py:297
  9.7 1.5 %collective-permute-start.7 = (bf16[120,1024]{1,0:T(8,128)(2,1)S(1)}, bf16[120,1024]{1,0:T(8,128)(2,1)S(1)}, u32[]{:S(2)}, u32[]{:S(2)}) collective-permute-start(bf16[120,1024]{1,0:T(8,128)(2,1)S(1)} %get-tuple-element.45), channel_id=1, source_target_pairs={{0,16},{1,17},{2,18},{3,19},{16,0},{17,1},{18,2},{19,3},{4,20},{5,... | collective-permute-start | bytes 737288 | tf_op jit(solution)/shard_map/ppermute | solution.py:297
  11.2 1.6 %shard_map.60 = (bf16[256,384]{1,0:T(8,128)(2,1)S(1)}, bf16[256,128]{1,0:T(8,128)(2,1)S(1)}) custom-call(s32[3]{0:T(128)S(1)} %pad_add_fusion.pos, bf16[512,512]{1,0:T(8,128)(2,1)} %bitcast.9, bf16[16,512]{1,0:T(8,128)(2,1)} %bitcast.10), custom_call_target="tpu_custom_call" | custom-call | bytes 802816 | tf_op jit(solution)/shard_map/pallas_call | solution.py:34
  12.8 2.1 %collective-permute-start.17 = (bf16[256,384]{1,0:T(8,128)(2,1)S(1)}, bf16[256,384]{1,0:T(8,128)(2,1)S(1)}, u32[]{:S(2)}, u32[]{:S(2)}) collective-permute-start(bf16[256,384]{1,0:T(8,128)(2,1)S(1)} %get-tuple-element.54.refs_0_), channel_id=1, source_target_pairs={{0,4},{4,0},{8,12},{12,8},{1,5},{5,1},{9,13},{13,9},{2,6},{6,2},{1... | collective-permute-start | bytes 589832 | tf_op jit(solution)/shard_map/ppermute | solution.py:264
  14.9 2.6 %collective-permute-start.18 = (bf16[256,384]{1,0:T(8,128)(2,1)S(1)}, bf16[256,384]{1,0:T(8,128)(2,1)S(1)}, u32[]{:S(2)}, u32[]{:S(2)}) collective-permute-start(bf16[256,384]{1,0:T(8,128)(2,1)S(1)} %get-tuple-element.54.refs_0_), channel_id=1, source_target_pairs={{0,8},{4,12},{8,0},{12,4},{1,9},{5,13},{9,1},{13,5},{2,10},{6,14},... | collective-permute-start | bytes 589832 | tf_op jit(solution)/shard_map/ppermute | solution.py:264
  17.5 2.3 %collective-permute-start.19 = (bf16[256,384]{1,0:T(8,128)(2,1)S(1)}, bf16[256,384]{1,0:T(8,128)(2,1)S(1)}, u32[]{:S(2)}, u32[]{:S(2)}) collective-permute-start(bf16[256,384]{1,0:T(8,128)(2,1)S(1)} %get-tuple-element.54.refs_0_), channel_id=1, source_target_pairs={{0,12},{4,8},{8,4},{12,0},{1,13},{5,9},{9,5},{13,1},{2,14},{6,10},... | collective-permute-start | bytes 589832 | tf_op jit(solution)/shard_map/ppermute | solution.py:264
  19.8 1.3 %shard_map.56 = (bf16[120,1024]{1,0:T(8,128)(2,1)S(1)}, bf16[120,1024]{1,0:T(8,128)(2,1)S(1)}, bf16[120,1024]{1,0:T(8,128)(2,1)S(1)}, bf16[120,1024]{1,0:T(8,128)(2,1)S(1)}) custom-call(s32[3]{0:T(128)S(1)} %pad_add_fusion.pos, bf16[256,192]{1,0:T(8,128)(2,1)S(1)} %get-tuple-element.36.pick, bf16[256,192]{1,0:T(8,128)(2,1)S(1)} %get-tuple-element.37.pick_pair, ...), custom_call_target="tpu_custom_call" | custom-call | flops 402653184 | bytes 2752512 | tf_op jit(solution)/shard_map/pallas_call | solution.py:34
  21.0 1.6 %collective-permute-start.2 = (bf16[120,1024]{1,0:T(8,128)(2,1)S(1)}, bf16[120,1024]{1,0:T(8,128)(2,1)S(1)}, u32[]{:S(2)}, u32[]{:S(2)}) collective-permute-start(bf16[120,1024]{1,0:T(8,128)(2,1)S(1)} %get-tuple-element.39), channel_id=1, source_target_pairs={{0,2},{1,3},{2,0},{3,1},{16,18},{17,19},{18,16},{19,17},{4,6},{5,7... | collective-permute-start | bytes 737288 | tf_op jit(solution)/shard_map/ppermute | solution.py:297
  22.6 0.6 shard_map.59.rows
  23.3 8.7 %collective-permute-done.18.refs_2_ = bf16[256,384]{1,0:T(8,128)(2,1)S(1)} collective-permute-done((bf16[256,384]{1,0:T(8,128)(2,1)S(1)}, bf16[256,384]{1,0:T(8,128)(2,1)S(1)}, u32[]{:S(2)}, u32[]{:S(2)}) %collective-permute-start.18) | collective-permute-done | bytes 196640 | tf_op jit(solution)/shard_map/ppermute | solution.py:264
  32.0 1.3 %shard_map.64 = (f32[512,128]{1,0:T(8,128)S(1)}, bf16[512,128]{1,0:T(8,128)(2,1)S(1)}, f32[512,256]{1,0:T(8,128)S(1)}, bf16[512,256]{1,0:T(8,128)(2,1)S(1)}) custom-call(s32[3]{0:T(128)S(1)} %pad_add_fusion.pos, bf16[512,1024]{1,0:T(8,128)(2,1)S(1)} %shard_map.59.rows, bf16[256,384]{1,0:T(8,128)(2,1)S(1)} %get-tuple-element.54.refs_0_, ...), custom_call_target="tpu_custom_call" | custom-call | flops 402653184 | bytes 3014656 | tf_op jit(solution)/shard_map/pallas_call | solution.py:34
  33.3 1.6 %collective-permute-start.25 = (bf16[512,256]{1,0:T(8,128)(2,1)S(1)}, bf16[512,256]{1,0:T(8,128)(2,1)S(1)}, u32[]{:S(2)}, u32[]{:S(2)}) collective-permute-start(bf16[512,256]{1,0:T(8,128)(2,1)S(1)} %get-tuple-element.62), channel_id=1, source_target_pairs={{0,16},{16,0},{1,17},{17,1},{2,18},{18,2},{3,19},{19,3},{4,20},{20... | collective-permute-start | bytes 786440 | tf_op jit(solution)/shard_map/ppermute | solution.py:328
  34.9 2.9 %collective-permute-start.9 = (bf16[256,128]{1,0:T(8,128)(2,1)S(1)}, bf16[256,128]{1,0:T(8,128)(2,1)S(1)}, u32[]{:S(2)}, u32[]{:S(2)}) collective-permute-start(bf16[256,128]{1,0:T(8,128)(2,1)S(1)} %get-tuple-element.47.refs_0_), channel_id=1, source_target_pairs={{0,4},{4,0},{8,12},{12,8},{1,5},{5,1},{9,13},{13,9},{2,6},{6,2},{1... | collective-permute-start | bytes 196616 | tf_op jit(solution)/shard_map/ppermute | solution.py:264
  37.7 0.5 collective-permute-start.3
  38.3 2.4 %collective-permute-start.4 = (bf16[120,1024]{1,0:T(8,128)(2,1)S(1)}, bf16[120,1024]{1,0:T(8,128)(2,1)S(1)}, u32[]{:S(2)}, u32[]{:S(2)}) collective-permute-start(bf16[120,1024]{1,0:T(8,128)(2,1)S(1)} %get-tuple-element.41), channel_id=1, source_target_pairs={{0,18},{1,19},{2,16},{3,17},{16,2},{17,3},{18,0},{19,1},{4,22},{5,... | collective-permute-start | bytes 737288 | tf_op jit(solution)/shard_map/ppermute | solution.py:297
  40.7 3.0 %collective-permute-start.10 = (bf16[256,128]{1,0:T(8,128)(2,1)S(1)}, bf16[256,128]{1,0:T(8,128)(2,1)S(1)}, u32[]{:S(2)}, u32[]{:S(2)}) collective-permute-start(bf16[256,128]{1,0:T(8,128)(2,1)S(1)} %get-tuple-element.47.refs_0_), channel_id=1, source_target_pairs={{0,8},{4,12},{8,0},{12,4},{1,9},{5,13},{9,1},{13,5},{2,10},{6,14},... | collective-permute-start | bytes 196616 | tf_op jit(solution)/shard_map/ppermute | solution.py:264
  43.7 4.1 %collective-permute-done.10.refs_2_ = bf16[256,128]{1,0:T(8,128)(2,1)S(1)} collective-permute-done((bf16[256,128]{1,0:T(8,128)(2,1)S(1)}, bf16[256,128]{1,0:T(8,128)(2,1)S(1)}, u32[]{:S(2)}, u32[]{:S(2)}) %collective-permute-start.10) | collective-permute-done | bytes 65568 | tf_op jit(solution)/shard_map/ppermute | solution.py:264
  47.8 1.2 %collective-permute-start.11 = (bf16[256,128]{1,0:T(8,128)(2,1)S(1)}, bf16[256,128]{1,0:T(8,128)(2,1)S(1)}, u32[]{:S(2)}, u32[]{:S(2)}) collective-permute-start(bf16[256,128]{1,0:T(8,128)(2,1)S(1)} %get-tuple-element.47.refs_0_), channel_id=1, source_target_pairs={{0,12},{4,8},{8,4},{12,0},{1,13},{5,9},{9,5},{13,1},{2,14},{6,10},... | collective-permute-start | bytes 196616 | tf_op jit(solution)/shard_map/ppermute | solution.py:264
  49.0 4.9 %collective-permute-done.11.refs_3_ = bf16[256,128]{1,0:T(8,128)(2,1)S(1)} collective-permute-done((bf16[256,128]{1,0:T(8,128)(2,1)S(1)}, bf16[256,128]{1,0:T(8,128)(2,1)S(1)}, u32[]{:S(2)}, u32[]{:S(2)}) %collective-permute-start.11) | collective-permute-done | bytes 65568 | tf_op jit(solution)/shard_map/ppermute | solution.py:264
  53.8 0.5 collective-permute-start.20
  54.3 1.0 %shard_map.61 = (f32[512,128]{1,0:T(8,128)S(1)}, bf16[512,128]{1,0:T(8,128)(2,1)S(1)}) custom-call(s32[3]{0:T(128)S(1)} %pad_add_fusion.pos, bf16[512,1024]{1,0:T(8,128)(2,1)S(1)} %shard_map.59.rows, bf16[256,128]{1,0:T(8,128)(2,1)S(1)} %get-tuple-element.47.refs_0_, bf16[256,128]{1,0:T(8,128)(2,1)S(1)} %collective-permute-done.9.refs_1_, ...), custom_call_target="tpu_custom_call" | custom-call | flops 134217728 | bytes 1703936 | tf_op jit(solution)/shard_map/pallas_call | solution.py:34
  55.4 1.6 %collective-permute-start.12 = (bf16[512,128]{1,0:T(8,128)(2,1)S(1)}, bf16[512,128]{1,0:T(8,128)(2,1)S(1)}, u32[]{:S(2)}, u32[]{:S(2)}) collective-permute-start(bf16[512,128]{1,0:T(8,128)(2,1)S(1)} %get-tuple-element.49), channel_id=1, source_target_pairs={{0,16},{16,0},{1,17},{17,1},{2,18},{18,2},{3,19},{19,3},{4,20},{20... | collective-permute-start | bytes 393224 | tf_op jit(solution)/shard_map/ppermute | solution.py:328
  56.9 0.9 %shard_map.57.turned = bf16[1024,512]{1,0:T(8,128)(2,1)S(1)} custom-call(s32[3]{0:T(128)S(1)} %pad_add_fusion.pos, bf16[120,1024]{1,0:T(8,128)(2,1)S(1)} %get-tuple-element.38.refs_0_, bf16[120,1024]{1,0:T(8,128)(2,1)S(1)} %collective-permute-done.2.refs_1_, bf16[120,1024]{1,0:T(8,128)(2,1)S(1)} %collective-permute-done.3.refs_2_, ...), custom_call_target="tpu_custom_call" | custom-call | bytes 2031616 | tf_op jit(solution)/shard_map/pallas_call | solution.py:34
  57.9 1.0 %shard_map.67 = (f32[256,256]{1,0:T(8,128)S(1)}, bf16[256,256]{1,0:T(8,128)(2,1)S(1)}, bf16[256,256]{1,0:T(8,128)(2,1)S(1)}, bf16[256,256]{1,0:T(8,128)(2,1)S(1)}) custom-call(s32[3]{0:T(128)S(1)} %pad_add_fusion.pos, bf16[1024,512]{1,0:T(8,128)(2,1)S(1)} %shard_map.57.turned, f32[512,256]{1,0:T(8,128)S(1)} %get-tuple-element.61.kept, ...), custom_call_target="tpu_custom_call" | custom-call | flops 268435456 | bytes 2490368 | tf_op jit(solution)/shard_map/pallas_call | solution.py:34
  58.9 1.3 %collective-permute-start.26 = (bf16[256,256]{1,0:T(8,128)(2,1)S(1)}, bf16[256,256]{1,0:T(8,128)(2,1)S(1)}, u32[]{:S(2)}, u32[]{:S(2)}) collective-permute-start(bf16[256,256]{1,0:T(8,128)(2,1)S(1)} %get-tuple-element.64), channel_id=1, source_target_pairs={{0,12},{4,8},{8,4},{12,0},{1,13},{5,9},{9,5},{13,1},{2,14},{6,10},... | collective-permute-start | bytes 393224 | tf_op jit(solution)/shard_map/ppermute | solution.py:342
  60.5 2.9 %collective-permute-start.28 = (bf16[256,256]{1,0:T(8,128)(2,1)S(1)}, bf16[256,256]{1,0:T(8,128)(2,1)S(1)}, u32[]{:S(2)}, u32[]{:S(2)}) collective-permute-start(bf16[256,256]{1,0:T(8,128)(2,1)S(1)} %get-tuple-element.66), channel_id=1, source_target_pairs={{0,8},{4,12},{8,0},{12,4},{1,9},{5,13},{9,1},{13,5},{2,10},{6,14},... | collective-permute-start | bytes 393224 | tf_op jit(solution)/shard_map/ppermute | solution.py:342
  63.4 1.0 %shard_map.65 = (f32[256,128]{1,0:T(8,128)S(1)}, bf16[256,128]{1,0:T(8,128)(2,1)S(1)}, bf16[256,128]{1,0:T(8,128)(2,1)S(1)}, bf16[256,128]{1,0:T(8,128)(2,1)S(1)}) custom-call(s32[3]{0:T(128)S(1)} %pad_add_fusion.pos, bf16[1024,512]{1,0:T(8,128)(2,1)S(1)} %shard_map.57.turned, f32[512,128]{1,0:T(8,128)S(1)} %get-tuple-element.55.kept, ...), custom_call_target="tpu_custom_call" | custom-call | flops 134217728 | bytes 1769472 | tf_op jit(solution)/shard_map/pallas_call | solution.py:34
  64.4 1.3 %collective-permute-start.21 = (bf16[256,128]{1,0:T(8,128)(2,1)S(1)}, bf16[256,128]{1,0:T(8,128)(2,1)S(1)}, u32[]{:S(2)}, u32[]{:S(2)}) collective-permute-start(bf16[256,128]{1,0:T(8,128)(2,1)S(1)} %get-tuple-element.58), channel_id=1, source_target_pairs={{0,12},{4,8},{8,4},{12,0},{1,13},{5,9},{9,5},{13,1},{2,14},{6,10},... | collective-permute-start | bytes 196616 | tf_op jit(solution)/shard_map/ppermute | solution.py:342
  65.7 1.0 %shard_map.62 = (f32[256,128]{1,0:T(8,128)S(1)}, bf16[256,128]{1,0:T(8,128)(2,1)S(1)}, bf16[256,128]{1,0:T(8,128)(2,1)S(1)}, bf16[256,128]{1,0:T(8,128)(2,1)S(1)}) custom-call(s32[3]{0:T(128)S(1)} %pad_add_fusion.pos, bf16[1024,512]{1,0:T(8,128)(2,1)S(1)} %shard_map.57.turned, f32[512,128]{1,0:T(8,128)S(1)} %get-tuple-element.48.kept, ...), custom_call_target="tpu_custom_call" | custom-call | flops 134217728 | bytes 1769472 | tf_op jit(solution)/shard_map/pallas_call | solution.py:34
  66.8 2.6 %collective-permute-start.13 = (bf16[256,128]{1,0:T(8,128)(2,1)S(1)}, bf16[256,128]{1,0:T(8,128)(2,1)S(1)}, u32[]{:S(2)}, u32[]{:S(2)}) collective-permute-start(bf16[256,128]{1,0:T(8,128)(2,1)S(1)} %get-tuple-element.51), channel_id=1, source_target_pairs={{0,12},{4,8},{8,4},{12,0},{1,13},{5,9},{9,5},{13,1},{2,14},{6,10},... | collective-permute-start | bytes 196616 | tf_op jit(solution)/shard_map/ppermute | solution.py:342
  69.4 1.1 %collective-permute-start.14 = (bf16[256,128]{1,0:T(8,128)(2,1)S(1)}, bf16[256,128]{1,0:T(8,128)(2,1)S(1)}, u32[]{:S(2)}, u32[]{:S(2)}) collective-permute-start(bf16[256,128]{1,0:T(8,128)(2,1)S(1)} %get-tuple-element.52), channel_id=1, source_target_pairs={{0,4},{4,0},{8,12},{12,8},{1,5},{5,1},{9,13},{13,9},{2,6},{6,2},{1... | collective-permute-start | bytes 196616 | tf_op jit(solution)/shard_map/ppermute | solution.py:342
  70.5 2.3 %collective-permute-done.28.refs_2_ = bf16[256,256]{1,0:T(8,128)(2,1)S(1)} collective-permute-done((bf16[256,256]{1,0:T(8,128)(2,1)S(1)}, bf16[256,256]{1,0:T(8,128)(2,1)S(1)}, u32[]{:S(2)}, u32[]{:S(2)}) %collective-permute-start.28) | collective-permute-done | bytes 131104 | tf_op jit(solution)/shard_map/ppermute | solution.py:342
  72.9 0.6 shard_map.68.refs_2_
  73.5 3.3 %collective-permute-start.15 = (bf16[256,128]{1,0:T(8,128)(2,1)S(1)}, bf16[256,128]{1,0:T(8,128)(2,1)S(1)}, u32[]{:S(2)}, u32[]{:S(2)}) collective-permute-start(bf16[256,128]{1,0:T(8,128)(2,1)S(1)} %get-tuple-element.53), channel_id=1, source_target_pairs={{0,8},{4,12},{8,0},{12,4},{1,9},{5,13},{9,1},{13,5},{2,10},{6,14},... | collective-permute-start | bytes 196616 | tf_op jit(solution)/shard_map/ppermute | solution.py:342
  76.8 2.2 %collective-permute-start.29 = (bf16[256,256]{1,0:T(8,128)(2,1)S(1)}, bf16[256,256]{1,0:T(8,128)(2,1)S(1)}, u32[]{:S(2)}, u32[]{:S(2)}) collective-permute-start(bf16[256,256]{1,0:T(8,128)(2,1)S(1)} %shard_map.68.refs_2_), channel_id=1, source_target_pairs={{0,16},{16,0},{1,17},{17,1},{2,18},{18,2},{3,19},{19,3},{4,20},{20... | collective-permute-start | bytes 393224 | tf_op jit(solution)/shard_map/ppermute | solution.py:347
  79.0 0.6 shard_map.66.refs_0_
  79.6 1.8 %collective-permute-start.24 = (bf16[256,128]{1,0:T(8,128)(2,1)S(1)}, bf16[256,128]{1,0:T(8,128)(2,1)S(1)}, u32[]{:S(2)}, u32[]{:S(2)}) collective-permute-start(bf16[256,128]{1,0:T(8,128)(2,1)S(1)} %shard_map.66.refs_0_), channel_id=1, source_target_pairs={{0,16},{16,0},{1,17},{17,1},{2,18},{18,2},{3,19},{19,3},{4,20},{20... | collective-permute-start | bytes 196616 | tf_op jit(solution)/shard_map/ppermute | solution.py:347
  81.4 0.6 shard_map.63.refs_4_
  82.0 0.3 collective-permute-start.16
  82.3 1.6 %collective-permute-done.24.refs_1_ = bf16[256,128]{1,0:T(8,128)(2,1)S(1)} collective-permute-done((bf16[256,128]{1,0:T(8,128)(2,1)S(1)}, bf16[256,128]{1,0:T(8,128)(2,1)S(1)}, u32[]{:S(2)}, u32[]{:S(2)}) %collective-permute-start.24) | collective-permute-done | bytes 65568 | tf_op jit(solution)/shard_map/ppermute | solution.py:347
  83.9 1.3 %shard_map.69.refs_1_ = bf16[512,512]{1,0:T(8,128)(2,1)} custom-call(s32[3]{0:T(128)S(1)} %pad_add_fusion.pos, bf16[256,128]{1,0:T(8,128)(2,1)S(1)} %shard_map.66.refs_0_, bf16[256,128]{1,0:T(8,128)(2,1)S(1)} %collective-permute-done.24.refs_1_, bf16[256,256]{1,0:T(8,128)(2,1)S(1)} %shard_map.68.refs_2_, ...), custom_call_target="tpu_custom_call" | custom-call | bytes 983040 | tf_op jit(solution)/shard_map/pallas_call | solution.py:34
  85.3 1.1 %collective-permute-done.16.refs_0_ = bf16[256,128]{1,0:T(8,128)(2,1)S(1)} collective-permute-done((bf16[256,128]{1,0:T(8,128)(2,1)S(1)}, bf16[256,128]{1,0:T(8,128)(2,1)S(1)}, u32[]{:S(2)}, u32[]{:S(2)}) %collective-permute-start.16) | collective-permute-done | bytes 65568 | tf_op jit(solution)/shard_map/ppermute | solution.py:347
  86.3 1.2 %shard_map.70 = bf16[512,512]{1,0:T(8,128)(2,1)} custom-call(s32[3]{0:T(128)S(1)} %pad_add_fusion.pos, bf16[256,128]{1,0:T(8,128)(2,1)S(1)} %collective-permute-done.16.refs_0_, bf16[512,512]{1,0:T(8,128)(2,1)} %shard_map.69.refs_1_), custom_call_target="tpu_custom_call", output_to_operand_aliasing={{}: (2, {})} | custom-call | bytes 1114112 | tf_op jit(solution)/shard_map/pallas_call | solution.py:34
  (33 shorter events, 0.8 us)
Async XLA Ops:
  0.0 0.7 copy-start.1
  0.0 5.4 %collective-permute-start.5 = (bf16[192,2048]{1,0:T(8,128)(2,1)}, bf16[192,2048]{1,0:T(8,128)(2,1)S(1)}, u32[]{:S(2)}, u32[]{:S(2)}) collective-permute-start(bf16[192,2048]{1,0:T(8,128)(2,1)} %rows.2), channel_id=1, source_target_pairs={{0,1},{1,0},{2,3},{3,2},{4,5},{5,4},{6,7},{7,6},{8,9},{9,8},{10,11... | collective-permute-start | bytes 2359304 | tf_op jit(solution)/shard_map/ppermute | solution.py:242
  0.5 14.4 %collective-permute-start.1 = (bf16[192,2048]{1,0:T(8,128)(2,1)}, bf16[192,2048]{1,0:T(8,128)(2,1)S(1)}, u32[]{:S(2)}, u32[]{:S(2)}) collective-permute-start(bf16[192,2048]{1,0:T(8,128)(2,1)} %rows.3), channel_id=1, source_target_pairs={{0,1},{1,0},{2,3},{3,2},{4,5},{5,4},{6,7},{7,6},{8,9},{9,8},{10,11... | collective-permute-start | bytes 2359304 | tf_op jit(solution)/shard_map/ppermute | solution.py:244
  0.7 3.1 %collective-permute-start = (s32[1,192]{1,0:T(1,128)S(1)}, s32[1,192]{1,0:T(1,128)S(1)}, u32[]{:S(2)}, u32[]{:S(2)}) collective-permute-start(s32[1,192]{1,0:T(1,128)S(1)} %bitcast.7), channel_id=1, source_target_pairs={{0,1},{1,0},{2,3},{3,2},{4,5},{5,4},{6,7},{7,6},{8,9},{9,8},{10,11... | collective-permute-start | bytes 2312 | tf_op jit(solution)/shard_map/ppermute | solution.py:243
  5.4 14.3 %copy-start = (bf16[192,2048]{1,0:T(8,128)(2,1)S(1)}, bf16[192,2048]{1,0:T(8,128)(2,1)}, u32[]{:S(2)}) copy-start(bf16[192,2048]{1,0:T(8,128)(2,1)} %rows.3) | copy-start | bytes 2359300
  6.7 10.7 %collective-permute-start.6 = (bf16[120,1024]{1,0:T(8,128)(2,1)S(1)}, bf16[120,1024]{1,0:T(8,128)(2,1)S(1)}, u32[]{:S(2)}, u32[]{:S(2)}) collective-permute-start(bf16[120,1024]{1,0:T(8,128)(2,1)S(1)} %get-tuple-element.44), channel_id=1, source_target_pairs={{0,2},{1,3},{2,0},{3,1},{16,18},{17,19},{18,16},{19,17},{4,6},{5,7... | collective-permute-start | bytes 737288 | tf_op jit(solution)/shard_map/ppermute | solution.py:297
  9.7 11.4 %collective-permute-start.7 = (bf16[120,1024]{1,0:T(8,128)(2,1)S(1)}, bf16[120,1024]{1,0:T(8,128)(2,1)S(1)}, u32[]{:S(2)}, u32[]{:S(2)}) collective-permute-start(bf16[120,1024]{1,0:T(8,128)(2,1)S(1)} %get-tuple-element.45), channel_id=1, source_target_pairs={{0,16},{1,17},{2,18},{3,19},{16,0},{17,1},{18,2},{19,3},{4,20},{5,... | collective-permute-start | bytes 737288 | tf_op jit(solution)/shard_map/ppermute | solution.py:297
  11.2 11.5 %collective-permute-start.8 = (bf16[120,1024]{1,0:T(8,128)(2,1)S(1)}, bf16[120,1024]{1,0:T(8,128)(2,1)S(1)}, u32[]{:S(2)}, u32[]{:S(2)}) collective-permute-start(bf16[120,1024]{1,0:T(8,128)(2,1)S(1)} %get-tuple-element.46), channel_id=1, source_target_pairs={{0,18},{1,19},{2,16},{3,17},{16,2},{17,3},{18,0},{19,1},{4,22},{5,... | collective-permute-start | bytes 737288 | tf_op jit(solution)/shard_map/ppermute | solution.py:297
  12.8 10.5 %collective-permute-start.17 = (bf16[256,384]{1,0:T(8,128)(2,1)S(1)}, bf16[256,384]{1,0:T(8,128)(2,1)S(1)}, u32[]{:S(2)}, u32[]{:S(2)}) collective-permute-start(bf16[256,384]{1,0:T(8,128)(2,1)S(1)} %get-tuple-element.54.refs_0_), channel_id=1, source_target_pairs={{0,4},{4,0},{8,12},{12,8},{1,5},{5,1},{9,13},{13,9},{2,6},{6,2},{1... | collective-permute-start | bytes 589832 | tf_op jit(solution)/shard_map/ppermute | solution.py:264
  14.9 17.1 %collective-permute-start.18 = (bf16[256,384]{1,0:T(8,128)(2,1)S(1)}, bf16[256,384]{1,0:T(8,128)(2,1)S(1)}, u32[]{:S(2)}, u32[]{:S(2)}) collective-permute-start(bf16[256,384]{1,0:T(8,128)(2,1)S(1)} %get-tuple-element.54.refs_0_), channel_id=1, source_target_pairs={{0,8},{4,12},{8,0},{12,4},{1,9},{5,13},{9,1},{13,5},{2,10},{6,14},... | collective-permute-start | bytes 589832 | tf_op jit(solution)/shard_map/ppermute | solution.py:264
  17.5 14.5 %collective-permute-start.19 = (bf16[256,384]{1,0:T(8,128)(2,1)S(1)}, bf16[256,384]{1,0:T(8,128)(2,1)S(1)}, u32[]{:S(2)}, u32[]{:S(2)}) collective-permute-start(bf16[256,384]{1,0:T(8,128)(2,1)S(1)} %get-tuple-element.54.refs_0_), channel_id=1, source_target_pairs={{0,12},{4,8},{8,4},{12,0},{1,13},{5,9},{9,5},{13,1},{2,14},{6,10},... | collective-permute-start | bytes 589832 | tf_op jit(solution)/shard_map/ppermute | solution.py:264
  21.0 34.3 %collective-permute-start.2 = (bf16[120,1024]{1,0:T(8,128)(2,1)S(1)}, bf16[120,1024]{1,0:T(8,128)(2,1)S(1)}, u32[]{:S(2)}, u32[]{:S(2)}) collective-permute-start(bf16[120,1024]{1,0:T(8,128)(2,1)S(1)} %get-tuple-element.39), channel_id=1, source_target_pairs={{0,2},{1,3},{2,0},{3,1},{16,18},{17,19},{18,16},{19,17},{4,6},{5,7... | collective-permute-start | bytes 737288 | tf_op jit(solution)/shard_map/ppermute | solution.py:297
  33.3 24.6 %collective-permute-start.25 = (bf16[512,256]{1,0:T(8,128)(2,1)S(1)}, bf16[512,256]{1,0:T(8,128)(2,1)S(1)}, u32[]{:S(2)}, u32[]{:S(2)}) collective-permute-start(bf16[512,256]{1,0:T(8,128)(2,1)S(1)} %get-tuple-element.62), channel_id=1, source_target_pairs={{0,16},{16,0},{1,17},{17,1},{2,18},{18,2},{3,19},{19,3},{4,20},{20... | collective-permute-start | bytes 786440 | tf_op jit(solution)/shard_map/ppermute | solution.py:328
  34.9 5.9 %collective-permute-start.9 = (bf16[256,128]{1,0:T(8,128)(2,1)S(1)}, bf16[256,128]{1,0:T(8,128)(2,1)S(1)}, u32[]{:S(2)}, u32[]{:S(2)}) collective-permute-start(bf16[256,128]{1,0:T(8,128)(2,1)S(1)} %get-tuple-element.47.refs_0_), channel_id=1, source_target_pairs={{0,4},{4,0},{8,12},{12,8},{1,5},{5,1},{9,13},{13,9},{2,6},{6,2},{1... | collective-permute-start | bytes 196616 | tf_op jit(solution)/shard_map/ppermute | solution.py:264
  37.7 19.2 %collective-permute-start.3 = (bf16[120,1024]{1,0:T(8,128)(2,1)S(1)}, bf16[120,1024]{1,0:T(8,128)(2,1)S(1)}, u32[]{:S(2)}, u32[]{:S(2)}) collective-permute-start(bf16[120,1024]{1,0:T(8,128)(2,1)S(1)} %get-tuple-element.40), channel_id=1, source_target_pairs={{0,16},{1,17},{2,18},{3,19},{16,0},{17,1},{18,2},{19,3},{4,20},{5,... | collective-permute-start | bytes 737288 | tf_op jit(solution)/shard_map/ppermute | solution.py:297
  38.3 18.7 %collective-permute-start.4 = (bf16[120,1024]{1,0:T(8,128)(2,1)S(1)}, bf16[120,1024]{1,0:T(8,128)(2,1)S(1)}, u32[]{:S(2)}, u32[]{:S(2)}) collective-permute-start(bf16[120,1024]{1,0:T(8,128)(2,1)S(1)} %get-tuple-element.41), channel_id=1, source_target_pairs={{0,18},{1,19},{2,16},{3,17},{16,2},{17,3},{18,0},{19,1},{4,22},{5,... | collective-permute-start | bytes 737288 | tf_op jit(solution)/shard_map/ppermute | solution.py:297
  40.7 7.0 %collective-permute-start.10 = (bf16[256,128]{1,0:T(8,128)(2,1)S(1)}, bf16[256,128]{1,0:T(8,128)(2,1)S(1)}, u32[]{:S(2)}, u32[]{:S(2)}) collective-permute-start(bf16[256,128]{1,0:T(8,128)(2,1)S(1)} %get-tuple-element.47.refs_0_), channel_id=1, source_target_pairs={{0,8},{4,12},{8,0},{12,4},{1,9},{5,13},{9,1},{13,5},{2,10},{6,14},... | collective-permute-start | bytes 196616 | tf_op jit(solution)/shard_map/ppermute | solution.py:264
  47.8 6.1 %collective-permute-start.11 = (bf16[256,128]{1,0:T(8,128)(2,1)S(1)}, bf16[256,128]{1,0:T(8,128)(2,1)S(1)}, u32[]{:S(2)}, u32[]{:S(2)}) collective-permute-start(bf16[256,128]{1,0:T(8,128)(2,1)S(1)} %get-tuple-element.47.refs_0_), channel_id=1, source_target_pairs={{0,12},{4,8},{8,4},{12,0},{1,13},{5,9},{9,5},{13,1},{2,14},{6,10},... | collective-permute-start | bytes 196616 | tf_op jit(solution)/shard_map/ppermute | solution.py:264
  53.8 9.5 %collective-permute-start.20 = (bf16[512,128]{1,0:T(8,128)(2,1)S(1)}, bf16[512,128]{1,0:T(8,128)(2,1)S(1)}, u32[]{:S(2)}, u32[]{:S(2)}) collective-permute-start(bf16[512,128]{1,0:T(8,128)(2,1)S(1)} %get-tuple-element.56), channel_id=1, source_target_pairs={{0,16},{16,0},{1,17},{17,1},{2,18},{18,2},{3,19},{19,3},{4,20},{20... | collective-permute-start | bytes 393224 | tf_op jit(solution)/shard_map/ppermute | solution.py:328
  55.4 10.3 %collective-permute-start.12 = (bf16[512,128]{1,0:T(8,128)(2,1)S(1)}, bf16[512,128]{1,0:T(8,128)(2,1)S(1)}, u32[]{:S(2)}, u32[]{:S(2)}) collective-permute-start(bf16[512,128]{1,0:T(8,128)(2,1)S(1)} %get-tuple-element.49), channel_id=1, source_target_pairs={{0,16},{16,0},{1,17},{17,1},{2,18},{18,2},{3,19},{19,3},{4,20},{20... | collective-permute-start | bytes 393224 | tf_op jit(solution)/shard_map/ppermute | solution.py:328
  58.9 7.9 %collective-permute-start.26 = (bf16[256,256]{1,0:T(8,128)(2,1)S(1)}, bf16[256,256]{1,0:T(8,128)(2,1)S(1)}, u32[]{:S(2)}, u32[]{:S(2)}) collective-permute-start(bf16[256,256]{1,0:T(8,128)(2,1)S(1)} %get-tuple-element.64), channel_id=1, source_target_pairs={{0,12},{4,8},{8,4},{12,0},{1,13},{5,9},{9,5},{13,1},{2,14},{6,10},... | collective-permute-start | bytes 393224 | tf_op jit(solution)/shard_map/ppermute | solution.py:342
  60.2 9.2 %collective-permute-start.27 = (bf16[256,256]{1,0:T(8,128)(2,1)S(1)}, bf16[256,256]{1,0:T(8,128)(2,1)S(1)}, u32[]{:S(2)}, u32[]{:S(2)}) collective-permute-start(bf16[256,256]{1,0:T(8,128)(2,1)S(1)} %get-tuple-element.65), channel_id=1, source_target_pairs={{0,4},{4,0},{8,12},{12,8},{1,5},{5,1},{9,13},{13,9},{2,6},{6,2},{1... | collective-permute-start | bytes 393224 | tf_op jit(solution)/shard_map/ppermute | solution.py:342
  60.5 12.4 %collective-permute-start.28 = (bf16[256,256]{1,0:T(8,128)(2,1)S(1)}, bf16[256,256]{1,0:T(8,128)(2,1)S(1)}, u32[]{:S(2)}, u32[]{:S(2)}) collective-permute-start(bf16[256,256]{1,0:T(8,128)(2,1)S(1)} %get-tuple-element.66), channel_id=1, source_target_pairs={{0,8},{4,12},{8,0},{12,4},{1,9},{5,13},{9,1},{13,5},{2,10},{6,14},... | collective-permute-start | bytes 393224 | tf_op jit(solution)/shard_map/ppermute | solution.py:342
  64.4 9.1 %collective-permute-start.21 = (bf16[256,128]{1,0:T(8,128)(2,1)S(1)}, bf16[256,128]{1,0:T(8,128)(2,1)S(1)}, u32[]{:S(2)}, u32[]{:S(2)}) collective-permute-start(bf16[256,128]{1,0:T(8,128)(2,1)S(1)} %get-tuple-element.58), channel_id=1, source_target_pairs={{0,12},{4,8},{8,4},{12,0},{1,13},{5,9},{9,5},{13,1},{2,14},{6,10},... | collective-permute-start | bytes 196616 | tf_op jit(solution)/shard_map/ppermute | solution.py:342
  65.7 11.1 %collective-permute-start.22 = (bf16[256,128]{1,0:T(8,128)(2,1)S(1)}, bf16[256,128]{1,0:T(8,128)(2,1)S(1)}, u32[]{:S(2)}, u32[]{:S(2)}) collective-permute-start(bf16[256,128]{1,0:T(8,128)(2,1)S(1)} %get-tuple-element.59), channel_id=1, source_target_pairs={{0,4},{4,0},{8,12},{12,8},{1,5},{5,1},{9,13},{13,9},{2,6},{6,2},{1... | collective-permute-start | bytes 196616 | tf_op jit(solution)/shard_map/ppermute | solution.py:342
  66.8 14.7 %collective-permute-start.13 = (bf16[256,128]{1,0:T(8,128)(2,1)S(1)}, bf16[256,128]{1,0:T(8,128)(2,1)S(1)}, u32[]{:S(2)}, u32[]{:S(2)}) collective-permute-start(bf16[256,128]{1,0:T(8,128)(2,1)S(1)} %get-tuple-element.51), channel_id=1, source_target_pairs={{0,12},{4,8},{8,4},{12,0},{1,13},{5,9},{9,5},{13,1},{2,14},{6,10},... | collective-permute-start | bytes 196616 | tf_op jit(solution)/shard_map/ppermute | solution.py:342
  69.4 12.0 %collective-permute-start.14 = (bf16[256,128]{1,0:T(8,128)(2,1)S(1)}, bf16[256,128]{1,0:T(8,128)(2,1)S(1)}, u32[]{:S(2)}, u32[]{:S(2)}) collective-permute-start(bf16[256,128]{1,0:T(8,128)(2,1)S(1)} %get-tuple-element.52), channel_id=1, source_target_pairs={{0,4},{4,0},{8,12},{12,8},{1,5},{5,1},{9,13},{13,9},{2,6},{6,2},{1... | collective-permute-start | bytes 196616 | tf_op jit(solution)/shard_map/ppermute | solution.py:342
  72.9 6.2 %collective-permute-start.23 = (bf16[256,128]{1,0:T(8,128)(2,1)S(1)}, bf16[256,128]{1,0:T(8,128)(2,1)S(1)}, u32[]{:S(2)}, u32[]{:S(2)}) collective-permute-start(bf16[256,128]{1,0:T(8,128)(2,1)S(1)} %get-tuple-element.60), channel_id=1, source_target_pairs={{0,8},{4,12},{8,0},{12,4},{1,9},{5,13},{9,1},{13,5},{2,10},{6,14},... | collective-permute-start | bytes 196616 | tf_op jit(solution)/shard_map/ppermute | solution.py:342
  73.5 8.0 %collective-permute-start.15 = (bf16[256,128]{1,0:T(8,128)(2,1)S(1)}, bf16[256,128]{1,0:T(8,128)(2,1)S(1)}, u32[]{:S(2)}, u32[]{:S(2)}) collective-permute-start(bf16[256,128]{1,0:T(8,128)(2,1)S(1)} %get-tuple-element.53), channel_id=1, source_target_pairs={{0,8},{4,12},{8,0},{12,4},{1,9},{5,13},{9,1},{13,5},{2,10},{6,14},... | collective-permute-start | bytes 196616 | tf_op jit(solution)/shard_map/ppermute | solution.py:342
  76.8 7.2 %collective-permute-start.29 = (bf16[256,256]{1,0:T(8,128)(2,1)S(1)}, bf16[256,256]{1,0:T(8,128)(2,1)S(1)}, u32[]{:S(2)}, u32[]{:S(2)}) collective-permute-start(bf16[256,256]{1,0:T(8,128)(2,1)S(1)} %shard_map.68.refs_2_), channel_id=1, source_target_pairs={{0,16},{16,0},{1,17},{17,1},{2,18},{18,2},{3,19},{19,3},{4,20},{20... | collective-permute-start | bytes 393224 | tf_op jit(solution)/shard_map/ppermute | solution.py:347
  79.6 4.3 %collective-permute-start.24 = (bf16[256,128]{1,0:T(8,128)(2,1)S(1)}, bf16[256,128]{1,0:T(8,128)(2,1)S(1)}, u32[]{:S(2)}, u32[]{:S(2)}) collective-permute-start(bf16[256,128]{1,0:T(8,128)(2,1)S(1)} %shard_map.66.refs_0_), channel_id=1, source_target_pairs={{0,16},{16,0},{1,17},{17,1},{2,18},{18,2},{3,19},{19,3},{4,20},{20... | collective-permute-start | bytes 196616 | tf_op jit(solution)/shard_map/ppermute | solution.py:347
  82.0 4.3 %collective-permute-start.16 = (bf16[256,128]{1,0:T(8,128)(2,1)S(1)}, bf16[256,128]{1,0:T(8,128)(2,1)S(1)}, u32[]{:S(2)}, u32[]{:S(2)}) collective-permute-start(bf16[256,128]{1,0:T(8,128)(2,1)S(1)} %shard_map.63.refs_4_), channel_id=1, source_target_pairs={{0,16},{16,0},{1,17},{17,1},{2,18},{18,2},{3,19},{19,3},{4,20},{20... | collective-permute-start | bytes 196616 | tf_op jit(solution)/shard_map/ppermute | solution.py:347

commit v5 on v4

--- a/solution.py
+++ b/solution.py
@@ -7,7 +7,7 @@
 from jax.sharding import PartitionSpec as P
 
 QB = 32
-SPLITS = ((1, 2), (1,))
+SPLITS = ((1, 1), (1, 1))
 F32 = jnp.float32
 BF16 = jnp.bfloat16
 
@@ -46,6 +46,18 @@
 
 def node_order(nodes):
     return [s for s in (3, 1, 2) if s < nodes] + list(range(4, nodes))
+
+
+def plan_of(nodes, aligned):
+    order = node_order(nodes)
+    every = order + [0]
+    chunks = sum(len(split) for split in SPLITS)
+    if not aligned:
+        return [every], [([i], every) for i in range(chunks)], [[i] for i in range(chunks)]
+    early, late = order[: nodes // 2], order[nodes // 2 :] + [0]
+    jobs = [([0], early), ([1], early), ([0, 1], late)]
+    jobs += [([i], every) for i in range(2, chunks)]
+    return [early, late], jobs, [[0, 1]] + [[i] for i in range(2, chunks)]
 
 
 def slots_of(copies, pairs):
@@ -110,22 +122,24 @@
         held = held + jnp.sum(marks, axis=1, keepdims=True)
 
 
-def place_rows(dims, stride, blocks, pos, picks, sources, outs):
-    copies, _, locals_ = dims
+def place_rows(dims, stride, columns, pos, picks, sources, outs):
+    copies, nodes, locals_ = dims
     pairs = locals_ // 2
-    rows = outs[0].shape[0]
-    width = sources[0].shape[1] // (copies * blocks)
-    for j in reversed(range(copies)):
-        which = traced_mate(pos[0], j, copies)
-        for b in range(blocks):
-            at = pl.multiple_of((b * copies + which) * width, 128)
-            got = sum(
-                jnp.dot(pick[...], source[:, pl.ds(at, width)], preferred_element_type=F32)
-                for pick, source in zip(picks, sources)
-            ).astype(BF16)
-            for k in range(pairs):
-                out = outs[j * pairs + k]
-                out[:, b * width : (b + 1) * width] = got[k * stride : k * stride + rows]
+    rows, width = outs[0].shape[0], outs[0].shape[1] // len(columns[0])
+    for g, group in enumerate(columns):
+        for j in reversed(range(copies)):
+            which = traced_mate(pos[0], j, copies)
+            for b, (relative, block) in enumerate(group):
+                if relative:
+                    block = traced_mate(pos[1], block, nodes)
+                at = pl.multiple_of((block * copies + which) * width, 128)
+                got = sum(
+                    jnp.dot(pick[...], source[:, pl.ds(at, width)], preferred_element_type=F32)
+                    for pick, source in zip(picks, sources)
+                ).astype(BF16)
+                for k in range(pairs):
+                    out = outs[(g * copies + j) * pairs + k]
+                    out[:, b * width : (b + 1) * width] = got[k * stride : k * stride + rows]
 
 
 def choose_body(dims, stride, pos, ids, ids_pair, rows, *refs):
@@ -136,8 +150,8 @@
     move.wait()
 
 
-def route_body(dims, stride, blocks, pos, pick, pick_pair, rows, rows_pair, *outs):
-    place_rows(dims, stride, blocks, pos, (pick, pick_pair), (rows, rows_pair), outs)
+def route_body(dims, stride, columns, pos, pick, pick_pair, rows, rows_pair, *outs):
+    place_rows(dims, stride, columns, pos, (pick, pick_pair), (rows, rows_pair), outs)
 
 
 def join_body(dims, stride, pos, *refs):
@@ -178,25 +192,44 @@
         begin = end
 
 
-def down_body(dims, factor, pos, turned, kept, *refs):
-    _, nodes, _ = dims
-    got, outs, act = refs[: -nodes - 1], refs[-nodes - 1 : -1], refs[-1]
-    pre = kept[...]
-    for part in got:
-        pre = pre + part[...].astype(F32)
-    act[...] = (pre * jax.nn.sigmoid(pre)).astype(BF16)
+def down_body(dims, factor, spots, sources, emits, pos, *refs):
+    nodes = dims[1]
+    tables = 1 + max(table for _, table, _ in spots)
+    turned, rest, act = refs[:tables], list(refs[tables:-1]), refs[-1]
+    begin = 0
+    used = sum(sources)
+    outs, kept_acts = rest[used : used + len(spots)], rest[used + len(spots) :]
+    for held, emit in zip(sources, emits):
+        if held and rest[0].dtype == F32:
+            pre = rest[0][...]
+            for part in rest[1:held]:
+                pre = pre + part[...].astype(F32)
+            value = (pre * jax.nn.sigmoid(pre)).astype(BF16)
+        else:
+            value = rest[0][...]
+        rest = rest[held:]
+        end = begin + value.shape[1]
+        act[:, begin:end] = value
+        if emit:
+            kept_acts[0][...] = value
+            kept_acts = kept_acts[1:]
+        begin = end
     mine = outs[0].shape[0]
-    for s in reversed(range(nodes)):
-        at = pl.multiple_of(traced_mate(pos[1], s, nodes) * mine, 16)
-        term = jnp.dot(turned[pl.ds(at, mine), :], act[...], preferred_element_type=F32)
-        outs[s][...] = (term * factor).astype(outs[s].dtype)
-
-
-def sum_body(pos, own, *refs):
-    total = own[...]
-    for part in refs[:-1]:
-        total = total + part[...].astype(F32)
-    refs[-1][...] = total.astype(BF16)
+    for (s, table, place), out in zip(spots, outs):
+        at = place * mine
+        if place < 0:
+            at = pl.multiple_of(traced_mate(pos[1], s, nodes) * mine, 16)
+        term = jnp.dot(turned[table][pl.ds(at, mine), :], act[...], preferred_element_type=F32)
+        out[...] = (term * factor).astype(out.dtype)
+
+
+def sum_body(begins, pos, own, *refs):
+    total, out = refs[-1], refs[-2]
+    total[...] = own[...]
+    for begin, part in zip(begins, refs[:-2]):
+        end = begin + part.shape[1]
+        total[:, begin:end] += part[...].astype(F32)
+    out[...] = total[...].astype(BF16)
 
 
 def lay_body(dims, spots, pos, *refs):
@@ -230,9 +263,13 @@
     everyone = copies * pairs * stride
     pos = jnp.stack([lax.axis_index(a) for a in ("dp", "node", "local")]).astype(jnp.int32)
 
-    blocks = nodes
-    if mine % 128:
-        blocks = 1
+    aligned = mine % 128 == 0
+    halves, jobs, outputs = plan_of(nodes, aligned)
+    if aligned:
+        columns_x = [[(False, b) for b in range(nodes)]]
+        columns_y = [[(True, s) for s in half] for half in halves]
+    else:
+        columns_x = columns_y = [[(False, 0)]]
         tokens, cotangent = (
             a.reshape(count, nodes, copies, mine).swapaxes(1, 2).reshape(count, features)
             for a in (tokens, cotangent)
@@ -273,17 +310,19 @@
         space=[pltpu.VMEM, pltpu.VMEM, pltpu.HBM],
     )
 
-    def route(rows, rows_pair):
-        return call(
-            functools.partial(route_body, dims, stride, blocks),
-            [shape(sent_rows, part, BF16)] * (copies * pairs),
+    def route(columns, rows, rows_pair):
+        pieces = call(
+            functools.partial(route_body, dims, stride, columns),
+            [shape(sent_rows, part // len(columns), BF16)] * (len(columns) * copies * pairs),
             pos,
             [*picks, rows, rows_pair],
             flops=4 * pairs * stride * count * features,
         )
-
-    pieces_x = route(tokens, tokens_pair)
-    pieces_y = route(cotangent, cotangent_pair)
+        step = copies * pairs
+        return [pieces[g * step : (g + 1) * step] for g in range(len(columns))]
+
+    (pieces_x,) = route(columns_x, tokens, tokens_pair)
+    pieces_y = route(columns_y, cotangent, cotangent_pair)
 
     def exchange(pieces):
         moved = list(pieces)
@@ -297,18 +336,23 @@
             moved[at] = lax.ppermute(pieces[at], ("dp", "local"), links)
         return moved
 
-    got_x = exchange(pieces_x)
-    got_dy = exchange(pieces_y)
     (rows_x,) = call(
-        functools.partial(join_body, dims, stride), [shape(everyone, part, BF16)], pos, got_x
-    )
-    (turned,) = call(
-        functools.partial(turn_body, dims, stride),
-        [shape(part, everyone, BF16)],
+        functools.partial(join_body, dims, stride),
+        [shape(everyone, part, BF16)],
         pos,
-        got_dy,
-        [pltpu.VMEM((everyone, part), BF16)],
-    )
+        exchange(pieces_x),
+    )
+    turned = []
+    for h, pieces in enumerate(pieces_y):
+        cols = part // len(pieces_y)
+        got_dy = exchange(pieces)
+        turned += call(
+            functools.partial(turn_body, dims, stride),
+            [shape(cols, everyone, BF16)],
+            pos,
+            got_dy,
+            [pltpu.VMEM((everyone, cols), BF16)],
+        )
     factor = float(count * copies * nodes) ** (-0.5)
     groups = []
     for i, split in enumerate(SPLITS):
@@ -322,34 +366,65 @@
             flops=2 * everyone * part * gathered[i],
         )
         groups += list(zip(widths, parts[::2], parts[1::2]))
-    finished = []
+    acts = []
     for wide, kept, sent in groups:
         if copies == 2:
-            others = [lax.ppermute(sent, "dp", [(0, 1), (1, 0)])]
+            acts.append([kept, lax.ppermute(sent, "dp", [(0, 1), (1, 0)])])
         else:
-            kept, others = lax.psum(kept, "dp"), []
+            acts.append([lax.psum(kept, "dp")])
+    owns, arrived = {}, {}
+    for n, (chunks, targets) in enumerate(jobs):
+        wide = sum(groups[i][0] for i in chunks)
+        tables = [h for h, half in enumerate(halves) if set(half) & set(targets)]
+        spots = []
+        for s in targets:
+            (h,) = [h for h in tables if s in halves[h]]
+            spots.append((s, tables.index(h), halves[h].index(s) if aligned else -1))
+        again = [any(i in other for other, _ in jobs[n + 1 :]) for i in chunks]
+        emits = [more and acts[i][0].dtype == F32 for i, more in zip(chunks, again)]
+        kinds = [shape(mine, wide, BF16 if s else F32) for s in targets]
+        kinds += [shape(everyone, groups[i][0], BF16) for i, emit in zip(chunks, emits) if emit]
         terms = call(
-            functools.partial(down_body, dims, factor),
-            [shape(mine, wide, F32)] + [shape(mine, wide, BF16)] * (nodes - 1),
+            functools.partial(down_body, dims, factor, spots, [len(acts[i]) for i in chunks], emits),
+            kinds,
             pos,
-            [turned, kept] + others,
+            [turned[h] for h in tables] + sum((acts[i] for i in chunks), []),
             [pltpu.VMEM((everyone, wide), BF16)],
-            flops=2 * everyone * part * wide,
-        )
-        arrived = []
-        for s in order:
+            flops=2 * everyone * len(targets) * mine * wide,
+        )
+        extra = list(terms[len(targets) :])
+        for i, emit in zip(chunks, emits):
+            if emit:
+                acts[i] = [extra.pop(0)]
+        (group,) = [g for g, members in enumerate(outputs) if chunks[0] in members]
+        begin = sum(groups[i][0] for i in outputs[group] if i < chunks[0])
+        for s, term in zip(targets, terms):
+            if s == 0:
+                owns[group] = term
+                continue
             links = [(a, mate(a, s, nodes)) for a in range(nodes)]
-            arrived.append(lax.ppermute(terms[s], "node", links))
-        (summed,) = call(sum_body, [shape(mine, wide, BF16)], pos, [terms[0]] + arrived)
+            moved = lax.ppermute(term, "node", links)
+            arrived.setdefault(group, []).append((begin, moved))
+    finished = []
+    for i in range(len(outputs)):
+        wide = owns[i].shape[1]
+        begins = [begin for begin, _ in arrived[i]]
+        (summed,) = call(
+            functools.partial(sum_body, begins),
+            [shape(mine, wide, BF16)],
+            pos,
+            [owns[i]] + [moved for _, moved in arrived[i]],
+            [pltpu.VMEM((mine, wide), F32)],
+        )
         finished.append(summed)
         for j in range(1, copies):
             links = [(a, mate(a, j, copies)) for a in range(copies)]
             finished.append(lax.ppermute(summed, "dp", links))
     spots = []
     begin = 0
-    for wide, _, _ in groups:
+    for i in range(len(outputs)):
         spots += [(j, begin) for j in range(copies)]
-        begin += wide
+        begin += owns[i].shape[1]
     early = len(finished) - copies + 1
     last = copies - 1
     (result,) = call(

time: 87.7 us -> 92.2 us (1.051)
  Pallas kernels: 17 us -> 19.5 us
  starting transfers between devices: 44.9 us -> 47.2 us
    ppermute x6 -> x9, waiting for transfers between devices: 0.02 us -> 7.43 us  [exchange(): moved[at] = lax.ppermute(pieces[at], ('dp', 'local'), links)]
    ppermute x6, waiting for transfers between devices: 17.6 us -> 11.2 us  [on_device(): lax.ppermute(chunk, 'node', [(a, mate(a, s, nodes)) for a in range(nodes)])]
    ppermute x12 -> x15, starting transfers between devices: 16.4 us -> 22.9 us  [the longest x11 18.8 us: on_device(): moved = lax.ppermute(term, 'node', links)]
    ppermute x3, starting transfers between devices: 4.4 us -> 1.66 us  [on_device(): finished.append(lax.ppermute(summed, 'dp', links))]
    ppermute x1, waiting for transfers between devices: 2.5 us -> 0.01 us  [on_device(): chosen_pair = lax.ppermute(chosen, 'local', swap)]
    pallas_call x16 -> x19, Pallas kernels: 17 us -> 19.5 us  [call(): pl.pallas_call(body, out_shape=outs, in_specs=[pl.BlockSpec(memory_space=...]
    ppermute x6, starting transfers between devices: 14 us -> 12.2 us  [on_device(): lax.ppermute(chunk, 'node', [(a, mate(a, s, nodes)) for a in range(nodes)])]
    ppermute x12 -> x15, waiting for transfers between devices: 2.41 us -> 3.71 us  [the longest x11 3.7 us: on_device(): moved = lax.ppermute(term, 'node', links)]
  transfers between devices with their start and end apart: 30 -> 36, of which waited for: 7 -> 10; matrix products, arithmetic and copies ran while one was open for 0% -> 0% of each run, Pallas kernels for 18% -> 20%
where the time goes in v5:
time: 92.2 us; the launch traced here: 91.9 us
  starting transfers between devices  47.2 us (51%)
  waiting for transfers between devices  24.9 us (27%)
  Pallas kernels  19.5 us (21%)
    pallas_call x19, Pallas kernels, call(): pl.pallas_call(body, out_shape=outs, in_specs=[pl.BlockSpec(memory_space=...  19.5 us
    ppermute x11, starting transfers between devices, on_device(): moved = lax.ppermute(term, 'node', links)  18.8 us
    ppermute x6, starting transfers between devices, on_device(): lax.ppermute(chunk, 'node', [(a, mate(a, s, nodes)) for a in range(nodes)])  12.2 us
    ppermute x6, waiting for transfers between devices, on_device(): lax.ppermute(chunk, 'node', [(a, mate(a, s, nodes)) for a in range(nodes)])  11.2 us
    ppermute x9, starting transfers between devices, exchange(): moved[at] = lax.ppermute(pieces[at], ('dp', 'local'), links)  9.92 us
    ppermute x9, waiting for transfers between devices, exchange(): moved[at] = lax.ppermute(pieces[at], ('dp', 'local'), links)  7.43 us
    ppermute x4, starting transfers between devices, on_device(): acts.append([kept, lax.ppermute(sent, 'dp', [(0, 1), (1, 0)])])  4.12 us
    ppermute x11, waiting for transfers between devices, on_device(): moved = lax.ppermute(term, 'node', links)  3.7 us
  transfers between devices with their start and end apart: 36, of which 10 were waited for; matrix products, arithmetic and copies ran while one was open for 0% of the time, Pallas kernels for 20%

profile of v5, /device:TPU:0, one launch (start us, length us, event | category | flops | bytes accessed | tf_op | source)
XLA Modules:
  0.0 91.9 jit_solution(8558023455073147481)
XLA Ops:
  0.6 1.6 %shard_map.61 = (bf16[256,256]{1,0:T(8,128)(2,1)S(1)}, bf16[256,256]{1,0:T(8,128)(2,1)S(1)}) custom-call(s32[3]{0:T(128)S(1)} %pad_add_fusion.pos, bf16[512,512]{1,0:T(8,128)(2,1)} %bitcast.9, bf16[16,512]{1,0:T(8,128)(2,1)} %bitcast.10), custom_call_target="tpu_custom_call" | custom-call | bytes 802816 | tf_op jit(solution)/shard_map/pallas_call | solution.py:34
  2.2 3.1 %collective-permute-start.12 = (bf16[256,256]{1,0:T(8,128)(2,1)S(1)}, bf16[256,256]{1,0:T(8,128)(2,1)S(1)}, u32[]{:S(2)}, u32[]{:S(2)}) collective-permute-start(bf16[256,256]{1,0:T(8,128)(2,1)S(1)} %get-tuple-element.61.refs_0_), channel_id=1, source_target_pairs={{0,4},{4,0},{8,12},{12,8},{1,5},{5,1},{9,13},{13,9},{2,6},{6,2},{1... | collective-permute-start | bytes 393224 | tf_op jit(solution)/shard_map/ppermute | solution.py:301
  5.3 2.6 %collective-permute-start.13 = (bf16[256,256]{1,0:T(8,128)(2,1)S(1)}, bf16[256,256]{1,0:T(8,128)(2,1)S(1)}, u32[]{:S(2)}, u32[]{:S(2)}) collective-permute-start(bf16[256,256]{1,0:T(8,128)(2,1)S(1)} %get-tuple-element.61.refs_0_), channel_id=1, source_target_pairs={{0,8},{4,12},{8,0},{12,4},{1,9},{5,13},{9,1},{13,5},{2,10},{6,14},... | collective-permute-start | bytes 393224 | tf_op jit(solution)/shard_map/ppermute | solution.py:301
  7.9 1.2 %collective-permute-start.14 = (bf16[256,256]{1,0:T(8,128)(2,1)S(1)}, bf16[256,256]{1,0:T(8,128)(2,1)S(1)}, u32[]{:S(2)}, u32[]{:S(2)}) collective-permute-start(bf16[256,256]{1,0:T(8,128)(2,1)S(1)} %get-tuple-element.61.refs_0_), channel_id=1, source_target_pairs={{0,12},{4,8},{8,4},{12,0},{1,13},{5,9},{9,5},{13,1},{2,14},{6,10},... | collective-permute-start | bytes 393224 | tf_op jit(solution)/shard_map/ppermute | solution.py:301
  9.1 1.7 %shard_map.55 = (bf16[256,192]{1,0:T(8,128)(2,1)S(1)}, bf16[256,192]{1,0:T(8,128)(2,1)S(1)}, bf16[192,2048]{1,0:T(8,128)(2,1)S(1)}) custom-call(s32[3]{0:T(128)S(1)} %pad_add_fusion.pos, s32[1,192]{1,0:T(1,128)S(1)} %bitcast.8, s32[1,192]{1,0:T(1,128)S(1)} %collective-permute-done.ids_pair, bf16[192,2048]{1,0:T(8,128)(2,1)} %rows.2), custom_call_target="tpu_custom_call" | custom-call | bytes 1771008 | tf_op jit(solution)/shard_map/pallas_call | solution.py:34
  11.4 1.3 %shard_map.59 = (bf16[120,1024]{1,0:T(8,128)(2,1)S(1)}, bf16[120,1024]{1,0:T(8,128)(2,1)S(1)}, bf16[120,1024]{1,0:T(8,128)(2,1)S(1)}, bf16[120,1024]{1,0:T(8,128)(2,1)S(1)}) custom-call(s32[3]{0:T(128)S(1)} %pad_add_fusion.pos, bf16[256,192]{1,0:T(8,128)(2,1)S(1)} %get-tuple-element.46.pick, bf16[256,192]{1,0:T(8,128)(2,1)S(1)} %get-tuple-element.47.pick_pair, ...), custom_call_target="tpu_custom_call" | custom-call | flops 402653184 | bytes 2752512 | tf_op jit(solution)/shard_map/pallas_call | solution.py:34
  12.7 1.6 %collective-permute-start.9 = (bf16[120,1024]{1,0:T(8,128)(2,1)S(1)}, bf16[120,1024]{1,0:T(8,128)(2,1)S(1)}, u32[]{:S(2)}, u32[]{:S(2)}) collective-permute-start(bf16[120,1024]{1,0:T(8,128)(2,1)S(1)} %get-tuple-element.58), channel_id=1, source_target_pairs={{0,2},{1,3},{2,0},{3,1},{16,18},{17,19},{18,16},{19,17},{4,6},{5,7... | collective-permute-start | bytes 737288 | tf_op jit(solution)/shard_map/ppermute | solution.py:336
  14.2 4.0 %collective-permute-done.13.refs_2_ = bf16[256,256]{1,0:T(8,128)(2,1)S(1)} collective-permute-done((bf16[256,256]{1,0:T(8,128)(2,1)S(1)}, bf16[256,256]{1,0:T(8,128)(2,1)S(1)}, u32[]{:S(2)}, u32[]{:S(2)}) %collective-permute-start.13) | collective-permute-done | bytes 131104 | tf_op jit(solution)/shard_map/ppermute | solution.py:301
  18.2 1.5 %collective-permute-start.10 = (bf16[120,1024]{1,0:T(8,128)(2,1)S(1)}, bf16[120,1024]{1,0:T(8,128)(2,1)S(1)}, u32[]{:S(2)}, u32[]{:S(2)}) collective-permute-start(bf16[120,1024]{1,0:T(8,128)(2,1)S(1)} %get-tuple-element.59), channel_id=1, source_target_pairs={{0,16},{1,17},{2,18},{3,19},{16,0},{17,1},{18,2},{19,3},{4,20},{5,... | collective-permute-start | bytes 737288 | tf_op jit(solution)/shard_map/ppermute | solution.py:336
  19.7 1.5 %collective-permute-start.11 = (bf16[120,1024]{1,0:T(8,128)(2,1)S(1)}, bf16[120,1024]{1,0:T(8,128)(2,1)S(1)}, u32[]{:S(2)}, u32[]{:S(2)}) collective-permute-start(bf16[120,1024]{1,0:T(8,128)(2,1)S(1)} %get-tuple-element.60), channel_id=1, source_target_pairs={{0,18},{1,19},{2,16},{3,17},{16,2},{17,3},{18,0},{19,1},{4,22},{5,... | collective-permute-start | bytes 737288 | tf_op jit(solution)/shard_map/ppermute | solution.py:336
  21.2 3.5 %collective-permute-start.21 = (bf16[256,256]{1,0:T(8,128)(2,1)S(1)}, bf16[256,256]{1,0:T(8,128)(2,1)S(1)}, u32[]{:S(2)}, u32[]{:S(2)}) collective-permute-start(bf16[256,256]{1,0:T(8,128)(2,1)S(1)} %get-tuple-element.68.refs_0_), channel_id=1, source_target_pairs={{0,8},{4,12},{8,0},{12,4},{1,9},{5,13},{9,1},{13,5},{2,10},{6,14},... | collective-permute-start | bytes 393224 | tf_op jit(solution)/shard_map/ppermute | solution.py:301
  24.8 1.2 %collective-permute-start.22 = (bf16[256,256]{1,0:T(8,128)(2,1)S(1)}, bf16[256,256]{1,0:T(8,128)(2,1)S(1)}, u32[]{:S(2)}, u32[]{:S(2)}) collective-permute-start(bf16[256,256]{1,0:T(8,128)(2,1)S(1)} %get-tuple-element.68.refs_0_), channel_id=1, source_target_pairs={{0,12},{4,8},{8,4},{12,0},{1,13},{5,9},{9,5},{13,1},{2,14},{6,10},... | collective-permute-start | bytes 393224 | tf_op jit(solution)/shard_map/ppermute | solution.py:301
  26.0 1.3 %shard_map.56 = (bf16[120,512]{1,0:T(8,128)(2,1)S(1)}, bf16[120,512]{1,0:T(8,128)(2,1)S(1)}, bf16[120,512]{1,0:T(8,128)(2,1)S(1)}, bf16[120,512]{1,0:T(8,128)(2,...) custom-call(s32[3]{0:T(128)S(1)} %pad_add_fusion.pos, ...), custom_call_target="tpu_custom_call" | custom-call | flops 402653184 | bytes 2752512 | tf_op jit(solution)/shard_map/pallas_call | solution.py:34
  27.2 7.2 %collective-permute-done.21.refs_2_ = bf16[256,256]{1,0:T(8,128)(2,1)S(1)} collective-permute-done((bf16[256,256]{1,0:T(8,128)(2,1)S(1)}, bf16[256,256]{1,0:T(8,128)(2,1)S(1)}, u32[]{:S(2)}, u32[]{:S(2)}) %collective-permute-start.21) | collective-permute-done | bytes 131104 | tf_op jit(solution)/shard_map/ppermute | solution.py:301
  35.5 2.4 %collective-permute-start.4 = (bf16[120,512]{1,0:T(8,128)(2,1)S(1)}, bf16[120,512]{1,0:T(8,128)(2,1)S(1)}, u32[]{:S(2)}, u32[]{:S(2)}) collective-permute-start(bf16[120,512]{1,0:T(8,128)(2,1)S(1)} %get-tuple-element.51), channel_id=1, source_target_pairs={{0,18},{1,19},{2,16},{3,17},{16,2},{17,3},{18,0},{19,1},{4,22},{5,... | collective-permute-start | bytes 368648 | tf_op jit(solution)/shard_map/ppermute | solution.py:336
  39.6 1.3 %shard_map.65 = (f32[512,128]{1,0:T(8,128)S(1)}, bf16[512,128]{1,0:T(8,128)(2,1)S(1)}, f32[512,128]{1,0:T(8,128)S(1)}, bf16[512,128]{1,0:T(8,128)(2,1)S(1)}) custom-call(s32[3]{0:T(128)S(1)} %pad_add_fusion.pos, bf16[512,1024]{1,0:T(8,128)(2,1)S(1)} %shard_map.60.rows, bf16[256,256]{1,0:T(8,128)(2,1)S(1)} %get-tuple-element.68.refs_0_, ...), custom_call_target="tpu_custom_call" | custom-call | flops 268435456 | bytes 2359296 | tf_op jit(solution)/shard_map/pallas_call | solution.py:34
  40.9 0.7 collective-permute-done.2.refs_1_
  41.6 0.9 collective-permute-start.23
  42.4 1.2 %collective-permute-start.24 = (bf16[512,128]{1,0:T(8,128)(2,1)S(1)}, bf16[512,128]{1,0:T(8,128)(2,1)S(1)}, u32[]{:S(2)}, u32[]{:S(2)}) collective-permute-start(bf16[512,128]{1,0:T(8,128)(2,1)S(1)} %get-tuple-element.73), channel_id=1, source_target_pairs={{0,16},{16,0},{1,17},{17,1},{2,18},{18,2},{3,19},{19,3},{4,20},{20... | collective-permute-start | bytes 393224 | tf_op jit(solution)/shard_map/ppermute | solution.py:372
  43.6 1.0 %collective-permute-done.4.refs_3_ = bf16[120,512]{1,0:T(8,128)(2,1)S(1)} collective-permute-done((bf16[120,512]{1,0:T(8,128)(2,1)S(1)}, bf16[120,512]{1,0:T(8,128)(2,1)S(1)}, u32[]{:S(2)}, u32[]{:S(2)}) %collective-permute-start.4) | collective-permute-done | bytes 122912 | tf_op jit(solution)/shard_map/ppermute | solution.py:336
  44.6 0.8 collective-permute-start.7
  45.4 1.3 %shard_map.62 = (f32[512,128]{1,0:T(8,128)S(1)}, bf16[512,128]{1,0:T(8,128)(2,1)S(1)}, f32[512,128]{1,0:T(8,128)S(1)}, bf16[512,128]{1,0:T(8,128)(2,1)S(1)}) custom-call(s32[3]{0:T(128)S(1)} %pad_add_fusion.pos, bf16[512,1024]{1,0:T(8,128)(2,1)S(1)} %shard_map.60.rows, bf16[256,256]{1,0:T(8,128)(2,1)S(1)} %get-tuple-element.61.refs_0_, ...), custom_call_target="tpu_custom_call" | custom-call | flops 268435456 | bytes 2359296 | tf_op jit(solution)/shard_map/pallas_call | solution.py:34
  46.7 1.2 %collective-permute-start.15 = (bf16[512,128]{1,0:T(8,128)(2,1)S(1)}, bf16[512,128]{1,0:T(8,128)(2,1)S(1)}, u32[]{:S(2)}, u32[]{:S(2)}) collective-permute-start(bf16[512,128]{1,0:T(8,128)(2,1)S(1)} %get-tuple-element.63), channel_id=1, source_target_pairs={{0,16},{16,0},{1,17},{17,1},{2,18},{18,2},{3,19},{19,3},{4,20},{20... | collective-permute-start | bytes 393224 | tf_op jit(solution)/shard_map/ppermute | solution.py:372
  47.9 0.9 collective-permute-start.31
  48.8 0.8 shard_map.57.refs_0_
  49.6 5.7 %collective-permute-done.7.refs_3_ = bf16[120,512]{1,0:T(8,128)(2,1)S(1)} collective-permute-done((bf16[120,512]{1,0:T(8,128)(2,1)S(1)}, bf16[120,512]{1,0:T(8,128)(2,1)S(1)}, u32[]{:S(2)}, u32[]{:S(2)}) %collective-permute-start.7) | collective-permute-done | bytes 122912 | tf_op jit(solution)/shard_map/ppermute | solution.py:336
  55.3 0.8 shard_map.58.refs_1_.refs_0_
  56.1 0.9 shard_map.66
  57.0 0.9 shard_map.67
  57.9 0.9 shard_map.68
  58.7 2.3 %collective-permute-start.29 = (bf16[256,256]{1,0:T(8,128)(2,1)S(1)}, bf16[256,256]{1,0:T(8,128)(2,1)S(1)}, u32[]{:S(2)}, u32[]{:S(2)}) collective-permute-start(bf16[256,256]{1,0:T(8,128)(2,1)S(1)} %get-tuple-element.80), channel_id=1, source_target_pairs={{0,8},{4,12},{8,0},{12,4},{1,9},{5,13},{9,1},{13,5},{2,10},{6,14},... | collective-permute-start | bytes 393224 | tf_op jit(solution)/shard_map/ppermute | solution.py:406
  61.1 1.3 %collective-permute-start.25 = (bf16[256,128]{1,0:T(8,128)(2,1)S(1)}, bf16[256,128]{1,0:T(8,128)(2,1)S(1)}, u32[]{:S(2)}, u32[]{:S(2)}) collective-permute-start(bf16[256,128]{1,0:T(8,128)(2,1)S(1)} %get-tuple-element.76), channel_id=1, source_target_pairs={{0,12},{4,8},{8,4},{12,0},{1,13},{5,9},{9,5},{13,1},{2,14},{6,10},... | collective-permute-start | bytes 196616 | tf_op jit(solution)/shard_map/ppermute | solution.py:406
  62.3 2.6 %collective-permute-start.27 = (bf16[256,128]{1,0:T(8,128)(2,1)S(1)}, bf16[256,128]{1,0:T(8,128)(2,1)S(1)}, u32[]{:S(2)}, u32[]{:S(2)}) collective-permute-start(bf16[256,128]{1,0:T(8,128)(2,1)S(1)} %get-tuple-element.78), channel_id=1, source_target_pairs={{0,12},{4,8},{8,4},{12,0},{1,13},{5,9},{9,5},{13,1},{2,14},{6,10},... | collective-permute-start | bytes 196616 | tf_op jit(solution)/shard_map/ppermute | solution.py:406
  64.9 1.1 %collective-permute-start.28 = (bf16[256,128]{1,0:T(8,128)(2,1)S(1)}, bf16[256,128]{1,0:T(8,128)(2,1)S(1)}, u32[]{:S(2)}, u32[]{:S(2)}) collective-permute-start(bf16[256,128]{1,0:T(8,128)(2,1)S(1)} %get-tuple-element.79), channel_id=1, source_target_pairs={{0,4},{4,0},{8,12},{12,8},{1,5},{5,1},{9,13},{13,9},{2,6},{6,2},{1... | collective-permute-start | bytes 196616 | tf_op jit(solution)/shard_map/ppermute | solution.py:406
  66.0 1.0 %shard_map.70 = (bf16[256,128]{1,0:T(8,128)(2,1)S(1)}, bf16[256,128]{1,0:T(8,128)(2,1)S(1)}, bf16[256,128]{1,0:T(8,128)(2,1)S(1)}, f32[256,128]{1,0:T(8,128)S(1)}) custom-call(s32[3]{0:T(128)S(1)} %pad_add_fusion.pos, bf16[512,512]{1,0:T(8,128)(2,1)S(1)} %shard_map.57.refs_0_, bf16[512,512]{1,0:T(8,128)(2,1)S(1)} %shard_map.58.refs_1_.refs_0_, ...), custom_call_target="tpu_custom_call" | custom-call | flops 134217728 | bytes 1769472 | tf_op jit(solution)/shard_map/pallas_call | solution.py:34
  67.1 0.7 collective-permute-done.25.refs_0_
  67.7 2.6 %collective-permute-start.32 = (bf16[256,128]{1,0:T(8,128)(2,1)S(1)}, bf16[256,128]{1,0:T(8,128)(2,1)S(1)}, u32[]{:S(2)}, u32[]{:S(2)}) collective-permute-start(bf16[256,128]{1,0:T(8,128)(2,1)S(1)} %get-tuple-element.84), channel_id=1, source_target_pairs={{0,12},{4,8},{8,4},{12,0},{1,13},{5,9},{9,5},{13,1},{2,14},{6,10},... | collective-permute-start | bytes 196616 | tf_op jit(solution)/shard_map/ppermute | solution.py:406
  70.4 3.6 %collective-permute-start.33 = (bf16[256,128]{1,0:T(8,128)(2,1)S(1)}, bf16[256,128]{1,0:T(8,128)(2,1)S(1)}, u32[]{:S(2)}, u32[]{:S(2)}) collective-permute-start(bf16[256,128]{1,0:T(8,128)(2,1)S(1)} %get-tuple-element.85), channel_id=1, source_target_pairs={{0,4},{4,0},{8,12},{12,8},{1,5},{5,1},{9,13},{13,9},{2,6},{6,2},{1... | collective-permute-start | bytes 196616 | tf_op jit(solution)/shard_map/ppermute | solution.py:406
  74.0 1.0 %shard_map.63 = (bf16[256,128]{1,0:T(8,128)(2,1)S(1)}, bf16[256,128]{1,0:T(8,128)(2,1)S(1)}, bf16[256,128]{1,0:T(8,128)(2,1)S(1)}, f32[256,128]{1,0:T(8,128)S(1)}) custom-call(s32[3]{0:T(128)S(1)} %pad_add_fusion.pos, bf16[512,512]{1,0:T(8,128)(2,1)S(1)} %shard_map.57.refs_0_, bf16[512,512]{1,0:T(8,128)(2,1)S(1)} %shard_map.58.refs_1_.refs_0_, ...), custom_call_target="tpu_custom_call" | custom-call | flops 134217728 | bytes 1769472 | tf_op jit(solution)/shard_map/pallas_call | solution.py:34
  75.1 2.2 %collective-permute-start.16 = (bf16[256,128]{1,0:T(8,128)(2,1)S(1)}, bf16[256,128]{1,0:T(8,128)(2,1)S(1)}, u32[]{:S(2)}, u32[]{:S(2)}) collective-permute-start(bf16[256,128]{1,0:T(8,128)(2,1)S(1)} %get-tuple-element.65), channel_id=1, source_target_pairs={{0,12},{4,8},{8,4},{12,0},{1,13},{5,9},{9,5},{13,1},{2,14},{6,10},... | collective-permute-start | bytes 196616 | tf_op jit(solution)/shard_map/ppermute | solution.py:406
  77.3 2.3 %collective-permute-start.34 = (bf16[256,128]{1,0:T(8,128)(2,1)S(1)}, bf16[256,128]{1,0:T(8,128)(2,1)S(1)}, u32[]{:S(2)}, u32[]{:S(2)}) collective-permute-start(bf16[256,128]{1,0:T(8,128)(2,1)S(1)} %get-tuple-element.86), channel_id=1, source_target_pairs={{0,8},{4,12},{8,0},{12,4},{1,9},{5,13},{9,1},{13,5},{2,10},{6,14},... | collective-permute-start | bytes 196616 | tf_op jit(solution)/shard_map/ppermute | solution.py:406
  80.1 0.8 collective-permute-start.18
  81.6 1.0 %collective-permute-done.34.refs_2_ = bf16[256,128]{1,0:T(8,128)(2,1)S(1)} collective-permute-done((bf16[256,128]{1,0:T(8,128)(2,1)S(1)}, bf16[256,128]{1,0:T(8,128)(2,1)S(1)}, u32[]{:S(2)}, u32[]{:S(2)}) %collective-permute-start.34) | collective-permute-done | bytes 65568 | tf_op jit(solution)/shard_map/ppermute | solution.py:406
  83.9 2.0 %collective-permute-done.18.refs_2_ = bf16[256,128]{1,0:T(8,128)(2,1)S(1)} collective-permute-done((bf16[256,128]{1,0:T(8,128)(2,1)S(1)}, bf16[256,128]{1,0:T(8,128)(2,1)S(1)}, u32[]{:S(2)}, u32[]{:S(2)}) %collective-permute-start.18) | collective-permute-done | bytes 65568 | tf_op jit(solution)/shard_map/ppermute | solution.py:406
  86.8 0.7 collective-permute-done.35.refs_3_
  87.5 1.3 %shard_map.72.refs_1_ = bf16[512,512]{1,0:T(8,128)(2,1)} custom-call(s32[3]{0:T(128)S(1)} %pad_add_fusion.pos, bf16[256,256]{1,0:T(8,128)(2,1)S(1)} %shard_map.69.refs_0_, bf16[256,256]{1,0:T(8,128)(2,1)S(1)} %collective-permute-done.30.refs_1_, bf16[256,128]{1,0:T(8,128)(2,1)S(1)} %shard_map.71.refs_2_, ...), custom_call_target="tpu_custom_call" | custom-call | bytes 983040 | tf_op jit(solution)/shard_map/pallas_call | solution.py:34
  88.9 1.9 %collective-permute-done.19.refs_0_ = bf16[256,128]{1,0:T(8,128)(2,1)S(1)} collective-permute-done((bf16[256,128]{1,0:T(8,128)(2,1)S(1)}, bf16[256,128]{1,0:T(8,128)(2,1)S(1)}, u32[]{:S(2)}, u32[]{:S(2)}) %collective-permute-start.19) | collective-permute-done | bytes 65568 | tf_op jit(solution)/shard_map/ppermute | solution.py:422
  90.7 1.2 %shard_map.73 = bf16[512,512]{1,0:T(8,128)(2,1)} custom-call(s32[3]{0:T(128)S(1)} %pad_add_fusion.pos, bf16[256,128]{1,0:T(8,128)(2,1)S(1)} %collective-permute-done.19.refs_0_, bf16[512,512]{1,0:T(8,128)(2,1)} %shard_map.72.refs_1_), custom_call_target="tpu_custom_call", output_to_operand_aliasing={{}: (2, {})} | custom-call | bytes 1114112 | tf_op jit(solution)/shard_map/pallas_call | solution.py:34
  (48 shorter events, 7.4 us)
Async XLA Ops:
  0.0 10.8 %collective-permute-start.8 = (bf16[192,2048]{1,0:T(8,128)(2,1)}, bf16[192,2048]{1,0:T(8,128)(2,1)S(1)}, u32[]{:S(2)}, u32[]{:S(2)}) collective-permute-start(bf16[192,2048]{1,0:T(8,128)(2,1)} %rows.2), channel_id=1, source_target_pairs={{0,1},{1,0},{2,3},{3,2},{4,5},{5,4},{6,7},{7,6},{8,9},{9,8},{10,11... | collective-permute-start | bytes 2359304 | tf_op jit(solution)/shard_map/ppermute | solution.py:279
  0.5 24.3 %collective-permute-start.1 = (bf16[192,2048]{1,0:T(8,128)(2,1)}, bf16[192,2048]{1,0:T(8,128)(2,1)S(1)}, u32[]{:S(2)}, u32[]{:S(2)}) collective-permute-start(bf16[192,2048]{1,0:T(8,128)(2,1)} %rows.3), channel_id=1, source_target_pairs={{0,1},{1,0},{2,3},{3,2},{4,5},{5,4},{6,7},{7,6},{8,9},{9,8},{10,11... | collective-permute-start | bytes 2359304 | tf_op jit(solution)/shard_map/ppermute | solution.py:281
  2.2 3.1 %copy-start.1 = (s32[192,1]{0,1:T(1,128)S(1)}, s32[192,1]{0,1:T(1,128)}, u32[]{:S(2)}) copy-start(s32[192,1]{0,1:T(1,128)} %param.7) | copy-start | bytes 2308
  2.2 10.5 %collective-permute-start.12 = (bf16[256,256]{1,0:T(8,128)(2,1)S(1)}, bf16[256,256]{1,0:T(8,128)(2,1)S(1)}, u32[]{:S(2)}, u32[]{:S(2)}) collective-permute-start(bf16[256,256]{1,0:T(8,128)(2,1)S(1)} %get-tuple-element.61.refs_0_), channel_id=1, source_target_pairs={{0,4},{4,0},{8,12},{12,8},{1,5},{5,1},{9,13},{13,9},{2,6},{6,2},{1... | collective-permute-start | bytes 393224 | tf_op jit(solution)/shard_map/ppermute | solution.py:301
  5.3 2.6 %collective-permute-start = (s32[1,192]{1,0:T(1,128)S(1)}, s32[1,192]{1,0:T(1,128)S(1)}, u32[]{:S(2)}, u32[]{:S(2)}) collective-permute-start(s32[1,192]{1,0:T(1,128)S(1)} %bitcast.7), channel_id=1, source_target_pairs={{0,1},{1,0},{2,3},{3,2},{4,5},{5,4},{6,7},{7,6},{8,9},{9,8},{10,11... | collective-permute-start | bytes 2312 | tf_op jit(solution)/shard_map/ppermute | solution.py:280
  5.3 12.9 %collective-permute-start.13 = (bf16[256,256]{1,0:T(8,128)(2,1)S(1)}, bf16[256,256]{1,0:T(8,128)(2,1)S(1)}, u32[]{:S(2)}, u32[]{:S(2)}) collective-permute-start(bf16[256,256]{1,0:T(8,128)(2,1)S(1)} %get-tuple-element.61.refs_0_), channel_id=1, source_target_pairs={{0,8},{4,12},{8,0},{12,4},{1,9},{5,13},{9,1},{13,5},{2,10},{6,14},... | collective-permute-start | bytes 393224 | tf_op jit(solution)/shard_map/ppermute | solution.py:301
  7.9 11.8 %collective-permute-start.14 = (bf16[256,256]{1,0:T(8,128)(2,1)S(1)}, bf16[256,256]{1,0:T(8,128)(2,1)S(1)}, u32[]{:S(2)}, u32[]{:S(2)}) collective-permute-start(bf16[256,256]{1,0:T(8,128)(2,1)S(1)} %get-tuple-element.61.refs_0_), channel_id=1, source_target_pairs={{0,12},{4,8},{8,4},{12,0},{1,13},{5,9},{9,5},{13,1},{2,14},{6,10},... | collective-permute-start | bytes 393224 | tf_op jit(solution)/shard_map/ppermute | solution.py:301
  10.8 10.4 %collective-permute-start.20 = (bf16[256,256]{1,0:T(8,128)(2,1)S(1)}, bf16[256,256]{1,0:T(8,128)(2,1)S(1)}, u32[]{:S(2)}, u32[]{:S(2)}) collective-permute-start(bf16[256,256]{1,0:T(8,128)(2,1)S(1)} %get-tuple-element.68.refs_0_), channel_id=1, source_target_pairs={{0,4},{4,0},{8,12},{12,8},{1,5},{5,1},{9,13},{13,9},{2,6},{6,2},{1... | collective-permute-start | bytes 393224 | tf_op jit(solution)/shard_map/ppermute | solution.py:301
  11.4 14.6 %copy-start = (bf16[192,2048]{1,0:T(8,128)(2,1)S(1)}, bf16[192,2048]{1,0:T(8,128)(2,1)}, u32[]{:S(2)}) copy-start(bf16[192,2048]{1,0:T(8,128)(2,1)} %rows.3) | copy-start | bytes 2359300
  12.7 22.8 %collective-permute-start.9 = (bf16[120,1024]{1,0:T(8,128)(2,1)S(1)}, bf16[120,1024]{1,0:T(8,128)(2,1)S(1)}, u32[]{:S(2)}, u32[]{:S(2)}) collective-permute-start(bf16[120,1024]{1,0:T(8,128)(2,1)S(1)} %get-tuple-element.58), channel_id=1, source_target_pairs={{0,2},{1,3},{2,0},{3,1},{16,18},{17,19},{18,16},{19,17},{4,6},{5,7... | collective-permute-start | bytes 737288 | tf_op jit(solution)/shard_map/ppermute | solution.py:336
  18.2 19.7 %collective-permute-start.10 = (bf16[120,1024]{1,0:T(8,128)(2,1)S(1)}, bf16[120,1024]{1,0:T(8,128)(2,1)S(1)}, u32[]{:S(2)}, u32[]{:S(2)}) collective-permute-start(bf16[120,1024]{1,0:T(8,128)(2,1)S(1)} %get-tuple-element.59), channel_id=1, source_target_pairs={{0,16},{1,17},{2,18},{3,19},{16,0},{17,1},{18,2},{19,3},{4,20},{5,... | collective-permute-start | bytes 737288 | tf_op jit(solution)/shard_map/ppermute | solution.py:336
  19.7 18.7 %collective-permute-start.11 = (bf16[120,1024]{1,0:T(8,128)(2,1)S(1)}, bf16[120,1024]{1,0:T(8,128)(2,1)S(1)}, u32[]{:S(2)}, u32[]{:S(2)}) collective-permute-start(bf16[120,1024]{1,0:T(8,128)(2,1)S(1)} %get-tuple-element.60), channel_id=1, source_target_pairs={{0,18},{1,19},{2,16},{3,17},{16,2},{17,3},{18,0},{19,1},{4,22},{5,... | collective-permute-start | bytes 737288 | tf_op jit(solution)/shard_map/ppermute | solution.py:336
  21.2 13.2 %collective-permute-start.21 = (bf16[256,256]{1,0:T(8,128)(2,1)S(1)}, bf16[256,256]{1,0:T(8,128)(2,1)S(1)}, u32[]{:S(2)}, u32[]{:S(2)}) collective-permute-start(bf16[256,256]{1,0:T(8,128)(2,1)S(1)} %get-tuple-element.68.refs_0_), channel_id=1, source_target_pairs={{0,8},{4,12},{8,0},{12,4},{1,9},{5,13},{9,1},{13,5},{2,10},{6,14},... | collective-permute-start | bytes 393224 | tf_op jit(solution)/shard_map/ppermute | solution.py:301
  24.8 10.2 %collective-permute-start.22 = (bf16[256,256]{1,0:T(8,128)(2,1)S(1)}, bf16[256,256]{1,0:T(8,128)(2,1)S(1)}, u32[]{:S(2)}, u32[]{:S(2)}) collective-permute-start(bf16[256,256]{1,0:T(8,128)(2,1)S(1)} %get-tuple-element.68.refs_0_), channel_id=1, source_target_pairs={{0,12},{4,8},{8,4},{12,0},{1,13},{5,9},{9,5},{13,1},{2,14},{6,10},... | collective-permute-start | bytes 393224 | tf_op jit(solution)/shard_map/ppermute | solution.py:301
  34.4 7.1 %collective-permute-start.2 = (bf16[120,512]{1,0:T(8,128)(2,1)S(1)}, bf16[120,512]{1,0:T(8,128)(2,1)S(1)}, u32[]{:S(2)}, u32[]{:S(2)}) collective-permute-start(bf16[120,512]{1,0:T(8,128)(2,1)S(1)} %get-tuple-element.49), channel_id=1, source_target_pairs={{0,2},{1,3},{2,0},{3,1},{16,18},{17,19},{18,16},{19,17},{4,6},{5,7... | collective-permute-start | bytes 368648 | tf_op jit(solution)/shard_map/ppermute | solution.py:336
  34.9 7.5 %collective-permute-start.3 = (bf16[120,512]{1,0:T(8,128)(2,1)S(1)}, bf16[120,512]{1,0:T(8,128)(2,1)S(1)}, u32[]{:S(2)}, u32[]{:S(2)}) collective-permute-start(bf16[120,512]{1,0:T(8,128)(2,1)S(1)} %get-tuple-element.50), channel_id=1, source_target_pairs={{0,16},{1,17},{2,18},{3,19},{16,0},{17,1},{18,2},{19,3},{4,20},{5,... | collective-permute-start | bytes 368648 | tf_op jit(solution)/shard_map/ppermute | solution.py:336
  35.5 9.1 %collective-permute-start.4 = (bf16[120,512]{1,0:T(8,128)(2,1)S(1)}, bf16[120,512]{1,0:T(8,128)(2,1)S(1)}, u32[]{:S(2)}, u32[]{:S(2)}) collective-permute-start(bf16[120,512]{1,0:T(8,128)(2,1)S(1)} %get-tuple-element.51), channel_id=1, source_target_pairs={{0,18},{1,19},{2,16},{3,17},{16,2},{17,3},{18,0},{19,1},{4,22},{5,... | collective-permute-start | bytes 368648 | tf_op jit(solution)/shard_map/ppermute | solution.py:336
  37.9 8.8 %collective-permute-start.5 = (bf16[120,512]{1,0:T(8,128)(2,1)S(1)}, bf16[120,512]{1,0:T(8,128)(2,1)S(1)}, u32[]{:S(2)}, u32[]{:S(2)}) collective-permute-start(bf16[120,512]{1,0:T(8,128)(2,1)S(1)} %get-tuple-element.53), channel_id=1, source_target_pairs={{0,2},{1,3},{2,0},{3,1},{16,18},{17,19},{18,16},{19,17},{4,6},{5,7... | collective-permute-start | bytes 368648 | tf_op jit(solution)/shard_map/ppermute | solution.py:336
  38.4 9.5 %collective-permute-start.6 = (bf16[120,512]{1,0:T(8,128)(2,1)S(1)}, bf16[120,512]{1,0:T(8,128)(2,1)S(1)}, u32[]{:S(2)}, u32[]{:S(2)}) collective-permute-start(bf16[120,512]{1,0:T(8,128)(2,1)S(1)} %get-tuple-element.54), channel_id=1, source_target_pairs={{0,16},{1,17},{2,18},{3,19},{16,0},{17,1},{18,2},{19,3},{4,20},{5,... | collective-permute-start | bytes 368648 | tf_op jit(solution)/shard_map/ppermute | solution.py:336
  41.6 14.5 %collective-permute-start.23 = (bf16[512,128]{1,0:T(8,128)(2,1)S(1)}, bf16[512,128]{1,0:T(8,128)(2,1)S(1)}, u32[]{:S(2)}, u32[]{:S(2)}) collective-permute-start(bf16[512,128]{1,0:T(8,128)(2,1)S(1)} %get-tuple-element.70), channel_id=1, source_target_pairs={{0,16},{16,0},{1,17},{17,1},{2,18},{18,2},{3,19},{19,3},{4,20},{20... | collective-permute-start | bytes 393224 | tf_op jit(solution)/shard_map/ppermute | solution.py:372
  42.4 14.5 %collective-permute-start.24 = (bf16[512,128]{1,0:T(8,128)(2,1)S(1)}, bf16[512,128]{1,0:T(8,128)(2,1)S(1)}, u32[]{:S(2)}, u32[]{:S(2)}) collective-permute-start(bf16[512,128]{1,0:T(8,128)(2,1)S(1)} %get-tuple-element.73), channel_id=1, source_target_pairs={{0,16},{16,0},{1,17},{17,1},{2,18},{18,2},{3,19},{19,3},{4,20},{20... | collective-permute-start | bytes 393224 | tf_op jit(solution)/shard_map/ppermute | solution.py:372
  44.6 10.7 %collective-permute-start.7 = (bf16[120,512]{1,0:T(8,128)(2,1)S(1)}, bf16[120,512]{1,0:T(8,128)(2,1)S(1)}, u32[]{:S(2)}, u32[]{:S(2)}) collective-permute-start(bf16[120,512]{1,0:T(8,128)(2,1)S(1)} %get-tuple-element.55), channel_id=1, source_target_pairs={{0,18},{1,19},{2,16},{3,17},{16,2},{17,3},{18,0},{19,1},{4,22},{5,... | collective-permute-start | bytes 368648 | tf_op jit(solution)/shard_map/ppermute | solution.py:336
  46.7 15.6 %collective-permute-start.15 = (bf16[512,128]{1,0:T(8,128)(2,1)S(1)}, bf16[512,128]{1,0:T(8,128)(2,1)S(1)}, u32[]{:S(2)}, u32[]{:S(2)}) collective-permute-start(bf16[512,128]{1,0:T(8,128)(2,1)S(1)} %get-tuple-element.63), channel_id=1, source_target_pairs={{0,16},{16,0},{1,17},{17,1},{2,18},{18,2},{3,19},{19,3},{4,20},{20... | collective-permute-start | bytes 393224 | tf_op jit(solution)/shard_map/ppermute | solution.py:372
  47.9 17.0 %collective-permute-start.31 = (bf16[512,128]{1,0:T(8,128)(2,1)S(1)}, bf16[512,128]{1,0:T(8,128)(2,1)S(1)}, u32[]{:S(2)}, u32[]{:S(2)}) collective-permute-start(bf16[512,128]{1,0:T(8,128)(2,1)S(1)} %get-tuple-element.82), channel_id=1, source_target_pairs={{0,16},{16,0},{1,17},{17,1},{2,18},{18,2},{3,19},{19,3},{4,20},{20... | collective-permute-start | bytes 393224 | tf_op jit(solution)/shard_map/ppermute | solution.py:372
  58.7 18.5 %collective-permute-start.29 = (bf16[256,256]{1,0:T(8,128)(2,1)S(1)}, bf16[256,256]{1,0:T(8,128)(2,1)S(1)}, u32[]{:S(2)}, u32[]{:S(2)}) collective-permute-start(bf16[256,256]{1,0:T(8,128)(2,1)S(1)} %get-tuple-element.80), channel_id=1, source_target_pairs={{0,8},{4,12},{8,0},{12,4},{1,9},{5,13},{9,1},{13,5},{2,10},{6,14},... | collective-permute-start | bytes 393224 | tf_op jit(solution)/shard_map/ppermute | solution.py:406
  61.1 6.7 %collective-permute-start.25 = (bf16[256,128]{1,0:T(8,128)(2,1)S(1)}, bf16[256,128]{1,0:T(8,128)(2,1)S(1)}, u32[]{:S(2)}, u32[]{:S(2)}) collective-permute-start(bf16[256,128]{1,0:T(8,128)(2,1)S(1)} %get-tuple-element.76), channel_id=1, source_target_pairs={{0,12},{4,8},{8,4},{12,0},{1,13},{5,9},{9,5},{13,1},{2,14},{6,10},... | collective-permute-start | bytes 196616 | tf_op jit(solution)/shard_map/ppermute | solution.py:406
  62.3 8.1 %collective-permute-start.26 = (bf16[256,128]{1,0:T(8,128)(2,1)S(1)}, bf16[256,128]{1,0:T(8,128)(2,1)S(1)}, u32[]{:S(2)}, u32[]{:S(2)}) collective-permute-start(bf16[256,128]{1,0:T(8,128)(2,1)S(1)} %get-tuple-element.77), channel_id=1, source_target_pairs={{0,4},{4,0},{8,12},{12,8},{1,5},{5,1},{9,13},{13,9},{2,6},{6,2},{1... | collective-permute-start | bytes 196616 | tf_op jit(solution)/shard_map/ppermute | solution.py:406
  62.3 12.7 %collective-permute-start.27 = (bf16[256,128]{1,0:T(8,128)(2,1)S(1)}, bf16[256,128]{1,0:T(8,128)(2,1)S(1)}, u32[]{:S(2)}, u32[]{:S(2)}) collective-permute-start(bf16[256,128]{1,0:T(8,128)(2,1)S(1)} %get-tuple-element.78), channel_id=1, source_target_pairs={{0,12},{4,8},{8,4},{12,0},{1,13},{5,9},{9,5},{13,1},{2,14},{6,10},... | collective-permute-start | bytes 196616 | tf_op jit(solution)/shard_map/ppermute | solution.py:406
  64.9 12.4 %collective-permute-start.28 = (bf16[256,128]{1,0:T(8,128)(2,1)S(1)}, bf16[256,128]{1,0:T(8,128)(2,1)S(1)}, u32[]{:S(2)}, u32[]{:S(2)}) collective-permute-start(bf16[256,128]{1,0:T(8,128)(2,1)S(1)} %get-tuple-element.79), channel_id=1, source_target_pairs={{0,4},{4,0},{8,12},{12,8},{1,5},{5,1},{9,13},{13,9},{2,6},{6,2},{1... | collective-permute-start | bytes 196616 | tf_op jit(solution)/shard_map/ppermute | solution.py:406
  67.7 12.4 %collective-permute-start.32 = (bf16[256,128]{1,0:T(8,128)(2,1)S(1)}, bf16[256,128]{1,0:T(8,128)(2,1)S(1)}, u32[]{:S(2)}, u32[]{:S(2)}) collective-permute-start(bf16[256,128]{1,0:T(8,128)(2,1)S(1)} %get-tuple-element.84), channel_id=1, source_target_pairs={{0,12},{4,8},{8,4},{12,0},{1,13},{5,9},{9,5},{13,1},{2,14},{6,10},... | collective-permute-start | bytes 196616 | tf_op jit(solution)/shard_map/ppermute | solution.py:406
  70.4 10.6 %collective-permute-start.33 = (bf16[256,128]{1,0:T(8,128)(2,1)S(1)}, bf16[256,128]{1,0:T(8,128)(2,1)S(1)}, u32[]{:S(2)}, u32[]{:S(2)}) collective-permute-start(bf16[256,128]{1,0:T(8,128)(2,1)S(1)} %get-tuple-element.85), channel_id=1, source_target_pairs={{0,4},{4,0},{8,12},{12,8},{1,5},{5,1},{9,13},{13,9},{2,6},{6,2},{1... | collective-permute-start | bytes 196616 | tf_op jit(solution)/shard_map/ppermute | solution.py:406
  75.1 8.8 %collective-permute-start.16 = (bf16[256,128]{1,0:T(8,128)(2,1)S(1)}, bf16[256,128]{1,0:T(8,128)(2,1)S(1)}, u32[]{:S(2)}, u32[]{:S(2)}) collective-permute-start(bf16[256,128]{1,0:T(8,128)(2,1)S(1)} %get-tuple-element.65), channel_id=1, source_target_pairs={{0,12},{4,8},{8,4},{12,0},{1,13},{5,9},{9,5},{13,1},{2,14},{6,10},... | collective-permute-start | bytes 196616 | tf_op jit(solution)/shard_map/ppermute | solution.py:406
  77.3 6.6 %collective-permute-start.17 = (bf16[256,128]{1,0:T(8,128)(2,1)S(1)}, bf16[256,128]{1,0:T(8,128)(2,1)S(1)}, u32[]{:S(2)}, u32[]{:S(2)}) collective-permute-start(bf16[256,128]{1,0:T(8,128)(2,1)S(1)} %get-tuple-element.66), channel_id=1, source_target_pairs={{0,4},{4,0},{8,12},{12,8},{1,5},{5,1},{9,13},{13,9},{2,6},{6,2},{1... | collective-permute-start | bytes 196616 | tf_op jit(solution)/shard_map/ppermute | solution.py:406
  77.3 5.3 %collective-permute-start.34 = (bf16[256,128]{1,0:T(8,128)(2,1)S(1)}, bf16[256,128]{1,0:T(8,128)(2,1)S(1)}, u32[]{:S(2)}, u32[]{:S(2)}) collective-permute-start(bf16[256,128]{1,0:T(8,128)(2,1)S(1)} %get-tuple-element.86), channel_id=1, source_target_pairs={{0,8},{4,12},{8,0},{12,4},{1,9},{5,13},{9,1},{13,5},{2,10},{6,14},... | collective-permute-start | bytes 196616 | tf_op jit(solution)/shard_map/ppermute | solution.py:406
  80.1 5.7 %collective-permute-start.18 = (bf16[256,128]{1,0:T(8,128)(2,1)S(1)}, bf16[256,128]{1,0:T(8,128)(2,1)S(1)}, u32[]{:S(2)}, u32[]{:S(2)}) collective-permute-start(bf16[256,128]{1,0:T(8,128)(2,1)S(1)} %get-tuple-element.67), channel_id=1, source_target_pairs={{0,8},{4,12},{8,0},{12,4},{1,9},{5,13},{9,1},{13,5},{2,10},{6,14},... | collective-permute-start | bytes 196616 | tf_op jit(solution)/shard_map/ppermute | solution.py:406
  81.0 6.6 %collective-permute-start.30 = (bf16[256,256]{1,0:T(8,128)(2,1)S(1)}, bf16[256,256]{1,0:T(8,128)(2,1)S(1)}, u32[]{:S(2)}, u32[]{:S(2)}) collective-permute-start(bf16[256,256]{1,0:T(8,128)(2,1)S(1)} %shard_map.69.refs_0_), channel_id=1, source_target_pairs={{0,16},{16,0},{1,17},{17,1},{2,18},{18,2},{3,19},{19,3},{4,20},{20... | collective-permute-start | bytes 393224 | tf_op jit(solution)/shard_map/ppermute | solution.py:422
  83.2 4.3 %collective-permute-start.35 = (bf16[256,128]{1,0:T(8,128)(2,1)S(1)}, bf16[256,128]{1,0:T(8,128)(2,1)S(1)}, u32[]{:S(2)}, u32[]{:S(2)}) collective-permute-start(bf16[256,128]{1,0:T(8,128)(2,1)S(1)} %shard_map.71.refs_2_), channel_id=1, source_target_pairs={{0,16},{16,0},{1,17},{17,1},{2,18},{18,2},{3,19},{19,3},{4,20},{20... | collective-permute-start | bytes 196616 | tf_op jit(solution)/shard_map/ppermute | solution.py:422
  86.4 4.3 %collective-permute-start.19 = (bf16[256,128]{1,0:T(8,128)(2,1)S(1)}, bf16[256,128]{1,0:T(8,128)(2,1)S(1)}, u32[]{:S(2)}, u32[]{:S(2)}) collective-permute-start(bf16[256,128]{1,0:T(8,128)(2,1)S(1)} %shard_map.64.refs_4_), channel_id=1, source_target_pairs={{0,16},{16,0},{1,17},{17,1},{2,18},{18,2},{3,19},{19,3},{4,20},{20... | collective-permute-start | bytes 196616 | tf_op jit(solution)/shard_map/ppermute | solution.py:422

commit v6 on v5

--- a/solution.py
+++ b/solution.py
@@ -7,7 +7,7 @@
 from jax.sharding import PartitionSpec as P
 
 QB = 32
-SPLITS = ((1, 1), (1, 1))
+SPLITS = ((1, 2, 1),)
 F32 = jnp.float32
 BF16 = jnp.bfloat16
 
@@ -48,16 +48,10 @@
     return [s for s in (3, 1, 2) if s < nodes] + list(range(4, nodes))
 
 
-def plan_of(nodes, aligned):
-    order = node_order(nodes)
-    every = order + [0]
-    chunks = sum(len(split) for split in SPLITS)
-    if not aligned:
-        return [every], [([i], every) for i in range(chunks)], [[i] for i in range(chunks)]
-    early, late = order[: nodes // 2], order[nodes // 2 :] + [0]
-    jobs = [([0], early), ([1], early), ([0, 1], late)]
-    jobs += [([i], every) for i in range(2, chunks)]
-    return [early, late], jobs, [[0, 1]] + [[i] for i in range(2, chunks)]
+def plan_of(nodes):
+    every = node_order(nodes) + [0]
+    chunks = range(sum(len(split) for split in SPLITS))
+    return [every], [([i], every) for i in chunks], [[i] for i in chunks]
 
 
 def slots_of(copies, pairs):
@@ -264,7 +258,7 @@
     pos = jnp.stack([lax.axis_index(a) for a in ("dp", "node", "local")]).astype(jnp.int32)
 
     aligned = mine % 128 == 0
-    halves, jobs, outputs = plan_of(nodes, aligned)
+    halves, jobs, outputs = plan_of(nodes)
     if aligned:
         columns_x = [[(False, b) for b in range(nodes)]]
         columns_y = [[(True, s) for s in half] for half in halves]

time: 92.2 us -> 89.3 us (0.969)
  waiting for transfers between devices: 24.9 us -> 30 us
  starting transfers between devices: 47.2 us -> 42.5 us
  Pallas kernels: 19.5 us -> 16.3 us
    ppermute x9 -> x6, waiting for transfers between devices: 7.43 us -> 21.5 us  [exchange(): moved[at] = lax.ppermute(pieces[at], ('dp', 'local'), links)]
    ppermute x6 -> x3, starting transfers between devices: 12.2 us -> 4.23 us  [on_device(): lax.ppermute(chunk, 'node', [(a, mate(a, s, nodes)) for a in range(nodes)])]
    ppermute x6 -> x3, waiting for transfers between devices: 11.2 us -> 4.33 us  [on_device(): lax.ppermute(chunk, 'node', [(a, mate(a, s, nodes)) for a in range(nodes)])]
    ppermute x11 -> x9, waiting for transfers between devices: 3.7 us -> 0.13 us  [on_device(): moved = lax.ppermute(term, 'node', links)]
    pallas_call x19 -> x15, Pallas kernels: 19.5 us -> 16.3 us  [call(): pl.pallas_call(body, out_shape=outs, in_specs=[pl.BlockSpec(memory_space=...]
    ppermute x11 -> x9, starting transfers between devices: 18.8 us -> 21.4 us  [on_device(): moved = lax.ppermute(term, 'node', links)]
    ppermute x1, waiting for transfers between devices: 0.01 us -> 2.5 us  [on_device(): chosen_pair = lax.ppermute(chosen, 'local', swap)]
    ppermute x3, starting transfers between devices: 1.66 us -> 3.64 us  [on_device(): finished.append(lax.ppermute(summed, 'dp', links))]
  transfers between devices with their start and end apart: 36 -> 27, of which waited for: 10 -> 9; matrix products, arithmetic and copies ran while one was open for 0% -> 0% of each run, Pallas kernels for 20% -> 17%
where the time goes in v6:
time: 89.3 us; the launch traced here: 89.1 us
  starting transfers between devices  42.5 us (48%)
  waiting for transfers between devices  30 us (34%)
  Pallas kernels  16.3 us (18%)
    ppermute x6, waiting for transfers between devices, exchange(): moved[at] = lax.ppermute(pieces[at], ('dp', 'local'), links)  21.5 us
    ppermute x9, starting transfers between devices, on_device(): moved = lax.ppermute(term, 'node', links)  21.4 us
    pallas_call x15, Pallas kernels, call(): pl.pallas_call(body, out_shape=outs, in_specs=[pl.BlockSpec(memory_space=...  16.3 us
    ppermute x6, starting transfers between devices, exchange(): moved[at] = lax.ppermute(pieces[at], ('dp', 'local'), links)  8.53 us
    ppermute x3, waiting for transfers between devices, on_device(): lax.ppermute(chunk, 'node', [(a, mate(a, s, nodes)) for a in range(nodes)])  4.33 us
    ppermute x3, starting transfers between devices, on_device(): lax.ppermute(chunk, 'node', [(a, mate(a, s, nodes)) for a in range(nodes)])  4.23 us
    ppermute x3, starting transfers between devices, on_device(): finished.append(lax.ppermute(summed, 'dp', links))  3.64 us
    ppermute x3, starting transfers between devices, on_device(): acts.append([kept, lax.ppermute(sent, 'dp', [(0, 1), (1, 0)])])  3.59 us
  transfers between devices with their start and end apart: 27, of which 9 were waited for; matrix products, arithmetic and copies ran while one was open for 0% of the time, Pallas kernels for 17%

profile of v6, /device:TPU:0, one launch (start us, length us, event | category | flops | bytes accessed | tf_op | source)
XLA Modules:
  0.0 89.1 jit_solution(13247500986425841204)
XLA Ops:
  0.0 0.5 collective-permute-start.5
  0.7 0.5 collective-permute-start
  1.2 2.5 %collective-permute-done.ids_pair = s32[1,192]{1,0:T(1,128)S(1)} collective-permute-done((s32[1,192]{1,0:T(1,128)S(1)}, s32[1,192]{1,0:T(1,128)S(1)}, u32[]{:S(2)}, u32[]{:S(2)}) %collective-permute-start) | collective-permute-done | bytes 800 | tf_op jit(solution)/shard_map/ppermute | solution.py:274
  3.7 1.7 %shard_map.55 = (bf16[256,192]{1,0:T(8,128)(2,1)S(1)}, bf16[256,192]{1,0:T(8,128)(2,1)S(1)}, bf16[192,2048]{1,0:T(8,128)(2,1)S(1)}) custom-call(s32[3]{0:T(128)S(1)} %pad_add_fusion.pos, s32[1,192]{1,0:T(1,128)S(1)} %bitcast.8, s32[1,192]{1,0:T(1,128)S(1)} %collective-permute-done.ids_pair, bf16[192,2048]{1,0:T(8,128)(2,1)} %rows.2), custom_call_target="tpu_custom_call" | custom-call | bytes 1771008 | tf_op jit(solution)/shard_map/pallas_call | solution.py:34
  5.4 1.3 %shard_map.58 = (bf16[120,1024]{1,0:T(8,128)(2,1)S(1)}, bf16[120,1024]{1,0:T(8,128)(2,1)S(1)}, bf16[120,1024]{1,0:T(8,128)(2,1)S(1)}, bf16[120,1024]{1,0:T(8,128)(2,1)S(1)}) custom-call(s32[3]{0:T(128)S(1)} %pad_add_fusion.pos, bf16[256,192]{1,0:T(8,128)(2,1)S(1)} %get-tuple-element.34.pick, bf16[256,192]{1,0:T(8,128)(2,1)S(1)} %get-tuple-element.35.pick_pair, ...), custom_call_target="tpu_custom_call" | custom-call | flops 402653184 | bytes 2752512 | tf_op jit(solution)/shard_map/pallas_call | solution.py:34
  6.7 2.9 %collective-permute-start.6 = (bf16[120,1024]{1,0:T(8,128)(2,1)S(1)}, bf16[120,1024]{1,0:T(8,128)(2,1)S(1)}, u32[]{:S(2)}, u32[]{:S(2)}) collective-permute-start(bf16[120,1024]{1,0:T(8,128)(2,1)S(1)} %get-tuple-element.42), channel_id=1, source_target_pairs={{0,2},{1,3},{2,0},{3,1},{16,18},{17,19},{18,16},{19,17},{4,6},{5,7... | collective-permute-start | bytes 737288 | tf_op jit(solution)/shard_map/ppermute | solution.py:330
  9.7 1.6 %shard_map.60.refs_0_ = bf16[256,512]{1,0:T(8,128)(2,1)S(1)} custom-call(s32[3]{0:T(128)S(1)} %pad_add_fusion.pos, bf16[512,512]{1,0:T(8,128)(2,1)} %bitcast.9, bf16[16,512]{1,0:T(8,128)(2,1)} %bitcast.10), custom_call_target="tpu_custom_call" | custom-call | bytes 802816 | tf_op jit(solution)/shard_map/pallas_call | solution.py:34
  11.3 2.6 %collective-permute-start.10 = (bf16[256,512]{1,0:T(8,128)(2,1)S(1)}, bf16[256,512]{1,0:T(8,128)(2,1)S(1)}, u32[]{:S(2)}, u32[]{:S(2)}) collective-permute-start(bf16[256,512]{1,0:T(8,128)(2,1)S(1)} %shard_map.60.refs_0_), channel_id=1, source_target_pairs={{0,8},{4,12},{8,0},{12,4},{1,9},{5,13},{9,1},{13,5},{2,10},{6,14},... | collective-permute-start | bytes 786440 | tf_op jit(solution)/shard_map/ppermute | solution.py:295
  13.9 1.3 %collective-permute-start.11 = (bf16[256,512]{1,0:T(8,128)(2,1)S(1)}, bf16[256,512]{1,0:T(8,128)(2,1)S(1)}, u32[]{:S(2)}, u32[]{:S(2)}) collective-permute-start(bf16[256,512]{1,0:T(8,128)(2,1)S(1)} %shard_map.60.refs_0_), channel_id=1, source_target_pairs={{0,12},{4,8},{8,4},{12,0},{1,13},{5,9},{9,5},{13,1},{2,14},{6,10},... | collective-permute-start | bytes 786440 | tf_op jit(solution)/shard_map/ppermute | solution.py:295
  15.2 0.2 collective-permute-start.9
  15.5 1.5 %collective-permute-start.7 = (bf16[120,1024]{1,0:T(8,128)(2,1)S(1)}, bf16[120,1024]{1,0:T(8,128)(2,1)S(1)}, u32[]{:S(2)}, u32[]{:S(2)}) collective-permute-start(bf16[120,1024]{1,0:T(8,128)(2,1)S(1)} %get-tuple-element.43), channel_id=1, source_target_pairs={{0,16},{1,17},{2,18},{3,19},{16,0},{17,1},{18,2},{19,3},{4,20},{5,... | collective-permute-start | bytes 737288 | tf_op jit(solution)/shard_map/ppermute | solution.py:330
  17.0 1.6 %collective-permute-start.8 = (bf16[120,1024]{1,0:T(8,128)(2,1)S(1)}, bf16[120,1024]{1,0:T(8,128)(2,1)S(1)}, u32[]{:S(2)}, u32[]{:S(2)}) collective-permute-start(bf16[120,1024]{1,0:T(8,128)(2,1)S(1)} %get-tuple-element.44), channel_id=1, source_target_pairs={{0,18},{1,19},{2,16},{3,17},{16,2},{17,3},{18,0},{19,1},{4,22},{5,... | collective-permute-start | bytes 737288 | tf_op jit(solution)/shard_map/ppermute | solution.py:330
  18.6 1.3 %shard_map.56 = (bf16[120,1024]{1,0:T(8,128)(2,1)S(1)}, bf16[120,1024]{1,0:T(8,128)(2,1)S(1)}, bf16[120,1024]{1,0:T(8,128)(2,1)S(1)}, bf16[120,1024]{1,0:T(8,128)(2,1)S(1)}) custom-call(s32[3]{0:T(128)S(1)} %pad_add_fusion.pos, bf16[256,192]{1,0:T(8,128)(2,1)S(1)} %get-tuple-element.34.pick, bf16[256,192]{1,0:T(8,128)(2,1)S(1)} %get-tuple-element.35.pick_pair, ...), custom_call_target="tpu_custom_call" | custom-call | flops 402653184 | bytes 2752512 | tf_op jit(solution)/shard_map/pallas_call | solution.py:34
  19.9 4.4 %collective-permute-done.7.refs_2_ = bf16[120,1024]{1,0:T(8,128)(2,1)S(1)} collective-permute-done((bf16[120,1024]{1,0:T(8,128)(2,1)S(1)}, bf16[120,1024]{1,0:T(8,128)(2,1)S(1)}, u32[]{:S(2)}, u32[]{:S(2)}) %collective-permute-start.7) | collective-permute-done | bytes 245792 | tf_op jit(solution)/shard_map/ppermute | solution.py:330
  24.3 0.5 collective-permute-start.2
  24.8 3.1 %collective-permute-done.8.refs_3_ = bf16[120,1024]{1,0:T(8,128)(2,1)S(1)} collective-permute-done((bf16[120,1024]{1,0:T(8,128)(2,1)S(1)}, bf16[120,1024]{1,0:T(8,128)(2,1)S(1)}, u32[]{:S(2)}, u32[]{:S(2)}) %collective-permute-start.8) | collective-permute-done | bytes 245792 | tf_op jit(solution)/shard_map/ppermute | solution.py:330
  28.0 0.6 shard_map.59.rows
  28.6 4.1 %collective-permute-done.10.refs_2_ = bf16[256,512]{1,0:T(8,128)(2,1)S(1)} collective-permute-done((bf16[256,512]{1,0:T(8,128)(2,1)S(1)}, bf16[256,512]{1,0:T(8,128)(2,1)S(1)}, u32[]{:S(2)}, u32[]{:S(2)}) %collective-permute-start.10) | collective-permute-done | bytes 262176 | tf_op jit(solution)/shard_map/ppermute | solution.py:295
  32.7 0.2 collective-permute-done.9.refs_1_
  32.9 1.6 %shard_map.61 = (f32[512,128]{1,0:T(8,128)S(1)}, bf16[512,128]{1,0:T(8,128)(2,1)S(1)}, f32[512,256]{1,0:T(8,128)S(1)}, bf16[512,256]{1,0:T(8,128)(2,1)S(1)}, f32...) custom-call(s32[3]{0:T(128)S(1)} %pad_add_fusion.pos, bf16[512,1024]{1,0:T(8,128)(2,1)S(1)} %shard_map.59.rows, ...), custom_call_target="tpu_custom_call" | custom-call | flops 536870912 | bytes 3670016 | tf_op jit(solution)/shard_map/pallas_call | solution.py:34
  34.5 1.6 %collective-permute-start.22 = (bf16[512,256]{1,0:T(8,128)(2,1)S(1)}, bf16[512,256]{1,0:T(8,128)(2,1)S(1)}, u32[]{:S(2)}, u32[]{:S(2)}) collective-permute-start(bf16[512,256]{1,0:T(8,128)(2,1)S(1)} %get-tuple-element.58), channel_id=1, source_target_pairs={{0,16},{16,0},{1,17},{17,1},{2,18},{18,2},{3,19},{19,3},{4,20},{20... | collective-permute-start | bytes 786440 | tf_op jit(solution)/shard_map/ppermute | solution.py:366
  36.1 0.5 collective-permute-start.3
  36.6 1.4 %collective-permute-start.4 = (bf16[120,1024]{1,0:T(8,128)(2,1)S(1)}, bf16[120,1024]{1,0:T(8,128)(2,1)S(1)}, u32[]{:S(2)}, u32[]{:S(2)}) collective-permute-start(bf16[120,1024]{1,0:T(8,128)(2,1)S(1)} %get-tuple-element.39), channel_id=1, source_target_pairs={{0,18},{1,19},{2,16},{3,17},{16,2},{17,3},{18,0},{19,1},{4,22},{5,... | collective-permute-start | bytes 737288 | tf_op jit(solution)/shard_map/ppermute | solution.py:330
  38.0 0.5 collective-permute-start.17
  38.5 1.5 %collective-permute-start.12 = (bf16[512,128]{1,0:T(8,128)(2,1)S(1)}, bf16[512,128]{1,0:T(8,128)(2,1)S(1)}, u32[]{:S(2)}, u32[]{:S(2)}) collective-permute-start(bf16[512,128]{1,0:T(8,128)(2,1)S(1)} %get-tuple-element.46), channel_id=1, source_target_pairs={{0,16},{16,0},{1,17},{17,1},{2,18},{18,2},{3,19},{19,3},{4,20},{20... | collective-permute-start | bytes 393224 | tf_op jit(solution)/shard_map/ppermute | solution.py:366
  40.1 9.0 %collective-permute-done.3.refs_2_ = bf16[120,1024]{1,0:T(8,128)(2,1)S(1)} collective-permute-done((bf16[120,1024]{1,0:T(8,128)(2,1)S(1)}, bf16[120,1024]{1,0:T(8,128)(2,1)S(1)}, u32[]{:S(2)}, u32[]{:S(2)}) %collective-permute-start.3) | collective-permute-done | bytes 245792 | tf_op jit(solution)/shard_map/ppermute | solution.py:330
  49.0 4.9 %collective-permute-done.4.refs_3_ = bf16[120,1024]{1,0:T(8,128)(2,1)S(1)} collective-permute-done((bf16[120,1024]{1,0:T(8,128)(2,1)S(1)}, bf16[120,1024]{1,0:T(8,128)(2,1)S(1)}, u32[]{:S(2)}, u32[]{:S(2)}) %collective-permute-start.4) | collective-permute-done | bytes 245792 | tf_op jit(solution)/shard_map/ppermute | solution.py:330
  54.0 0.9 %shard_map.57.refs_0_ = bf16[1024,512]{1,0:T(8,128)(2,1)S(1)} custom-call(s32[3]{0:T(128)S(1)} %pad_add_fusion.pos, bf16[120,1024]{1,0:T(8,128)(2,1)S(1)} %get-tuple-element.36.refs_0_, bf16[120,1024]{1,0:T(8,128)(2,1)S(1)} %collective-permute-done.2.refs_1_, bf16[120,1024]{1,0:T(8,128)(2,1)S(1)} %collective-permute-done.3.refs_2_, ...), custom_call_target="tpu_custom_call" | custom-call | bytes 2031616 | tf_op jit(solution)/shard_map/pallas_call | solution.py:34
  54.9 1.0 %shard_map.66 = (bf16[256,256]{1,0:T(8,128)(2,1)S(1)}, bf16[256,256]{1,0:T(8,128)(2,1)S(1)}, bf16[256,256]{1,0:T(8,128)(2,1)S(1)}, f32[256,256]{1,0:T(8,128)S(1)}) custom-call(s32[3]{0:T(128)S(1)} %pad_add_fusion.pos, bf16[1024,512]{1,0:T(8,128)(2,1)S(1)} %shard_map.57.refs_0_, f32[512,256]{1,0:T(8,128)S(1)} %get-tuple-element.57.refs_1_, ...), custom_call_target="tpu_custom_call" | custom-call | flops 268435456 | bytes 2490368 | tf_op jit(solution)/shard_map/pallas_call | solution.py:34
  55.9 3.8 %collective-permute-start.23 = (bf16[256,256]{1,0:T(8,128)(2,1)S(1)}, bf16[256,256]{1,0:T(8,128)(2,1)S(1)}, u32[]{:S(2)}, u32[]{:S(2)}) collective-permute-start(bf16[256,256]{1,0:T(8,128)(2,1)S(1)} %get-tuple-element.60), channel_id=1, source_target_pairs={{0,12},{4,8},{8,4},{12,0},{1,13},{5,9},{9,5},{13,1},{2,14},{6,10},... | collective-permute-start | bytes 393224 | tf_op jit(solution)/shard_map/ppermute | solution.py:400
  59.7 4.0 %collective-permute-start.24 = (bf16[256,256]{1,0:T(8,128)(2,1)S(1)}, bf16[256,256]{1,0:T(8,128)(2,1)S(1)}, u32[]{:S(2)}, u32[]{:S(2)}) collective-permute-start(bf16[256,256]{1,0:T(8,128)(2,1)S(1)} %get-tuple-element.61), channel_id=1, source_target_pairs={{0,4},{4,0},{8,12},{12,8},{1,5},{5,1},{9,13},{13,9},{2,6},{6,2},{1... | collective-permute-start | bytes 393224 | tf_op jit(solution)/shard_map/ppermute | solution.py:400
  63.7 1.0 %shard_map.64 = (bf16[256,128]{1,0:T(8,128)(2,1)S(1)}, bf16[256,128]{1,0:T(8,128)(2,1)S(1)}, bf16[256,128]{1,0:T(8,128)(2,1)S(1)}, f32[256,128]{1,0:T(8,128)S(1)}) custom-call(s32[3]{0:T(128)S(1)} %pad_add_fusion.pos, bf16[1024,512]{1,0:T(8,128)(2,1)S(1)} %shard_map.57.refs_0_, f32[512,128]{1,0:T(8,128)S(1)} %get-tuple-element.51.refs_1_, ...), custom_call_target="tpu_custom_call" | custom-call | flops 134217728 | bytes 1769472 | tf_op jit(solution)/shard_map/pallas_call | solution.py:34
  64.7 2.4 %collective-permute-start.18 = (bf16[256,128]{1,0:T(8,128)(2,1)S(1)}, bf16[256,128]{1,0:T(8,128)(2,1)S(1)}, u32[]{:S(2)}, u32[]{:S(2)}) collective-permute-start(bf16[256,128]{1,0:T(8,128)(2,1)S(1)} %get-tuple-element.54), channel_id=1, source_target_pairs={{0,12},{4,8},{8,4},{12,0},{1,13},{5,9},{9,5},{13,1},{2,14},{6,10},... | collective-permute-start | bytes 196616 | tf_op jit(solution)/shard_map/ppermute | solution.py:400
  67.2 1.1 %collective-permute-start.19 = (bf16[256,128]{1,0:T(8,128)(2,1)S(1)}, bf16[256,128]{1,0:T(8,128)(2,1)S(1)}, u32[]{:S(2)}, u32[]{:S(2)}) collective-permute-start(bf16[256,128]{1,0:T(8,128)(2,1)S(1)} %get-tuple-element.55), channel_id=1, source_target_pairs={{0,4},{4,0},{8,12},{12,8},{1,5},{5,1},{9,13},{13,9},{2,6},{6,2},{1... | collective-permute-start | bytes 196616 | tf_op jit(solution)/shard_map/ppermute | solution.py:400
  68.3 1.0 %shard_map.62 = (bf16[256,128]{1,0:T(8,128)(2,1)S(1)}, bf16[256,128]{1,0:T(8,128)(2,1)S(1)}, bf16[256,128]{1,0:T(8,128)(2,1)S(1)}, f32[256,128]{1,0:T(8,128)S(1)}) custom-call(s32[3]{0:T(128)S(1)} %pad_add_fusion.pos, bf16[1024,512]{1,0:T(8,128)(2,1)S(1)} %shard_map.57.refs_0_, f32[512,128]{1,0:T(8,128)S(1)} %get-tuple-element.45.refs_1_, ...), custom_call_target="tpu_custom_call" | custom-call | flops 134217728 | bytes 1769472 | tf_op jit(solution)/shard_map/pallas_call | solution.py:34
  69.3 5.8 %collective-permute-start.20 = (bf16[256,128]{1,0:T(8,128)(2,1)S(1)}, bf16[256,128]{1,0:T(8,128)(2,1)S(1)}, u32[]{:S(2)}, u32[]{:S(2)}) collective-permute-start(bf16[256,128]{1,0:T(8,128)(2,1)S(1)} %get-tuple-element.56), channel_id=1, source_target_pairs={{0,8},{4,12},{8,0},{12,4},{1,9},{5,13},{9,1},{13,5},{2,10},{6,14},... | collective-permute-start | bytes 196616 | tf_op jit(solution)/shard_map/ppermute | solution.py:400
  75.1 0.5 collective-permute-start.13
  75.7 0.3 collective-permute-start.14
  76.0 0.6 shard_map.67.refs_2_
  76.6 3.6 %collective-permute-start.15 = (bf16[256,128]{1,0:T(8,128)(2,1)S(1)}, bf16[256,128]{1,0:T(8,128)(2,1)S(1)}, u32[]{:S(2)}, u32[]{:S(2)}) collective-permute-start(bf16[256,128]{1,0:T(8,128)(2,1)S(1)} %get-tuple-element.50), channel_id=1, source_target_pairs={{0,8},{4,12},{8,0},{12,4},{1,9},{5,13},{9,1},{13,5},{2,10},{6,14},... | collective-permute-start | bytes 196616 | tf_op jit(solution)/shard_map/ppermute | solution.py:400
  80.2 1.5 %collective-permute-start.26 = (bf16[256,256]{1,0:T(8,128)(2,1)S(1)}, bf16[256,256]{1,0:T(8,128)(2,1)S(1)}, u32[]{:S(2)}, u32[]{:S(2)}) collective-permute-start(bf16[256,256]{1,0:T(8,128)(2,1)S(1)} %shard_map.67.refs_2_), channel_id=1, source_target_pairs={{0,16},{16,0},{1,17},{17,1},{2,18},{18,2},{3,19},{19,3},{4,20},{20... | collective-permute-start | bytes 393224 | tf_op jit(solution)/shard_map/ppermute | solution.py:416
  81.7 0.6 shard_map.65.refs_0_
  82.3 0.6 collective-permute-start.21
  82.9 0.6 shard_map.63.refs_4_
  83.5 1.5 %collective-permute-start.16 = (bf16[256,128]{1,0:T(8,128)(2,1)S(1)}, bf16[256,128]{1,0:T(8,128)(2,1)S(1)}, u32[]{:S(2)}, u32[]{:S(2)}) collective-permute-start(bf16[256,128]{1,0:T(8,128)(2,1)S(1)} %shard_map.63.refs_4_), channel_id=1, source_target_pairs={{0,16},{16,0},{1,17},{17,1},{2,18},{18,2},{3,19},{19,3},{4,20},{20... | collective-permute-start | bytes 196616 | tf_op jit(solution)/shard_map/ppermute | solution.py:416
  85.0 1.6 %collective-permute-done.21.refs_1_ = bf16[256,128]{1,0:T(8,128)(2,1)S(1)} collective-permute-done((bf16[256,128]{1,0:T(8,128)(2,1)S(1)}, bf16[256,128]{1,0:T(8,128)(2,1)S(1)}, u32[]{:S(2)}, u32[]{:S(2)}) %collective-permute-start.21) | collective-permute-done | bytes 65568 | tf_op jit(solution)/shard_map/ppermute | solution.py:416
  86.6 1.3 %shard_map.68.refs_1_ = bf16[512,512]{1,0:T(8,128)(2,1)} custom-call(s32[3]{0:T(128)S(1)} %pad_add_fusion.pos, bf16[256,128]{1,0:T(8,128)(2,1)S(1)} %shard_map.65.refs_0_, bf16[256,128]{1,0:T(8,128)(2,1)S(1)} %collective-permute-done.21.refs_1_, bf16[256,256]{1,0:T(8,128)(2,1)S(1)} %shard_map.67.refs_2_, ...), custom_call_target="tpu_custom_call" | custom-call | bytes 983040 | tf_op jit(solution)/shard_map/pallas_call | solution.py:34
  88.0 1.2 %shard_map.69 = bf16[512,512]{1,0:T(8,128)(2,1)} custom-call(s32[3]{0:T(128)S(1)} %pad_add_fusion.pos, bf16[256,128]{1,0:T(8,128)(2,1)S(1)} %collective-permute-done.16.refs_0_, bf16[512,512]{1,0:T(8,128)(2,1)} %shard_map.68.refs_1_), custom_call_target="tpu_custom_call", output_to_operand_aliasing={{}: (2, {})} | custom-call | bytes 1114112 | tf_op jit(solution)/shard_map/pallas_call | solution.py:34
  (26 shorter events, 0.4 us)
Async XLA Ops:
  0.0 0.7 copy-start.1
  0.0 5.4 %collective-permute-start.5 = (bf16[192,2048]{1,0:T(8,128)(2,1)}, bf16[192,2048]{1,0:T(8,128)(2,1)S(1)}, u32[]{:S(2)}, u32[]{:S(2)}) collective-permute-start(bf16[192,2048]{1,0:T(8,128)(2,1)} %rows.2), channel_id=1, source_target_pairs={{0,1},{1,0},{2,3},{3,2},{4,5},{5,4},{6,7},{7,6},{8,9},{9,8},{10,11... | collective-permute-start | bytes 2359304 | tf_op jit(solution)/shard_map/ppermute | solution.py:273
  0.5 15.0 %collective-permute-start.1 = (bf16[192,2048]{1,0:T(8,128)(2,1)}, bf16[192,2048]{1,0:T(8,128)(2,1)S(1)}, u32[]{:S(2)}, u32[]{:S(2)}) collective-permute-start(bf16[192,2048]{1,0:T(8,128)(2,1)} %rows.3), channel_id=1, source_target_pairs={{0,1},{1,0},{2,3},{3,2},{4,5},{5,4},{6,7},{7,6},{8,9},{9,8},{10,11... | collective-permute-start | bytes 2359304 | tf_op jit(solution)/shard_map/ppermute | solution.py:275
  0.7 3.1 %collective-permute-start = (s32[1,192]{1,0:T(1,128)S(1)}, s32[1,192]{1,0:T(1,128)S(1)}, u32[]{:S(2)}, u32[]{:S(2)}) collective-permute-start(s32[1,192]{1,0:T(1,128)S(1)} %bitcast.7), channel_id=1, source_target_pairs={{0,1},{1,0},{2,3},{3,2},{4,5},{5,4},{6,7},{7,6},{8,9},{9,8},{10,11... | collective-permute-start | bytes 2312 | tf_op jit(solution)/shard_map/ppermute | solution.py:274
  6.7 11.9 %copy-start = (bf16[192,2048]{1,0:T(8,128)(2,1)S(1)}, bf16[192,2048]{1,0:T(8,128)(2,1)}, u32[]{:S(2)}) copy-start(bf16[192,2048]{1,0:T(8,128)(2,1)} %rows.3) | copy-start | bytes 2359300
  6.7 10.3 %collective-permute-start.6 = (bf16[120,1024]{1,0:T(8,128)(2,1)S(1)}, bf16[120,1024]{1,0:T(8,128)(2,1)S(1)}, u32[]{:S(2)}, u32[]{:S(2)}) collective-permute-start(bf16[120,1024]{1,0:T(8,128)(2,1)S(1)} %get-tuple-element.42), channel_id=1, source_target_pairs={{0,2},{1,3},{2,0},{3,1},{16,18},{17,19},{18,16},{19,17},{4,6},{5,7... | collective-permute-start | bytes 737288 | tf_op jit(solution)/shard_map/ppermute | solution.py:330
  11.3 21.4 %collective-permute-start.10 = (bf16[256,512]{1,0:T(8,128)(2,1)S(1)}, bf16[256,512]{1,0:T(8,128)(2,1)S(1)}, u32[]{:S(2)}, u32[]{:S(2)}) collective-permute-start(bf16[256,512]{1,0:T(8,128)(2,1)S(1)} %shard_map.60.refs_0_), channel_id=1, source_target_pairs={{0,8},{4,12},{8,0},{12,4},{1,9},{5,13},{9,1},{13,5},{2,10},{6,14},... | collective-permute-start | bytes 786440 | tf_op jit(solution)/shard_map/ppermute | solution.py:295
  13.9 18.8 %collective-permute-start.11 = (bf16[256,512]{1,0:T(8,128)(2,1)S(1)}, bf16[256,512]{1,0:T(8,128)(2,1)S(1)}, u32[]{:S(2)}, u32[]{:S(2)}) collective-permute-start(bf16[256,512]{1,0:T(8,128)(2,1)S(1)} %shard_map.60.refs_0_), channel_id=1, source_target_pairs={{0,12},{4,8},{8,4},{12,0},{1,13},{5,9},{9,5},{13,1},{2,14},{6,10},... | collective-permute-start | bytes 786440 | tf_op jit(solution)/shard_map/ppermute | solution.py:295
  15.2 17.7 %collective-permute-start.9 = (bf16[256,512]{1,0:T(8,128)(2,1)S(1)}, bf16[256,512]{1,0:T(8,128)(2,1)S(1)}, u32[]{:S(2)}, u32[]{:S(2)}) collective-permute-start(bf16[256,512]{1,0:T(8,128)(2,1)S(1)} %shard_map.60.refs_0_), channel_id=1, source_target_pairs={{0,4},{4,0},{8,12},{12,8},{1,5},{5,1},{9,13},{13,9},{2,6},{6,2},{1... | collective-permute-start | bytes 786440 | tf_op jit(solution)/shard_map/ppermute | solution.py:295
  15.5 8.8 %collective-permute-start.7 = (bf16[120,1024]{1,0:T(8,128)(2,1)S(1)}, bf16[120,1024]{1,0:T(8,128)(2,1)S(1)}, u32[]{:S(2)}, u32[]{:S(2)}) collective-permute-start(bf16[120,1024]{1,0:T(8,128)(2,1)S(1)} %get-tuple-element.43), channel_id=1, source_target_pairs={{0,16},{1,17},{2,18},{3,19},{16,0},{17,1},{18,2},{19,3},{4,20},{5,... | collective-permute-start | bytes 737288 | tf_op jit(solution)/shard_map/ppermute | solution.py:330
  17.0 11.0 %collective-permute-start.8 = (bf16[120,1024]{1,0:T(8,128)(2,1)S(1)}, bf16[120,1024]{1,0:T(8,128)(2,1)S(1)}, u32[]{:S(2)}, u32[]{:S(2)}) collective-permute-start(bf16[120,1024]{1,0:T(8,128)(2,1)S(1)} %get-tuple-element.44), channel_id=1, source_target_pairs={{0,18},{1,19},{2,16},{3,17},{16,2},{17,3},{18,0},{19,1},{4,22},{5,... | collective-permute-start | bytes 737288 | tf_op jit(solution)/shard_map/ppermute | solution.py:330
  24.3 14.2 %collective-permute-start.2 = (bf16[120,1024]{1,0:T(8,128)(2,1)S(1)}, bf16[120,1024]{1,0:T(8,128)(2,1)S(1)}, u32[]{:S(2)}, u32[]{:S(2)}) collective-permute-start(bf16[120,1024]{1,0:T(8,128)(2,1)S(1)} %get-tuple-element.37), channel_id=1, source_target_pairs={{0,2},{1,3},{2,0},{3,1},{16,18},{17,19},{18,16},{19,17},{4,6},{5,7... | collective-permute-start | bytes 737288 | tf_op jit(solution)/shard_map/ppermute | solution.py:330
  34.5 20.4 %collective-permute-start.22 = (bf16[512,256]{1,0:T(8,128)(2,1)S(1)}, bf16[512,256]{1,0:T(8,128)(2,1)S(1)}, u32[]{:S(2)}, u32[]{:S(2)}) collective-permute-start(bf16[512,256]{1,0:T(8,128)(2,1)S(1)} %get-tuple-element.58), channel_id=1, source_target_pairs={{0,16},{16,0},{1,17},{17,1},{2,18},{18,2},{3,19},{19,3},{4,20},{20... | collective-permute-start | bytes 786440 | tf_op jit(solution)/shard_map/ppermute | solution.py:366
  36.1 12.9 %collective-permute-start.3 = (bf16[120,1024]{1,0:T(8,128)(2,1)S(1)}, bf16[120,1024]{1,0:T(8,128)(2,1)S(1)}, u32[]{:S(2)}, u32[]{:S(2)}) collective-permute-start(bf16[120,1024]{1,0:T(8,128)(2,1)S(1)} %get-tuple-element.38), channel_id=1, source_target_pairs={{0,16},{1,17},{2,18},{3,19},{16,0},{17,1},{18,2},{19,3},{4,20},{5,... | collective-permute-start | bytes 737288 | tf_op jit(solution)/shard_map/ppermute | solution.py:330
  36.6 17.4 %collective-permute-start.4 = (bf16[120,1024]{1,0:T(8,128)(2,1)S(1)}, bf16[120,1024]{1,0:T(8,128)(2,1)S(1)}, u32[]{:S(2)}, u32[]{:S(2)}) collective-permute-start(bf16[120,1024]{1,0:T(8,128)(2,1)S(1)} %get-tuple-element.39), channel_id=1, source_target_pairs={{0,18},{1,19},{2,16},{3,17},{16,2},{17,3},{18,0},{19,1},{4,22},{5,... | collective-permute-start | bytes 737288 | tf_op jit(solution)/shard_map/ppermute | solution.py:330
  38.0 25.7 %collective-permute-start.17 = (bf16[512,128]{1,0:T(8,128)(2,1)S(1)}, bf16[512,128]{1,0:T(8,128)(2,1)S(1)}, u32[]{:S(2)}, u32[]{:S(2)}) collective-permute-start(bf16[512,128]{1,0:T(8,128)(2,1)S(1)} %get-tuple-element.52), channel_id=1, source_target_pairs={{0,16},{16,0},{1,17},{17,1},{2,18},{18,2},{3,19},{19,3},{4,20},{20... | collective-permute-start | bytes 393224 | tf_op jit(solution)/shard_map/ppermute | solution.py:366
  38.5 28.6 %collective-permute-start.12 = (bf16[512,128]{1,0:T(8,128)(2,1)S(1)}, bf16[512,128]{1,0:T(8,128)(2,1)S(1)}, u32[]{:S(2)}, u32[]{:S(2)}) collective-permute-start(bf16[512,128]{1,0:T(8,128)(2,1)S(1)} %get-tuple-element.46), channel_id=1, source_target_pairs={{0,16},{16,0},{1,17},{17,1},{2,18},{18,2},{3,19},{19,3},{4,20},{20... | collective-permute-start | bytes 393224 | tf_op jit(solution)/shard_map/ppermute | solution.py:366
  55.9 13.4 %collective-permute-start.23 = (bf16[256,256]{1,0:T(8,128)(2,1)S(1)}, bf16[256,256]{1,0:T(8,128)(2,1)S(1)}, u32[]{:S(2)}, u32[]{:S(2)}) collective-permute-start(bf16[256,256]{1,0:T(8,128)(2,1)S(1)} %get-tuple-element.60), channel_id=1, source_target_pairs={{0,12},{4,8},{8,4},{12,0},{1,13},{5,9},{9,5},{13,1},{2,14},{6,10},... | collective-permute-start | bytes 393224 | tf_op jit(solution)/shard_map/ppermute | solution.py:400
  59.7 15.4 %collective-permute-start.24 = (bf16[256,256]{1,0:T(8,128)(2,1)S(1)}, bf16[256,256]{1,0:T(8,128)(2,1)S(1)}, u32[]{:S(2)}, u32[]{:S(2)}) collective-permute-start(bf16[256,256]{1,0:T(8,128)(2,1)S(1)} %get-tuple-element.61), channel_id=1, source_target_pairs={{0,4},{4,0},{8,12},{12,8},{1,5},{5,1},{9,13},{13,9},{2,6},{6,2},{1... | collective-permute-start | bytes 393224 | tf_op jit(solution)/shard_map/ppermute | solution.py:400
  63.7 12.1 %collective-permute-start.25 = (bf16[256,256]{1,0:T(8,128)(2,1)S(1)}, bf16[256,256]{1,0:T(8,128)(2,1)S(1)}, u32[]{:S(2)}, u32[]{:S(2)}) collective-permute-start(bf16[256,256]{1,0:T(8,128)(2,1)S(1)} %get-tuple-element.62), channel_id=1, source_target_pairs={{0,8},{4,12},{8,0},{12,4},{1,9},{5,13},{9,1},{13,5},{2,10},{6,14},... | collective-permute-start | bytes 393224 | tf_op jit(solution)/shard_map/ppermute | solution.py:400
  64.7 11.9 %collective-permute-start.18 = (bf16[256,128]{1,0:T(8,128)(2,1)S(1)}, bf16[256,128]{1,0:T(8,128)(2,1)S(1)}, u32[]{:S(2)}, u32[]{:S(2)}) collective-permute-start(bf16[256,128]{1,0:T(8,128)(2,1)S(1)} %get-tuple-element.54), channel_id=1, source_target_pairs={{0,12},{4,8},{8,4},{12,0},{1,13},{5,9},{9,5},{13,1},{2,14},{6,10},... | collective-permute-start | bytes 196616 | tf_op jit(solution)/shard_map/ppermute | solution.py:400
  67.2 13.0 %collective-permute-start.19 = (bf16[256,128]{1,0:T(8,128)(2,1)S(1)}, bf16[256,128]{1,0:T(8,128)(2,1)S(1)}, u32[]{:S(2)}, u32[]{:S(2)}) collective-permute-start(bf16[256,128]{1,0:T(8,128)(2,1)S(1)} %get-tuple-element.55), channel_id=1, source_target_pairs={{0,4},{4,0},{8,12},{12,8},{1,5},{5,1},{9,13},{13,9},{2,6},{6,2},{1... | collective-permute-start | bytes 196616 | tf_op jit(solution)/shard_map/ppermute | solution.py:400
  69.3 12.3 %collective-permute-start.20 = (bf16[256,128]{1,0:T(8,128)(2,1)S(1)}, bf16[256,128]{1,0:T(8,128)(2,1)S(1)}, u32[]{:S(2)}, u32[]{:S(2)}) collective-permute-start(bf16[256,128]{1,0:T(8,128)(2,1)S(1)} %get-tuple-element.56), channel_id=1, source_target_pairs={{0,8},{4,12},{8,0},{12,4},{1,9},{5,13},{9,1},{13,5},{2,10},{6,14},... | collective-permute-start | bytes 196616 | tf_op jit(solution)/shard_map/ppermute | solution.py:400
  75.1 7.8 %collective-permute-start.13 = (bf16[256,128]{1,0:T(8,128)(2,1)S(1)}, bf16[256,128]{1,0:T(8,128)(2,1)S(1)}, u32[]{:S(2)}, u32[]{:S(2)}) collective-permute-start(bf16[256,128]{1,0:T(8,128)(2,1)S(1)} %get-tuple-element.48), channel_id=1, source_target_pairs={{0,12},{4,8},{8,4},{12,0},{1,13},{5,9},{9,5},{13,1},{2,14},{6,10},... | collective-permute-start | bytes 196616 | tf_op jit(solution)/shard_map/ppermute | solution.py:400
  75.7 7.1 %collective-permute-start.14 = (bf16[256,128]{1,0:T(8,128)(2,1)S(1)}, bf16[256,128]{1,0:T(8,128)(2,1)S(1)}, u32[]{:S(2)}, u32[]{:S(2)}) collective-permute-start(bf16[256,128]{1,0:T(8,128)(2,1)S(1)} %get-tuple-element.49), channel_id=1, source_target_pairs={{0,4},{4,0},{8,12},{12,8},{1,5},{5,1},{9,13},{13,9},{2,6},{6,2},{1... | collective-permute-start | bytes 196616 | tf_op jit(solution)/shard_map/ppermute | solution.py:400
  76.6 6.3 %collective-permute-start.15 = (bf16[256,128]{1,0:T(8,128)(2,1)S(1)}, bf16[256,128]{1,0:T(8,128)(2,1)S(1)}, u32[]{:S(2)}, u32[]{:S(2)}) collective-permute-start(bf16[256,128]{1,0:T(8,128)(2,1)S(1)} %get-tuple-element.50), channel_id=1, source_target_pairs={{0,8},{4,12},{8,0},{12,4},{1,9},{5,13},{9,1},{13,5},{2,10},{6,14},... | collective-permute-start | bytes 196616 | tf_op jit(solution)/shard_map/ppermute | solution.py:400
  80.2 6.4 %collective-permute-start.26 = (bf16[256,256]{1,0:T(8,128)(2,1)S(1)}, bf16[256,256]{1,0:T(8,128)(2,1)S(1)}, u32[]{:S(2)}, u32[]{:S(2)}) collective-permute-start(bf16[256,256]{1,0:T(8,128)(2,1)S(1)} %shard_map.67.refs_2_), channel_id=1, source_target_pairs={{0,16},{16,0},{1,17},{17,1},{2,18},{18,2},{3,19},{19,3},{4,20},{20... | collective-permute-start | bytes 393224 | tf_op jit(solution)/shard_map/ppermute | solution.py:416
  82.3 4.3 %collective-permute-start.21 = (bf16[256,128]{1,0:T(8,128)(2,1)S(1)}, bf16[256,128]{1,0:T(8,128)(2,1)S(1)}, u32[]{:S(2)}, u32[]{:S(2)}) collective-permute-start(bf16[256,128]{1,0:T(8,128)(2,1)S(1)} %shard_map.65.refs_0_), channel_id=1, source_target_pairs={{0,16},{16,0},{1,17},{17,1},{2,18},{18,2},{3,19},{19,3},{4,20},{20... | collective-permute-start | bytes 196616 | tf_op jit(solution)/shard_map/ppermute | solution.py:416
  83.5 4.5 %collective-permute-start.16 = (bf16[256,128]{1,0:T(8,128)(2,1)S(1)}, bf16[256,128]{1,0:T(8,128)(2,1)S(1)}, u32[]{:S(2)}, u32[]{:S(2)}) collective-permute-start(bf16[256,128]{1,0:T(8,128)(2,1)S(1)} %shard_map.63.refs_4_), channel_id=1, source_target_pairs={{0,16},{16,0},{1,17},{17,1},{2,18},{18,2},{3,19},{19,3},{4,20},{20... | collective-permute-start | bytes 196616 | tf_op jit(solution)/shard_map/ppermute | solution.py:416

commit v7 on v5

--- a/solution.py
+++ b/solution.py
@@ -7,7 +7,7 @@
 from jax.sharding import PartitionSpec as P
 
 QB = 32
-SPLITS = ((1, 1), (1, 1))
+SPLITS = ((2,), (1, 1))
 F32 = jnp.float32
 BF16 = jnp.bfloat16
 
@@ -55,14 +55,13 @@
     if not aligned:
         return [every], [([i], every) for i in range(chunks)], [[i] for i in range(chunks)]
     early, late = order[: nodes // 2], order[nodes // 2 :] + [0]
-    jobs = [([0], early), ([1], early), ([0, 1], late)]
-    jobs += [([i], every) for i in range(2, chunks)]
-    return [early, late], jobs, [[0, 1]] + [[i] for i in range(2, chunks)]
+    jobs = [([0], early), ([0], late)] + [([i], every) for i in range(1, chunks)]
+    return [early, late], jobs, [[i] for i in range(chunks)]
 
 
 def slots_of(copies, pairs):
-    slots = [(j, k) for k in reversed(range(pairs)) for j in reversed(range(copies))]
-    return [slot for slot in slots if slot != (0, 0)]
+    slots = [(j, k) for k in range(pairs) for j in range(copies) if j or k]
+    return sorted(slots, key=lambda slot: -(slot[0] > 0) - (slot[1] > 0))
 
 
 def shape(rows, cols, dtype):
@@ -425,25 +424,27 @@
     for i in range(len(outputs)):
         spots += [(j, begin) for j in range(copies)]
         begin += owns[i].shape[1]
-    early = len(finished) - copies + 1
-    last = copies - 1
+    items = list(zip(finished, spots))
+    sure = copies * max(0, len(outputs) - 2)
+    soon = [item for i, item in enumerate(items) if i < sure or item[1][0] == 0]
+    late = [item for i, item in enumerate(items) if i >= sure and item[1][0] > 0]
     (result,) = call(
-        functools.partial(lay_body, dims, spots[:early]),
+        functools.partial(lay_body, dims, [spot for _, spot in soon]),
         [shape(shard, hidden, BF16)],
         pos,
-        finished[:early],
-        [pltpu.SemaphoreType.DMA((early,))],
+        [value for value, _ in soon],
+        [pltpu.SemaphoreType.DMA((len(soon),))],
         target=pltpu.HBM,
     )
     (result,) = call(
-        functools.partial(lay_body, dims, spots[early:]),
+        functools.partial(lay_body, dims, [spot for _, spot in late]),
         [shape(shard, hidden, BF16)],
         pos,
-        finished[early:] + [result],
-        [pltpu.SemaphoreType.DMA((last,))],
-        space=[pltpu.VMEM] * last + [pltpu.HBM],
+        [value for value, _ in late] + [result],
+        [pltpu.SemaphoreType.DMA((len(late),))],
+        space=[pltpu.VMEM] * len(late) + [pltpu.HBM],
         target=pltpu.HBM,
-        aliases={last + 1: 0},
+        aliases={len(late) + 1: 0},
     )
     return result[None]
 

time: 92.2 us -> 88.8 us (0.963)
  waiting for transfers between devices: 24.9 us -> 14.1 us
  starting transfers between devices: 47.2 us -> 55.7 us
  Pallas kernels: 19.5 us -> 18.2 us
    ppermute x6, waiting for transfers between devices: 11.2 us -> 5.11 us  [on_device(): lax.ppermute(chunk, 'node', [(a, mate(a, s, nodes)) for a in range(nodes)])]
    ppermute x11 -> x9, waiting for transfers between devices: 3.7 us -> 0.17 us  [on_device(): moved = lax.ppermute(term, 'node', links)]
    ppermute x9, waiting for transfers between devices: 7.43 us -> 4.14 us  [exchange(): moved[at] = lax.ppermute(pieces[at], ('dp', 'local'), links)]
    ppermute x9, starting transfers between devices: 9.92 us -> 12.6 us  [exchange(): moved[at] = lax.ppermute(pieces[at], ('dp', 'local'), links)]
    ppermute x1, waiting for transfers between devices: 0.01 us -> 2.5 us  [on_device(): chosen_pair = lax.ppermute(chosen, 'local', swap)]
    ppermute x3, starting transfers between devices: 1.66 us -> 3.82 us  [on_device(): finished.append(lax.ppermute(summed, 'dp', links))]
    ppermute x6, starting transfers between devices: 12.2 us -> 14.3 us  [on_device(): lax.ppermute(chunk, 'node', [(a, mate(a, s, nodes)) for a in range(nodes)])]
    ppermute x11 -> x9, starting transfers between devices: 18.8 us -> 20.3 us  [on_device(): moved = lax.ppermute(term, 'node', links)]
  transfers between devices with their start and end apart: 36 -> 33, of which waited for: 10 -> 10; matrix products, arithmetic and copies ran while one was open for 0% -> 0% of each run, Pallas kernels for 20% -> 19%
where the time goes in v7:
time: 88.8 us; the launch traced here: 88.5 us
  starting transfers between devices  55.7 us (63%)
  Pallas kernels  18.2 us (20%)
  waiting for transfers between devices  14.1 us (16%)
    ppermute x9, starting transfers between devices, on_device(): moved = lax.ppermute(term, 'node', links)  20.3 us
    pallas_call x18, Pallas kernels, call(): pl.pallas_call(body, out_shape=outs, in_specs=[pl.BlockSpec(memory_space=...  18.2 us
    ppermute x6, starting transfers between devices, on_device(): lax.ppermute(chunk, 'node', [(a, mate(a, s, nodes)) for a in range(nodes)])  14.3 us
    ppermute x9, starting transfers between devices, exchange(): moved[at] = lax.ppermute(pieces[at], ('dp', 'local'), links)  12.6 us
    ppermute x6, waiting for transfers between devices, on_device(): lax.ppermute(chunk, 'node', [(a, mate(a, s, nodes)) for a in range(nodes)])  5.11 us
    ppermute x9, waiting for transfers between devices, exchange(): moved[at] = lax.ppermute(pieces[at], ('dp', 'local'), links)  4.14 us
    ppermute x3, starting transfers between devices, on_device(): finished.append(lax.ppermute(summed, 'dp', links))  3.82 us
    ppermute x3, starting transfers between devices, on_device(): acts.append([kept, lax.ppermute(sent, 'dp', [(0, 1), (1, 0)])])  3.63 us
  transfers between devices with their start and end apart: 33, of which 10 were waited for; matrix products, arithmetic and copies ran while one was open for 0% of the time, Pallas kernels for 19%

profile of v7, /device:TPU:0, one launch (start us, length us, event | category | flops | bytes accessed | tf_op | source)
XLA Modules:
  0.0 88.5 jit_solution(18242322380640883247)
XLA Ops:
  1.2 2.5 %collective-permute-done.ids_pair = s32[1,192]{1,0:T(1,128)S(1)} collective-permute-done((s32[1,192]{1,0:T(1,128)S(1)}, s32[1,192]{1,0:T(1,128)S(1)}, u32[]{:S(2)}, u32[]{:S(2)}) %collective-permute-start) | collective-permute-done | bytes 800 | tf_op jit(solution)/shard_map/ppermute | solution.py:279
  3.7 1.7 %shard_map.55 = (bf16[256,192]{1,0:T(8,128)(2,1)S(1)}, bf16[256,192]{1,0:T(8,128)(2,1)S(1)}, bf16[192,2048]{1,0:T(8,128)(2,1)S(1)}) custom-call(s32[3]{0:T(128)S(1)} %pad_add_fusion.pos, s32[1,192]{1,0:T(1,128)S(1)} %bitcast.8, s32[1,192]{1,0:T(1,128)S(1)} %collective-permute-done.ids_pair, bf16[192,2048]{1,0:T(8,128)(2,1)} %rows.2), custom_call_target="tpu_custom_call" | custom-call | bytes 1771008 | tf_op jit(solution)/shard_map/pallas_call | solution.py:34
  5.4 1.3 %shard_map.59 = (bf16[120,1024]{1,0:T(8,128)(2,1)S(1)}, bf16[120,1024]{1,0:T(8,128)(2,1)S(1)}, bf16[120,1024]{1,0:T(8,128)(2,1)S(1)}, bf16[120,1024]{1,0:T(8,128)(2,1)S(1)}) custom-call(s32[3]{0:T(128)S(1)} %pad_add_fusion.pos, bf16[256,192]{1,0:T(8,128)(2,1)S(1)} %get-tuple-element.41.pick, bf16[256,192]{1,0:T(8,128)(2,1)S(1)} %get-tuple-element.42.pick_pair, ...), custom_call_target="tpu_custom_call" | custom-call | flops 402653184 | bytes 2752512 | tf_op jit(solution)/shard_map/pallas_call | solution.py:34
  6.7 2.9 %collective-permute-start.9 = (bf16[120,1024]{1,0:T(8,128)(2,1)S(1)}, bf16[120,1024]{1,0:T(8,128)(2,1)S(1)}, u32[]{:S(2)}, u32[]{:S(2)}) collective-permute-start(bf16[120,1024]{1,0:T(8,128)(2,1)S(1)} %get-tuple-element.53), channel_id=1, source_target_pairs={{0,2},{1,3},{2,0},{3,1},{16,18},{17,19},{18,16},{19,17},{4,6},{5,7... | collective-permute-start | bytes 737288 | tf_op jit(solution)/shard_map/ppermute | solution.py:335
  9.7 1.5 %collective-permute-start.10 = (bf16[120,1024]{1,0:T(8,128)(2,1)S(1)}, bf16[120,1024]{1,0:T(8,128)(2,1)S(1)}, u32[]{:S(2)}, u32[]{:S(2)}) collective-permute-start(bf16[120,1024]{1,0:T(8,128)(2,1)S(1)} %get-tuple-element.54), channel_id=1, source_target_pairs={{0,16},{1,17},{2,18},{3,19},{16,0},{17,1},{18,2},{19,3},{4,20},{5,... | collective-permute-start | bytes 737288 | tf_op jit(solution)/shard_map/ppermute | solution.py:335
  11.2 1.6 %shard_map.61 = (bf16[256,256]{1,0:T(8,128)(2,1)S(1)}, bf16[256,256]{1,0:T(8,128)(2,1)S(1)}) custom-call(s32[3]{0:T(128)S(1)} %pad_add_fusion.pos, bf16[512,512]{1,0:T(8,128)(2,1)} %bitcast.9, bf16[16,512]{1,0:T(8,128)(2,1)} %bitcast.10), custom_call_target="tpu_custom_call" | custom-call | bytes 802816 | tf_op jit(solution)/shard_map/pallas_call | solution.py:34
  12.8 2.1 %collective-permute-start.25 = (bf16[256,256]{1,0:T(8,128)(2,1)S(1)}, bf16[256,256]{1,0:T(8,128)(2,1)S(1)}, u32[]{:S(2)}, u32[]{:S(2)}) collective-permute-start(bf16[256,256]{1,0:T(8,128)(2,1)S(1)} %get-tuple-element.69.refs_0_), channel_id=1, source_target_pairs={{0,4},{4,0},{8,12},{12,8},{1,5},{5,1},{9,13},{13,9},{2,6},{6,2},{1... | collective-permute-start | bytes 393224 | tf_op jit(solution)/shard_map/ppermute | solution.py:300
  14.8 1.1 %collective-permute-done.9.refs_1_ = bf16[120,1024]{1,0:T(8,128)(2,1)S(1)} collective-permute-done((bf16[120,1024]{1,0:T(8,128)(2,1)S(1)}, bf16[120,1024]{1,0:T(8,128)(2,1)S(1)}, u32[]{:S(2)}, u32[]{:S(2)}) %collective-permute-start.9) | collective-permute-done | bytes 245792 | tf_op jit(solution)/shard_map/ppermute | solution.py:335
  15.9 2.8 %collective-permute-start.26 = (bf16[256,256]{1,0:T(8,128)(2,1)S(1)}, bf16[256,256]{1,0:T(8,128)(2,1)S(1)}, u32[]{:S(2)}, u32[]{:S(2)}) collective-permute-start(bf16[256,256]{1,0:T(8,128)(2,1)S(1)} %get-tuple-element.69.refs_0_), channel_id=1, source_target_pairs={{0,8},{4,12},{8,0},{12,4},{1,9},{5,13},{9,1},{13,5},{2,10},{6,14},... | collective-permute-start | bytes 393224 | tf_op jit(solution)/shard_map/ppermute | solution.py:300
  18.7 3.4 %collective-permute-start.27 = (bf16[256,256]{1,0:T(8,128)(2,1)S(1)}, bf16[256,256]{1,0:T(8,128)(2,1)S(1)}, u32[]{:S(2)}, u32[]{:S(2)}) collective-permute-start(bf16[256,256]{1,0:T(8,128)(2,1)S(1)} %get-tuple-element.69.refs_0_), channel_id=1, source_target_pairs={{0,12},{4,8},{8,4},{12,0},{1,13},{5,9},{9,5},{13,1},{2,14},{6,10},... | collective-permute-start | bytes 393224 | tf_op jit(solution)/shard_map/ppermute | solution.py:300
  22.4 1.7 %collective-permute-start.12 = (bf16[256,256]{1,0:T(8,128)(2,1)S(1)}, bf16[256,256]{1,0:T(8,128)(2,1)S(1)}, u32[]{:S(2)}, u32[]{:S(2)}) collective-permute-start(bf16[256,256]{1,0:T(8,128)(2,1)S(1)} %get-tuple-element.56.refs_0_), channel_id=1, source_target_pairs={{0,4},{4,0},{8,12},{12,8},{1,5},{5,1},{9,13},{13,9},{2,6},{6,2},{1... | collective-permute-start | bytes 393224 | tf_op jit(solution)/shard_map/ppermute | solution.py:300
  24.2 0.6 shard_map.60.rows
  24.8 2.7 %collective-permute-start.13 = (bf16[256,256]{1,0:T(8,128)(2,1)S(1)}, bf16[256,256]{1,0:T(8,128)(2,1)S(1)}, u32[]{:S(2)}, u32[]{:S(2)}) collective-permute-start(bf16[256,256]{1,0:T(8,128)(2,1)S(1)} %get-tuple-element.56.refs_0_), channel_id=1, source_target_pairs={{0,8},{4,12},{8,0},{12,4},{1,9},{5,13},{9,1},{13,5},{2,10},{6,14},... | collective-permute-start | bytes 393224 | tf_op jit(solution)/shard_map/ppermute | solution.py:300
  27.5 2.6 %collective-permute-done.26.refs_2_ = bf16[256,256]{1,0:T(8,128)(2,1)S(1)} collective-permute-done((bf16[256,256]{1,0:T(8,128)(2,1)S(1)}, bf16[256,256]{1,0:T(8,128)(2,1)S(1)}, u32[]{:S(2)}, u32[]{:S(2)}) %collective-permute-start.26) | collective-permute-done | bytes 131104 | tf_op jit(solution)/shard_map/ppermute | solution.py:300
  30.0 1.7 %collective-permute-start.14 = (bf16[256,256]{1,0:T(8,128)(2,1)S(1)}, bf16[256,256]{1,0:T(8,128)(2,1)S(1)}, u32[]{:S(2)}, u32[]{:S(2)}) collective-permute-start(bf16[256,256]{1,0:T(8,128)(2,1)S(1)} %get-tuple-element.56.refs_0_), channel_id=1, source_target_pairs={{0,12},{4,8},{8,4},{12,0},{1,13},{5,9},{9,5},{13,1},{2,14},{6,10},... | collective-permute-start | bytes 393224 | tf_op jit(solution)/shard_map/ppermute | solution.py:300
  31.7 1.0 %shard_map.67 = (f32[512,256]{1,0:T(8,128)S(1)}, bf16[512,256]{1,0:T(8,128)(2,1)S(1)}) custom-call(s32[3]{0:T(128)S(1)} %pad_add_fusion.pos, bf16[512,1024]{1,0:T(8,128)(2,1)S(1)} %shard_map.60.rows, bf16[256,256]{1,0:T(8,128)(2,1)S(1)} %get-tuple-element.69.refs_0_, bf16[256,256]{1,0:T(8,128)(2,1)S(1)} %collective-permute-done.25.refs_1_, ...), custom_call_target="tpu_custom_call" | custom-call | flops 268435456 | bytes 2359296 | tf_op jit(solution)/shard_map/pallas_call | solution.py:34
  32.7 1.5 %collective-permute-start.28 = (bf16[512,256]{1,0:T(8,128)(2,1)S(1)}, bf16[512,256]{1,0:T(8,128)(2,1)S(1)}, u32[]{:S(2)}, u32[]{:S(2)}) collective-permute-start(bf16[512,256]{1,0:T(8,128)(2,1)S(1)} %get-tuple-element.71), channel_id=1, source_target_pairs={{0,16},{16,0},{1,17},{17,1},{2,18},{18,2},{3,19},{19,3},{4,20},{20... | collective-permute-start | bytes 786440 | tf_op jit(solution)/shard_map/ppermute | solution.py:371
  34.3 1.3 %shard_map.56 = (bf16[120,512]{1,0:T(8,128)(2,1)S(1)}, bf16[120,512]{1,0:T(8,128)(2,1)S(1)}, bf16[120,512]{1,0:T(8,128)(2,1)S(1)}, bf16[120,512]{1,0:T(8,128)(2,...) custom-call(s32[3]{0:T(128)S(1)} %pad_add_fusion.pos, ...), custom_call_target="tpu_custom_call" | custom-call | flops 402653184 | bytes 2752512 | tf_op jit(solution)/shard_map/pallas_call | solution.py:34
  35.6 1.2 %collective-permute-start.2 = (bf16[120,512]{1,0:T(8,128)(2,1)S(1)}, bf16[120,512]{1,0:T(8,128)(2,1)S(1)}, u32[]{:S(2)}, u32[]{:S(2)}) collective-permute-start(bf16[120,512]{1,0:T(8,128)(2,1)S(1)} %get-tuple-element.44), channel_id=1, source_target_pairs={{0,2},{1,3},{2,0},{3,1},{16,18},{17,19},{18,16},{19,17},{4,6},{5,7... | collective-permute-start | bytes 368648 | tf_op jit(solution)/shard_map/ppermute | solution.py:335
  37.3 2.5 %collective-permute-done.13.refs_2_ = bf16[256,256]{1,0:T(8,128)(2,1)S(1)} collective-permute-done((bf16[256,256]{1,0:T(8,128)(2,1)S(1)}, bf16[256,256]{1,0:T(8,128)(2,1)S(1)}, u32[]{:S(2)}, u32[]{:S(2)}) %collective-permute-start.13) | collective-permute-done | bytes 131104 | tf_op jit(solution)/shard_map/ppermute | solution.py:300
  39.9 2.5 %collective-permute-start.4 = (bf16[120,512]{1,0:T(8,128)(2,1)S(1)}, bf16[120,512]{1,0:T(8,128)(2,1)S(1)}, u32[]{:S(2)}, u32[]{:S(2)}) collective-permute-start(bf16[120,512]{1,0:T(8,128)(2,1)S(1)} %get-tuple-element.46), channel_id=1, source_target_pairs={{0,18},{1,19},{2,16},{3,17},{16,2},{17,3},{18,0},{19,1},{4,22},{5,... | collective-permute-start | bytes 368648 | tf_op jit(solution)/shard_map/ppermute | solution.py:335
  43.8 2.9 %collective-permute-start.7 = (bf16[120,512]{1,0:T(8,128)(2,1)S(1)}, bf16[120,512]{1,0:T(8,128)(2,1)S(1)}, u32[]{:S(2)}, u32[]{:S(2)}) collective-permute-start(bf16[120,512]{1,0:T(8,128)(2,1)S(1)} %get-tuple-element.50), channel_id=1, source_target_pairs={{0,18},{1,19},{2,16},{3,17},{16,2},{17,3},{18,0},{19,1},{4,22},{5,... | collective-permute-start | bytes 368648 | tf_op jit(solution)/shard_map/ppermute | solution.py:335
  46.7 1.3 %shard_map.62 = (f32[512,128]{1,0:T(8,128)S(1)}, bf16[512,128]{1,0:T(8,128)(2,1)S(1)}, f32[512,128]{1,0:T(8,128)S(1)}, bf16[512,128]{1,0:T(8,128)(2,1)S(1)}) custom-call(s32[3]{0:T(128)S(1)} %pad_add_fusion.pos, bf16[512,1024]{1,0:T(8,128)(2,1)S(1)} %shard_map.60.rows, bf16[256,256]{1,0:T(8,128)(2,1)S(1)} %get-tuple-element.56.refs_0_, ...), custom_call_target="tpu_custom_call" | custom-call | flops 268435456 | bytes 2359296 | tf_op jit(solution)/shard_map/pallas_call | solution.py:34
  48.0 1.4 %collective-permute-start.15 = (bf16[512,128]{1,0:T(8,128)(2,1)S(1)}, bf16[512,128]{1,0:T(8,128)(2,1)S(1)}, u32[]{:S(2)}, u32[]{:S(2)}) collective-permute-start(bf16[512,128]{1,0:T(8,128)(2,1)S(1)} %get-tuple-element.58), channel_id=1, source_target_pairs={{0,16},{16,0},{1,17},{17,1},{2,18},{18,2},{3,19},{19,3},{4,20},{20... | collective-permute-start | bytes 393224 | tf_op jit(solution)/shard_map/ppermute | solution.py:371
  49.3 0.7 collective-permute-start.20
  50.1 0.8 shard_map.57.refs_0_
  50.8 2.2 %collective-permute-done.7.refs_3_ = bf16[120,512]{1,0:T(8,128)(2,1)S(1)} collective-permute-done((bf16[120,512]{1,0:T(8,128)(2,1)S(1)}, bf16[120,512]{1,0:T(8,128)(2,1)S(1)}, u32[]{:S(2)}, u32[]{:S(2)}) %collective-permute-start.7) | collective-permute-done | bytes 122912 | tf_op jit(solution)/shard_map/ppermute | solution.py:335
  53.1 0.8 shard_map.58.refs_1_.refs_0_
  53.9 0.9 shard_map.68
  54.7 1.8 %collective-permute-start.29 = (bf16[256,256]{1,0:T(8,128)(2,1)S(1)}, bf16[256,256]{1,0:T(8,128)(2,1)S(1)}, u32[]{:S(2)}, u32[]{:S(2)}) collective-permute-start(bf16[256,256]{1,0:T(8,128)(2,1)S(1)} %get-tuple-element.74), channel_id=1, source_target_pairs={{0,12},{4,8},{8,4},{12,0},{1,13},{5,9},{9,5},{13,1},{2,14},{6,10},... | collective-permute-start | bytes 393224 | tf_op jit(solution)/shard_map/ppermute | solution.py:405
  56.6 6.0 %collective-permute-start.30 = (bf16[256,256]{1,0:T(8,128)(2,1)S(1)}, bf16[256,256]{1,0:T(8,128)(2,1)S(1)}, u32[]{:S(2)}, u32[]{:S(2)}) collective-permute-start(bf16[256,256]{1,0:T(8,128)(2,1)S(1)} %get-tuple-element.75), channel_id=1, source_target_pairs={{0,4},{4,0},{8,12},{12,8},{1,5},{5,1},{9,13},{13,9},{2,6},{6,2},{1... | collective-permute-start | bytes 393224 | tf_op jit(solution)/shard_map/ppermute | solution.py:405
  62.5 0.8 shard_map.69
  63.6 1.0 %shard_map.63 = (bf16[256,128]{1,0:T(8,128)(2,1)S(1)}, bf16[256,128]{1,0:T(8,128)(2,1)S(1)}, bf16[256,128]{1,0:T(8,128)(2,1)S(1)}, f32[256,128]{1,0:T(8,128)S(1)}) custom-call(s32[3]{0:T(128)S(1)} %pad_add_fusion.pos, bf16[512,512]{1,0:T(8,128)(2,1)S(1)} %shard_map.57.refs_0_, bf16[512,512]{1,0:T(8,128)(2,1)S(1)} %shard_map.58.refs_1_.refs_0_, ...), custom_call_target="tpu_custom_call" | custom-call | flops 134217728 | bytes 1769472 | tf_op jit(solution)/shard_map/pallas_call | solution.py:34
  64.6 2.3 %collective-permute-start.16 = (bf16[256,128]{1,0:T(8,128)(2,1)S(1)}, bf16[256,128]{1,0:T(8,128)(2,1)S(1)}, u32[]{:S(2)}, u32[]{:S(2)}) collective-permute-start(bf16[256,128]{1,0:T(8,128)(2,1)S(1)} %get-tuple-element.60), channel_id=1, source_target_pairs={{0,12},{4,8},{8,4},{12,0},{1,13},{5,9},{9,5},{13,1},{2,14},{6,10},... | collective-permute-start | bytes 196616 | tf_op jit(solution)/shard_map/ppermute | solution.py:405
  66.9 1.1 %collective-permute-start.17 = (bf16[256,128]{1,0:T(8,128)(2,1)S(1)}, bf16[256,128]{1,0:T(8,128)(2,1)S(1)}, u32[]{:S(2)}, u32[]{:S(2)}) collective-permute-start(bf16[256,128]{1,0:T(8,128)(2,1)S(1)} %get-tuple-element.61), channel_id=1, source_target_pairs={{0,4},{4,0},{8,12},{12,8},{1,5},{5,1},{9,13},{13,9},{2,6},{6,2},{1... | collective-permute-start | bytes 196616 | tf_op jit(solution)/shard_map/ppermute | solution.py:405
  68.0 1.0 %shard_map.65 = (bf16[256,128]{1,0:T(8,128)(2,1)S(1)}, bf16[256,128]{1,0:T(8,128)(2,1)S(1)}, bf16[256,128]{1,0:T(8,128)(2,1)S(1)}, f32[256,128]{1,0:T(8,128)S(1)}) custom-call(s32[3]{0:T(128)S(1)} %pad_add_fusion.pos, bf16[512,512]{1,0:T(8,128)(2,1)S(1)} %shard_map.57.refs_0_, bf16[512,512]{1,0:T(8,128)(2,1)S(1)} %shard_map.58.refs_1_.refs_0_, ...), custom_call_target="tpu_custom_call" | custom-call | flops 134217728 | bytes 1769472 | tf_op jit(solution)/shard_map/pallas_call | solution.py:34
  69.1 4.4 %collective-permute-start.18 = (bf16[256,128]{1,0:T(8,128)(2,1)S(1)}, bf16[256,128]{1,0:T(8,128)(2,1)S(1)}, u32[]{:S(2)}, u32[]{:S(2)}) collective-permute-start(bf16[256,128]{1,0:T(8,128)(2,1)S(1)} %get-tuple-element.62), channel_id=1, source_target_pairs={{0,8},{4,12},{8,0},{12,4},{1,9},{5,13},{9,1},{13,5},{2,10},{6,14},... | collective-permute-start | bytes 196616 | tf_op jit(solution)/shard_map/ppermute | solution.py:405
  73.4 2.0 %collective-permute-start.21 = (bf16[256,128]{1,0:T(8,128)(2,1)S(1)}, bf16[256,128]{1,0:T(8,128)(2,1)S(1)}, u32[]{:S(2)}, u32[]{:S(2)}) collective-permute-start(bf16[256,128]{1,0:T(8,128)(2,1)S(1)} %get-tuple-element.66), channel_id=1, source_target_pairs={{0,12},{4,8},{8,4},{12,0},{1,13},{5,9},{9,5},{13,1},{2,14},{6,10},... | collective-permute-start | bytes 196616 | tf_op jit(solution)/shard_map/ppermute | solution.py:405
  75.4 0.6 shard_map.70.refs_0_
  76.0 2.6 %collective-permute-start.23 = (bf16[256,128]{1,0:T(8,128)(2,1)S(1)}, bf16[256,128]{1,0:T(8,128)(2,1)S(1)}, u32[]{:S(2)}, u32[]{:S(2)}) collective-permute-start(bf16[256,128]{1,0:T(8,128)(2,1)S(1)} %get-tuple-element.68), channel_id=1, source_target_pairs={{0,8},{4,12},{8,0},{12,4},{1,9},{5,13},{9,1},{13,5},{2,10},{6,14},... | collective-permute-start | bytes 196616 | tf_op jit(solution)/shard_map/ppermute | solution.py:405
  78.7 1.5 %collective-permute-start.32 = (bf16[256,256]{1,0:T(8,128)(2,1)S(1)}, bf16[256,256]{1,0:T(8,128)(2,1)S(1)}, u32[]{:S(2)}, u32[]{:S(2)}) collective-permute-start(bf16[256,256]{1,0:T(8,128)(2,1)S(1)} %shard_map.70.refs_0_), channel_id=1, source_target_pairs={{0,16},{16,0},{1,17},{17,1},{2,18},{18,2},{3,19},{19,3},{4,20},{20... | collective-permute-start | bytes 393224 | tf_op jit(solution)/shard_map/ppermute | solution.py:421
  80.3 0.6 shard_map.64.refs_2_
  80.9 1.5 %collective-permute-start.19 = (bf16[256,128]{1,0:T(8,128)(2,1)S(1)}, bf16[256,128]{1,0:T(8,128)(2,1)S(1)}, u32[]{:S(2)}, u32[]{:S(2)}) collective-permute-start(bf16[256,128]{1,0:T(8,128)(2,1)S(1)} %shard_map.64.refs_2_), channel_id=1, source_target_pairs={{0,16},{16,0},{1,17},{17,1},{2,18},{18,2},{3,19},{19,3},{4,20},{20... | collective-permute-start | bytes 196616 | tf_op jit(solution)/shard_map/ppermute | solution.py:421
  82.4 0.6 shard_map.66.refs_3_
  83.0 0.8 collective-permute-start.24
  83.8 1.3 %shard_map.71.refs_2_ = bf16[512,512]{1,0:T(8,128)(2,1)} custom-call(s32[3]{0:T(128)S(1)} %pad_add_fusion.pos, bf16[256,256]{1,0:T(8,128)(2,1)S(1)} %shard_map.70.refs_0_, bf16[256,256]{1,0:T(8,128)(2,1)S(1)} %collective-permute-done.32.refs_1_, bf16[256,128]{1,0:T(8,128)(2,1)S(1)} %shard_map.64.refs_2_, bf16[256,128]{1,0:T(8,128)(2,1)S(1)} %shard_map.66.refs_3_), custom_call_target="tpu_custom_call" | custom-call | bytes 917504 | tf_op jit(solution)/shard_map/pallas_call | solution.py:34
  85.2 2.1 %collective-permute-done.24.refs_1_ = bf16[256,128]{1,0:T(8,128)(2,1)S(1)} collective-permute-done((bf16[256,128]{1,0:T(8,128)(2,1)S(1)}, bf16[256,128]{1,0:T(8,128)(2,1)S(1)}, u32[]{:S(2)}, u32[]{:S(2)}) %collective-permute-start.24) | collective-permute-done | bytes 65568 | tf_op jit(solution)/shard_map/ppermute | solution.py:421
  87.3 1.2 %shard_map.72 = bf16[512,512]{1,0:T(8,128)(2,1)} custom-call(s32[3]{0:T(128)S(1)} %pad_add_fusion.pos, bf16[256,128]{1,0:T(8,128)(2,1)S(1)} %collective-permute-done.19.refs_0_, bf16[256,128]{1,0:T(8,128)(2,1)S(1)} %collective-permute-done.24.refs_1_, bf16[512,512]{1,0:T(8,128)(2,1)} %shard_map.71.refs_2_), custom_call_target="tpu_custom_call", output_to_operand_aliasing={{}: (3, {})} | custom-call | bytes 1179648 | tf_op jit(solution)/shard_map/pallas_call | solution.py:34
  (41 shorter events, 4.0 us)
Async XLA Ops:
  0.0 0.7 copy-start.1
  0.0 5.4 %collective-permute-start.8 = (bf16[192,2048]{1,0:T(8,128)(2,1)}, bf16[192,2048]{1,0:T(8,128)(2,1)S(1)}, u32[]{:S(2)}, u32[]{:S(2)}) collective-permute-start(bf16[192,2048]{1,0:T(8,128)(2,1)} %rows.2), channel_id=1, source_target_pairs={{0,1},{1,0},{2,3},{3,2},{4,5},{5,4},{6,7},{7,6},{8,9},{9,8},{10,11... | collective-permute-start | bytes 2359304 | tf_op jit(solution)/shard_map/ppermute | solution.py:278
  0.5 33.8 %collective-permute-start.1 = (bf16[192,2048]{1,0:T(8,128)(2,1)}, bf16[192,2048]{1,0:T(8,128)(2,1)S(1)}, u32[]{:S(2)}, u32[]{:S(2)}) collective-permute-start(bf16[192,2048]{1,0:T(8,128)(2,1)} %rows.3), channel_id=1, source_target_pairs={{0,1},{1,0},{2,3},{3,2},{4,5},{5,4},{6,7},{7,6},{8,9},{9,8},{10,11... | collective-permute-start | bytes 2359304 | tf_op jit(solution)/shard_map/ppermute | solution.py:280
  0.7 3.1 %collective-permute-start = (s32[1,192]{1,0:T(1,128)S(1)}, s32[1,192]{1,0:T(1,128)S(1)}, u32[]{:S(2)}, u32[]{:S(2)}) collective-permute-start(s32[1,192]{1,0:T(1,128)S(1)} %bitcast.7), channel_id=1, source_target_pairs={{0,1},{1,0},{2,3},{3,2},{4,5},{5,4},{6,7},{7,6},{8,9},{9,8},{10,11... | collective-permute-start | bytes 2312 | tf_op jit(solution)/shard_map/ppermute | solution.py:279
  6.7 9.2 %collective-permute-start.9 = (bf16[120,1024]{1,0:T(8,128)(2,1)S(1)}, bf16[120,1024]{1,0:T(8,128)(2,1)S(1)}, u32[]{:S(2)}, u32[]{:S(2)}) collective-permute-start(bf16[120,1024]{1,0:T(8,128)(2,1)S(1)} %get-tuple-element.53), channel_id=1, source_target_pairs={{0,2},{1,3},{2,0},{3,1},{16,18},{17,19},{18,16},{19,17},{4,6},{5,7... | collective-permute-start | bytes 737288 | tf_op jit(solution)/shard_map/ppermute | solution.py:335
  9.7 9.1 %collective-permute-start.10 = (bf16[120,1024]{1,0:T(8,128)(2,1)S(1)}, bf16[120,1024]{1,0:T(8,128)(2,1)S(1)}, u32[]{:S(2)}, u32[]{:S(2)}) collective-permute-start(bf16[120,1024]{1,0:T(8,128)(2,1)S(1)} %get-tuple-element.54), channel_id=1, source_target_pairs={{0,16},{1,17},{2,18},{3,19},{16,0},{17,1},{18,2},{19,3},{4,20},{5,... | collective-permute-start | bytes 737288 | tf_op jit(solution)/shard_map/ppermute | solution.py:335
  11.2 11.3 %collective-permute-start.11 = (bf16[120,1024]{1,0:T(8,128)(2,1)S(1)}, bf16[120,1024]{1,0:T(8,128)(2,1)S(1)}, u32[]{:S(2)}, u32[]{:S(2)}) collective-permute-start(bf16[120,1024]{1,0:T(8,128)(2,1)S(1)} %get-tuple-element.55), channel_id=1, source_target_pairs={{0,18},{1,19},{2,16},{3,17},{16,2},{17,3},{18,0},{19,1},{4,22},{5,... | collective-permute-start | bytes 737288 | tf_op jit(solution)/shard_map/ppermute | solution.py:335
  12.8 12.0 %collective-permute-start.25 = (bf16[256,256]{1,0:T(8,128)(2,1)S(1)}, bf16[256,256]{1,0:T(8,128)(2,1)S(1)}, u32[]{:S(2)}, u32[]{:S(2)}) collective-permute-start(bf16[256,256]{1,0:T(8,128)(2,1)S(1)} %get-tuple-element.69.refs_0_), channel_id=1, source_target_pairs={{0,4},{4,0},{8,12},{12,8},{1,5},{5,1},{9,13},{13,9},{2,6},{6,2},{1... | collective-permute-start | bytes 393224 | tf_op jit(solution)/shard_map/ppermute | solution.py:300
  15.9 14.1 %collective-permute-start.26 = (bf16[256,256]{1,0:T(8,128)(2,1)S(1)}, bf16[256,256]{1,0:T(8,128)(2,1)S(1)}, u32[]{:S(2)}, u32[]{:S(2)}) collective-permute-start(bf16[256,256]{1,0:T(8,128)(2,1)S(1)} %get-tuple-element.69.refs_0_), channel_id=1, source_target_pairs={{0,8},{4,12},{8,0},{12,4},{1,9},{5,13},{9,1},{13,5},{2,10},{6,14},... | collective-permute-start | bytes 393224 | tf_op jit(solution)/shard_map/ppermute | solution.py:300
  18.7 13.0 %collective-permute-start.27 = (bf16[256,256]{1,0:T(8,128)(2,1)S(1)}, bf16[256,256]{1,0:T(8,128)(2,1)S(1)}, u32[]{:S(2)}, u32[]{:S(2)}) collective-permute-start(bf16[256,256]{1,0:T(8,128)(2,1)S(1)} %get-tuple-element.69.refs_0_), channel_id=1, source_target_pairs={{0,12},{4,8},{8,4},{12,0},{1,13},{5,9},{9,5},{13,1},{2,14},{6,10},... | collective-permute-start | bytes 393224 | tf_op jit(solution)/shard_map/ppermute | solution.py:300
  22.4 14.3 %collective-permute-start.12 = (bf16[256,256]{1,0:T(8,128)(2,1)S(1)}, bf16[256,256]{1,0:T(8,128)(2,1)S(1)}, u32[]{:S(2)}, u32[]{:S(2)}) collective-permute-start(bf16[256,256]{1,0:T(8,128)(2,1)S(1)} %get-tuple-element.56.refs_0_), channel_id=1, source_target_pairs={{0,4},{4,0},{8,12},{12,8},{1,5},{5,1},{9,13},{13,9},{2,6},{6,2},{1... | collective-permute-start | bytes 393224 | tf_op jit(solution)/shard_map/ppermute | solution.py:300
  24.8 9.5 %copy-start = (bf16[192,2048]{1,0:T(8,128)(2,1)S(1)}, bf16[192,2048]{1,0:T(8,128)(2,1)}, u32[]{:S(2)}) copy-start(bf16[192,2048]{1,0:T(8,128)(2,1)} %rows.3) | copy-start | bytes 2359300
  24.8 15.0 %collective-permute-start.13 = (bf16[256,256]{1,0:T(8,128)(2,1)S(1)}, bf16[256,256]{1,0:T(8,128)(2,1)S(1)}, u32[]{:S(2)}, u32[]{:S(2)}) collective-permute-start(bf16[256,256]{1,0:T(8,128)(2,1)S(1)} %get-tuple-element.56.refs_0_), channel_id=1, source_target_pairs={{0,8},{4,12},{8,0},{12,4},{1,9},{5,13},{9,1},{13,5},{2,10},{6,14},... | collective-permute-start | bytes 393224 | tf_op jit(solution)/shard_map/ppermute | solution.py:300
  30.0 12.4 %collective-permute-start.14 = (bf16[256,256]{1,0:T(8,128)(2,1)S(1)}, bf16[256,256]{1,0:T(8,128)(2,1)S(1)}, u32[]{:S(2)}, u32[]{:S(2)}) collective-permute-start(bf16[256,256]{1,0:T(8,128)(2,1)S(1)} %get-tuple-element.56.refs_0_), channel_id=1, source_target_pairs={{0,12},{4,8},{8,4},{12,0},{1,13},{5,9},{9,5},{13,1},{2,14},{6,10},... | collective-permute-start | bytes 393224 | tf_op jit(solution)/shard_map/ppermute | solution.py:300
  32.7 21.1 %collective-permute-start.28 = (bf16[512,256]{1,0:T(8,128)(2,1)S(1)}, bf16[512,256]{1,0:T(8,128)(2,1)S(1)}, u32[]{:S(2)}, u32[]{:S(2)}) collective-permute-start(bf16[512,256]{1,0:T(8,128)(2,1)S(1)} %get-tuple-element.71), channel_id=1, source_target_pairs={{0,16},{16,0},{1,17},{17,1},{2,18},{18,2},{3,19},{19,3},{4,20},{20... | collective-permute-start | bytes 786440 | tf_op jit(solution)/shard_map/ppermute | solution.py:371
  35.6 7.3 %collective-permute-start.2 = (bf16[120,512]{1,0:T(8,128)(2,1)S(1)}, bf16[120,512]{1,0:T(8,128)(2,1)S(1)}, u32[]{:S(2)}, u32[]{:S(2)}) collective-permute-start(bf16[120,512]{1,0:T(8,128)(2,1)S(1)} %get-tuple-element.44), channel_id=1, source_target_pairs={{0,2},{1,3},{2,0},{3,1},{16,18},{17,19},{18,16},{19,17},{4,6},{5,7... | collective-permute-start | bytes 368648 | tf_op jit(solution)/shard_map/ppermute | solution.py:335
  36.8 7.0 %collective-permute-start.3 = (bf16[120,512]{1,0:T(8,128)(2,1)S(1)}, bf16[120,512]{1,0:T(8,128)(2,1)S(1)}, u32[]{:S(2)}, u32[]{:S(2)}) collective-permute-start(bf16[120,512]{1,0:T(8,128)(2,1)S(1)} %get-tuple-element.45), channel_id=1, source_target_pairs={{0,16},{1,17},{2,18},{3,19},{16,0},{17,1},{18,2},{19,3},{4,20},{5,... | collective-permute-start | bytes 368648 | tf_op jit(solution)/shard_map/ppermute | solution.py:335
  39.9 8.1 %collective-permute-start.4 = (bf16[120,512]{1,0:T(8,128)(2,1)S(1)}, bf16[120,512]{1,0:T(8,128)(2,1)S(1)}, u32[]{:S(2)}, u32[]{:S(2)}) collective-permute-start(bf16[120,512]{1,0:T(8,128)(2,1)S(1)} %get-tuple-element.46), channel_id=1, source_target_pairs={{0,18},{1,19},{2,16},{3,17},{16,2},{17,3},{18,0},{19,1},{4,22},{5,... | collective-permute-start | bytes 368648 | tf_op jit(solution)/shard_map/ppermute | solution.py:335
  42.4 6.9 %collective-permute-start.5 = (bf16[120,512]{1,0:T(8,128)(2,1)S(1)}, bf16[120,512]{1,0:T(8,128)(2,1)S(1)}, u32[]{:S(2)}, u32[]{:S(2)}) collective-permute-start(bf16[120,512]{1,0:T(8,128)(2,1)S(1)} %get-tuple-element.48), channel_id=1, source_target_pairs={{0,2},{1,3},{2,0},{3,1},{16,18},{17,19},{18,16},{19,17},{4,6},{5,7... | collective-permute-start | bytes 368648 | tf_op jit(solution)/shard_map/ppermute | solution.py:335
  42.9 7.9 %collective-permute-start.6 = (bf16[120,512]{1,0:T(8,128)(2,1)S(1)}, bf16[120,512]{1,0:T(8,128)(2,1)S(1)}, u32[]{:S(2)}, u32[]{:S(2)}) collective-permute-start(bf16[120,512]{1,0:T(8,128)(2,1)S(1)} %get-tuple-element.49), channel_id=1, source_target_pairs={{0,16},{1,17},{2,18},{3,19},{16,0},{17,1},{18,2},{19,3},{4,20},{5,... | collective-permute-start | bytes 368648 | tf_op jit(solution)/shard_map/ppermute | solution.py:335
  43.8 9.3 %collective-permute-start.7 = (bf16[120,512]{1,0:T(8,128)(2,1)S(1)}, bf16[120,512]{1,0:T(8,128)(2,1)S(1)}, u32[]{:S(2)}, u32[]{:S(2)}) collective-permute-start(bf16[120,512]{1,0:T(8,128)(2,1)S(1)} %get-tuple-element.50), channel_id=1, source_target_pairs={{0,18},{1,19},{2,16},{3,17},{16,2},{17,3},{18,0},{19,1},{4,22},{5,... | collective-permute-start | bytes 368648 | tf_op jit(solution)/shard_map/ppermute | solution.py:335
  48.0 15.6 %collective-permute-start.15 = (bf16[512,128]{1,0:T(8,128)(2,1)S(1)}, bf16[512,128]{1,0:T(8,128)(2,1)S(1)}, u32[]{:S(2)}, u32[]{:S(2)}) collective-permute-start(bf16[512,128]{1,0:T(8,128)(2,1)S(1)} %get-tuple-element.58), channel_id=1, source_target_pairs={{0,16},{16,0},{1,17},{17,1},{2,18},{18,2},{3,19},{19,3},{4,20},{20... | collective-permute-start | bytes 393224 | tf_op jit(solution)/shard_map/ppermute | solution.py:371
  49.3 17.6 %collective-permute-start.20 = (bf16[512,128]{1,0:T(8,128)(2,1)S(1)}, bf16[512,128]{1,0:T(8,128)(2,1)S(1)}, u32[]{:S(2)}, u32[]{:S(2)}) collective-permute-start(bf16[512,128]{1,0:T(8,128)(2,1)S(1)} %get-tuple-element.64), channel_id=1, source_target_pairs={{0,16},{16,0},{1,17},{17,1},{2,18},{18,2},{3,19},{19,3},{4,20},{20... | collective-permute-start | bytes 393224 | tf_op jit(solution)/shard_map/ppermute | solution.py:371
  54.7 14.3 %collective-permute-start.29 = (bf16[256,256]{1,0:T(8,128)(2,1)S(1)}, bf16[256,256]{1,0:T(8,128)(2,1)S(1)}, u32[]{:S(2)}, u32[]{:S(2)}) collective-permute-start(bf16[256,256]{1,0:T(8,128)(2,1)S(1)} %get-tuple-element.74), channel_id=1, source_target_pairs={{0,12},{4,8},{8,4},{12,0},{1,13},{5,9},{9,5},{13,1},{2,14},{6,10},... | collective-permute-start | bytes 393224 | tf_op jit(solution)/shard_map/ppermute | solution.py:405
  56.6 16.9 %collective-permute-start.30 = (bf16[256,256]{1,0:T(8,128)(2,1)S(1)}, bf16[256,256]{1,0:T(8,128)(2,1)S(1)}, u32[]{:S(2)}, u32[]{:S(2)}) collective-permute-start(bf16[256,256]{1,0:T(8,128)(2,1)S(1)} %get-tuple-element.75), channel_id=1, source_target_pairs={{0,4},{4,0},{8,12},{12,8},{1,5},{5,1},{9,13},{13,9},{2,6},{6,2},{1... | collective-permute-start | bytes 393224 | tf_op jit(solution)/shard_map/ppermute | solution.py:405
  63.4 12.0 %collective-permute-start.31 = (bf16[256,256]{1,0:T(8,128)(2,1)S(1)}, bf16[256,256]{1,0:T(8,128)(2,1)S(1)}, u32[]{:S(2)}, u32[]{:S(2)}) collective-permute-start(bf16[256,256]{1,0:T(8,128)(2,1)S(1)} %get-tuple-element.76), channel_id=1, source_target_pairs={{0,8},{4,12},{8,0},{12,4},{1,9},{5,13},{9,1},{13,5},{2,10},{6,14},... | collective-permute-start | bytes 393224 | tf_op jit(solution)/shard_map/ppermute | solution.py:405
  64.6 11.4 %collective-permute-start.16 = (bf16[256,128]{1,0:T(8,128)(2,1)S(1)}, bf16[256,128]{1,0:T(8,128)(2,1)S(1)}, u32[]{:S(2)}, u32[]{:S(2)}) collective-permute-start(bf16[256,128]{1,0:T(8,128)(2,1)S(1)} %get-tuple-element.60), channel_id=1, source_target_pairs={{0,12},{4,8},{8,4},{12,0},{1,13},{5,9},{9,5},{13,1},{2,14},{6,10},... | collective-permute-start | bytes 196616 | tf_op jit(solution)/shard_map/ppermute | solution.py:405
  66.9 11.7 %collective-permute-start.17 = (bf16[256,128]{1,0:T(8,128)(2,1)S(1)}, bf16[256,128]{1,0:T(8,128)(2,1)S(1)}, u32[]{:S(2)}, u32[]{:S(2)}) collective-permute-start(bf16[256,128]{1,0:T(8,128)(2,1)S(1)} %get-tuple-element.61), channel_id=1, source_target_pairs={{0,4},{4,0},{8,12},{12,8},{1,5},{5,1},{9,13},{13,9},{2,6},{6,2},{1... | collective-permute-start | bytes 196616 | tf_op jit(solution)/shard_map/ppermute | solution.py:405
  69.1 11.2 %collective-permute-start.18 = (bf16[256,128]{1,0:T(8,128)(2,1)S(1)}, bf16[256,128]{1,0:T(8,128)(2,1)S(1)}, u32[]{:S(2)}, u32[]{:S(2)}) collective-permute-start(bf16[256,128]{1,0:T(8,128)(2,1)S(1)} %get-tuple-element.62), channel_id=1, source_target_pairs={{0,8},{4,12},{8,0},{12,4},{1,9},{5,13},{9,1},{13,5},{2,10},{6,14},... | collective-permute-start | bytes 196616 | tf_op jit(solution)/shard_map/ppermute | solution.py:405
  73.4 8.9 %collective-permute-start.21 = (bf16[256,128]{1,0:T(8,128)(2,1)S(1)}, bf16[256,128]{1,0:T(8,128)(2,1)S(1)}, u32[]{:S(2)}, u32[]{:S(2)}) collective-permute-start(bf16[256,128]{1,0:T(8,128)(2,1)S(1)} %get-tuple-element.66), channel_id=1, source_target_pairs={{0,12},{4,8},{8,4},{12,0},{1,13},{5,9},{9,5},{13,1},{2,14},{6,10},... | collective-permute-start | bytes 196616 | tf_op jit(solution)/shard_map/ppermute | solution.py:405
  75.4 7.0 %collective-permute-start.22 = (bf16[256,128]{1,0:T(8,128)(2,1)S(1)}, bf16[256,128]{1,0:T(8,128)(2,1)S(1)}, u32[]{:S(2)}, u32[]{:S(2)}) collective-permute-start(bf16[256,128]{1,0:T(8,128)(2,1)S(1)} %get-tuple-element.67), channel_id=1, source_target_pairs={{0,4},{4,0},{8,12},{12,8},{1,5},{5,1},{9,13},{13,9},{2,6},{6,2},{1... | collective-permute-start | bytes 196616 | tf_op jit(solution)/shard_map/ppermute | solution.py:405
  76.0 6.4 %collective-permute-start.23 = (bf16[256,128]{1,0:T(8,128)(2,1)S(1)}, bf16[256,128]{1,0:T(8,128)(2,1)S(1)}, u32[]{:S(2)}, u32[]{:S(2)}) collective-permute-start(bf16[256,128]{1,0:T(8,128)(2,1)S(1)} %get-tuple-element.68), channel_id=1, source_target_pairs={{0,8},{4,12},{8,0},{12,4},{1,9},{5,13},{9,1},{13,5},{2,10},{6,14},... | collective-permute-start | bytes 196616 | tf_op jit(solution)/shard_map/ppermute | solution.py:405
  78.7 5.1 %collective-permute-start.32 = (bf16[256,256]{1,0:T(8,128)(2,1)S(1)}, bf16[256,256]{1,0:T(8,128)(2,1)S(1)}, u32[]{:S(2)}, u32[]{:S(2)}) collective-permute-start(bf16[256,256]{1,0:T(8,128)(2,1)S(1)} %shard_map.70.refs_0_), channel_id=1, source_target_pairs={{0,16},{16,0},{1,17},{17,1},{2,18},{18,2},{3,19},{19,3},{4,20},{20... | collective-permute-start | bytes 393224 | tf_op jit(solution)/shard_map/ppermute | solution.py:421
  80.9 4.3 %collective-permute-start.19 = (bf16[256,128]{1,0:T(8,128)(2,1)S(1)}, bf16[256,128]{1,0:T(8,128)(2,1)S(1)}, u32[]{:S(2)}, u32[]{:S(2)}) collective-permute-start(bf16[256,128]{1,0:T(8,128)(2,1)S(1)} %shard_map.64.refs_2_), channel_id=1, source_target_pairs={{0,16},{16,0},{1,17},{17,1},{2,18},{18,2},{3,19},{19,3},{4,20},{20... | collective-permute-start | bytes 196616 | tf_op jit(solution)/shard_map/ppermute | solution.py:421
  83.0 4.3 %collective-permute-start.24 = (bf16[256,128]{1,0:T(8,128)(2,1)S(1)}, bf16[256,128]{1,0:T(8,128)(2,1)S(1)}, u32[]{:S(2)}, u32[]{:S(2)}) collective-permute-start(bf16[256,128]{1,0:T(8,128)(2,1)S(1)} %shard_map.66.refs_3_), channel_id=1, source_target_pairs={{0,16},{16,0},{1,17},{17,1},{2,18},{18,2},{3,19},{19,3},{4,20},{20... | collective-permute-start | bytes 196616 | tf_op jit(solution)/shard_map/ppermute | solution.py:421

commit v8 on v7

--- a/solution.py
+++ b/solution.py
@@ -68,22 +68,27 @@
     return jax.ShapeDtypeStruct((rows, cols), dtype)
 
 
-def dequant_body(pos, codes, scales, *refs):
-    outs, (raw, steps, wide, sems) = refs[:-4], refs[-4:]
+def prep_body(dims, stride, pos, ids, ids_pair, rows, codes, scales, *refs):
+    picks, near, outs = refs[:2], refs[2], refs[3:-4]
+    raw, steps, wide, sems = refs[-4:]
     mine, ff = raw.shape
     at = pl.multiple_of(pos[0] * mine, 16)
-    first = pltpu.make_async_copy(codes.at[pl.ds(at, mine), :], raw, sems.at[0])
-    second = pltpu.make_async_copy(scales, steps, sems.at[1])
-    first.start()
-    second.start()
-    second.wait()
+    moves = [
+        pltpu.make_async_copy(scales, steps, sems.at[0]),
+        pltpu.make_async_copy(codes.at[pl.ds(at, mine), :], raw, sems.at[1]),
+        pltpu.make_async_copy(rows, near, sems.at[2]),
+    ]
+    for move in moves:
+        move.start()
+    select_body(dims, stride, pos, ids, ids_pair, *picks)
+    moves[0].wait()
     wide[...] = steps[...].astype(F32)
     used = max(1, mine // QB)
     begin = lax.div(pos[0] * mine, jnp.int32(QB))
     if used % 8 == 0:
         begin = pl.multiple_of(begin, 8)
     factors = wide[pl.ds(begin, used), :]
-    first.wait()
+    moves[1].wait()
     blocks = raw[...].astype(F32).reshape(used, mine // used, ff)
     kept = (blocks * factors[:, None, :]).astype(BF16).reshape(mine, ff)
     begin = 0
@@ -91,6 +96,7 @@
         end = begin + out.shape[1]
         out[...] = kept[:, begin:end]
         begin = end
+    moves[2].wait()
 
 
 def select_body(dims, stride, pos, ids, ids_pair, *picks):
@@ -141,14 +147,6 @@
                     out[:, b * width : (b + 1) * width] = got[k * stride : k * stride + rows]
 
 
-def choose_body(dims, stride, pos, ids, ids_pair, rows, *refs):
-    picks, near, sem = refs[:2], refs[2], refs[3]
-    move = pltpu.make_async_copy(rows, near, sem)
-    move.start()
-    select_body(dims, stride, pos, ids, ids_pair, *picks)
-    move.wait()
-
-
 def route_body(dims, stride, columns, pos, pick, pick_pair, rows, rows_pair, *outs):
     place_rows(dims, stride, columns, pos, (pick, pick_pair), (rows, rows_pair), outs)
 
@@ -175,9 +173,14 @@
     out[...] = jnp.transpose(held[...])
 
 
-def up_body(dims, pos, rows, *refs):
-    _, nodes, _ = dims
-    weights, outs, held = refs[:nodes], refs[nodes:-1], refs[-1]
+def up_body(dims, stride, given, pos, *refs):
+    nodes = dims[1]
+    pieces, weights, held = refs[:given], refs[given : given + nodes], refs[-1]
+    outs = refs[given + nodes : -1]
+    rows = pieces[0]
+    if given > 1:
+        rows, outs = outs[0], outs[1:]
+        join_body(dims, stride, pos, *pieces, rows)
     mine = weights[0].shape[0]
     for s in range(nodes):
         at = pl.multiple_of(traced_origin(pos[1], s, nodes) * mine, 16)
@@ -279,19 +282,22 @@
     chosen_pair = lax.ppermute(chosen, "local", swap)
     cotangent_pair = lax.ppermute(cotangent, "local", swap)
 
-    weights = call(
-        dequant_body,
-        [shape(mine, w, BF16) for w in gathered],
+    far = [pltpu.with_memory_space_constraint(a, pltpu.HBM) for a in (tokens, w1_codes[0], w1_scales[0])]
+    near = [shape(pairs * stride, count, BF16)] * 2 + [shape(count, features, BF16)]
+    first, second, tokens, *weights = call(
+        functools.partial(prep_body, dims, stride),
+        near + [shape(mine, w, BF16) for w in gathered],
         pos,
-        [pltpu.with_memory_space_constraint(a[0], pltpu.HBM) for a in (w1_codes, w1_scales)],
+        [chosen, chosen_pair] + far,
         [
             pltpu.VMEM((mine, hidden), BF16),
             pltpu.VMEM((shard // QB, hidden), BF16),
             pltpu.VMEM((shard // QB, hidden), F32),
-            pltpu.SemaphoreType.DMA((2,)),
+            pltpu.SemaphoreType.DMA((3,)),
         ],
-        space=pltpu.HBM,
+        space=[pltpu.VMEM] * 2 + [pltpu.HBM] * 3,
     )
+    picks = [first, second]
     order = node_order(nodes)
     held = []
     for chunk in weights:
@@ -299,15 +305,6 @@
         for s in order:
             got[s] = lax.ppermute(chunk, "node", [(a, mate(a, s, nodes)) for a in range(nodes)])
         held.append([got[s] for s in range(nodes)])
-
-    *picks, tokens = call(
-        functools.partial(choose_body, dims, stride),
-        [shape(pairs * stride, count, BF16)] * 2 + [shape(count, features, BF16)],
-        pos,
-        [chosen, chosen_pair, pltpu.with_memory_space_constraint(tokens, pltpu.HBM)],
-        [pltpu.SemaphoreType.DMA],
-        space=[pltpu.VMEM, pltpu.VMEM, pltpu.HBM],
-    )
 
     def route(columns, rows, rows_pair):
         pieces = call(
@@ -335,12 +332,7 @@
             moved[at] = lax.ppermute(pieces[at], ("dp", "local"), links)
         return moved
 
-    (rows_x,) = call(
-        functools.partial(join_body, dims, stride),
-        [shape(everyone, part, BF16)],
-        pos,
-        exchange(pieces_x),
-    )
+    rows_x = exchange(pieces_x)
     turned = []
     for h, pieces in enumerate(pieces_y):
         cols = part // len(pieces_y)
@@ -356,14 +348,17 @@
     groups = []
     for i, split in enumerate(SPLITS):
         widths = [unit * share for share in split]
+        joined = [shape(everyone, part, BF16)] if len(rows_x) > 1 else []
         parts = call(
-            functools.partial(up_body, dims),
-            [shape(everyone, w, kind) for w in widths for kind in (F32, BF16)],
+            functools.partial(up_body, dims, stride, len(rows_x)),
+            joined + [shape(everyone, w, kind) for w in widths for kind in (F32, BF16)],
             pos,
-            [rows_x] + held[i],
+            list(rows_x) + held[i],
             [pltpu.VMEM((part, gathered[i]), BF16)],
             flops=2 * everyone * part * gathered[i],
         )
+        if joined:
+            rows_x, parts = parts[:1], parts[1:]
         groups += list(zip(widths, parts[::2], parts[1::2]))
     acts = []
     for wide, kept, sent in groups:

time: 88.8 us -> 82.6 us (0.930)
  starting transfers between devices: 55.7 us -> 47.8 us
  waiting for transfers between devices: 14.1 us -> 17.9 us
  Pallas kernels: 18.2 us -> 16.3 us
    ppermute x9, starting transfers between devices: 20.3 us -> 15.3 us  [on_device(): moved = lax.ppermute(term, 'node', links)]
    ppermute x9, waiting for transfers between devices: 0.17 us -> 4.12 us  [on_device(): moved = lax.ppermute(term, 'node', links)]
    ppermute x6, waiting for transfers between devices: 5.11 us -> 7.13 us  [on_device(): lax.ppermute(chunk, 'node', [(a, mate(a, s, nodes)) for a in range(nodes)])]
    pallas_call x18 -> x16, Pallas kernels: 18.2 us -> 16.3 us  [call(): pl.pallas_call(body, out_shape=outs, in_specs=[pl.BlockSpec(memory_space=...]
    ppermute x6, starting transfers between devices: 14.3 us -> 12.4 us  [on_device(): lax.ppermute(chunk, 'node', [(a, mate(a, s, nodes)) for a in range(nodes)])]
    ppermute x9, waiting for transfers between devices: 4.14 us -> 2.33 us  [exchange(): moved[at] = lax.ppermute(pieces[at], ('dp', 'local'), links)]
  transfers between devices with their start and end apart: 33 -> 33, of which waited for: 10 -> 9; matrix products, arithmetic and copies ran while one was open for 0% -> 0% of each run, Pallas kernels for 19% -> 18%
where the time goes in v8:
time: 82.6 us; the launch traced here: 82.3 us
  starting transfers between devices  47.8 us (58%)
  waiting for transfers between devices  17.9 us (22%)
  Pallas kernels  16.3 us (20%)
    pallas_call x16, Pallas kernels, call(): pl.pallas_call(body, out_shape=outs, in_specs=[pl.BlockSpec(memory_space=...  16.3 us
    ppermute x9, starting transfers between devices, on_device(): moved = lax.ppermute(term, 'node', links)  15.3 us
    ppermute x6, starting transfers between devices, on_device(): lax.ppermute(chunk, 'node', [(a, mate(a, s, nodes)) for a in range(nodes)])  12.4 us
    ppermute x9, starting transfers between devices, exchange(): moved[at] = lax.ppermute(pieces[at], ('dp', 'local'), links)  12 us
    ppermute x6, waiting for transfers between devices, on_device(): lax.ppermute(chunk, 'node', [(a, mate(a, s, nodes)) for a in range(nodes)])  7.13 us
    ppermute x9, waiting for transfers between devices, on_device(): moved = lax.ppermute(term, 'node', links)  4.12 us
    ppermute x3, starting transfers between devices, on_device(): acts.append([kept, lax.ppermute(sent, 'dp', [(0, 1), (1, 0)])])  3.65 us
    ppermute x3, starting transfers between devices, on_device(): finished.append(lax.ppermute(summed, 'dp', links))  3.37 us
  transfers between devices with their start and end apart: 33, of which 9 were waited for; matrix products, arithmetic and copies ran while one was open for 0% of the time, Pallas kernels for 18%

profile of v8, /device:TPU:0, one launch (start us, length us, event | category | flops | bytes accessed | tf_op | source)
XLA Modules:
  0.0 82.3 jit_solution(4342039467160621574)
XLA Ops:
  1.2 2.5 %collective-permute-done.ids_pair = s32[1,192]{1,0:T(1,128)S(1)} collective-permute-done((s32[1,192]{1,0:T(1,128)S(1)}, s32[1,192]{1,0:T(1,128)S(1)}, u32[]{:S(2)}, u32[]{:S(2)}) %collective-permute-start) | collective-permute-done | bytes 800 | tf_op jit(solution)/shard_map/ppermute | solution.py:282
  3.7 1.8 %shard_map.55 = (bf16[256,192]{1,0:T(8,128)(2,1)S(1)}, bf16[256,192]{1,0:T(8,128)(2,1)S(1)}, bf16[192,2048]{1,0:T(8,128)(2,1)S(1)}, bf16[256,256]{1,0:T(8,128)(2,1)S(1)}, bf16[256,256]{1,0:T(8,128)(2,1)S(1)}) custom-call(s32[3]{0:T(128)S(1)} %pad_add_fusion.pos, s32[1,192]{1,0:T(1,128)S(1)} %bitcast.8, s32[1,192]{1,0:T(1,128)S(1)} %collective-permute-done.ids_pair, ...), custom_call_target="tpu_custom_call" | custom-call | bytes 2573824 | tf_op jit(solution)/shard_map/pallas_call | solution.py:34
  5.6 3.0 %collective-permute-start.12 = (bf16[256,256]{1,0:T(8,128)(2,1)S(1)}, bf16[256,256]{1,0:T(8,128)(2,1)S(1)}, u32[]{:S(2)}, u32[]{:S(2)}) collective-permute-start(bf16[256,256]{1,0:T(8,128)(2,1)S(1)} %get-tuple-element.57.refs_4_), channel_id=1, source_target_pairs={{0,4},{4,0},{8,12},{12,8},{1,5},{5,1},{9,13},{13,9},{2,6},{6,2},{1... | collective-permute-start | bytes 393224 | tf_op jit(solution)/shard_map/ppermute | solution.py:306
  8.6 2.6 %collective-permute-start.13 = (bf16[256,256]{1,0:T(8,128)(2,1)S(1)}, bf16[256,256]{1,0:T(8,128)(2,1)S(1)}, u32[]{:S(2)}, u32[]{:S(2)}) collective-permute-start(bf16[256,256]{1,0:T(8,128)(2,1)S(1)} %get-tuple-element.57.refs_4_), channel_id=1, source_target_pairs={{0,8},{4,12},{8,0},{12,4},{1,9},{5,13},{9,1},{13,5},{2,10},{6,14},... | collective-permute-start | bytes 393224 | tf_op jit(solution)/shard_map/ppermute | solution.py:306
  11.1 1.3 %shard_map.59 = (bf16[120,1024]{1,0:T(8,128)(2,1)S(1)}, bf16[120,1024]{1,0:T(8,128)(2,1)S(1)}, bf16[120,1024]{1,0:T(8,128)(2,1)S(1)}, bf16[120,1024]{1,0:T(8,128)(2,1)S(1)}) custom-call(s32[3]{0:T(128)S(1)} %pad_add_fusion.pos, bf16[256,192]{1,0:T(8,128)(2,1)S(1)} %get-tuple-element.42.pick, bf16[256,192]{1,0:T(8,128)(2,1)S(1)} %get-tuple-element.43.pick_pair, ...), custom_call_target="tpu_custom_call" | custom-call | flops 402653184 | bytes 2752512 | tf_op jit(solution)/shard_map/pallas_call | solution.py:34
  12.4 1.6 %collective-permute-start.10 = (bf16[120,1024]{1,0:T(8,128)(2,1)S(1)}, bf16[120,1024]{1,0:T(8,128)(2,1)S(1)}, u32[]{:S(2)}, u32[]{:S(2)}) collective-permute-start(bf16[120,1024]{1,0:T(8,128)(2,1)S(1)} %get-tuple-element.55), channel_id=1, source_target_pairs={{0,16},{1,17},{2,18},{3,19},{16,0},{17,1},{18,2},{19,3},{4,20},{5,... | collective-permute-start | bytes 737288 | tf_op jit(solution)/shard_map/ppermute | solution.py:332
  14.0 1.5 %collective-permute-start.11 = (bf16[120,1024]{1,0:T(8,128)(2,1)S(1)}, bf16[120,1024]{1,0:T(8,128)(2,1)S(1)}, u32[]{:S(2)}, u32[]{:S(2)}) collective-permute-start(bf16[120,1024]{1,0:T(8,128)(2,1)S(1)} %get-tuple-element.56), channel_id=1, source_target_pairs={{0,18},{1,19},{2,16},{3,17},{16,2},{17,3},{18,0},{19,1},{4,22},{5,... | collective-permute-start | bytes 737288 | tf_op jit(solution)/shard_map/ppermute | solution.py:332
  15.5 0.9 %collective-permute-start.9 = (bf16[120,1024]{1,0:T(8,128)(2,1)S(1)}, bf16[120,1024]{1,0:T(8,128)(2,1)S(1)}, u32[]{:S(2)}, u32[]{:S(2)}) collective-permute-start(bf16[120,1024]{1,0:T(8,128)(2,1)S(1)} %get-tuple-element.54), channel_id=1, source_target_pairs={{0,2},{1,3},{2,0},{3,1},{16,18},{17,19},{18,16},{19,17},{4,6},{5,7... | collective-permute-start | bytes 737288 | tf_op jit(solution)/shard_map/ppermute | solution.py:332
  16.4 1.2 %collective-permute-done.13.refs_6_ = bf16[256,256]{1,0:T(8,128)(2,1)S(1)} collective-permute-done((bf16[256,256]{1,0:T(8,128)(2,1)S(1)}, bf16[256,256]{1,0:T(8,128)(2,1)S(1)}, u32[]{:S(2)}, u32[]{:S(2)}) %collective-permute-start.13) | collective-permute-done | bytes 131104 | tf_op jit(solution)/shard_map/ppermute | solution.py:306
  17.6 2.5 %collective-permute-start.14 = (bf16[256,256]{1,0:T(8,128)(2,1)S(1)}, bf16[256,256]{1,0:T(8,128)(2,1)S(1)}, u32[]{:S(2)}, u32[]{:S(2)}) collective-permute-start(bf16[256,256]{1,0:T(8,128)(2,1)S(1)} %get-tuple-element.57.refs_4_), channel_id=1, source_target_pairs={{0,12},{4,8},{8,4},{12,0},{1,13},{5,9},{9,5},{13,1},{2,14},{6,10},... | collective-permute-start | bytes 393224 | tf_op jit(solution)/shard_map/ppermute | solution.py:306
  20.0 4.4 %collective-permute-done.14.refs_7_ = bf16[256,256]{1,0:T(8,128)(2,1)S(1)} collective-permute-done((bf16[256,256]{1,0:T(8,128)(2,1)S(1)}, bf16[256,256]{1,0:T(8,128)(2,1)S(1)}, u32[]{:S(2)}, u32[]{:S(2)}) %collective-permute-start.14) | collective-permute-done | bytes 131104 | tf_op jit(solution)/shard_map/ppermute | solution.py:306
  24.5 1.0 %collective-permute-start.15 = (bf16[256,256]{1,0:T(8,128)(2,1)S(1)}, bf16[256,256]{1,0:T(8,128)(2,1)S(1)}, u32[]{:S(2)}, u32[]{:S(2)}) collective-permute-start(bf16[256,256]{1,0:T(8,128)(2,1)S(1)} %get-tuple-element.59.refs_1_), channel_id=1, source_target_pairs={{0,4},{4,0},{8,12},{12,8},{1,5},{5,1},{9,13},{13,9},{2,6},{6,2},{1... | collective-permute-start | bytes 393224 | tf_op jit(solution)/shard_map/ppermute | solution.py:306
  25.5 1.9 %collective-permute-start.16 = (bf16[256,256]{1,0:T(8,128)(2,1)S(1)}, bf16[256,256]{1,0:T(8,128)(2,1)S(1)}, u32[]{:S(2)}, u32[]{:S(2)}) collective-permute-start(bf16[256,256]{1,0:T(8,128)(2,1)S(1)} %get-tuple-element.59.refs_1_), channel_id=1, source_target_pairs={{0,8},{4,12},{8,0},{12,4},{1,9},{5,13},{9,1},{13,5},{2,10},{6,14},... | collective-permute-start | bytes 393224 | tf_op jit(solution)/shard_map/ppermute | solution.py:306
  27.4 1.5 %collective-permute-start.17 = (bf16[256,256]{1,0:T(8,128)(2,1)S(1)}, bf16[256,256]{1,0:T(8,128)(2,1)S(1)}, u32[]{:S(2)}, u32[]{:S(2)}) collective-permute-start(bf16[256,256]{1,0:T(8,128)(2,1)S(1)} %get-tuple-element.59.refs_1_), channel_id=1, source_target_pairs={{0,12},{4,8},{8,4},{12,0},{1,13},{5,9},{9,5},{13,1},{2,14},{6,10},... | collective-permute-start | bytes 393224 | tf_op jit(solution)/shard_map/ppermute | solution.py:306
  28.9 1.1 %shard_map.60 = (bf16[512,1024]{1,0:T(8,128)(2,1)S(1)}, f32[512,256]{1,0:T(8,128)S(1)}, bf16[512,256]{1,0:T(8,128)(2,1)S(1)}) custom-call(s32[3]{0:T(128)S(1)} %pad_add_fusion.pos, bf16[120,1024]{1,0:T(8,128)(2,1)S(1)} %get-tuple-element.53.refs_0_, bf16[120,1024]{1,0:T(8,128)(2,1)S(1)} %collective-permute-done.9.refs_1_, ...), custom_call_target="tpu_custom_call" | custom-call | flops 268435456 | bytes 3342336 | tf_op jit(solution)/shard_map/pallas_call | solution.py:34
  29.9 1.6 %collective-permute-start.28 = (bf16[512,256]{1,0:T(8,128)(2,1)S(1)}, bf16[512,256]{1,0:T(8,128)(2,1)S(1)}, u32[]{:S(2)}, u32[]{:S(2)}) collective-permute-start(bf16[512,256]{1,0:T(8,128)(2,1)S(1)} %get-tuple-element.73), channel_id=1, source_target_pairs={{0,16},{16,0},{1,17},{17,1},{2,18},{18,2},{3,19},{19,3},{4,20},{20... | collective-permute-start | bytes 786440 | tf_op jit(solution)/shard_map/ppermute | solution.py:366
  31.5 1.3 %shard_map.56 = (bf16[120,512]{1,0:T(8,128)(2,1)S(1)}, bf16[120,512]{1,0:T(8,128)(2,1)S(1)}, bf16[120,512]{1,0:T(8,128)(2,1)S(1)}, bf16[120,512]{1,0:T(8,128)(2,...) custom-call(s32[3]{0:T(128)S(1)} %pad_add_fusion.pos, ...), custom_call_target="tpu_custom_call" | custom-call | flops 402653184 | bytes 2752512 | tf_op jit(solution)/shard_map/pallas_call | solution.py:34
  32.8 1.6 %collective-permute-start.2 = (bf16[120,512]{1,0:T(8,128)(2,1)S(1)}, bf16[120,512]{1,0:T(8,128)(2,1)S(1)}, u32[]{:S(2)}, u32[]{:S(2)}) collective-permute-start(bf16[120,512]{1,0:T(8,128)(2,1)S(1)} %get-tuple-element.45), channel_id=1, source_target_pairs={{0,2},{1,3},{2,0},{3,1},{16,18},{17,19},{18,16},{19,17},{4,6},{5,7... | collective-permute-start | bytes 368648 | tf_op jit(solution)/shard_map/ppermute | solution.py:332
  34.4 0.5 collective-permute-start.3
  34.9 1.5 %collective-permute-done.16.refs_3_ = bf16[256,256]{1,0:T(8,128)(2,1)S(1)} collective-permute-done((bf16[256,256]{1,0:T(8,128)(2,1)S(1)}, bf16[256,256]{1,0:T(8,128)(2,1)S(1)}, u32[]{:S(2)}, u32[]{:S(2)}) %collective-permute-start.16) | collective-permute-done | bytes 131104 | tf_op jit(solution)/shard_map/ppermute | solution.py:306
  36.4 2.4 %collective-permute-start.4 = (bf16[120,512]{1,0:T(8,128)(2,1)S(1)}, bf16[120,512]{1,0:T(8,128)(2,1)S(1)}, u32[]{:S(2)}, u32[]{:S(2)}) collective-permute-start(bf16[120,512]{1,0:T(8,128)(2,1)S(1)} %get-tuple-element.47), channel_id=1, source_target_pairs={{0,18},{1,19},{2,16},{3,17},{16,2},{17,3},{18,0},{19,1},{4,22},{5,... | collective-permute-start | bytes 368648 | tf_op jit(solution)/shard_map/ppermute | solution.py:332
  39.4 0.5 collective-permute-start.6
  39.9 1.9 %collective-permute-done.3.refs_2_ = bf16[120,512]{1,0:T(8,128)(2,1)S(1)} collective-permute-done((bf16[120,512]{1,0:T(8,128)(2,1)S(1)}, bf16[120,512]{1,0:T(8,128)(2,1)S(1)}, u32[]{:S(2)}, u32[]{:S(2)}) %collective-permute-start.3) | collective-permute-done | bytes 122912 | tf_op jit(solution)/shard_map/ppermute | solution.py:332
  41.8 2.4 %collective-permute-start.7 = (bf16[120,512]{1,0:T(8,128)(2,1)S(1)}, bf16[120,512]{1,0:T(8,128)(2,1)S(1)}, u32[]{:S(2)}, u32[]{:S(2)}) collective-permute-start(bf16[120,512]{1,0:T(8,128)(2,1)S(1)} %get-tuple-element.51), channel_id=1, source_target_pairs={{0,18},{1,19},{2,16},{3,17},{16,2},{17,3},{18,0},{19,1},{4,22},{5,... | collective-permute-start | bytes 368648 | tf_op jit(solution)/shard_map/ppermute | solution.py:332
  44.3 1.3 %shard_map.61 = (f32[512,128]{1,0:T(8,128)S(1)}, bf16[512,128]{1,0:T(8,128)(2,1)S(1)}, f32[512,128]{1,0:T(8,128)S(1)}, bf16[512,128]{1,0:T(8,128)(2,1)S(1)}) custom-call(s32[3]{0:T(128)S(1)} %pad_add_fusion.pos, bf16[512,1024]{1,0:T(8,128)(2,1)S(1)} %get-tuple-element.58.refs_0_, bf16[256,256]{1,0:T(8,128)(2,1)S(1)} %get-tuple-element.59.refs_1_, ...), custom_call_target="tpu_custom_call" | custom-call | flops 268435456 | bytes 2359296 | tf_op jit(solution)/shard_map/pallas_call | solution.py:34
  45.5 1.3 %collective-permute-start.23 = (bf16[512,128]{1,0:T(8,128)(2,1)S(1)}, bf16[512,128]{1,0:T(8,128)(2,1)S(1)}, u32[]{:S(2)}, u32[]{:S(2)}) collective-permute-start(bf16[512,128]{1,0:T(8,128)(2,1)S(1)} %get-tuple-element.67), channel_id=1, source_target_pairs={{0,16},{16,0},{1,17},{17,1},{2,18},{18,2},{3,19},{19,3},{4,20},{20... | collective-permute-start | bytes 393224 | tf_op jit(solution)/shard_map/ppermute | solution.py:366
  46.9 0.8 collective-permute-start.18
  47.6 0.8 shard_map.57.refs_0_
  48.8 0.8 shard_map.58.refs_1_.refs_0_
  49.6 0.9 %shard_map.66 = (bf16[256,256]{1,0:T(8,128)(2,1)S(1)}, bf16[256,256]{1,0:T(8,128)(2,1)S(1)}, bf16[512,256]{1,0:T(8,128)(2,1)S(1)}) custom-call(s32[3]{0:T(128)S(1)} %pad_add_fusion.pos, bf16[512,512]{1,0:T(8,128)(2,1)S(1)} %shard_map.57.refs_0_, f32[512,256]{1,0:T(8,128)S(1)} %get-tuple-element.72.refs_1_, bf16[512,256]{1,0:T(8,128)(2,1)S(1)} %collective-permute-done.28.refs_2_), custom_call_target="tpu_custom_call" | custom-call | flops 134217728 | bytes 1835008 | tf_op jit(solution)/shard_map/pallas_call | solution.py:34
  50.5 0.8 %shard_map.67 = (bf16[256,256]{1,0:T(8,128)(2,1)S(1)}, f32[256,256]{1,0:T(8,128)S(1)}) custom-call(s32[3]{0:T(128)S(1)} %pad_add_fusion.pos, bf16[512,512]{1,0:T(8,128)(2,1)S(1)} %shard_map.58.refs_1_.refs_0_, bf16[512,256]{1,0:T(8,128)(2,1)S(1)} %get-tuple-element.74.refs_1_), custom_call_target="tpu_custom_call" | custom-call | flops 134217728 | bytes 1179648 | tf_op jit(solution)/shard_map/pallas_call | solution.py:34
  51.6 4.0 %collective-permute-start.29 = (bf16[256,256]{1,0:T(8,128)(2,1)S(1)}, bf16[256,256]{1,0:T(8,128)(2,1)S(1)}, u32[]{:S(2)}, u32[]{:S(2)}) collective-permute-start(bf16[256,256]{1,0:T(8,128)(2,1)S(1)} %get-tuple-element.76), channel_id=1, source_target_pairs={{0,12},{4,8},{8,4},{12,0},{1,13},{5,9},{9,5},{13,1},{2,14},{6,10},... | collective-permute-start | bytes 393224 | tf_op jit(solution)/shard_map/ppermute | solution.py:400
  56.1 1.0 %shard_map.64 = (bf16[256,128]{1,0:T(8,128)(2,1)S(1)}, bf16[256,128]{1,0:T(8,128)(2,1)S(1)}, bf16[256,128]{1,0:T(8,128)(2,1)S(1)}, f32[256,128]{1,0:T(8,128)S(1)}) custom-call(s32[3]{0:T(128)S(1)} %pad_add_fusion.pos, bf16[512,512]{1,0:T(8,128)(2,1)S(1)} %shard_map.57.refs_0_, bf16[512,512]{1,0:T(8,128)(2,1)S(1)} %shard_map.58.refs_1_.refs_0_, ...), custom_call_target="tpu_custom_call" | custom-call | flops 134217728 | bytes 1769472 | tf_op jit(solution)/shard_map/pallas_call | solution.py:34
  57.1 3.0 %collective-permute-start.24 = (bf16[256,128]{1,0:T(8,128)(2,1)S(1)}, bf16[256,128]{1,0:T(8,128)(2,1)S(1)}, u32[]{:S(2)}, u32[]{:S(2)}) collective-permute-start(bf16[256,128]{1,0:T(8,128)(2,1)S(1)} %get-tuple-element.69), channel_id=1, source_target_pairs={{0,12},{4,8},{8,4},{12,0},{1,13},{5,9},{9,5},{13,1},{2,14},{6,10},... | collective-permute-start | bytes 196616 | tf_op jit(solution)/shard_map/ppermute | solution.py:400
  60.1 1.0 %shard_map.62 = (bf16[256,128]{1,0:T(8,128)(2,1)S(1)}, bf16[256,128]{1,0:T(8,128)(2,1)S(1)}, bf16[256,128]{1,0:T(8,128)(2,1)S(1)}, f32[256,128]{1,0:T(8,128)S(1)}) custom-call(s32[3]{0:T(128)S(1)} %pad_add_fusion.pos, bf16[512,512]{1,0:T(8,128)(2,1)S(1)} %shard_map.57.refs_0_, bf16[512,512]{1,0:T(8,128)(2,1)S(1)} %shard_map.58.refs_1_.refs_0_, ...), custom_call_target="tpu_custom_call" | custom-call | flops 134217728 | bytes 1769472 | tf_op jit(solution)/shard_map/pallas_call | solution.py:34
  61.2 1.6 %collective-permute-done.31.refs_2_ = bf16[256,256]{1,0:T(8,128)(2,1)S(1)} collective-permute-done((bf16[256,256]{1,0:T(8,128)(2,1)S(1)}, bf16[256,256]{1,0:T(8,128)(2,1)S(1)}, u32[]{:S(2)}, u32[]{:S(2)}) %collective-permute-start.31) | collective-permute-done | bytes 131104 | tf_op jit(solution)/shard_map/ppermute | solution.py:400
  62.8 3.6 %collective-permute-start.19 = (bf16[256,128]{1,0:T(8,128)(2,1)S(1)}, bf16[256,128]{1,0:T(8,128)(2,1)S(1)}, u32[]{:S(2)}, u32[]{:S(2)}) collective-permute-start(bf16[256,128]{1,0:T(8,128)(2,1)S(1)} %get-tuple-element.63), channel_id=1, source_target_pairs={{0,12},{4,8},{8,4},{12,0},{1,13},{5,9},{9,5},{13,1},{2,14},{6,10},... | collective-permute-start | bytes 196616 | tf_op jit(solution)/shard_map/ppermute | solution.py:400
  66.4 3.9 %collective-permute-start.20 = (bf16[256,128]{1,0:T(8,128)(2,1)S(1)}, bf16[256,128]{1,0:T(8,128)(2,1)S(1)}, u32[]{:S(2)}, u32[]{:S(2)}) collective-permute-start(bf16[256,128]{1,0:T(8,128)(2,1)S(1)} %get-tuple-element.64), channel_id=1, source_target_pairs={{0,4},{4,0},{8,12},{12,8},{1,5},{5,1},{9,13},{13,9},{2,6},{6,2},{1... | collective-permute-start | bytes 196616 | tf_op jit(solution)/shard_map/ppermute | solution.py:400
  70.2 0.6 shard_map.68.refs_0_
  70.9 1.2 %collective-permute-start.32 = (bf16[256,256]{1,0:T(8,128)(2,1)S(1)}, bf16[256,256]{1,0:T(8,128)(2,1)S(1)}, u32[]{:S(2)}, u32[]{:S(2)}) collective-permute-start(bf16[256,256]{1,0:T(8,128)(2,1)S(1)} %shard_map.68.refs_0_), channel_id=1, source_target_pairs={{0,16},{16,0},{1,17},{17,1},{2,18},{18,2},{3,19},{19,3},{4,20},{20... | collective-permute-start | bytes 393224 | tf_op jit(solution)/shard_map/ppermute | solution.py:416
  72.2 0.6 shard_map.65.refs_3_
  72.7 0.9 %collective-permute-start.27 = (bf16[256,128]{1,0:T(8,128)(2,1)S(1)}, bf16[256,128]{1,0:T(8,128)(2,1)S(1)}, u32[]{:S(2)}, u32[]{:S(2)}) collective-permute-start(bf16[256,128]{1,0:T(8,128)(2,1)S(1)} %shard_map.65.refs_3_), channel_id=1, source_target_pairs={{0,16},{16,0},{1,17},{17,1},{2,18},{18,2},{3,19},{19,3},{4,20},{20... | collective-permute-start | bytes 196616 | tf_op jit(solution)/shard_map/ppermute | solution.py:416
  73.7 2.5 %collective-permute-done.21.refs_2_ = bf16[256,128]{1,0:T(8,128)(2,1)S(1)} collective-permute-done((bf16[256,128]{1,0:T(8,128)(2,1)S(1)}, bf16[256,128]{1,0:T(8,128)(2,1)S(1)}, u32[]{:S(2)}, u32[]{:S(2)}) %collective-permute-start.21) | collective-permute-done | bytes 65568 | tf_op jit(solution)/shard_map/ppermute | solution.py:400
  76.2 0.6 shard_map.63.refs_2_
  76.8 1.2 %collective-permute-start.22 = (bf16[256,128]{1,0:T(8,128)(2,1)S(1)}, bf16[256,128]{1,0:T(8,128)(2,1)S(1)}, u32[]{:S(2)}, u32[]{:S(2)}) collective-permute-start(bf16[256,128]{1,0:T(8,128)(2,1)S(1)} %shard_map.63.refs_2_), channel_id=1, source_target_pairs={{0,16},{16,0},{1,17},{17,1},{2,18},{18,2},{3,19},{19,3},{4,20},{20... | collective-permute-start | bytes 196616 | tf_op jit(solution)/shard_map/ppermute | solution.py:416
  78.0 1.3 %shard_map.69.refs_2_ = bf16[512,512]{1,0:T(8,128)(2,1)} custom-call(s32[3]{0:T(128)S(1)} %pad_add_fusion.pos, bf16[256,256]{1,0:T(8,128)(2,1)S(1)} %shard_map.68.refs_0_, bf16[256,256]{1,0:T(8,128)(2,1)S(1)} %collective-permute-done.32.refs_1_, bf16[256,128]{1,0:T(8,128)(2,1)S(1)} %shard_map.63.refs_2_, bf16[256,128]{1,0:T(8,128)(2,1)S(1)} %shard_map.65.refs_3_), custom_call_target="tpu_custom_call" | custom-call | bytes 917504 | tf_op jit(solution)/shard_map/pallas_call | solution.py:34
  79.4 1.8 %collective-permute-done.22.refs_0_ = bf16[256,128]{1,0:T(8,128)(2,1)S(1)} collective-permute-done((bf16[256,128]{1,0:T(8,128)(2,1)S(1)}, bf16[256,128]{1,0:T(8,128)(2,1)S(1)}, u32[]{:S(2)}, u32[]{:S(2)}) %collective-permute-start.22) | collective-permute-done | bytes 65568 | tf_op jit(solution)/shard_map/ppermute | solution.py:416
  81.1 1.2 %shard_map.70 = bf16[512,512]{1,0:T(8,128)(2,1)} custom-call(s32[3]{0:T(128)S(1)} %pad_add_fusion.pos, bf16[256,128]{1,0:T(8,128)(2,1)S(1)} %collective-permute-done.22.refs_0_, bf16[256,128]{1,0:T(8,128)(2,1)S(1)} %collective-permute-done.27.refs_1_, bf16[512,512]{1,0:T(8,128)(2,1)} %shard_map.69.refs_2_), custom_call_target="tpu_custom_call", output_to_operand_aliasing={{}: (3, {})} | custom-call | bytes 1179648 | tf_op jit(solution)/shard_map/pallas_call | solution.py:34
  (39 shorter events, 3.0 us)
Async XLA Ops:
  0.0 0.7 copy-start.1
  0.0 11.1 %collective-permute-start.8 = (bf16[192,2048]{1,0:T(8,128)(2,1)}, bf16[192,2048]{1,0:T(8,128)(2,1)S(1)}, u32[]{:S(2)}, u32[]{:S(2)}) collective-permute-start(bf16[192,2048]{1,0:T(8,128)(2,1)} %rows.2), channel_id=1, source_target_pairs={{0,1},{1,0},{2,3},{3,2},{4,5},{5,4},{6,7},{7,6},{8,9},{9,8},{10,11... | collective-permute-start | bytes 2359304 | tf_op jit(solution)/shard_map/ppermute | solution.py:281
  0.5 31.0 %collective-permute-start.1 = (bf16[192,2048]{1,0:T(8,128)(2,1)}, bf16[192,2048]{1,0:T(8,128)(2,1)S(1)}, u32[]{:S(2)}, u32[]{:S(2)}) collective-permute-start(bf16[192,2048]{1,0:T(8,128)(2,1)} %rows.3), channel_id=1, source_target_pairs={{0,1},{1,0},{2,3},{3,2},{4,5},{5,4},{6,7},{7,6},{8,9},{9,8},{10,11... | collective-permute-start | bytes 2359304 | tf_op jit(solution)/shard_map/ppermute | solution.py:283
  0.7 3.1 %collective-permute-start = (s32[1,192]{1,0:T(1,128)S(1)}, s32[1,192]{1,0:T(1,128)S(1)}, u32[]{:S(2)}, u32[]{:S(2)}) collective-permute-start(s32[1,192]{1,0:T(1,128)S(1)} %bitcast.7), channel_id=1, source_target_pairs={{0,1},{1,0},{2,3},{3,2},{4,5},{5,4},{6,7},{7,6},{8,9},{9,8},{10,11... | collective-permute-start | bytes 2312 | tf_op jit(solution)/shard_map/ppermute | solution.py:282
  5.6 9.9 %collective-permute-start.12 = (bf16[256,256]{1,0:T(8,128)(2,1)S(1)}, bf16[256,256]{1,0:T(8,128)(2,1)S(1)}, u32[]{:S(2)}, u32[]{:S(2)}) collective-permute-start(bf16[256,256]{1,0:T(8,128)(2,1)S(1)} %get-tuple-element.57.refs_4_), channel_id=1, source_target_pairs={{0,4},{4,0},{8,12},{12,8},{1,5},{5,1},{9,13},{13,9},{2,6},{6,2},{1... | collective-permute-start | bytes 393224 | tf_op jit(solution)/shard_map/ppermute | solution.py:306
  8.6 9.0 %collective-permute-start.13 = (bf16[256,256]{1,0:T(8,128)(2,1)S(1)}, bf16[256,256]{1,0:T(8,128)(2,1)S(1)}, u32[]{:S(2)}, u32[]{:S(2)}) collective-permute-start(bf16[256,256]{1,0:T(8,128)(2,1)S(1)} %get-tuple-element.57.refs_4_), channel_id=1, source_target_pairs={{0,8},{4,12},{8,0},{12,4},{1,9},{5,13},{9,1},{13,5},{2,10},{6,14},... | collective-permute-start | bytes 393224 | tf_op jit(solution)/shard_map/ppermute | solution.py:306
  12.4 19.1 %copy-start = (bf16[192,2048]{1,0:T(8,128)(2,1)S(1)}, bf16[192,2048]{1,0:T(8,128)(2,1)}, u32[]{:S(2)}) copy-start(bf16[192,2048]{1,0:T(8,128)(2,1)} %rows.3) | copy-start | bytes 2359300
  12.4 13.0 %collective-permute-start.10 = (bf16[120,1024]{1,0:T(8,128)(2,1)S(1)}, bf16[120,1024]{1,0:T(8,128)(2,1)S(1)}, u32[]{:S(2)}, u32[]{:S(2)}) collective-permute-start(bf16[120,1024]{1,0:T(8,128)(2,1)S(1)} %get-tuple-element.55), channel_id=1, source_target_pairs={{0,16},{1,17},{2,18},{3,19},{16,0},{17,1},{18,2},{19,3},{4,20},{5,... | collective-permute-start | bytes 737288 | tf_op jit(solution)/shard_map/ppermute | solution.py:332
  14.0 13.4 %collective-permute-start.11 = (bf16[120,1024]{1,0:T(8,128)(2,1)S(1)}, bf16[120,1024]{1,0:T(8,128)(2,1)S(1)}, u32[]{:S(2)}, u32[]{:S(2)}) collective-permute-start(bf16[120,1024]{1,0:T(8,128)(2,1)S(1)} %get-tuple-element.56), channel_id=1, source_target_pairs={{0,18},{1,19},{2,16},{3,17},{16,2},{17,3},{18,0},{19,1},{4,22},{5,... | collective-permute-start | bytes 737288 | tf_op jit(solution)/shard_map/ppermute | solution.py:332
  15.5 13.4 %collective-permute-start.9 = (bf16[120,1024]{1,0:T(8,128)(2,1)S(1)}, bf16[120,1024]{1,0:T(8,128)(2,1)S(1)}, u32[]{:S(2)}, u32[]{:S(2)}) collective-permute-start(bf16[120,1024]{1,0:T(8,128)(2,1)S(1)} %get-tuple-element.54), channel_id=1, source_target_pairs={{0,2},{1,3},{2,0},{3,1},{16,18},{17,19},{18,16},{19,17},{4,6},{5,7... | collective-permute-start | bytes 737288 | tf_op jit(solution)/shard_map/ppermute | solution.py:332
  17.6 6.9 %collective-permute-start.14 = (bf16[256,256]{1,0:T(8,128)(2,1)S(1)}, bf16[256,256]{1,0:T(8,128)(2,1)S(1)}, u32[]{:S(2)}, u32[]{:S(2)}) collective-permute-start(bf16[256,256]{1,0:T(8,128)(2,1)S(1)} %get-tuple-element.57.refs_4_), channel_id=1, source_target_pairs={{0,12},{4,8},{8,4},{12,0},{1,13},{5,9},{9,5},{13,1},{2,14},{6,10},... | collective-permute-start | bytes 393224 | tf_op jit(solution)/shard_map/ppermute | solution.py:306
  24.5 9.9 %collective-permute-start.15 = (bf16[256,256]{1,0:T(8,128)(2,1)S(1)}, bf16[256,256]{1,0:T(8,128)(2,1)S(1)}, u32[]{:S(2)}, u32[]{:S(2)}) collective-permute-start(bf16[256,256]{1,0:T(8,128)(2,1)S(1)} %get-tuple-element.59.refs_1_), channel_id=1, source_target_pairs={{0,4},{4,0},{8,12},{12,8},{1,5},{5,1},{9,13},{13,9},{2,6},{6,2},{1... | collective-permute-start | bytes 393224 | tf_op jit(solution)/shard_map/ppermute | solution.py:306
  25.5 10.9 %collective-permute-start.16 = (bf16[256,256]{1,0:T(8,128)(2,1)S(1)}, bf16[256,256]{1,0:T(8,128)(2,1)S(1)}, u32[]{:S(2)}, u32[]{:S(2)}) collective-permute-start(bf16[256,256]{1,0:T(8,128)(2,1)S(1)} %get-tuple-element.59.refs_1_), channel_id=1, source_target_pairs={{0,8},{4,12},{8,0},{12,4},{1,9},{5,13},{9,1},{13,5},{2,10},{6,14},... | collective-permute-start | bytes 393224 | tf_op jit(solution)/shard_map/ppermute | solution.py:306
  27.4 11.5 %collective-permute-start.17 = (bf16[256,256]{1,0:T(8,128)(2,1)S(1)}, bf16[256,256]{1,0:T(8,128)(2,1)S(1)}, u32[]{:S(2)}, u32[]{:S(2)}) collective-permute-start(bf16[256,256]{1,0:T(8,128)(2,1)S(1)} %get-tuple-element.59.refs_1_), channel_id=1, source_target_pairs={{0,12},{4,8},{8,4},{12,0},{1,13},{5,9},{9,5},{13,1},{2,14},{6,10},... | collective-permute-start | bytes 393224 | tf_op jit(solution)/shard_map/ppermute | solution.py:306
  29.9 19.7 %collective-permute-start.28 = (bf16[512,256]{1,0:T(8,128)(2,1)S(1)}, bf16[512,256]{1,0:T(8,128)(2,1)S(1)}, u32[]{:S(2)}, u32[]{:S(2)}) collective-permute-start(bf16[512,256]{1,0:T(8,128)(2,1)S(1)} %get-tuple-element.73), channel_id=1, source_target_pairs={{0,16},{16,0},{1,17},{17,1},{2,18},{18,2},{3,19},{19,3},{4,20},{20... | collective-permute-start | bytes 786440 | tf_op jit(solution)/shard_map/ppermute | solution.py:366
  32.8 6.6 %collective-permute-start.2 = (bf16[120,512]{1,0:T(8,128)(2,1)S(1)}, bf16[120,512]{1,0:T(8,128)(2,1)S(1)}, u32[]{:S(2)}, u32[]{:S(2)}) collective-permute-start(bf16[120,512]{1,0:T(8,128)(2,1)S(1)} %get-tuple-element.45), channel_id=1, source_target_pairs={{0,2},{1,3},{2,0},{3,1},{16,18},{17,19},{18,16},{19,17},{4,6},{5,7... | collective-permute-start | bytes 368648 | tf_op jit(solution)/shard_map/ppermute | solution.py:332
  34.4 7.5 %collective-permute-start.3 = (bf16[120,512]{1,0:T(8,128)(2,1)S(1)}, bf16[120,512]{1,0:T(8,128)(2,1)S(1)}, u32[]{:S(2)}, u32[]{:S(2)}) collective-permute-start(bf16[120,512]{1,0:T(8,128)(2,1)S(1)} %get-tuple-element.46), channel_id=1, source_target_pairs={{0,16},{1,17},{2,18},{3,19},{16,0},{17,1},{18,2},{19,3},{4,20},{5,... | collective-permute-start | bytes 368648 | tf_op jit(solution)/shard_map/ppermute | solution.py:332
  36.4 9.1 %collective-permute-start.4 = (bf16[120,512]{1,0:T(8,128)(2,1)S(1)}, bf16[120,512]{1,0:T(8,128)(2,1)S(1)}, u32[]{:S(2)}, u32[]{:S(2)}) collective-permute-start(bf16[120,512]{1,0:T(8,128)(2,1)S(1)} %get-tuple-element.47), channel_id=1, source_target_pairs={{0,18},{1,19},{2,16},{3,17},{16,2},{17,3},{18,0},{19,1},{4,22},{5,... | collective-permute-start | bytes 368648 | tf_op jit(solution)/shard_map/ppermute | solution.py:332
  38.8 8.0 %collective-permute-start.5 = (bf16[120,512]{1,0:T(8,128)(2,1)S(1)}, bf16[120,512]{1,0:T(8,128)(2,1)S(1)}, u32[]{:S(2)}, u32[]{:S(2)}) collective-permute-start(bf16[120,512]{1,0:T(8,128)(2,1)S(1)} %get-tuple-element.49), channel_id=1, source_target_pairs={{0,2},{1,3},{2,0},{3,1},{16,18},{17,19},{18,16},{19,17},{4,6},{5,7... | collective-permute-start | bytes 368648 | tf_op jit(solution)/shard_map/ppermute | solution.py:332
  39.4 9.1 %collective-permute-start.6 = (bf16[120,512]{1,0:T(8,128)(2,1)S(1)}, bf16[120,512]{1,0:T(8,128)(2,1)S(1)}, u32[]{:S(2)}, u32[]{:S(2)}) collective-permute-start(bf16[120,512]{1,0:T(8,128)(2,1)S(1)} %get-tuple-element.50), channel_id=1, source_target_pairs={{0,16},{1,17},{2,18},{3,19},{16,0},{17,1},{18,2},{19,3},{4,20},{5,... | collective-permute-start | bytes 368648 | tf_op jit(solution)/shard_map/ppermute | solution.py:332
  41.8 7.0 %collective-permute-start.7 = (bf16[120,512]{1,0:T(8,128)(2,1)S(1)}, bf16[120,512]{1,0:T(8,128)(2,1)S(1)}, u32[]{:S(2)}, u32[]{:S(2)}) collective-permute-start(bf16[120,512]{1,0:T(8,128)(2,1)S(1)} %get-tuple-element.51), channel_id=1, source_target_pairs={{0,18},{1,19},{2,16},{3,17},{16,2},{17,3},{18,0},{19,1},{4,22},{5,... | collective-permute-start | bytes 368648 | tf_op jit(solution)/shard_map/ppermute | solution.py:332
  45.5 10.6 %collective-permute-start.23 = (bf16[512,128]{1,0:T(8,128)(2,1)S(1)}, bf16[512,128]{1,0:T(8,128)(2,1)S(1)}, u32[]{:S(2)}, u32[]{:S(2)}) collective-permute-start(bf16[512,128]{1,0:T(8,128)(2,1)S(1)} %get-tuple-element.67), channel_id=1, source_target_pairs={{0,16},{16,0},{1,17},{17,1},{2,18},{18,2},{3,19},{19,3},{4,20},{20... | collective-permute-start | bytes 393224 | tf_op jit(solution)/shard_map/ppermute | solution.py:366
  46.9 13.2 %collective-permute-start.18 = (bf16[512,128]{1,0:T(8,128)(2,1)S(1)}, bf16[512,128]{1,0:T(8,128)(2,1)S(1)}, u32[]{:S(2)}, u32[]{:S(2)}) collective-permute-start(bf16[512,128]{1,0:T(8,128)(2,1)S(1)} %get-tuple-element.61), channel_id=1, source_target_pairs={{0,16},{16,0},{1,17},{17,1},{2,18},{18,2},{3,19},{19,3},{4,20},{20... | collective-permute-start | bytes 393224 | tf_op jit(solution)/shard_map/ppermute | solution.py:366
  51.3 11.4 %collective-permute-start.31 = (bf16[256,256]{1,0:T(8,128)(2,1)S(1)}, bf16[256,256]{1,0:T(8,128)(2,1)S(1)}, u32[]{:S(2)}, u32[]{:S(2)}) collective-permute-start(bf16[256,256]{1,0:T(8,128)(2,1)S(1)} %get-tuple-element.78), channel_id=1, source_target_pairs={{0,8},{4,12},{8,0},{12,4},{1,9},{5,13},{9,1},{13,5},{2,10},{6,14},... | collective-permute-start | bytes 393224 | tf_op jit(solution)/shard_map/ppermute | solution.py:400
  51.6 11.2 %collective-permute-start.29 = (bf16[256,256]{1,0:T(8,128)(2,1)S(1)}, bf16[256,256]{1,0:T(8,128)(2,1)S(1)}, u32[]{:S(2)}, u32[]{:S(2)}) collective-permute-start(bf16[256,256]{1,0:T(8,128)(2,1)S(1)} %get-tuple-element.76), channel_id=1, source_target_pairs={{0,12},{4,8},{8,4},{12,0},{1,13},{5,9},{9,5},{13,1},{2,14},{6,10},... | collective-permute-start | bytes 393224 | tf_op jit(solution)/shard_map/ppermute | solution.py:400
  55.6 10.7 %collective-permute-start.30 = (bf16[256,256]{1,0:T(8,128)(2,1)S(1)}, bf16[256,256]{1,0:T(8,128)(2,1)S(1)}, u32[]{:S(2)}, u32[]{:S(2)}) collective-permute-start(bf16[256,256]{1,0:T(8,128)(2,1)S(1)} %get-tuple-element.77), channel_id=1, source_target_pairs={{0,4},{4,0},{8,12},{12,8},{1,5},{5,1},{9,13},{13,9},{2,6},{6,2},{1... | collective-permute-start | bytes 393224 | tf_op jit(solution)/shard_map/ppermute | solution.py:400
  57.1 13.7 %collective-permute-start.24 = (bf16[256,128]{1,0:T(8,128)(2,1)S(1)}, bf16[256,128]{1,0:T(8,128)(2,1)S(1)}, u32[]{:S(2)}, u32[]{:S(2)}) collective-permute-start(bf16[256,128]{1,0:T(8,128)(2,1)S(1)} %get-tuple-element.69), channel_id=1, source_target_pairs={{0,12},{4,8},{8,4},{12,0},{1,13},{5,9},{9,5},{13,1},{2,14},{6,10},... | collective-permute-start | bytes 196616 | tf_op jit(solution)/shard_map/ppermute | solution.py:400
  60.1 10.8 %collective-permute-start.25 = (bf16[256,128]{1,0:T(8,128)(2,1)S(1)}, bf16[256,128]{1,0:T(8,128)(2,1)S(1)}, u32[]{:S(2)}, u32[]{:S(2)}) collective-permute-start(bf16[256,128]{1,0:T(8,128)(2,1)S(1)} %get-tuple-element.70), channel_id=1, source_target_pairs={{0,4},{4,0},{8,12},{12,8},{1,5},{5,1},{9,13},{13,9},{2,6},{6,2},{1... | collective-permute-start | bytes 196616 | tf_op jit(solution)/shard_map/ppermute | solution.py:400
  62.7 9.4 %collective-permute-start.26 = (bf16[256,128]{1,0:T(8,128)(2,1)S(1)}, bf16[256,128]{1,0:T(8,128)(2,1)S(1)}, u32[]{:S(2)}, u32[]{:S(2)}) collective-permute-start(bf16[256,128]{1,0:T(8,128)(2,1)S(1)} %get-tuple-element.71), channel_id=1, source_target_pairs={{0,8},{4,12},{8,0},{12,4},{1,9},{5,13},{9,1},{13,5},{2,10},{6,14},... | collective-permute-start | bytes 196616 | tf_op jit(solution)/shard_map/ppermute | solution.py:400
  62.8 10.9 %collective-permute-start.19 = (bf16[256,128]{1,0:T(8,128)(2,1)S(1)}, bf16[256,128]{1,0:T(8,128)(2,1)S(1)}, u32[]{:S(2)}, u32[]{:S(2)}) collective-permute-start(bf16[256,128]{1,0:T(8,128)(2,1)S(1)} %get-tuple-element.63), channel_id=1, source_target_pairs={{0,12},{4,8},{8,4},{12,0},{1,13},{5,9},{9,5},{13,1},{2,14},{6,10},... | collective-permute-start | bytes 196616 | tf_op jit(solution)/shard_map/ppermute | solution.py:400
  66.4 7.3 %collective-permute-start.20 = (bf16[256,128]{1,0:T(8,128)(2,1)S(1)}, bf16[256,128]{1,0:T(8,128)(2,1)S(1)}, u32[]{:S(2)}, u32[]{:S(2)}) collective-permute-start(bf16[256,128]{1,0:T(8,128)(2,1)S(1)} %get-tuple-element.64), channel_id=1, source_target_pairs={{0,4},{4,0},{8,12},{12,8},{1,5},{5,1},{9,13},{13,9},{2,6},{6,2},{1... | collective-permute-start | bytes 196616 | tf_op jit(solution)/shard_map/ppermute | solution.py:400
  70.9 5.4 %collective-permute-start.21 = (bf16[256,128]{1,0:T(8,128)(2,1)S(1)}, bf16[256,128]{1,0:T(8,128)(2,1)S(1)}, u32[]{:S(2)}, u32[]{:S(2)}) collective-permute-start(bf16[256,128]{1,0:T(8,128)(2,1)S(1)} %get-tuple-element.65), channel_id=1, source_target_pairs={{0,8},{4,12},{8,0},{12,4},{1,9},{5,13},{9,1},{13,5},{2,10},{6,14},... | collective-permute-start | bytes 196616 | tf_op jit(solution)/shard_map/ppermute | solution.py:400
  70.9 7.1 %collective-permute-start.32 = (bf16[256,256]{1,0:T(8,128)(2,1)S(1)}, bf16[256,256]{1,0:T(8,128)(2,1)S(1)}, u32[]{:S(2)}, u32[]{:S(2)}) collective-permute-start(bf16[256,256]{1,0:T(8,128)(2,1)S(1)} %shard_map.68.refs_0_), channel_id=1, source_target_pairs={{0,16},{16,0},{1,17},{17,1},{2,18},{18,2},{3,19},{19,3},{4,20},{20... | collective-permute-start | bytes 393224 | tf_op jit(solution)/shard_map/ppermute | solution.py:416
  72.7 6.6 %collective-permute-start.27 = (bf16[256,128]{1,0:T(8,128)(2,1)S(1)}, bf16[256,128]{1,0:T(8,128)(2,1)S(1)}, u32[]{:S(2)}, u32[]{:S(2)}) collective-permute-start(bf16[256,128]{1,0:T(8,128)(2,1)S(1)} %shard_map.65.refs_3_), channel_id=1, source_target_pairs={{0,16},{16,0},{1,17},{17,1},{2,18},{18,2},{3,19},{19,3},{4,20},{20... | collective-permute-start | bytes 196616 | tf_op jit(solution)/shard_map/ppermute | solution.py:416
  76.8 4.3 %collective-permute-start.22 = (bf16[256,128]{1,0:T(8,128)(2,1)S(1)}, bf16[256,128]{1,0:T(8,128)(2,1)S(1)}, u32[]{:S(2)}, u32[]{:S(2)}) collective-permute-start(bf16[256,128]{1,0:T(8,128)(2,1)S(1)} %shard_map.63.refs_2_), channel_id=1, source_target_pairs={{0,16},{16,0},{1,17},{17,1},{2,18},{18,2},{3,19},{19,3},{4,20},{20... | collective-permute-start | bytes 196616 | tf_op jit(solution)/shard_map/ppermute | solution.py:416

commit v9 on v8

--- a/solution.py
+++ b/solution.py
@@ -26,22 +26,25 @@
     return lax.rem(i + (size - k), size)
 
 
-def call(body, outs, scalars, args, scratch=(), flops=0, space=pltpu.VMEM, target=pltpu.VMEM, aliases=None):
+def call(body, outs, args, scratch=(), flops=0, space=pltpu.VMEM, target=pltpu.VMEM, aliases=None):
     moved = sum(a.size * a.dtype.itemsize for a in args)
     moved += sum(o.size * o.dtype.itemsize for o in outs)
     spaces = space if isinstance(space, list) else [space] * len(args)
     room = 2 * moved + (8 << 20)
+
+    def kernel(*refs):
+        body([lax.axis_index(name) for name in ("dp", "node", "local")], *refs)
+
     return pl.pallas_call(
-        body,
+        kernel,
         out_shape=outs,
-        in_specs=[pl.BlockSpec(memory_space=pltpu.SMEM)]
-        + [pl.BlockSpec(memory_space=kind) for kind in spaces],
+        in_specs=[pl.BlockSpec(memory_space=kind) for kind in spaces],
         out_specs=[pl.BlockSpec(memory_space=target)] * len(outs),
         scratch_shapes=list(scratch),
         input_output_aliases=aliases or {},
         compiler_params=pltpu.CompilerParams(vmem_limit_bytes=min(room, 60 << 20)),
         cost_estimate=pl.CostEstimate(flops=flops, bytes_accessed=moved, transcendentals=0),
-    )(scalars, *args)
+    )(*args)
 
 
 def node_order(nodes):
@@ -263,7 +266,6 @@
     unit = hidden // sum(sum(split) for split in SPLITS)
     gathered = [unit * sum(split) for split in SPLITS]
     everyone = copies * pairs * stride
-    pos = jnp.stack([lax.axis_index(a) for a in ("dp", "node", "local")]).astype(jnp.int32)
 
     aligned = mine % 128 == 0
     halves, jobs, outputs = plan_of(nodes, aligned)
@@ -287,7 +289,6 @@
     first, second, tokens, *weights = call(
         functools.partial(prep_body, dims, stride),
         near + [shape(mine, w, BF16) for w in gathered],
-        pos,
         [chosen, chosen_pair] + far,
         [
             pltpu.VMEM((mine, hidden), BF16),
@@ -310,7 +311,6 @@
         pieces = call(
             functools.partial(route_body, dims, stride, columns),
             [shape(sent_rows, part // len(columns), BF16)] * (len(columns) * copies * pairs),
-            pos,
             [*picks, rows, rows_pair],
             flops=4 * pairs * stride * count * features,
         )
@@ -340,7 +340,6 @@
         turned += call(
             functools.partial(turn_body, dims, stride),
             [shape(cols, everyone, BF16)],
-            pos,
             got_dy,
             [pltpu.VMEM((everyone, cols), BF16)],
         )
@@ -352,7 +351,6 @@
         parts = call(
             functools.partial(up_body, dims, stride, len(rows_x)),
             joined + [shape(everyone, w, kind) for w in widths for kind in (F32, BF16)],
-            pos,
             list(rows_x) + held[i],
             [pltpu.VMEM((part, gathered[i]), BF16)],
             flops=2 * everyone * part * gathered[i],
@@ -381,7 +379,6 @@
         terms = call(
             functools.partial(down_body, dims, factor, spots, [len(acts[i]) for i in chunks], emits),
             kinds,
-            pos,
             [turned[h] for h in tables] + sum((acts[i] for i in chunks), []),
             [pltpu.VMEM((everyone, wide), BF16)],
             flops=2 * everyone * len(targets) * mine * wide,
@@ -406,7 +403,6 @@
         (summed,) = call(
             functools.partial(sum_body, begins),
             [shape(mine, wide, BF16)],
-            pos,
             [owns[i]] + [moved for _, moved in arrived[i]],
             [pltpu.VMEM((mine, wide), F32)],
         )
@@ -426,7 +422,6 @@
     (result,) = call(
         functools.partial(lay_body, dims, [spot for _, spot in soon]),
         [shape(shard, hidden, BF16)],
-        pos,
         [value for value, _ in soon],
         [pltpu.SemaphoreType.DMA((len(soon),))],
         target=pltpu.HBM,
@@ -434,12 +429,11 @@
     (result,) = call(
         functools.partial(lay_body, dims, [spot for _, spot in late]),
         [shape(shard, hidden, BF16)],
-        pos,
         [value for value, _ in late] + [result],
         [pltpu.SemaphoreType.DMA((len(late),))],
         space=[pltpu.VMEM] * len(late) + [pltpu.HBM],
         target=pltpu.HBM,
-        aliases={len(late) + 1: 0},
+        aliases={len(late): 0},
     )
     return result[None]
 

time: 82.6 us -> 78.3 us (0.948)
  Pallas kernels: 16.3 us -> 7.6 us
  waiting for transfers between devices: 17.9 us -> 22 us
    pallas_call x16, Pallas kernels: 16.3 us -> 7.6 us  [call(): pl.pallas_call(kernel, out_shape=outs, in_specs=[pl.BlockSpec(memory_spac...]
    ppermute x9, waiting for transfers between devices: 4.12 us -> 5.62 us  [on_device(): moved = lax.ppermute(term, 'node', links)]
    ppermute x6, waiting for transfers between devices: 7.13 us -> 8.21 us  [on_device(): lax.ppermute(chunk, 'node', [(a, mate(a, s, nodes)) for a in range(nodes)])]
    ppermute x3, waiting for transfers between devices: 1.79 us -> 2.7 us  [on_device(): finished.append(lax.ppermute(summed, 'dp', links))]
  transfers between devices with their start and end apart: 33 -> 33, of which waited for: 9 -> 11; matrix products, arithmetic and copies ran while one was open for 0% -> 0% of each run, Pallas kernels for 18% -> 9%
where the time goes in v9:
time: 78.3 us; the launch traced here: 78.1 us
  starting transfers between devices  48.2 us (62%)
  waiting for transfers between devices  22 us (28%)
  Pallas kernels  7.6 us (10%)
    ppermute x9, starting transfers between devices, on_device(): moved = lax.ppermute(term, 'node', links)  15.6 us
    ppermute x9, starting transfers between devices, exchange(): moved[at] = lax.ppermute(pieces[at], ('dp', 'local'), links)  12.6 us
    ppermute x6, starting transfers between devices, on_device(): lax.ppermute(chunk, 'node', [(a, mate(a, s, nodes)) for a in range(nodes)])  12.4 us
    ppermute x6, waiting for transfers between devices, on_device(): lax.ppermute(chunk, 'node', [(a, mate(a, s, nodes)) for a in range(nodes)])  8.21 us
    pallas_call x16, Pallas kernels, call(): pl.pallas_call(kernel, out_shape=outs, in_specs=[pl.BlockSpec(memory_spac...  7.6 us
    ppermute x9, waiting for transfers between devices, on_device(): moved = lax.ppermute(term, 'node', links)  5.62 us
    ppermute x3, starting transfers between devices, on_device(): acts.append([kept, lax.ppermute(sent, 'dp', [(0, 1), (1, 0)])])  3.58 us
    ppermute x3, starting transfers between devices, on_device(): finished.append(lax.ppermute(summed, 'dp', links))  2.94 us
  transfers between devices with their start and end apart: 33, of which 11 were waited for; matrix products, arithmetic and copies ran while one was open for 0% of the time, Pallas kernels for 9%

profile of v9, /device:TPU:0, one launch (start us, length us, event | category | flops | bytes accessed | tf_op | source)
XLA Modules:
  0.0 78.1 jit_solution(12689311144457889083)
XLA Ops:
  0.0 0.5 collective-permute-start.8
  0.7 0.5 collective-permute-start
  1.2 2.6 %collective-permute-done.refs_1_ = s32[1,192]{1,0:T(1,128)S(1)} collective-permute-done((s32[1,192]{1,0:T(1,128)S(1)}, s32[1,192]{1,0:T(1,128)S(1)}, u32[]{:S(2)}, u32[]{:S(2)}) %collective-permute-start) | collective-permute-done | bytes 800 | tf_op jit(solution)/shard_map/ppermute | solution.py:284
  3.7 1.3 %shard_map.55 = (bf16[256,192]{1,0:T(8,128)(2,1)S(1)}, bf16[256,192]{1,0:T(8,128)(2,1)S(1)}, bf16[192,2048]{1,0:T(8,128)(2,1)S(1)}, bf16[256,256]{1,0:T(8,128)(2,1)S(1)}, bf16[256,256]{1,0:T(8,128)(2,1)S(1)}) custom-call(s32[1,192]{1,0:T(1,128)S(1)} %bitcast.5, s32[1,192]{1,0:T(1,128)S(1)} %collective-permute-done.refs_1_, bf16[192,2048]{1,0:T(8,128)(2,1)} %refs_2_.2, ...), custom_call_target="tpu_custom_call" | custom-call | bytes 2573824 | tf_op jit(solution)/shard_map/pallas_call | solution.py:38
  5.0 3.0 %collective-permute-start.12 = (bf16[256,256]{1,0:T(8,128)(2,1)S(1)}, bf16[256,256]{1,0:T(8,128)(2,1)S(1)}, u32[]{:S(2)}, u32[]{:S(2)}) collective-permute-start(bf16[256,256]{1,0:T(8,128)(2,1)S(1)} %get-tuple-element.57.refs_4_), channel_id=1, source_target_pairs={{0,4},{4,0},{8,12},{12,8},{1,5},{5,1},{9,13},{13,9},{2,6},{6,2},{1... | collective-permute-start | bytes 393224 | tf_op jit(solution)/shard_map/ppermute | solution.py:307
  8.0 2.6 %collective-permute-start.13 = (bf16[256,256]{1,0:T(8,128)(2,1)S(1)}, bf16[256,256]{1,0:T(8,128)(2,1)S(1)}, u32[]{:S(2)}, u32[]{:S(2)}) collective-permute-start(bf16[256,256]{1,0:T(8,128)(2,1)S(1)} %get-tuple-element.57.refs_4_), channel_id=1, source_target_pairs={{0,8},{4,12},{8,0},{12,4},{1,9},{5,13},{9,1},{13,5},{2,10},{6,14},... | collective-permute-start | bytes 393224 | tf_op jit(solution)/shard_map/ppermute | solution.py:307
  10.6 0.7 shard_map.59
  11.3 1.6 %collective-permute-start.10 = (bf16[120,1024]{1,0:T(8,128)(2,1)S(1)}, bf16[120,1024]{1,0:T(8,128)(2,1)S(1)}, u32[]{:S(2)}, u32[]{:S(2)}) collective-permute-start(bf16[120,1024]{1,0:T(8,128)(2,1)S(1)} %get-tuple-element.55), channel_id=1, source_target_pairs={{0,16},{1,17},{2,18},{3,19},{16,0},{17,1},{18,2},{19,3},{4,20},{5,... | collective-permute-start | bytes 737288 | tf_op jit(solution)/shard_map/ppermute | solution.py:332
  12.9 1.5 %collective-permute-start.11 = (bf16[120,1024]{1,0:T(8,128)(2,1)S(1)}, bf16[120,1024]{1,0:T(8,128)(2,1)S(1)}, u32[]{:S(2)}, u32[]{:S(2)}) collective-permute-start(bf16[120,1024]{1,0:T(8,128)(2,1)S(1)} %get-tuple-element.56), channel_id=1, source_target_pairs={{0,18},{1,19},{2,16},{3,17},{16,2},{17,3},{18,0},{19,1},{4,22},{5,... | collective-permute-start | bytes 737288 | tf_op jit(solution)/shard_map/ppermute | solution.py:332
  14.4 1.4 %collective-permute-start.9 = (bf16[120,1024]{1,0:T(8,128)(2,1)S(1)}, bf16[120,1024]{1,0:T(8,128)(2,1)S(1)}, u32[]{:S(2)}, u32[]{:S(2)}) collective-permute-start(bf16[120,1024]{1,0:T(8,128)(2,1)S(1)} %get-tuple-element.54), channel_id=1, source_target_pairs={{0,2},{1,3},{2,0},{3,1},{16,18},{17,19},{18,16},{19,17},{4,6},{5,7... | collective-permute-start | bytes 737288 | tf_op jit(solution)/shard_map/ppermute | solution.py:332
  15.8 1.2 %collective-permute-done.13.refs_6_ = bf16[256,256]{1,0:T(8,128)(2,1)S(1)} collective-permute-done((bf16[256,256]{1,0:T(8,128)(2,1)S(1)}, bf16[256,256]{1,0:T(8,128)(2,1)S(1)}, u32[]{:S(2)}, u32[]{:S(2)}) %collective-permute-start.13) | collective-permute-done | bytes 131104 | tf_op jit(solution)/shard_map/ppermute | solution.py:307
  17.0 2.5 %collective-permute-start.14 = (bf16[256,256]{1,0:T(8,128)(2,1)S(1)}, bf16[256,256]{1,0:T(8,128)(2,1)S(1)}, u32[]{:S(2)}, u32[]{:S(2)}) collective-permute-start(bf16[256,256]{1,0:T(8,128)(2,1)S(1)} %get-tuple-element.57.refs_4_), channel_id=1, source_target_pairs={{0,12},{4,8},{8,4},{12,0},{1,13},{5,9},{9,5},{13,1},{2,14},{6,10},... | collective-permute-start | bytes 393224 | tf_op jit(solution)/shard_map/ppermute | solution.py:307
  19.5 4.4 %collective-permute-done.14.refs_7_ = bf16[256,256]{1,0:T(8,128)(2,1)S(1)} collective-permute-done((bf16[256,256]{1,0:T(8,128)(2,1)S(1)}, bf16[256,256]{1,0:T(8,128)(2,1)S(1)}, u32[]{:S(2)}, u32[]{:S(2)}) %collective-permute-start.14) | collective-permute-done | bytes 131104 | tf_op jit(solution)/shard_map/ppermute | solution.py:307
  23.9 1.0 %collective-permute-start.15 = (bf16[256,256]{1,0:T(8,128)(2,1)S(1)}, bf16[256,256]{1,0:T(8,128)(2,1)S(1)}, u32[]{:S(2)}, u32[]{:S(2)}) collective-permute-start(bf16[256,256]{1,0:T(8,128)(2,1)S(1)} %get-tuple-element.59.refs_1_), channel_id=1, source_target_pairs={{0,4},{4,0},{8,12},{12,8},{1,5},{5,1},{9,13},{13,9},{2,6},{6,2},{1... | collective-permute-start | bytes 393224 | tf_op jit(solution)/shard_map/ppermute | solution.py:307
  24.9 1.9 %collective-permute-start.16 = (bf16[256,256]{1,0:T(8,128)(2,1)S(1)}, bf16[256,256]{1,0:T(8,128)(2,1)S(1)}, u32[]{:S(2)}, u32[]{:S(2)}) collective-permute-start(bf16[256,256]{1,0:T(8,128)(2,1)S(1)} %get-tuple-element.59.refs_1_), channel_id=1, source_target_pairs={{0,8},{4,12},{8,0},{12,4},{1,9},{5,13},{9,1},{13,5},{2,10},{6,14},... | collective-permute-start | bytes 393224 | tf_op jit(solution)/shard_map/ppermute | solution.py:307
  26.8 1.5 %collective-permute-start.17 = (bf16[256,256]{1,0:T(8,128)(2,1)S(1)}, bf16[256,256]{1,0:T(8,128)(2,1)S(1)}, u32[]{:S(2)}, u32[]{:S(2)}) collective-permute-start(bf16[256,256]{1,0:T(8,128)(2,1)S(1)} %get-tuple-element.59.refs_1_), channel_id=1, source_target_pairs={{0,12},{4,8},{8,4},{12,0},{1,13},{5,9},{9,5},{13,1},{2,14},{6,10},... | collective-permute-start | bytes 393224 | tf_op jit(solution)/shard_map/ppermute | solution.py:307
  28.3 0.5 shard_map.60
  28.9 1.6 %collective-permute-start.28 = (bf16[512,256]{1,0:T(8,128)(2,1)S(1)}, bf16[512,256]{1,0:T(8,128)(2,1)S(1)}, u32[]{:S(2)}, u32[]{:S(2)}) collective-permute-start(bf16[512,256]{1,0:T(8,128)(2,1)S(1)} %get-tuple-element.73), channel_id=1, source_target_pairs={{0,16},{16,0},{1,17},{17,1},{2,18},{18,2},{3,19},{19,3},{4,20},{20... | collective-permute-start | bytes 786440 | tf_op jit(solution)/shard_map/ppermute | solution.py:364
  30.4 0.7 shard_map.56
  31.2 1.6 %collective-permute-start.2 = (bf16[120,512]{1,0:T(8,128)(2,1)S(1)}, bf16[120,512]{1,0:T(8,128)(2,1)S(1)}, u32[]{:S(2)}, u32[]{:S(2)}) collective-permute-start(bf16[120,512]{1,0:T(8,128)(2,1)S(1)} %get-tuple-element.45), channel_id=1, source_target_pairs={{0,2},{1,3},{2,0},{3,1},{16,18},{17,19},{18,16},{19,17},{4,6},{5,7... | collective-permute-start | bytes 368648 | tf_op jit(solution)/shard_map/ppermute | solution.py:332
  32.7 0.5 collective-permute-start.3
  33.3 2.6 %collective-permute-done.16.refs_3_ = bf16[256,256]{1,0:T(8,128)(2,1)S(1)} collective-permute-done((bf16[256,256]{1,0:T(8,128)(2,1)S(1)}, bf16[256,256]{1,0:T(8,128)(2,1)S(1)}, u32[]{:S(2)}, u32[]{:S(2)}) %collective-permute-start.16) | collective-permute-done | bytes 131104 | tf_op jit(solution)/shard_map/ppermute | solution.py:307
  35.9 2.4 %collective-permute-start.4 = (bf16[120,512]{1,0:T(8,128)(2,1)S(1)}, bf16[120,512]{1,0:T(8,128)(2,1)S(1)}, u32[]{:S(2)}, u32[]{:S(2)}) collective-permute-start(bf16[120,512]{1,0:T(8,128)(2,1)S(1)} %get-tuple-element.47), channel_id=1, source_target_pairs={{0,18},{1,19},{2,16},{3,17},{16,2},{17,3},{18,0},{19,1},{4,22},{5,... | collective-permute-start | bytes 368648 | tf_op jit(solution)/shard_map/ppermute | solution.py:332
  38.3 0.5 collective-permute-start.5
  38.8 0.5 collective-permute-start.6
  39.4 1.1 %collective-permute-done.3.refs_2_ = bf16[120,512]{1,0:T(8,128)(2,1)S(1)} collective-permute-done((bf16[120,512]{1,0:T(8,128)(2,1)S(1)}, bf16[120,512]{1,0:T(8,128)(2,1)S(1)}, u32[]{:S(2)}, u32[]{:S(2)}) %collective-permute-start.3) | collective-permute-done | bytes 122912 | tf_op jit(solution)/shard_map/ppermute | solution.py:332
  40.5 2.5 %collective-permute-start.7 = (bf16[120,512]{1,0:T(8,128)(2,1)S(1)}, bf16[120,512]{1,0:T(8,128)(2,1)S(1)}, u32[]{:S(2)}, u32[]{:S(2)}) collective-permute-start(bf16[120,512]{1,0:T(8,128)(2,1)S(1)} %get-tuple-element.51), channel_id=1, source_target_pairs={{0,18},{1,19},{2,16},{3,17},{16,2},{17,3},{18,0},{19,1},{4,22},{5,... | collective-permute-start | bytes 368648 | tf_op jit(solution)/shard_map/ppermute | solution.py:332
  43.0 0.7 shard_map.61
  44.1 1.5 %collective-permute-start.23 = (bf16[512,128]{1,0:T(8,128)(2,1)S(1)}, bf16[512,128]{1,0:T(8,128)(2,1)S(1)}, u32[]{:S(2)}, u32[]{:S(2)}) collective-permute-start(bf16[512,128]{1,0:T(8,128)(2,1)S(1)} %get-tuple-element.67), channel_id=1, source_target_pairs={{0,16},{16,0},{1,17},{17,1},{2,18},{18,2},{3,19},{19,3},{4,20},{20... | collective-permute-start | bytes 393224 | tf_op jit(solution)/shard_map/ppermute | solution.py:364
  45.6 0.5 collective-permute-start.18
  46.4 1.3 %collective-permute-done.7.refs_3_ = bf16[120,512]{1,0:T(8,128)(2,1)S(1)} collective-permute-done((bf16[120,512]{1,0:T(8,128)(2,1)S(1)}, bf16[120,512]{1,0:T(8,128)(2,1)S(1)}, u32[]{:S(2)}, u32[]{:S(2)}) %collective-permute-start.7) | collective-permute-done | bytes 122912 | tf_op jit(solution)/shard_map/ppermute | solution.py:332
  48.6 0.8 %collective-permute-start.31 = (bf16[256,256]{1,0:T(8,128)(2,1)S(1)}, bf16[256,256]{1,0:T(8,128)(2,1)S(1)}, u32[]{:S(2)}, u32[]{:S(2)}) collective-permute-start(bf16[256,256]{1,0:T(8,128)(2,1)S(1)} %get-tuple-element.78), channel_id=1, source_target_pairs={{0,8},{4,12},{8,0},{12,4},{1,9},{5,13},{9,1},{13,5},{2,10},{6,14},... | collective-permute-start | bytes 393224 | tf_op jit(solution)/shard_map/ppermute | solution.py:397
  49.5 3.2 %collective-permute-start.29 = (bf16[256,256]{1,0:T(8,128)(2,1)S(1)}, bf16[256,256]{1,0:T(8,128)(2,1)S(1)}, u32[]{:S(2)}, u32[]{:S(2)}) collective-permute-start(bf16[256,256]{1,0:T(8,128)(2,1)S(1)} %get-tuple-element.76), channel_id=1, source_target_pairs={{0,12},{4,8},{8,4},{12,0},{1,13},{5,9},{9,5},{13,1},{2,14},{6,10},... | collective-permute-start | bytes 393224 | tf_op jit(solution)/shard_map/ppermute | solution.py:397
  52.7 0.5 collective-permute-start.30
  53.2 0.5 shard_map.64
  53.6 3.0 %collective-permute-start.24 = (bf16[256,128]{1,0:T(8,128)(2,1)S(1)}, bf16[256,128]{1,0:T(8,128)(2,1)S(1)}, u32[]{:S(2)}, u32[]{:S(2)}) collective-permute-start(bf16[256,128]{1,0:T(8,128)(2,1)S(1)} %get-tuple-element.69), channel_id=1, source_target_pairs={{0,12},{4,8},{8,4},{12,0},{1,13},{5,9},{9,5},{13,1},{2,14},{6,10},... | collective-permute-start | bytes 196616 | tf_op jit(solution)/shard_map/ppermute | solution.py:397
  56.6 0.5 shard_map.62
  57.1 3.8 %collective-permute-done.31.refs_3_ = bf16[256,256]{1,0:T(8,128)(2,1)S(1)} collective-permute-done((bf16[256,256]{1,0:T(8,128)(2,1)S(1)}, bf16[256,256]{1,0:T(8,128)(2,1)S(1)}, u32[]{:S(2)}, u32[]{:S(2)}) %collective-permute-start.31) | collective-permute-done | bytes 131104 | tf_op jit(solution)/shard_map/ppermute | solution.py:397
  60.9 2.8 %collective-permute-start.19 = (bf16[256,128]{1,0:T(8,128)(2,1)S(1)}, bf16[256,128]{1,0:T(8,128)(2,1)S(1)}, u32[]{:S(2)}, u32[]{:S(2)}) collective-permute-start(bf16[256,128]{1,0:T(8,128)(2,1)S(1)} %get-tuple-element.63), channel_id=1, source_target_pairs={{0,12},{4,8},{8,4},{12,0},{1,13},{5,9},{9,5},{13,1},{2,14},{6,10},... | collective-permute-start | bytes 196616 | tf_op jit(solution)/shard_map/ppermute | solution.py:397
  63.7 3.9 %collective-permute-start.20 = (bf16[256,128]{1,0:T(8,128)(2,1)S(1)}, bf16[256,128]{1,0:T(8,128)(2,1)S(1)}, u32[]{:S(2)}, u32[]{:S(2)}) collective-permute-start(bf16[256,128]{1,0:T(8,128)(2,1)S(1)} %get-tuple-element.64), channel_id=1, source_target_pairs={{0,4},{4,0},{8,12},{12,8},{1,5},{5,1},{9,13},{13,9},{2,6},{6,2},{1... | collective-permute-start | bytes 196616 | tf_op jit(solution)/shard_map/ppermute | solution.py:397
  67.7 1.4 %collective-permute-start.21 = (bf16[256,128]{1,0:T(8,128)(2,1)S(1)}, bf16[256,128]{1,0:T(8,128)(2,1)S(1)}, u32[]{:S(2)}, u32[]{:S(2)}) collective-permute-start(bf16[256,128]{1,0:T(8,128)(2,1)S(1)} %get-tuple-element.65), channel_id=1, source_target_pairs={{0,8},{4,12},{8,0},{12,4},{1,9},{5,13},{9,1},{13,5},{2,10},{6,14},... | collective-permute-start | bytes 196616 | tf_op jit(solution)/shard_map/ppermute | solution.py:397
  69.1 0.9 %collective-permute-start.32 = (bf16[256,256]{1,0:T(8,128)(2,1)S(1)}, bf16[256,256]{1,0:T(8,128)(2,1)S(1)}, u32[]{:S(2)}, u32[]{:S(2)}) collective-permute-start(bf16[256,256]{1,0:T(8,128)(2,1)S(1)} %shard_map.68.refs_0_), channel_id=1, source_target_pairs={{0,16},{16,0},{1,17},{17,1},{2,18},{18,2},{3,19},{19,3},{4,20},{20... | collective-permute-start | bytes 393224 | tf_op jit(solution)/shard_map/ppermute | solution.py:412
  70.0 1.2 %collective-permute-start.27 = (bf16[256,128]{1,0:T(8,128)(2,1)S(1)}, bf16[256,128]{1,0:T(8,128)(2,1)S(1)}, u32[]{:S(2)}, u32[]{:S(2)}) collective-permute-start(bf16[256,128]{1,0:T(8,128)(2,1)S(1)} %shard_map.65.refs_3_), channel_id=1, source_target_pairs={{0,16},{16,0},{1,17},{17,1},{2,18},{18,2},{3,19},{19,3},{4,20},{20... | collective-permute-start | bytes 196616 | tf_op jit(solution)/shard_map/ppermute | solution.py:412
  71.2 1.8 %collective-permute-done.21.refs_3_ = bf16[256,128]{1,0:T(8,128)(2,1)S(1)} collective-permute-done((bf16[256,128]{1,0:T(8,128)(2,1)S(1)}, bf16[256,128]{1,0:T(8,128)(2,1)S(1)}, u32[]{:S(2)}, u32[]{:S(2)}) %collective-permute-start.21) | collective-permute-done | bytes 65568 | tf_op jit(solution)/shard_map/ppermute | solution.py:397
  73.1 0.8 %collective-permute-start.22 = (bf16[256,128]{1,0:T(8,128)(2,1)S(1)}, bf16[256,128]{1,0:T(8,128)(2,1)S(1)}, u32[]{:S(2)}, u32[]{:S(2)}) collective-permute-start(bf16[256,128]{1,0:T(8,128)(2,1)S(1)} %shard_map.63.refs_2_), channel_id=1, source_target_pairs={{0,16},{16,0},{1,17},{17,1},{2,18},{18,2},{3,19},{19,3},{4,20},{20... | collective-permute-start | bytes 196616 | tf_op jit(solution)/shard_map/ppermute | solution.py:412
  74.0 0.8 shard_map.69.refs_2_
  74.8 2.6 %collective-permute-done.22.refs_0_ = bf16[256,128]{1,0:T(8,128)(2,1)S(1)} collective-permute-done((bf16[256,128]{1,0:T(8,128)(2,1)S(1)}, bf16[256,128]{1,0:T(8,128)(2,1)S(1)}, u32[]{:S(2)}, u32[]{:S(2)}) %collective-permute-start.22) | collective-permute-done | bytes 65568 | tf_op jit(solution)/shard_map/ppermute | solution.py:412
  77.4 0.7 shard_map.70
  (38 shorter events, 2.0 us)
Async XLA Ops:
  0.0 0.7 copy-start.1
  0.0 10.6 %collective-permute-start.8 = (bf16[192,2048]{1,0:T(8,128)(2,1)}, bf16[192,2048]{1,0:T(8,128)(2,1)S(1)}, u32[]{:S(2)}, u32[]{:S(2)}) collective-permute-start(bf16[192,2048]{1,0:T(8,128)(2,1)} %refs_2_.2), channel_id=1, source_target_pairs={{0,1},{1,0},{2,3},{3,2},{4,5},{5,4},{6,7},{7,6},{8,9},{9,8},{10,11... | collective-permute-start | bytes 2359304 | tf_op jit(solution)/shard_map/ppermute | solution.py:283
  0.5 29.9 %collective-permute-start.1 = (bf16[192,2048]{1,0:T(8,128)(2,1)}, bf16[192,2048]{1,0:T(8,128)(2,1)S(1)}, u32[]{:S(2)}, u32[]{:S(2)}) collective-permute-start(bf16[192,2048]{1,0:T(8,128)(2,1)} %refs_2_.3), channel_id=1, source_target_pairs={{0,1},{1,0},{2,3},{3,2},{4,5},{5,4},{6,7},{7,6},{8,9},{9,8},{10,11... | collective-permute-start | bytes 2359304 | tf_op jit(solution)/shard_map/ppermute | solution.py:285
  0.7 3.1 %collective-permute-start = (s32[1,192]{1,0:T(1,128)S(1)}, s32[1,192]{1,0:T(1,128)S(1)}, u32[]{:S(2)}, u32[]{:S(2)}) collective-permute-start(s32[1,192]{1,0:T(1,128)S(1)} %bitcast.4), channel_id=1, source_target_pairs={{0,1},{1,0},{2,3},{3,2},{4,5},{5,4},{6,7},{7,6},{8,9},{9,8},{10,11... | collective-permute-start | bytes 2312 | tf_op jit(solution)/shard_map/ppermute | solution.py:284
  5.0 9.4 %collective-permute-start.12 = (bf16[256,256]{1,0:T(8,128)(2,1)S(1)}, bf16[256,256]{1,0:T(8,128)(2,1)S(1)}, u32[]{:S(2)}, u32[]{:S(2)}) collective-permute-start(bf16[256,256]{1,0:T(8,128)(2,1)S(1)} %get-tuple-element.57.refs_4_), channel_id=1, source_target_pairs={{0,4},{4,0},{8,12},{12,8},{1,5},{5,1},{9,13},{13,9},{2,6},{6,2},{1... | collective-permute-start | bytes 393224 | tf_op jit(solution)/shard_map/ppermute | solution.py:307
  8.0 9.0 %collective-permute-start.13 = (bf16[256,256]{1,0:T(8,128)(2,1)S(1)}, bf16[256,256]{1,0:T(8,128)(2,1)S(1)}, u32[]{:S(2)}, u32[]{:S(2)}) collective-permute-start(bf16[256,256]{1,0:T(8,128)(2,1)S(1)} %get-tuple-element.57.refs_4_), channel_id=1, source_target_pairs={{0,8},{4,12},{8,0},{12,4},{1,9},{5,13},{9,1},{13,5},{2,10},{6,14},... | collective-permute-start | bytes 393224 | tf_op jit(solution)/shard_map/ppermute | solution.py:307
  11.3 19.1 %copy-start = (bf16[192,2048]{1,0:T(8,128)(2,1)S(1)}, bf16[192,2048]{1,0:T(8,128)(2,1)}, u32[]{:S(2)}) copy-start(bf16[192,2048]{1,0:T(8,128)(2,1)} %refs_2_.3) | copy-start | bytes 2359300
  11.3 13.6 %collective-permute-start.10 = (bf16[120,1024]{1,0:T(8,128)(2,1)S(1)}, bf16[120,1024]{1,0:T(8,128)(2,1)S(1)}, u32[]{:S(2)}, u32[]{:S(2)}) collective-permute-start(bf16[120,1024]{1,0:T(8,128)(2,1)S(1)} %get-tuple-element.55), channel_id=1, source_target_pairs={{0,16},{1,17},{2,18},{3,19},{16,0},{17,1},{18,2},{19,3},{4,20},{5,... | collective-permute-start | bytes 737288 | tf_op jit(solution)/shard_map/ppermute | solution.py:332
  12.9 13.9 %collective-permute-start.11 = (bf16[120,1024]{1,0:T(8,128)(2,1)S(1)}, bf16[120,1024]{1,0:T(8,128)(2,1)S(1)}, u32[]{:S(2)}, u32[]{:S(2)}) collective-permute-start(bf16[120,1024]{1,0:T(8,128)(2,1)S(1)} %get-tuple-element.56), channel_id=1, source_target_pairs={{0,18},{1,19},{2,16},{3,17},{16,2},{17,3},{18,0},{19,1},{4,22},{5,... | collective-permute-start | bytes 737288 | tf_op jit(solution)/shard_map/ppermute | solution.py:332
  14.4 13.9 %collective-permute-start.9 = (bf16[120,1024]{1,0:T(8,128)(2,1)S(1)}, bf16[120,1024]{1,0:T(8,128)(2,1)S(1)}, u32[]{:S(2)}, u32[]{:S(2)}) collective-permute-start(bf16[120,1024]{1,0:T(8,128)(2,1)S(1)} %get-tuple-element.54), channel_id=1, source_target_pairs={{0,2},{1,3},{2,0},{3,1},{16,18},{17,19},{18,16},{19,17},{4,6},{5,7... | collective-permute-start | bytes 737288 | tf_op jit(solution)/shard_map/ppermute | solution.py:332
  17.0 6.9 %collective-permute-start.14 = (bf16[256,256]{1,0:T(8,128)(2,1)S(1)}, bf16[256,256]{1,0:T(8,128)(2,1)S(1)}, u32[]{:S(2)}, u32[]{:S(2)}) collective-permute-start(bf16[256,256]{1,0:T(8,128)(2,1)S(1)} %get-tuple-element.57.refs_4_), channel_id=1, source_target_pairs={{0,12},{4,8},{8,4},{12,0},{1,13},{5,9},{9,5},{13,1},{2,14},{6,10},... | collective-permute-start | bytes 393224 | tf_op jit(solution)/shard_map/ppermute | solution.py:307
  23.9 8.8 %collective-permute-start.15 = (bf16[256,256]{1,0:T(8,128)(2,1)S(1)}, bf16[256,256]{1,0:T(8,128)(2,1)S(1)}, u32[]{:S(2)}, u32[]{:S(2)}) collective-permute-start(bf16[256,256]{1,0:T(8,128)(2,1)S(1)} %get-tuple-element.59.refs_1_), channel_id=1, source_target_pairs={{0,4},{4,0},{8,12},{12,8},{1,5},{5,1},{9,13},{13,9},{2,6},{6,2},{1... | collective-permute-start | bytes 393224 | tf_op jit(solution)/shard_map/ppermute | solution.py:307
  24.9 10.9 %collective-permute-start.16 = (bf16[256,256]{1,0:T(8,128)(2,1)S(1)}, bf16[256,256]{1,0:T(8,128)(2,1)S(1)}, u32[]{:S(2)}, u32[]{:S(2)}) collective-permute-start(bf16[256,256]{1,0:T(8,128)(2,1)S(1)} %get-tuple-element.59.refs_1_), channel_id=1, source_target_pairs={{0,8},{4,12},{8,0},{12,4},{1,9},{5,13},{9,1},{13,5},{2,10},{6,14},... | collective-permute-start | bytes 393224 | tf_op jit(solution)/shard_map/ppermute | solution.py:307
  26.8 11.5 %collective-permute-start.17 = (bf16[256,256]{1,0:T(8,128)(2,1)S(1)}, bf16[256,256]{1,0:T(8,128)(2,1)S(1)}, u32[]{:S(2)}, u32[]{:S(2)}) collective-permute-start(bf16[256,256]{1,0:T(8,128)(2,1)S(1)} %get-tuple-element.59.refs_1_), channel_id=1, source_target_pairs={{0,12},{4,8},{8,4},{12,0},{1,13},{5,9},{9,5},{13,1},{2,14},{6,10},... | collective-permute-start | bytes 393224 | tf_op jit(solution)/shard_map/ppermute | solution.py:307
  28.9 19.1 %collective-permute-start.28 = (bf16[512,256]{1,0:T(8,128)(2,1)S(1)}, bf16[512,256]{1,0:T(8,128)(2,1)S(1)}, u32[]{:S(2)}, u32[]{:S(2)}) collective-permute-start(bf16[512,256]{1,0:T(8,128)(2,1)S(1)} %get-tuple-element.73), channel_id=1, source_target_pairs={{0,16},{16,0},{1,17},{17,1},{2,18},{18,2},{3,19},{19,3},{4,20},{20... | collective-permute-start | bytes 786440 | tf_op jit(solution)/shard_map/ppermute | solution.py:364
  31.2 7.7 %collective-permute-start.2 = (bf16[120,512]{1,0:T(8,128)(2,1)S(1)}, bf16[120,512]{1,0:T(8,128)(2,1)S(1)}, u32[]{:S(2)}, u32[]{:S(2)}) collective-permute-start(bf16[120,512]{1,0:T(8,128)(2,1)S(1)} %get-tuple-element.45), channel_id=1, source_target_pairs={{0,2},{1,3},{2,0},{3,1},{16,18},{17,19},{18,16},{19,17},{4,6},{5,7... | collective-permute-start | bytes 368648 | tf_op jit(solution)/shard_map/ppermute | solution.py:332
  32.7 7.7 %collective-permute-start.3 = (bf16[120,512]{1,0:T(8,128)(2,1)S(1)}, bf16[120,512]{1,0:T(8,128)(2,1)S(1)}, u32[]{:S(2)}, u32[]{:S(2)}) collective-permute-start(bf16[120,512]{1,0:T(8,128)(2,1)S(1)} %get-tuple-element.46), channel_id=1, source_target_pairs={{0,16},{1,17},{2,18},{3,19},{16,0},{17,1},{18,2},{19,3},{4,20},{5,... | collective-permute-start | bytes 368648 | tf_op jit(solution)/shard_map/ppermute | solution.py:332
  35.9 8.3 %collective-permute-start.4 = (bf16[120,512]{1,0:T(8,128)(2,1)S(1)}, bf16[120,512]{1,0:T(8,128)(2,1)S(1)}, u32[]{:S(2)}, u32[]{:S(2)}) collective-permute-start(bf16[120,512]{1,0:T(8,128)(2,1)S(1)} %get-tuple-element.47), channel_id=1, source_target_pairs={{0,18},{1,19},{2,16},{3,17},{16,2},{17,3},{18,0},{19,1},{4,22},{5,... | collective-permute-start | bytes 368648 | tf_op jit(solution)/shard_map/ppermute | solution.py:332
  38.3 7.3 %collective-permute-start.5 = (bf16[120,512]{1,0:T(8,128)(2,1)S(1)}, bf16[120,512]{1,0:T(8,128)(2,1)S(1)}, u32[]{:S(2)}, u32[]{:S(2)}) collective-permute-start(bf16[120,512]{1,0:T(8,128)(2,1)S(1)} %get-tuple-element.49), channel_id=1, source_target_pairs={{0,2},{1,3},{2,0},{3,1},{16,18},{17,19},{18,16},{19,17},{4,6},{5,7... | collective-permute-start | bytes 368648 | tf_op jit(solution)/shard_map/ppermute | solution.py:332
  38.8 7.6 %collective-permute-start.6 = (bf16[120,512]{1,0:T(8,128)(2,1)S(1)}, bf16[120,512]{1,0:T(8,128)(2,1)S(1)}, u32[]{:S(2)}, u32[]{:S(2)}) collective-permute-start(bf16[120,512]{1,0:T(8,128)(2,1)S(1)} %get-tuple-element.50), channel_id=1, source_target_pairs={{0,16},{1,17},{2,18},{3,19},{16,0},{17,1},{18,2},{19,3},{4,20},{5,... | collective-permute-start | bytes 368648 | tf_op jit(solution)/shard_map/ppermute | solution.py:332
  40.5 7.3 %collective-permute-start.7 = (bf16[120,512]{1,0:T(8,128)(2,1)S(1)}, bf16[120,512]{1,0:T(8,128)(2,1)S(1)}, u32[]{:S(2)}, u32[]{:S(2)}) collective-permute-start(bf16[120,512]{1,0:T(8,128)(2,1)S(1)} %get-tuple-element.51), channel_id=1, source_target_pairs={{0,18},{1,19},{2,16},{3,17},{16,2},{17,3},{18,0},{19,1},{4,22},{5,... | collective-permute-start | bytes 368648 | tf_op jit(solution)/shard_map/ppermute | solution.py:332
  44.1 9.0 %collective-permute-start.23 = (bf16[512,128]{1,0:T(8,128)(2,1)S(1)}, bf16[512,128]{1,0:T(8,128)(2,1)S(1)}, u32[]{:S(2)}, u32[]{:S(2)}) collective-permute-start(bf16[512,128]{1,0:T(8,128)(2,1)S(1)} %get-tuple-element.67), channel_id=1, source_target_pairs={{0,16},{16,0},{1,17},{17,1},{2,18},{18,2},{3,19},{19,3},{4,20},{20... | collective-permute-start | bytes 393224 | tf_op jit(solution)/shard_map/ppermute | solution.py:364
  45.6 11.0 %collective-permute-start.18 = (bf16[512,128]{1,0:T(8,128)(2,1)S(1)}, bf16[512,128]{1,0:T(8,128)(2,1)S(1)}, u32[]{:S(2)}, u32[]{:S(2)}) collective-permute-start(bf16[512,128]{1,0:T(8,128)(2,1)S(1)} %get-tuple-element.61), channel_id=1, source_target_pairs={{0,16},{16,0},{1,17},{17,1},{2,18},{18,2},{3,19},{19,3},{4,20},{20... | collective-permute-start | bytes 393224 | tf_op jit(solution)/shard_map/ppermute | solution.py:364
  48.6 12.2 %collective-permute-start.31 = (bf16[256,256]{1,0:T(8,128)(2,1)S(1)}, bf16[256,256]{1,0:T(8,128)(2,1)S(1)}, u32[]{:S(2)}, u32[]{:S(2)}) collective-permute-start(bf16[256,256]{1,0:T(8,128)(2,1)S(1)} %get-tuple-element.78), channel_id=1, source_target_pairs={{0,8},{4,12},{8,0},{12,4},{1,9},{5,13},{9,1},{13,5},{2,10},{6,14},... | collective-permute-start | bytes 393224 | tf_op jit(solution)/shard_map/ppermute | solution.py:397
  49.5 11.4 %collective-permute-start.29 = (bf16[256,256]{1,0:T(8,128)(2,1)S(1)}, bf16[256,256]{1,0:T(8,128)(2,1)S(1)}, u32[]{:S(2)}, u32[]{:S(2)}) collective-permute-start(bf16[256,256]{1,0:T(8,128)(2,1)S(1)} %get-tuple-element.76), channel_id=1, source_target_pairs={{0,12},{4,8},{8,4},{12,0},{1,13},{5,9},{9,5},{13,1},{2,14},{6,10},... | collective-permute-start | bytes 393224 | tf_op jit(solution)/shard_map/ppermute | solution.py:397
  52.7 11.1 %collective-permute-start.30 = (bf16[256,256]{1,0:T(8,128)(2,1)S(1)}, bf16[256,256]{1,0:T(8,128)(2,1)S(1)}, u32[]{:S(2)}, u32[]{:S(2)}) collective-permute-start(bf16[256,256]{1,0:T(8,128)(2,1)S(1)} %get-tuple-element.77), channel_id=1, source_target_pairs={{0,4},{4,0},{8,12},{12,8},{1,5},{5,1},{9,13},{13,9},{2,6},{6,2},{1... | collective-permute-start | bytes 393224 | tf_op jit(solution)/shard_map/ppermute | solution.py:397
  53.6 14.0 %collective-permute-start.24 = (bf16[256,128]{1,0:T(8,128)(2,1)S(1)}, bf16[256,128]{1,0:T(8,128)(2,1)S(1)}, u32[]{:S(2)}, u32[]{:S(2)}) collective-permute-start(bf16[256,128]{1,0:T(8,128)(2,1)S(1)} %get-tuple-element.69), channel_id=1, source_target_pairs={{0,12},{4,8},{8,4},{12,0},{1,13},{5,9},{9,5},{13,1},{2,14},{6,10},... | collective-permute-start | bytes 196616 | tf_op jit(solution)/shard_map/ppermute | solution.py:397
  56.6 12.4 %collective-permute-start.25 = (bf16[256,128]{1,0:T(8,128)(2,1)S(1)}, bf16[256,128]{1,0:T(8,128)(2,1)S(1)}, u32[]{:S(2)}, u32[]{:S(2)}) collective-permute-start(bf16[256,128]{1,0:T(8,128)(2,1)S(1)} %get-tuple-element.70), channel_id=1, source_target_pairs={{0,4},{4,0},{8,12},{12,8},{1,5},{5,1},{9,13},{13,9},{2,6},{6,2},{1... | collective-permute-start | bytes 196616 | tf_op jit(solution)/shard_map/ppermute | solution.py:397
  60.9 9.0 %collective-permute-start.26 = (bf16[256,128]{1,0:T(8,128)(2,1)S(1)}, bf16[256,128]{1,0:T(8,128)(2,1)S(1)}, u32[]{:S(2)}, u32[]{:S(2)}) collective-permute-start(bf16[256,128]{1,0:T(8,128)(2,1)S(1)} %get-tuple-element.71), channel_id=1, source_target_pairs={{0,8},{4,12},{8,0},{12,4},{1,9},{5,13},{9,1},{13,5},{2,10},{6,14},... | collective-permute-start | bytes 196616 | tf_op jit(solution)/shard_map/ppermute | solution.py:397
  60.9 10.3 %collective-permute-start.19 = (bf16[256,128]{1,0:T(8,128)(2,1)S(1)}, bf16[256,128]{1,0:T(8,128)(2,1)S(1)}, u32[]{:S(2)}, u32[]{:S(2)}) collective-permute-start(bf16[256,128]{1,0:T(8,128)(2,1)S(1)} %get-tuple-element.63), channel_id=1, source_target_pairs={{0,12},{4,8},{8,4},{12,0},{1,13},{5,9},{9,5},{13,1},{2,14},{6,10},... | collective-permute-start | bytes 196616 | tf_op jit(solution)/shard_map/ppermute | solution.py:397
  63.7 7.5 %collective-permute-start.20 = (bf16[256,128]{1,0:T(8,128)(2,1)S(1)}, bf16[256,128]{1,0:T(8,128)(2,1)S(1)}, u32[]{:S(2)}, u32[]{:S(2)}) collective-permute-start(bf16[256,128]{1,0:T(8,128)(2,1)S(1)} %get-tuple-element.64), channel_id=1, source_target_pairs={{0,4},{4,0},{8,12},{12,8},{1,5},{5,1},{9,13},{13,9},{2,6},{6,2},{1... | collective-permute-start | bytes 196616 | tf_op jit(solution)/shard_map/ppermute | solution.py:397
  67.7 5.4 %collective-permute-start.21 = (bf16[256,128]{1,0:T(8,128)(2,1)S(1)}, bf16[256,128]{1,0:T(8,128)(2,1)S(1)}, u32[]{:S(2)}, u32[]{:S(2)}) collective-permute-start(bf16[256,128]{1,0:T(8,128)(2,1)S(1)} %get-tuple-element.65), channel_id=1, source_target_pairs={{0,8},{4,12},{8,0},{12,4},{1,9},{5,13},{9,1},{13,5},{2,10},{6,14},... | collective-permute-start | bytes 196616 | tf_op jit(solution)/shard_map/ppermute | solution.py:397
  69.1 5.0 %collective-permute-start.32 = (bf16[256,256]{1,0:T(8,128)(2,1)S(1)}, bf16[256,256]{1,0:T(8,128)(2,1)S(1)}, u32[]{:S(2)}, u32[]{:S(2)}) collective-permute-start(bf16[256,256]{1,0:T(8,128)(2,1)S(1)} %shard_map.68.refs_0_), channel_id=1, source_target_pairs={{0,16},{16,0},{1,17},{17,1},{2,18},{18,2},{3,19},{19,3},{4,20},{20... | collective-permute-start | bytes 393224 | tf_op jit(solution)/shard_map/ppermute | solution.py:412
  70.0 4.8 %collective-permute-start.27 = (bf16[256,128]{1,0:T(8,128)(2,1)S(1)}, bf16[256,128]{1,0:T(8,128)(2,1)S(1)}, u32[]{:S(2)}, u32[]{:S(2)}) collective-permute-start(bf16[256,128]{1,0:T(8,128)(2,1)S(1)} %shard_map.65.refs_3_), channel_id=1, source_target_pairs={{0,16},{16,0},{1,17},{17,1},{2,18},{18,2},{3,19},{19,3},{4,20},{20... | collective-permute-start | bytes 196616 | tf_op jit(solution)/shard_map/ppermute | solution.py:412
  73.1 4.3 %collective-permute-start.22 = (bf16[256,128]{1,0:T(8,128)(2,1)S(1)}, bf16[256,128]{1,0:T(8,128)(2,1)S(1)}, u32[]{:S(2)}, u32[]{:S(2)}) collective-permute-start(bf16[256,128]{1,0:T(8,128)(2,1)S(1)} %shard_map.63.refs_2_), channel_id=1, source_target_pairs={{0,16},{16,0},{1,17},{17,1},{2,18},{18,2},{3,19},{19,3},{4,20},{20... | collective-permute-start | bytes 196616 | tf_op jit(solution)/shard_map/ppermute | solution.py:412

commit v10 on v9

--- a/solution.py
+++ b/solution.py
@@ -7,7 +7,7 @@
 from jax.sharding import PartitionSpec as P
 
 QB = 32
-SPLITS = ((2,), (1, 1))
+SPLITS = ((1, 1), (1, 1))
 F32 = jnp.float32
 BF16 = jnp.bfloat16
 
@@ -58,8 +58,9 @@
     if not aligned:
         return [every], [([i], every) for i in range(chunks)], [[i] for i in range(chunks)]
     early, late = order[: nodes // 2], order[nodes // 2 :] + [0]
-    jobs = [([0], early), ([0], late)] + [([i], every) for i in range(1, chunks)]
-    return [early, late], jobs, [[i] for i in range(chunks)]
+    jobs = [([0], early), ([1], early), ([0, 1], late)]
+    jobs += [([i], every) for i in range(2, chunks)]
+    return [early, late], jobs, [[0, 1]] + [[i] for i in range(2, chunks)]
 
 
 def slots_of(copies, pairs):

time: 78.3 us -> 86.3 us (1.10)
  starting transfers between devices: 48.2 us -> 52.1 us
  waiting for transfers between devices: 22 us -> 25.4 us
    ppermute x6, waiting for transfers between devices: 8.21 us -> 14.2 us  [on_device(): lax.ppermute(chunk, 'node', [(a, mate(a, s, nodes)) for a in range(nodes)])]
    ppermute x9 -> x11, starting transfers between devices: 15.6 us -> 21.3 us  [on_device(): moved = lax.ppermute(term, 'node', links)]
    ppermute x9 -> x11, waiting for transfers between devices: 5.62 us -> 1.11 us  [on_device(): moved = lax.ppermute(term, 'node', links)]
    ppermute x9, waiting for transfers between devices: 2.86 us -> 5.92 us  [exchange(): moved[at] = lax.ppermute(pieces[at], ('dp', 'local'), links)]
    ppermute x6, starting transfers between devices: 12.4 us -> 9.72 us  [on_device(): lax.ppermute(chunk, 'node', [(a, mate(a, s, nodes)) for a in range(nodes)])]
    ppermute x3, waiting for transfers between devices: 2.7 us -> 1.64 us  [on_device(): finished.append(lax.ppermute(summed, 'dp', links))]
    ppermute x3, starting transfers between devices: 2.94 us -> 4 us  [on_device(): finished.append(lax.ppermute(summed, 'dp', links))]
    pallas_call x16 -> x17, Pallas kernels: 7.6 us -> 8.24 us  [call(): pl.pallas_call(kernel, out_shape=outs, in_specs=[pl.BlockSpec(memory_spac...]
  transfers between devices with their start and end apart: 33 -> 36, of which waited for: 11 -> 10; matrix products, arithmetic and copies ran while one was open for 0% -> 0% of each run, Pallas kernels for 9% -> 9%
where the time goes in v10:
time: 86.3 us; the launch traced here: 86.1 us
  starting transfers between devices  52.1 us (60%)
  waiting for transfers between devices  25.4 us (29%)
  Pallas kernels  8.24 us (10%)
    ppermute x11, starting transfers between devices, on_device(): moved = lax.ppermute(term, 'node', links)  21.3 us
    ppermute x6, waiting for transfers between devices, on_device(): lax.ppermute(chunk, 'node', [(a, mate(a, s, nodes)) for a in range(nodes)])  14.2 us
    ppermute x9, starting transfers between devices, exchange(): moved[at] = lax.ppermute(pieces[at], ('dp', 'local'), links)  11.8 us
    ppermute x6, starting transfers between devices, on_device(): lax.ppermute(chunk, 'node', [(a, mate(a, s, nodes)) for a in range(nodes)])  9.72 us
    pallas_call x17, Pallas kernels, call(): pl.pallas_call(kernel, out_shape=outs, in_specs=[pl.BlockSpec(memory_spac...  8.24 us
    ppermute x9, waiting for transfers between devices, exchange(): moved[at] = lax.ppermute(pieces[at], ('dp', 'local'), links)  5.92 us
    ppermute x4, starting transfers between devices, on_device(): acts.append([kept, lax.ppermute(sent, 'dp', [(0, 1), (1, 0)])])  4.18 us
    ppermute x3, starting transfers between devices, on_device(): finished.append(lax.ppermute(summed, 'dp', links))  4 us
  transfers between devices with their start and end apart: 36, of which 10 were waited for; matrix products, arithmetic and copies ran while one was open for 0% of the time, Pallas kernels for 9%

profile of v10, /device:TPU:0, one launch (start us, length us, event | category | flops | bytes accessed | tf_op | source)
XLA Modules:
  0.0 86.1 jit_solution(9167556412874431730)
XLA Ops:
  0.0 0.5 collective-permute-start.8
  0.7 0.5 collective-permute-start
  1.2 2.6 %collective-permute-done.refs_1_ = s32[1,192]{1,0:T(1,128)S(1)} collective-permute-done((s32[1,192]{1,0:T(1,128)S(1)}, s32[1,192]{1,0:T(1,128)S(1)}, u32[]{:S(2)}, u32[]{:S(2)}) %collective-permute-start) | collective-permute-done | bytes 800 | tf_op jit(solution)/shard_map/ppermute | solution.py:285
  3.7 1.3 %shard_map.55 = (bf16[256,192]{1,0:T(8,128)(2,1)S(1)}, bf16[256,192]{1,0:T(8,128)(2,1)S(1)}, bf16[192,2048]{1,0:T(8,128)(2,1)S(1)}, bf16[256,256]{1,0:T(8,128)(2,1)S(1)}, bf16[256,256]{1,0:T(8,128)(2,1)S(1)}) custom-call(s32[1,192]{1,0:T(1,128)S(1)} %bitcast.5, s32[1,192]{1,0:T(1,128)S(1)} %collective-permute-done.refs_1_, bf16[192,2048]{1,0:T(8,128)(2,1)} %refs_2_.2, ...), custom_call_target="tpu_custom_call" | custom-call | bytes 2573824 | tf_op jit(solution)/shard_map/pallas_call | solution.py:38
  5.0 3.0 %collective-permute-start.12 = (bf16[256,256]{1,0:T(8,128)(2,1)S(1)}, bf16[256,256]{1,0:T(8,128)(2,1)S(1)}, u32[]{:S(2)}, u32[]{:S(2)}) collective-permute-start(bf16[256,256]{1,0:T(8,128)(2,1)S(1)} %get-tuple-element.62.refs_4_), channel_id=1, source_target_pairs={{0,4},{4,0},{8,12},{12,8},{1,5},{5,1},{9,13},{13,9},{2,6},{6,2},{1... | collective-permute-start | bytes 393224 | tf_op jit(solution)/shard_map/ppermute | solution.py:308
  8.0 2.6 %collective-permute-start.13 = (bf16[256,256]{1,0:T(8,128)(2,1)S(1)}, bf16[256,256]{1,0:T(8,128)(2,1)S(1)}, u32[]{:S(2)}, u32[]{:S(2)}) collective-permute-start(bf16[256,256]{1,0:T(8,128)(2,1)S(1)} %get-tuple-element.62.refs_4_), channel_id=1, source_target_pairs={{0,8},{4,12},{8,0},{12,4},{1,9},{5,13},{9,1},{13,5},{2,10},{6,14},... | collective-permute-start | bytes 393224 | tf_op jit(solution)/shard_map/ppermute | solution.py:308
  10.6 0.9 %collective-permute-start.15 = (bf16[256,256]{1,0:T(8,128)(2,1)S(1)}, bf16[256,256]{1,0:T(8,128)(2,1)S(1)}, u32[]{:S(2)}, u32[]{:S(2)}) collective-permute-start(bf16[256,256]{1,0:T(8,128)(2,1)S(1)} %get-tuple-element.64.refs_1_), channel_id=1, source_target_pairs={{0,4},{4,0},{8,12},{12,8},{1,5},{5,1},{9,13},{13,9},{2,6},{6,2},{1... | collective-permute-start | bytes 393224 | tf_op jit(solution)/shard_map/ppermute | solution.py:308
  11.5 0.7 shard_map.59
  12.2 1.9 %collective-permute-done.12.refs_5_ = bf16[256,256]{1,0:T(8,128)(2,1)S(1)} collective-permute-done((bf16[256,256]{1,0:T(8,128)(2,1)S(1)}, bf16[256,256]{1,0:T(8,128)(2,1)S(1)}, u32[]{:S(2)}, u32[]{:S(2)}) %collective-permute-start.12) | collective-permute-done | bytes 131104 | tf_op jit(solution)/shard_map/ppermute | solution.py:308
  14.2 1.9 %collective-permute-start.10 = (bf16[120,1024]{1,0:T(8,128)(2,1)S(1)}, bf16[120,1024]{1,0:T(8,128)(2,1)S(1)}, u32[]{:S(2)}, u32[]{:S(2)}) collective-permute-start(bf16[120,1024]{1,0:T(8,128)(2,1)S(1)} %get-tuple-element.60), channel_id=1, source_target_pairs={{0,16},{1,17},{2,18},{3,19},{16,0},{17,1},{18,2},{19,3},{4,20},{5,... | collective-permute-start | bytes 737288 | tf_op jit(solution)/shard_map/ppermute | solution.py:333
  16.1 4.8 %collective-permute-done.13.refs_6_ = bf16[256,256]{1,0:T(8,128)(2,1)S(1)} collective-permute-done((bf16[256,256]{1,0:T(8,128)(2,1)S(1)}, bf16[256,256]{1,0:T(8,128)(2,1)S(1)}, u32[]{:S(2)}, u32[]{:S(2)}) %collective-permute-start.13) | collective-permute-done | bytes 131104 | tf_op jit(solution)/shard_map/ppermute | solution.py:308
  20.9 2.5 %collective-permute-start.11 = (bf16[120,1024]{1,0:T(8,128)(2,1)S(1)}, bf16[120,1024]{1,0:T(8,128)(2,1)S(1)}, u32[]{:S(2)}, u32[]{:S(2)}) collective-permute-start(bf16[120,1024]{1,0:T(8,128)(2,1)S(1)} %get-tuple-element.61), channel_id=1, source_target_pairs={{0,18},{1,19},{2,16},{3,17},{16,2},{17,3},{18,0},{19,1},{4,22},{5,... | collective-permute-start | bytes 737288 | tf_op jit(solution)/shard_map/ppermute | solution.py:333
  23.4 0.5 collective-permute-start.9
  23.9 1.9 %collective-permute-start.16 = (bf16[256,256]{1,0:T(8,128)(2,1)S(1)}, bf16[256,256]{1,0:T(8,128)(2,1)S(1)}, u32[]{:S(2)}, u32[]{:S(2)}) collective-permute-start(bf16[256,256]{1,0:T(8,128)(2,1)S(1)} %get-tuple-element.64.refs_1_), channel_id=1, source_target_pairs={{0,8},{4,12},{8,0},{12,4},{1,9},{5,13},{9,1},{13,5},{2,10},{6,14},... | collective-permute-start | bytes 393224 | tf_op jit(solution)/shard_map/ppermute | solution.py:308
  25.8 1.3 %collective-permute-start.17 = (bf16[256,256]{1,0:T(8,128)(2,1)S(1)}, bf16[256,256]{1,0:T(8,128)(2,1)S(1)}, u32[]{:S(2)}, u32[]{:S(2)}) collective-permute-start(bf16[256,256]{1,0:T(8,128)(2,1)S(1)} %get-tuple-element.64.refs_1_), channel_id=1, source_target_pairs={{0,12},{4,8},{8,4},{12,0},{1,13},{5,9},{9,5},{13,1},{2,14},{6,10},... | collective-permute-start | bytes 393224 | tf_op jit(solution)/shard_map/ppermute | solution.py:308
  27.1 0.7 shard_map.56
  27.9 7.4 %collective-permute-done.16.refs_3_ = bf16[256,256]{1,0:T(8,128)(2,1)S(1)} collective-permute-done((bf16[256,256]{1,0:T(8,128)(2,1)S(1)}, bf16[256,256]{1,0:T(8,128)(2,1)S(1)}, u32[]{:S(2)}, u32[]{:S(2)}) %collective-permute-start.16) | collective-permute-done | bytes 131104 | tf_op jit(solution)/shard_map/ppermute | solution.py:308
  35.3 0.5 collective-permute-start.2
  35.8 1.5 %collective-permute-start.3 = (bf16[120,512]{1,0:T(8,128)(2,1)S(1)}, bf16[120,512]{1,0:T(8,128)(2,1)S(1)}, u32[]{:S(2)}, u32[]{:S(2)}) collective-permute-start(bf16[120,512]{1,0:T(8,128)(2,1)S(1)} %get-tuple-element.51), channel_id=1, source_target_pairs={{0,16},{1,17},{2,18},{3,19},{16,0},{17,1},{18,2},{19,3},{4,20},{5,... | collective-permute-start | bytes 368648 | tf_op jit(solution)/shard_map/ppermute | solution.py:333
  37.3 1.5 %collective-permute-start.4 = (bf16[120,512]{1,0:T(8,128)(2,1)S(1)}, bf16[120,512]{1,0:T(8,128)(2,1)S(1)}, u32[]{:S(2)}, u32[]{:S(2)}) collective-permute-start(bf16[120,512]{1,0:T(8,128)(2,1)S(1)} %get-tuple-element.52), channel_id=1, source_target_pairs={{0,18},{1,19},{2,16},{3,17},{16,2},{17,3},{18,0},{19,1},{4,22},{5,... | collective-permute-start | bytes 368648 | tf_op jit(solution)/shard_map/ppermute | solution.py:333
  38.8 0.5 collective-permute-start.5
  39.3 1.5 %collective-permute-start.6 = (bf16[120,512]{1,0:T(8,128)(2,1)S(1)}, bf16[120,512]{1,0:T(8,128)(2,1)S(1)}, u32[]{:S(2)}, u32[]{:S(2)}) collective-permute-start(bf16[120,512]{1,0:T(8,128)(2,1)S(1)} %get-tuple-element.55), channel_id=1, source_target_pairs={{0,16},{1,17},{2,18},{3,19},{16,0},{17,1},{18,2},{19,3},{4,20},{5,... | collective-permute-start | bytes 368648 | tf_op jit(solution)/shard_map/ppermute | solution.py:333
  40.8 0.8 shard_map.60
  41.6 0.6 collective-permute-start.29
  42.2 1.5 %collective-permute-start.28 = (bf16[512,128]{1,0:T(8,128)(2,1)S(1)}, bf16[512,128]{1,0:T(8,128)(2,1)S(1)}, u32[]{:S(2)}, u32[]{:S(2)}) collective-permute-start(bf16[512,128]{1,0:T(8,128)(2,1)S(1)} %get-tuple-element.78), channel_id=1, source_target_pairs={{0,16},{16,0},{1,17},{17,1},{2,18},{18,2},{3,19},{19,3},{4,20},{20... | collective-permute-start | bytes 393224 | tf_op jit(solution)/shard_map/ppermute | solution.py:365
  43.7 2.0 %collective-permute-done.4.refs_3_ = bf16[120,512]{1,0:T(8,128)(2,1)S(1)} collective-permute-done((bf16[120,512]{1,0:T(8,128)(2,1)S(1)}, bf16[120,512]{1,0:T(8,128)(2,1)S(1)}, u32[]{:S(2)}, u32[]{:S(2)}) %collective-permute-start.4) | collective-permute-done | bytes 122912 | tf_op jit(solution)/shard_map/ppermute | solution.py:333
  45.7 1.4 %collective-permute-start.7 = (bf16[120,512]{1,0:T(8,128)(2,1)S(1)}, bf16[120,512]{1,0:T(8,128)(2,1)S(1)}, u32[]{:S(2)}, u32[]{:S(2)}) collective-permute-start(bf16[120,512]{1,0:T(8,128)(2,1)S(1)} %get-tuple-element.56), channel_id=1, source_target_pairs={{0,18},{1,19},{2,16},{3,17},{16,2},{17,3},{18,0},{19,1},{4,22},{5,... | collective-permute-start | bytes 368648 | tf_op jit(solution)/shard_map/ppermute | solution.py:333
  47.1 0.7 shard_map.61
  47.9 0.5 collective-permute-start.23
  48.4 1.6 %collective-permute-start.18 = (bf16[512,128]{1,0:T(8,128)(2,1)S(1)}, bf16[512,128]{1,0:T(8,128)(2,1)S(1)}, u32[]{:S(2)}, u32[]{:S(2)}) collective-permute-start(bf16[512,128]{1,0:T(8,128)(2,1)S(1)} %get-tuple-element.66), channel_id=1, source_target_pairs={{0,16},{16,0},{1,17},{17,1},{2,18},{18,2},{3,19},{19,3},{4,20},{20... | collective-permute-start | bytes 393224 | tf_op jit(solution)/shard_map/ppermute | solution.py:365
  50.2 3.9 %collective-permute-done.7.refs_3_ = bf16[120,512]{1,0:T(8,128)(2,1)S(1)} collective-permute-done((bf16[120,512]{1,0:T(8,128)(2,1)S(1)}, bf16[120,512]{1,0:T(8,128)(2,1)S(1)}, u32[]{:S(2)}, u32[]{:S(2)}) %collective-permute-start.7) | collective-permute-done | bytes 122912 | tf_op jit(solution)/shard_map/ppermute | solution.py:333
  55.4 4.0 %collective-permute-start.34 = (bf16[256,256]{1,0:T(8,128)(2,1)S(1)}, bf16[256,256]{1,0:T(8,128)(2,1)S(1)}, u32[]{:S(2)}, u32[]{:S(2)}) collective-permute-start(bf16[256,256]{1,0:T(8,128)(2,1)S(1)} %get-tuple-element.88), channel_id=1, source_target_pairs={{0,8},{4,12},{8,0},{12,4},{1,9},{5,13},{9,1},{13,5},{2,10},{6,14},... | collective-permute-start | bytes 393224 | tf_op jit(solution)/shard_map/ppermute | solution.py:398
  59.4 1.0 %collective-permute-start.32 = (bf16[256,128]{1,0:T(8,128)(2,1)S(1)}, bf16[256,128]{1,0:T(8,128)(2,1)S(1)}, u32[]{:S(2)}, u32[]{:S(2)}) collective-permute-start(bf16[256,128]{1,0:T(8,128)(2,1)S(1)} %get-tuple-element.86), channel_id=1, source_target_pairs={{0,12},{4,8},{8,4},{12,0},{1,13},{5,9},{9,5},{13,1},{2,14},{6,10},... | collective-permute-start | bytes 196616 | tf_op jit(solution)/shard_map/ppermute | solution.py:398
  60.5 2.8 %collective-permute-start.30 = (bf16[256,128]{1,0:T(8,128)(2,1)S(1)}, bf16[256,128]{1,0:T(8,128)(2,1)S(1)}, u32[]{:S(2)}, u32[]{:S(2)}) collective-permute-start(bf16[256,128]{1,0:T(8,128)(2,1)S(1)} %get-tuple-element.84), channel_id=1, source_target_pairs={{0,12},{4,8},{8,4},{12,0},{1,13},{5,9},{9,5},{13,1},{2,14},{6,10},... | collective-permute-start | bytes 196616 | tf_op jit(solution)/shard_map/ppermute | solution.py:398
  63.2 1.1 %collective-permute-start.31 = (bf16[256,128]{1,0:T(8,128)(2,1)S(1)}, bf16[256,128]{1,0:T(8,128)(2,1)S(1)}, u32[]{:S(2)}, u32[]{:S(2)}) collective-permute-start(bf16[256,128]{1,0:T(8,128)(2,1)S(1)} %get-tuple-element.85), channel_id=1, source_target_pairs={{0,4},{4,0},{8,12},{12,8},{1,5},{5,1},{9,13},{13,9},{2,6},{6,2},{1... | collective-permute-start | bytes 196616 | tf_op jit(solution)/shard_map/ppermute | solution.py:398
  64.9 1.0 %collective-permute-done.32.refs_3_ = bf16[256,128]{1,0:T(8,128)(2,1)S(1)} collective-permute-done((bf16[256,128]{1,0:T(8,128)(2,1)S(1)}, bf16[256,128]{1,0:T(8,128)(2,1)S(1)}, u32[]{:S(2)}, u32[]{:S(2)}) %collective-permute-start.32) | collective-permute-done | bytes 65568 | tf_op jit(solution)/shard_map/ppermute | solution.py:398
  65.8 1.5 %collective-permute-start.24 = (bf16[256,128]{1,0:T(8,128)(2,1)S(1)}, bf16[256,128]{1,0:T(8,128)(2,1)S(1)}, u32[]{:S(2)}, u32[]{:S(2)}) collective-permute-start(bf16[256,128]{1,0:T(8,128)(2,1)S(1)} %get-tuple-element.74), channel_id=1, source_target_pairs={{0,12},{4,8},{8,4},{12,0},{1,13},{5,9},{9,5},{13,1},{2,14},{6,10},... | collective-permute-start | bytes 196616 | tf_op jit(solution)/shard_map/ppermute | solution.py:398
  67.4 3.9 %collective-permute-start.25 = (bf16[256,128]{1,0:T(8,128)(2,1)S(1)}, bf16[256,128]{1,0:T(8,128)(2,1)S(1)}, u32[]{:S(2)}, u32[]{:S(2)}) collective-permute-start(bf16[256,128]{1,0:T(8,128)(2,1)S(1)} %get-tuple-element.75), channel_id=1, source_target_pairs={{0,4},{4,0},{8,12},{12,8},{1,5},{5,1},{9,13},{13,9},{2,6},{6,2},{1... | collective-permute-start | bytes 196616 | tf_op jit(solution)/shard_map/ppermute | solution.py:398
  71.8 2.4 %collective-permute-start.26 = (bf16[256,128]{1,0:T(8,128)(2,1)S(1)}, bf16[256,128]{1,0:T(8,128)(2,1)S(1)}, u32[]{:S(2)}, u32[]{:S(2)}) collective-permute-start(bf16[256,128]{1,0:T(8,128)(2,1)S(1)} %get-tuple-element.76), channel_id=1, source_target_pairs={{0,8},{4,12},{8,0},{12,4},{1,9},{5,13},{9,1},{13,5},{2,10},{6,14},... | collective-permute-start | bytes 196616 | tf_op jit(solution)/shard_map/ppermute | solution.py:398
  74.7 0.7 collective-permute-start.20
  75.4 3.3 %collective-permute-start.21 = (bf16[256,128]{1,0:T(8,128)(2,1)S(1)}, bf16[256,128]{1,0:T(8,128)(2,1)S(1)}, u32[]{:S(2)}, u32[]{:S(2)}) collective-permute-start(bf16[256,128]{1,0:T(8,128)(2,1)S(1)} %get-tuple-element.70), channel_id=1, source_target_pairs={{0,8},{4,12},{8,0},{12,4},{1,9},{5,13},{9,1},{13,5},{2,10},{6,14},... | collective-permute-start | bytes 196616 | tf_op jit(solution)/shard_map/ppermute | solution.py:398
  78.8 0.8 collective-permute-start.35
  79.6 1.3 %collective-permute-start.27 = (bf16[256,128]{1,0:T(8,128)(2,1)S(1)}, bf16[256,128]{1,0:T(8,128)(2,1)S(1)}, u32[]{:S(2)}, u32[]{:S(2)}) collective-permute-start(bf16[256,128]{1,0:T(8,128)(2,1)S(1)} %shard_map.65.refs_3_), channel_id=1, source_target_pairs={{0,16},{16,0},{1,17},{17,1},{2,18},{18,2},{3,19},{19,3},{4,20},{20... | collective-permute-start | bytes 196616 | tf_op jit(solution)/shard_map/ppermute | solution.py:413
  81.1 1.9 %collective-permute-start.22 = (bf16[256,128]{1,0:T(8,128)(2,1)S(1)}, bf16[256,128]{1,0:T(8,128)(2,1)S(1)}, u32[]{:S(2)}, u32[]{:S(2)}) collective-permute-start(bf16[256,128]{1,0:T(8,128)(2,1)S(1)} %shard_map.63.refs_2_), channel_id=1, source_target_pairs={{0,16},{16,0},{1,17},{17,1},{2,18},{18,2},{3,19},{19,3},{4,20},{20... | collective-permute-start | bytes 196616 | tf_op jit(solution)/shard_map/ppermute | solution.py:413
  83.0 0.8 collective-permute-done.35.refs_1_
  83.7 0.8 shard_map.70.refs_2_
  84.5 0.9 %collective-permute-done.22.refs_0_ = bf16[256,128]{1,0:T(8,128)(2,1)S(1)} collective-permute-done((bf16[256,128]{1,0:T(8,128)(2,1)S(1)}, bf16[256,128]{1,0:T(8,128)(2,1)S(1)}, u32[]{:S(2)}, u32[]{:S(2)}) %collective-permute-start.22) | collective-permute-done | bytes 65568 | tf_op jit(solution)/shard_map/ppermute | solution.py:413
  85.4 0.7 shard_map.71
  (45 shorter events, 3.4 us)
Async XLA Ops:
  0.0 0.7 copy-start.1
  0.0 10.6 %collective-permute-start.8 = (bf16[192,2048]{1,0:T(8,128)(2,1)}, bf16[192,2048]{1,0:T(8,128)(2,1)S(1)}, u32[]{:S(2)}, u32[]{:S(2)}) collective-permute-start(bf16[192,2048]{1,0:T(8,128)(2,1)} %refs_2_.2), channel_id=1, source_target_pairs={{0,1},{1,0},{2,3},{3,2},{4,5},{5,4},{6,7},{7,6},{8,9},{9,8},{10,11... | collective-permute-start | bytes 2359304 | tf_op jit(solution)/shard_map/ppermute | solution.py:284
  0.5 25.3 %collective-permute-start.1 = (bf16[192,2048]{1,0:T(8,128)(2,1)}, bf16[192,2048]{1,0:T(8,128)(2,1)S(1)}, u32[]{:S(2)}, u32[]{:S(2)}) collective-permute-start(bf16[192,2048]{1,0:T(8,128)(2,1)} %refs_2_.3), channel_id=1, source_target_pairs={{0,1},{1,0},{2,3},{3,2},{4,5},{5,4},{6,7},{7,6},{8,9},{9,8},{10,11... | collective-permute-start | bytes 2359304 | tf_op jit(solution)/shard_map/ppermute | solution.py:286
  0.7 3.1 %collective-permute-start = (s32[1,192]{1,0:T(1,128)S(1)}, s32[1,192]{1,0:T(1,128)S(1)}, u32[]{:S(2)}, u32[]{:S(2)}) collective-permute-start(s32[1,192]{1,0:T(1,128)S(1)} %bitcast.4), channel_id=1, source_target_pairs={{0,1},{1,0},{2,3},{3,2},{4,5},{5,4},{6,7},{7,6},{8,9},{9,8},{10,11... | collective-permute-start | bytes 2312 | tf_op jit(solution)/shard_map/ppermute | solution.py:285
  5.0 9.1 %collective-permute-start.12 = (bf16[256,256]{1,0:T(8,128)(2,1)S(1)}, bf16[256,256]{1,0:T(8,128)(2,1)S(1)}, u32[]{:S(2)}, u32[]{:S(2)}) collective-permute-start(bf16[256,256]{1,0:T(8,128)(2,1)S(1)} %get-tuple-element.62.refs_4_), channel_id=1, source_target_pairs={{0,4},{4,0},{8,12},{12,8},{1,5},{5,1},{9,13},{13,9},{2,6},{6,2},{1... | collective-permute-start | bytes 393224 | tf_op jit(solution)/shard_map/ppermute | solution.py:308
  8.0 12.9 %collective-permute-start.13 = (bf16[256,256]{1,0:T(8,128)(2,1)S(1)}, bf16[256,256]{1,0:T(8,128)(2,1)S(1)}, u32[]{:S(2)}, u32[]{:S(2)}) collective-permute-start(bf16[256,256]{1,0:T(8,128)(2,1)S(1)} %get-tuple-element.62.refs_4_), channel_id=1, source_target_pairs={{0,8},{4,12},{8,0},{12,4},{1,9},{5,13},{9,1},{13,5},{2,10},{6,14},... | collective-permute-start | bytes 393224 | tf_op jit(solution)/shard_map/ppermute | solution.py:308
  10.6 12.8 %collective-permute-start.14 = (bf16[256,256]{1,0:T(8,128)(2,1)S(1)}, bf16[256,256]{1,0:T(8,128)(2,1)S(1)}, u32[]{:S(2)}, u32[]{:S(2)}) collective-permute-start(bf16[256,256]{1,0:T(8,128)(2,1)S(1)} %get-tuple-element.62.refs_4_), channel_id=1, source_target_pairs={{0,12},{4,8},{8,4},{12,0},{1,13},{5,9},{9,5},{13,1},{2,14},{6,10},... | collective-permute-start | bytes 393224 | tf_op jit(solution)/shard_map/ppermute | solution.py:308
  10.6 13.3 %collective-permute-start.15 = (bf16[256,256]{1,0:T(8,128)(2,1)S(1)}, bf16[256,256]{1,0:T(8,128)(2,1)S(1)}, u32[]{:S(2)}, u32[]{:S(2)}) collective-permute-start(bf16[256,256]{1,0:T(8,128)(2,1)S(1)} %get-tuple-element.64.refs_1_), channel_id=1, source_target_pairs={{0,4},{4,0},{8,12},{12,8},{1,5},{5,1},{9,13},{13,9},{2,6},{6,2},{1... | collective-permute-start | bytes 393224 | tf_op jit(solution)/shard_map/ppermute | solution.py:308
  11.5 15.6 %copy-start = (bf16[192,2048]{1,0:T(8,128)(2,1)S(1)}, bf16[192,2048]{1,0:T(8,128)(2,1)}, u32[]{:S(2)}) copy-start(bf16[192,2048]{1,0:T(8,128)(2,1)} %refs_2_.3) | copy-start | bytes 2359300
  14.2 23.1 %collective-permute-start.10 = (bf16[120,1024]{1,0:T(8,128)(2,1)S(1)}, bf16[120,1024]{1,0:T(8,128)(2,1)S(1)}, u32[]{:S(2)}, u32[]{:S(2)}) collective-permute-start(bf16[120,1024]{1,0:T(8,128)(2,1)S(1)} %get-tuple-element.60), channel_id=1, source_target_pairs={{0,16},{1,17},{2,18},{3,19},{16,0},{17,1},{18,2},{19,3},{4,20},{5,... | collective-permute-start | bytes 737288 | tf_op jit(solution)/shard_map/ppermute | solution.py:333
  20.9 17.9 %collective-permute-start.11 = (bf16[120,1024]{1,0:T(8,128)(2,1)S(1)}, bf16[120,1024]{1,0:T(8,128)(2,1)S(1)}, u32[]{:S(2)}, u32[]{:S(2)}) collective-permute-start(bf16[120,1024]{1,0:T(8,128)(2,1)S(1)} %get-tuple-element.61), channel_id=1, source_target_pairs={{0,18},{1,19},{2,16},{3,17},{16,2},{17,3},{18,0},{19,1},{4,22},{5,... | collective-permute-start | bytes 737288 | tf_op jit(solution)/shard_map/ppermute | solution.py:333
  23.4 15.9 %collective-permute-start.9 = (bf16[120,1024]{1,0:T(8,128)(2,1)S(1)}, bf16[120,1024]{1,0:T(8,128)(2,1)S(1)}, u32[]{:S(2)}, u32[]{:S(2)}) collective-permute-start(bf16[120,1024]{1,0:T(8,128)(2,1)S(1)} %get-tuple-element.59), channel_id=1, source_target_pairs={{0,2},{1,3},{2,0},{3,1},{16,18},{17,19},{18,16},{19,17},{4,6},{5,7... | collective-permute-start | bytes 737288 | tf_op jit(solution)/shard_map/ppermute | solution.py:333
  23.9 11.4 %collective-permute-start.16 = (bf16[256,256]{1,0:T(8,128)(2,1)S(1)}, bf16[256,256]{1,0:T(8,128)(2,1)S(1)}, u32[]{:S(2)}, u32[]{:S(2)}) collective-permute-start(bf16[256,256]{1,0:T(8,128)(2,1)S(1)} %get-tuple-element.64.refs_1_), channel_id=1, source_target_pairs={{0,8},{4,12},{8,0},{12,4},{1,9},{5,13},{9,1},{13,5},{2,10},{6,14},... | collective-permute-start | bytes 393224 | tf_op jit(solution)/shard_map/ppermute | solution.py:308
  25.8 10.0 %collective-permute-start.17 = (bf16[256,256]{1,0:T(8,128)(2,1)S(1)}, bf16[256,256]{1,0:T(8,128)(2,1)S(1)}, u32[]{:S(2)}, u32[]{:S(2)}) collective-permute-start(bf16[256,256]{1,0:T(8,128)(2,1)S(1)} %get-tuple-element.64.refs_1_), channel_id=1, source_target_pairs={{0,12},{4,8},{8,4},{12,0},{1,13},{5,9},{9,5},{13,1},{2,14},{6,10},... | collective-permute-start | bytes 393224 | tf_op jit(solution)/shard_map/ppermute | solution.py:308
  35.3 6.3 %collective-permute-start.2 = (bf16[120,512]{1,0:T(8,128)(2,1)S(1)}, bf16[120,512]{1,0:T(8,128)(2,1)S(1)}, u32[]{:S(2)}, u32[]{:S(2)}) collective-permute-start(bf16[120,512]{1,0:T(8,128)(2,1)S(1)} %get-tuple-element.50), channel_id=1, source_target_pairs={{0,2},{1,3},{2,0},{3,1},{16,18},{17,19},{18,16},{19,17},{4,6},{5,7... | collective-permute-start | bytes 368648 | tf_op jit(solution)/shard_map/ppermute | solution.py:333
  35.8 6.4 %collective-permute-start.3 = (bf16[120,512]{1,0:T(8,128)(2,1)S(1)}, bf16[120,512]{1,0:T(8,128)(2,1)S(1)}, u32[]{:S(2)}, u32[]{:S(2)}) collective-permute-start(bf16[120,512]{1,0:T(8,128)(2,1)S(1)} %get-tuple-element.51), channel_id=1, source_target_pairs={{0,16},{1,17},{2,18},{3,19},{16,0},{17,1},{18,2},{19,3},{4,20},{5,... | collective-permute-start | bytes 368648 | tf_op jit(solution)/shard_map/ppermute | solution.py:333
  37.3 8.4 %collective-permute-start.4 = (bf16[120,512]{1,0:T(8,128)(2,1)S(1)}, bf16[120,512]{1,0:T(8,128)(2,1)S(1)}, u32[]{:S(2)}, u32[]{:S(2)}) collective-permute-start(bf16[120,512]{1,0:T(8,128)(2,1)S(1)} %get-tuple-element.52), channel_id=1, source_target_pairs={{0,18},{1,19},{2,16},{3,17},{16,2},{17,3},{18,0},{19,1},{4,22},{5,... | collective-permute-start | bytes 368648 | tf_op jit(solution)/shard_map/ppermute | solution.py:333
  38.8 9.1 %collective-permute-start.5 = (bf16[120,512]{1,0:T(8,128)(2,1)S(1)}, bf16[120,512]{1,0:T(8,128)(2,1)S(1)}, u32[]{:S(2)}, u32[]{:S(2)}) collective-permute-start(bf16[120,512]{1,0:T(8,128)(2,1)S(1)} %get-tuple-element.54), channel_id=1, source_target_pairs={{0,2},{1,3},{2,0},{3,1},{16,18},{17,19},{18,16},{19,17},{4,6},{5,7... | collective-permute-start | bytes 368648 | tf_op jit(solution)/shard_map/ppermute | solution.py:333
  39.3 9.1 %collective-permute-start.6 = (bf16[120,512]{1,0:T(8,128)(2,1)S(1)}, bf16[120,512]{1,0:T(8,128)(2,1)S(1)}, u32[]{:S(2)}, u32[]{:S(2)}) collective-permute-start(bf16[120,512]{1,0:T(8,128)(2,1)S(1)} %get-tuple-element.55), channel_id=1, source_target_pairs={{0,16},{1,17},{2,18},{3,19},{16,0},{17,1},{18,2},{19,3},{4,20},{5,... | collective-permute-start | bytes 368648 | tf_op jit(solution)/shard_map/ppermute | solution.py:333
  41.6 12.8 %collective-permute-start.29 = (bf16[512,128]{1,0:T(8,128)(2,1)S(1)}, bf16[512,128]{1,0:T(8,128)(2,1)S(1)}, u32[]{:S(2)}, u32[]{:S(2)}) collective-permute-start(bf16[512,128]{1,0:T(8,128)(2,1)S(1)} %get-tuple-element.81), channel_id=1, source_target_pairs={{0,16},{16,0},{1,17},{17,1},{2,18},{18,2},{3,19},{19,3},{4,20},{20... | collective-permute-start | bytes 393224 | tf_op jit(solution)/shard_map/ppermute | solution.py:365
  42.2 12.5 %collective-permute-start.28 = (bf16[512,128]{1,0:T(8,128)(2,1)S(1)}, bf16[512,128]{1,0:T(8,128)(2,1)S(1)}, u32[]{:S(2)}, u32[]{:S(2)}) collective-permute-start(bf16[512,128]{1,0:T(8,128)(2,1)S(1)} %get-tuple-element.78), channel_id=1, source_target_pairs={{0,16},{16,0},{1,17},{17,1},{2,18},{18,2},{3,19},{19,3},{4,20},{20... | collective-permute-start | bytes 393224 | tf_op jit(solution)/shard_map/ppermute | solution.py:365
  45.7 8.4 %collective-permute-start.7 = (bf16[120,512]{1,0:T(8,128)(2,1)S(1)}, bf16[120,512]{1,0:T(8,128)(2,1)S(1)}, u32[]{:S(2)}, u32[]{:S(2)}) collective-permute-start(bf16[120,512]{1,0:T(8,128)(2,1)S(1)} %get-tuple-element.56), channel_id=1, source_target_pairs={{0,18},{1,19},{2,16},{3,17},{16,2},{17,3},{18,0},{19,1},{4,22},{5,... | collective-permute-start | bytes 368648 | tf_op jit(solution)/shard_map/ppermute | solution.py:333
  47.9 12.6 %collective-permute-start.23 = (bf16[512,128]{1,0:T(8,128)(2,1)S(1)}, bf16[512,128]{1,0:T(8,128)(2,1)S(1)}, u32[]{:S(2)}, u32[]{:S(2)}) collective-permute-start(bf16[512,128]{1,0:T(8,128)(2,1)S(1)} %get-tuple-element.72), channel_id=1, source_target_pairs={{0,16},{16,0},{1,17},{17,1},{2,18},{18,2},{3,19},{19,3},{4,20},{20... | collective-permute-start | bytes 393224 | tf_op jit(solution)/shard_map/ppermute | solution.py:365
  48.4 14.9 %collective-permute-start.18 = (bf16[512,128]{1,0:T(8,128)(2,1)S(1)}, bf16[512,128]{1,0:T(8,128)(2,1)S(1)}, u32[]{:S(2)}, u32[]{:S(2)}) collective-permute-start(bf16[512,128]{1,0:T(8,128)(2,1)S(1)} %get-tuple-element.66), channel_id=1, source_target_pairs={{0,16},{16,0},{1,17},{17,1},{2,18},{18,2},{3,19},{19,3},{4,20},{20... | collective-permute-start | bytes 393224 | tf_op jit(solution)/shard_map/ppermute | solution.py:365
  55.4 19.3 %collective-permute-start.34 = (bf16[256,256]{1,0:T(8,128)(2,1)S(1)}, bf16[256,256]{1,0:T(8,128)(2,1)S(1)}, u32[]{:S(2)}, u32[]{:S(2)}) collective-permute-start(bf16[256,256]{1,0:T(8,128)(2,1)S(1)} %get-tuple-element.88), channel_id=1, source_target_pairs={{0,8},{4,12},{8,0},{12,4},{1,9},{5,13},{9,1},{13,5},{2,10},{6,14},... | collective-permute-start | bytes 393224 | tf_op jit(solution)/shard_map/ppermute | solution.py:398
  59.4 6.4 %collective-permute-start.32 = (bf16[256,128]{1,0:T(8,128)(2,1)S(1)}, bf16[256,128]{1,0:T(8,128)(2,1)S(1)}, u32[]{:S(2)}, u32[]{:S(2)}) collective-permute-start(bf16[256,128]{1,0:T(8,128)(2,1)S(1)} %get-tuple-element.86), channel_id=1, source_target_pairs={{0,12},{4,8},{8,4},{12,0},{1,13},{5,9},{9,5},{13,1},{2,14},{6,10},... | collective-permute-start | bytes 196616 | tf_op jit(solution)/shard_map/ppermute | solution.py:398
  60.4 6.9 %collective-permute-start.33 = (bf16[256,128]{1,0:T(8,128)(2,1)S(1)}, bf16[256,128]{1,0:T(8,128)(2,1)S(1)}, u32[]{:S(2)}, u32[]{:S(2)}) collective-permute-start(bf16[256,128]{1,0:T(8,128)(2,1)S(1)} %get-tuple-element.87), channel_id=1, source_target_pairs={{0,4},{4,0},{8,12},{12,8},{1,5},{5,1},{9,13},{13,9},{2,6},{6,2},{1... | collective-permute-start | bytes 196616 | tf_op jit(solution)/shard_map/ppermute | solution.py:398
  60.5 11.3 %collective-permute-start.30 = (bf16[256,128]{1,0:T(8,128)(2,1)S(1)}, bf16[256,128]{1,0:T(8,128)(2,1)S(1)}, u32[]{:S(2)}, u32[]{:S(2)}) collective-permute-start(bf16[256,128]{1,0:T(8,128)(2,1)S(1)} %get-tuple-element.84), channel_id=1, source_target_pairs={{0,12},{4,8},{8,4},{12,0},{1,13},{5,9},{9,5},{13,1},{2,14},{6,10},... | collective-permute-start | bytes 196616 | tf_op jit(solution)/shard_map/ppermute | solution.py:398
  63.2 11.0 %collective-permute-start.31 = (bf16[256,128]{1,0:T(8,128)(2,1)S(1)}, bf16[256,128]{1,0:T(8,128)(2,1)S(1)}, u32[]{:S(2)}, u32[]{:S(2)}) collective-permute-start(bf16[256,128]{1,0:T(8,128)(2,1)S(1)} %get-tuple-element.85), channel_id=1, source_target_pairs={{0,4},{4,0},{8,12},{12,8},{1,5},{5,1},{9,13},{13,9},{2,6},{6,2},{1... | collective-permute-start | bytes 196616 | tf_op jit(solution)/shard_map/ppermute | solution.py:398
  65.8 9.6 %collective-permute-start.24 = (bf16[256,128]{1,0:T(8,128)(2,1)S(1)}, bf16[256,128]{1,0:T(8,128)(2,1)S(1)}, u32[]{:S(2)}, u32[]{:S(2)}) collective-permute-start(bf16[256,128]{1,0:T(8,128)(2,1)S(1)} %get-tuple-element.74), channel_id=1, source_target_pairs={{0,12},{4,8},{8,4},{12,0},{1,13},{5,9},{9,5},{13,1},{2,14},{6,10},... | collective-permute-start | bytes 196616 | tf_op jit(solution)/shard_map/ppermute | solution.py:398
  67.4 11.4 %collective-permute-start.25 = (bf16[256,128]{1,0:T(8,128)(2,1)S(1)}, bf16[256,128]{1,0:T(8,128)(2,1)S(1)}, u32[]{:S(2)}, u32[]{:S(2)}) collective-permute-start(bf16[256,128]{1,0:T(8,128)(2,1)S(1)} %get-tuple-element.75), channel_id=1, source_target_pairs={{0,4},{4,0},{8,12},{12,8},{1,5},{5,1},{9,13},{13,9},{2,6},{6,2},{1... | collective-permute-start | bytes 196616 | tf_op jit(solution)/shard_map/ppermute | solution.py:398
  71.8 7.8 %collective-permute-start.26 = (bf16[256,128]{1,0:T(8,128)(2,1)S(1)}, bf16[256,128]{1,0:T(8,128)(2,1)S(1)}, u32[]{:S(2)}, u32[]{:S(2)}) collective-permute-start(bf16[256,128]{1,0:T(8,128)(2,1)S(1)} %get-tuple-element.76), channel_id=1, source_target_pairs={{0,8},{4,12},{8,0},{12,4},{1,9},{5,13},{9,1},{13,5},{2,10},{6,14},... | collective-permute-start | bytes 196616 | tf_op jit(solution)/shard_map/ppermute | solution.py:398
  74.2 6.7 %collective-permute-start.19 = (bf16[256,128]{1,0:T(8,128)(2,1)S(1)}, bf16[256,128]{1,0:T(8,128)(2,1)S(1)}, u32[]{:S(2)}, u32[]{:S(2)}) collective-permute-start(bf16[256,128]{1,0:T(8,128)(2,1)S(1)} %get-tuple-element.68), channel_id=1, source_target_pairs={{0,12},{4,8},{8,4},{12,0},{1,13},{5,9},{9,5},{13,1},{2,14},{6,10},... | collective-permute-start | bytes 196616 | tf_op jit(solution)/shard_map/ppermute | solution.py:398
  74.7 6.2 %collective-permute-start.20 = (bf16[256,128]{1,0:T(8,128)(2,1)S(1)}, bf16[256,128]{1,0:T(8,128)(2,1)S(1)}, u32[]{:S(2)}, u32[]{:S(2)}) collective-permute-start(bf16[256,128]{1,0:T(8,128)(2,1)S(1)} %get-tuple-element.69), channel_id=1, source_target_pairs={{0,4},{4,0},{8,12},{12,8},{1,5},{5,1},{9,13},{13,9},{2,6},{6,2},{1... | collective-permute-start | bytes 196616 | tf_op jit(solution)/shard_map/ppermute | solution.py:398
  75.4 5.6 %collective-permute-start.21 = (bf16[256,128]{1,0:T(8,128)(2,1)S(1)}, bf16[256,128]{1,0:T(8,128)(2,1)S(1)}, u32[]{:S(2)}, u32[]{:S(2)}) collective-permute-start(bf16[256,128]{1,0:T(8,128)(2,1)S(1)} %get-tuple-element.70), channel_id=1, source_target_pairs={{0,8},{4,12},{8,0},{12,4},{1,9},{5,13},{9,1},{13,5},{2,10},{6,14},... | collective-permute-start | bytes 196616 | tf_op jit(solution)/shard_map/ppermute | solution.py:398
  78.8 5.0 %collective-permute-start.35 = (bf16[256,256]{1,0:T(8,128)(2,1)S(1)}, bf16[256,256]{1,0:T(8,128)(2,1)S(1)}, u32[]{:S(2)}, u32[]{:S(2)}) collective-permute-start(bf16[256,256]{1,0:T(8,128)(2,1)S(1)} %shard_map.69.refs_0_), channel_id=1, source_target_pairs={{0,16},{16,0},{1,17},{17,1},{2,18},{18,2},{3,19},{19,3},{4,20},{20... | collective-permute-start | bytes 393224 | tf_op jit(solution)/shard_map/ppermute | solution.py:413
  79.6 4.9 %collective-permute-start.27 = (bf16[256,128]{1,0:T(8,128)(2,1)S(1)}, bf16[256,128]{1,0:T(8,128)(2,1)S(1)}, u32[]{:S(2)}, u32[]{:S(2)}) collective-permute-start(bf16[256,128]{1,0:T(8,128)(2,1)S(1)} %shard_map.65.refs_3_), channel_id=1, source_target_pairs={{0,16},{16,0},{1,17},{17,1},{2,18},{18,2},{3,19},{19,3},{4,20},{20... | collective-permute-start | bytes 196616 | tf_op jit(solution)/shard_map/ppermute | solution.py:413
  81.1 4.3 %collective-permute-start.22 = (bf16[256,128]{1,0:T(8,128)(2,1)S(1)}, bf16[256,128]{1,0:T(8,128)(2,1)S(1)}, u32[]{:S(2)}, u32[]{:S(2)}) collective-permute-start(bf16[256,128]{1,0:T(8,128)(2,1)S(1)} %shard_map.63.refs_2_), channel_id=1, source_target_pairs={{0,16},{16,0},{1,17},{17,1},{2,18},{18,2},{3,19},{19,3},{4,20},{20... | collective-permute-start | bytes 196616 | tf_op jit(solution)/shard_map/ppermute | solution.py:413

commit v11 on v9

--- a/solution.py
+++ b/solution.py
@@ -71,8 +71,8 @@
     return jax.ShapeDtypeStruct((rows, cols), dtype)
 
 
-def prep_body(dims, stride, pos, ids, ids_pair, rows, codes, scales, *refs):
-    picks, near, outs = refs[:2], refs[2], refs[3:-4]
+def prep_body(pos, rows, codes, scales, *refs):
+    near, outs = refs[0], refs[1:-4]
     raw, steps, wide, sems = refs[-4:]
     mine, ff = raw.shape
     at = pl.multiple_of(pos[0] * mine, 16)
@@ -83,7 +83,6 @@
     ]
     for move in moves:
         move.start()
-    select_body(dims, stride, pos, ids, ids_pair, *picks)
     moves[0].wait()
     wide[...] = steps[...].astype(F32)
     used = max(1, mine // QB)
@@ -285,20 +284,23 @@
     cotangent_pair = lax.ppermute(cotangent, "local", swap)
 
     far = [pltpu.with_memory_space_constraint(a, pltpu.HBM) for a in (tokens, w1_codes[0], w1_scales[0])]
-    near = [shape(pairs * stride, count, BF16)] * 2 + [shape(count, features, BF16)]
-    first, second, tokens, *weights = call(
-        functools.partial(prep_body, dims, stride),
-        near + [shape(mine, w, BF16) for w in gathered],
-        [chosen, chosen_pair] + far,
+    tokens, *weights = call(
+        prep_body,
+        [shape(count, features, BF16)] + [shape(mine, w, BF16) for w in gathered],
+        far,
         [
             pltpu.VMEM((mine, hidden), BF16),
             pltpu.VMEM((shard // QB, hidden), BF16),
             pltpu.VMEM((shard // QB, hidden), F32),
             pltpu.SemaphoreType.DMA((3,)),
         ],
-        space=[pltpu.VMEM] * 2 + [pltpu.HBM] * 3,
+        space=pltpu.HBM,
     )
-    picks = [first, second]
+    picks = call(
+        functools.partial(select_body, dims, stride),
+        [shape(pairs * stride, count, BF16)] * 2,
+        [chosen, chosen_pair],
+    )
     order = node_order(nodes)
     held = []
     for chunk in weights:

time: 78.3 us -> 74.4 us (0.950)
  starting transfers between devices: 48.2 us -> 45.2 us
  waiting for transfers between devices: 22 us -> 20.9 us
    ppermute x9, waiting for transfers between devices: 2.86 us -> 5.38 us  [exchange(): moved[at] = lax.ppermute(pieces[at], ('dp', 'local'), links)]
    ppermute x9, starting transfers between devices: 15.6 us -> 13.6 us  [on_device(): moved = lax.ppermute(term, 'node', links)]
    ppermute x9, starting transfers between devices: 12.6 us -> 10.8 us  [exchange(): moved[at] = lax.ppermute(pieces[at], ('dp', 'local'), links)]
    ppermute x3, starting transfers between devices: 2.94 us -> 4.52 us  [on_device(): finished.append(lax.ppermute(summed, 'dp', links))]
    ppermute x1, waiting for transfers between devices: 2.57 us -> 1.16 us  [on_device(): chosen_pair = lax.ppermute(chosen, 'local', swap)]
    ppermute x3, waiting for transfers between devices: 2.7 us -> 1.47 us  [on_device(): finished.append(lax.ppermute(summed, 'dp', links))]
    pallas_call x16 -> x17, Pallas kernels: 7.6 us -> 7.86 us  [call(): pl.pallas_call(kernel, out_shape=outs, in_specs=[pl.BlockSpec(memory_spac...]
  transfers between devices with their start and end apart: 33 -> 33, of which waited for: 11 -> 15; matrix products, arithmetic and copies ran while one was open for 0% -> 0% of each run, Pallas kernels for 9% -> 10%
where the time goes in v11:
time: 74.4 us; the launch traced here: 74.2 us
  starting transfers between devices  45.2 us (61%)
  waiting for transfers between devices  20.9 us (28%)
  Pallas kernels  7.86 us (11%)
    ppermute x9, starting transfers between devices, on_device(): moved = lax.ppermute(term, 'node', links)  13.6 us
    ppermute x6, starting transfers between devices, on_device(): lax.ppermute(chunk, 'node', [(a, mate(a, s, nodes)) for a in range(nodes)])  12.1 us
    ppermute x9, starting transfers between devices, exchange(): moved[at] = lax.ppermute(pieces[at], ('dp', 'local'), links)  10.8 us
    pallas_call x17, Pallas kernels, call(): pl.pallas_call(kernel, out_shape=outs, in_specs=[pl.BlockSpec(memory_spac...  7.86 us
    ppermute x6, waiting for transfers between devices, on_device(): lax.ppermute(chunk, 'node', [(a, mate(a, s, nodes)) for a in range(nodes)])  7.78 us
    ppermute x9, waiting for transfers between devices, exchange(): moved[at] = lax.ppermute(pieces[at], ('dp', 'local'), links)  5.38 us
    ppermute x9, waiting for transfers between devices, on_device(): moved = lax.ppermute(term, 'node', links)  5.13 us
    ppermute x3, starting transfers between devices, on_device(): finished.append(lax.ppermute(summed, 'dp', links))  4.52 us
  transfers between devices with their start and end apart: 33, of which 15 were waited for; matrix products, arithmetic and copies ran while one was open for 0% of the time, Pallas kernels for 10%

profile of v11, /device:TPU:0, one launch (start us, length us, event | category | flops | bytes accessed | tf_op | source)
XLA Modules:
  0.0 74.2 jit_solution(4490944589078348292)
XLA Ops:
  0.0 0.5 collective-permute-start.8
  0.5 1.3 %shard_map.59 = (bf16[192,2048]{1,0:T(8,128)(2,1)S(1)}, bf16[256,256]{1,0:T(8,128)(2,1)S(1)}, bf16[256,256]{1,0:T(8,128)(2,1)S(1)}) custom-call(bf16[192,2048]{1,0:T(8,128)(2,1)} %refs_0_.1, bf16[512,512]{1,0:T(8,128)(2,1)} %bitcast.6, bf16[16,512]{1,0:T(8,128)(2,1)} %bitcast.7), custom_call_target="tpu_custom_call" | custom-call | bytes 2375680 | tf_op jit(solution)/shard_map/pallas_call | solution.py:38
  1.8 3.1 %collective-permute-start.12 = (bf16[256,256]{1,0:T(8,128)(2,1)S(1)}, bf16[256,256]{1,0:T(8,128)(2,1)S(1)}, u32[]{:S(2)}, u32[]{:S(2)}) collective-permute-start(bf16[256,256]{1,0:T(8,128)(2,1)S(1)} %get-tuple-element.57.refs_4_), channel_id=1, source_target_pairs={{0,4},{4,0},{8,12},{12,8},{1,5},{5,1},{9,13},{13,9},{2,6},{6,2},{1... | collective-permute-start | bytes 393224 | tf_op jit(solution)/shard_map/ppermute | solution.py:309
  4.9 2.6 %collective-permute-start.13 = (bf16[256,256]{1,0:T(8,128)(2,1)S(1)}, bf16[256,256]{1,0:T(8,128)(2,1)S(1)}, u32[]{:S(2)}, u32[]{:S(2)}) collective-permute-start(bf16[256,256]{1,0:T(8,128)(2,1)S(1)} %get-tuple-element.57.refs_4_), channel_id=1, source_target_pairs={{0,8},{4,12},{8,0},{12,4},{1,9},{5,13},{9,1},{13,5},{2,10},{6,14},... | collective-permute-start | bytes 393224 | tf_op jit(solution)/shard_map/ppermute | solution.py:309
  7.5 1.2 %collective-permute-done.refs_1_ = s32[1,192]{1,0:T(1,128)S(1)} collective-permute-done((s32[1,192]{1,0:T(1,128)S(1)}, s32[1,192]{1,0:T(1,128)S(1)}, u32[]{:S(2)}, u32[]{:S(2)}) %collective-permute-start) | collective-permute-done | bytes 800 | tf_op jit(solution)/shard_map/ppermute | solution.py:283
  8.9 0.7 shard_map.60
  9.7 1.6 %collective-permute-start.10 = (bf16[120,1024]{1,0:T(8,128)(2,1)S(1)}, bf16[120,1024]{1,0:T(8,128)(2,1)S(1)}, u32[]{:S(2)}, u32[]{:S(2)}) collective-permute-start(bf16[120,1024]{1,0:T(8,128)(2,1)S(1)} %get-tuple-element.55), channel_id=1, source_target_pairs={{0,16},{1,17},{2,18},{3,19},{16,0},{17,1},{18,2},{19,3},{4,20},{5,... | collective-permute-start | bytes 737288 | tf_op jit(solution)/shard_map/ppermute | solution.py:334
  11.2 1.5 %collective-permute-start.11 = (bf16[120,1024]{1,0:T(8,128)(2,1)S(1)}, bf16[120,1024]{1,0:T(8,128)(2,1)S(1)}, u32[]{:S(2)}, u32[]{:S(2)}) collective-permute-start(bf16[120,1024]{1,0:T(8,128)(2,1)S(1)} %get-tuple-element.56), channel_id=1, source_target_pairs={{0,18},{1,19},{2,16},{3,17},{16,2},{17,3},{18,0},{19,1},{4,22},{5,... | collective-permute-start | bytes 737288 | tf_op jit(solution)/shard_map/ppermute | solution.py:334
  12.7 0.5 collective-permute-start.9
  13.2 0.6 collective-permute-done.13.refs_6_
  13.8 2.5 %collective-permute-start.14 = (bf16[256,256]{1,0:T(8,128)(2,1)S(1)}, bf16[256,256]{1,0:T(8,128)(2,1)S(1)}, u32[]{:S(2)}, u32[]{:S(2)}) collective-permute-start(bf16[256,256]{1,0:T(8,128)(2,1)S(1)} %get-tuple-element.57.refs_4_), channel_id=1, source_target_pairs={{0,12},{4,8},{8,4},{12,0},{1,13},{5,9},{9,5},{13,1},{2,14},{6,10},... | collective-permute-start | bytes 393224 | tf_op jit(solution)/shard_map/ppermute | solution.py:309
  16.3 4.4 %collective-permute-done.14.refs_7_ = bf16[256,256]{1,0:T(8,128)(2,1)S(1)} collective-permute-done((bf16[256,256]{1,0:T(8,128)(2,1)S(1)}, bf16[256,256]{1,0:T(8,128)(2,1)S(1)}, u32[]{:S(2)}, u32[]{:S(2)}) %collective-permute-start.14) | collective-permute-done | bytes 131104 | tf_op jit(solution)/shard_map/ppermute | solution.py:309
  20.7 1.1 %collective-permute-start.15 = (bf16[256,256]{1,0:T(8,128)(2,1)S(1)}, bf16[256,256]{1,0:T(8,128)(2,1)S(1)}, u32[]{:S(2)}, u32[]{:S(2)}) collective-permute-start(bf16[256,256]{1,0:T(8,128)(2,1)S(1)} %get-tuple-element.59.refs_1_), channel_id=1, source_target_pairs={{0,4},{4,0},{8,12},{12,8},{1,5},{5,1},{9,13},{13,9},{2,6},{6,2},{1... | collective-permute-start | bytes 393224 | tf_op jit(solution)/shard_map/ppermute | solution.py:309
  21.7 1.9 %collective-permute-start.16 = (bf16[256,256]{1,0:T(8,128)(2,1)S(1)}, bf16[256,256]{1,0:T(8,128)(2,1)S(1)}, u32[]{:S(2)}, u32[]{:S(2)}) collective-permute-start(bf16[256,256]{1,0:T(8,128)(2,1)S(1)} %get-tuple-element.59.refs_1_), channel_id=1, source_target_pairs={{0,8},{4,12},{8,0},{12,4},{1,9},{5,13},{9,1},{13,5},{2,10},{6,14},... | collective-permute-start | bytes 393224 | tf_op jit(solution)/shard_map/ppermute | solution.py:309
  23.7 0.4 collective-permute-done.11.refs_3_
  24.1 1.0 %collective-permute-start.17 = (bf16[256,256]{1,0:T(8,128)(2,1)S(1)}, bf16[256,256]{1,0:T(8,128)(2,1)S(1)}, u32[]{:S(2)}, u32[]{:S(2)}) collective-permute-start(bf16[256,256]{1,0:T(8,128)(2,1)S(1)} %get-tuple-element.59.refs_1_), channel_id=1, source_target_pairs={{0,12},{4,8},{8,4},{12,0},{1,13},{5,9},{9,5},{13,1},{2,14},{6,10},... | collective-permute-start | bytes 393224 | tf_op jit(solution)/shard_map/ppermute | solution.py:309
  25.0 0.4 collective-permute-done.9.refs_1_
  25.5 0.5 shard_map.61
  26.0 1.6 %collective-permute-start.28 = (bf16[512,256]{1,0:T(8,128)(2,1)S(1)}, bf16[512,256]{1,0:T(8,128)(2,1)S(1)}, u32[]{:S(2)}, u32[]{:S(2)}) collective-permute-start(bf16[512,256]{1,0:T(8,128)(2,1)S(1)} %get-tuple-element.73), channel_id=1, source_target_pairs={{0,16},{16,0},{1,17},{17,1},{2,18},{18,2},{3,19},{19,3},{4,20},{20... | collective-permute-start | bytes 786440 | tf_op jit(solution)/shard_map/ppermute | solution.py:366
  27.6 0.7 shard_map.56
  28.3 1.2 %collective-permute-start.2 = (bf16[120,512]{1,0:T(8,128)(2,1)S(1)}, bf16[120,512]{1,0:T(8,128)(2,1)S(1)}, u32[]{:S(2)}, u32[]{:S(2)}) collective-permute-start(bf16[120,512]{1,0:T(8,128)(2,1)S(1)} %get-tuple-element.45), channel_id=1, source_target_pairs={{0,2},{1,3},{2,0},{3,1},{16,18},{17,19},{18,16},{19,17},{4,6},{5,7... | collective-permute-start | bytes 368648 | tf_op jit(solution)/shard_map/ppermute | solution.py:334
  29.5 0.5 collective-permute-start.3
  30.0 2.8 %collective-permute-done.16.refs_3_ = bf16[256,256]{1,0:T(8,128)(2,1)S(1)} collective-permute-done((bf16[256,256]{1,0:T(8,128)(2,1)S(1)}, bf16[256,256]{1,0:T(8,128)(2,1)S(1)}, u32[]{:S(2)}, u32[]{:S(2)}) %collective-permute-start.16) | collective-permute-done | bytes 131104 | tf_op jit(solution)/shard_map/ppermute | solution.py:309
  32.8 1.6 %collective-permute-start.4 = (bf16[120,512]{1,0:T(8,128)(2,1)S(1)}, bf16[120,512]{1,0:T(8,128)(2,1)S(1)}, u32[]{:S(2)}, u32[]{:S(2)}) collective-permute-start(bf16[120,512]{1,0:T(8,128)(2,1)S(1)} %get-tuple-element.47), channel_id=1, source_target_pairs={{0,18},{1,19},{2,16},{3,17},{16,2},{17,3},{18,0},{19,1},{4,22},{5,... | collective-permute-start | bytes 368648 | tf_op jit(solution)/shard_map/ppermute | solution.py:334
  34.5 1.3 %collective-permute-start.5 = (bf16[120,512]{1,0:T(8,128)(2,1)S(1)}, bf16[120,512]{1,0:T(8,128)(2,1)S(1)}, u32[]{:S(2)}, u32[]{:S(2)}) collective-permute-start(bf16[120,512]{1,0:T(8,128)(2,1)S(1)} %get-tuple-element.49), channel_id=1, source_target_pairs={{0,2},{1,3},{2,0},{3,1},{16,18},{17,19},{18,16},{19,17},{4,6},{5,7... | collective-permute-start | bytes 368648 | tf_op jit(solution)/shard_map/ppermute | solution.py:334
  35.8 0.5 collective-permute-start.6
  36.3 1.5 %collective-permute-done.3.refs_2_ = bf16[120,512]{1,0:T(8,128)(2,1)S(1)} collective-permute-done((bf16[120,512]{1,0:T(8,128)(2,1)S(1)}, bf16[120,512]{1,0:T(8,128)(2,1)S(1)}, u32[]{:S(2)}, u32[]{:S(2)}) %collective-permute-start.3) | collective-permute-done | bytes 122912 | tf_op jit(solution)/shard_map/ppermute | solution.py:334
  37.9 2.0 %collective-permute-start.7 = (bf16[120,512]{1,0:T(8,128)(2,1)S(1)}, bf16[120,512]{1,0:T(8,128)(2,1)S(1)}, u32[]{:S(2)}, u32[]{:S(2)}) collective-permute-start(bf16[120,512]{1,0:T(8,128)(2,1)S(1)} %get-tuple-element.51), channel_id=1, source_target_pairs={{0,18},{1,19},{2,16},{3,17},{16,2},{17,3},{18,0},{19,1},{4,22},{5,... | collective-permute-start | bytes 368648 | tf_op jit(solution)/shard_map/ppermute | solution.py:334
  39.9 0.7 %shard_map.62 = (f32[512,128]{1,0:T(8,128)S(1)}, bf16[512,128]{1,0:T(8,128)(2,1)S(1)}, f32[512,128]{1,0:T(8,128)S(1)}, bf16[512,128]{1,0:T(8,128)(2,1)S(1)}) custom-call(bf16[512,1024]{1,0:T(8,128)(2,1)S(1)} %get-tuple-element.58.refs_0_, bf16[256,256]{1,0:T(8,128)(2,1)S(1)} %get-tuple-element.59.refs_1_, ...), custom_call_target="tpu_custom_call" | custom-call | flops 268435456 | bytes 2359296 | tf_op jit(solution)/shard_map/pallas_call | solution.py:38
  40.7 1.9 %collective-permute-start.23 = (bf16[512,128]{1,0:T(8,128)(2,1)S(1)}, bf16[512,128]{1,0:T(8,128)(2,1)S(1)}, u32[]{:S(2)}, u32[]{:S(2)}) collective-permute-start(bf16[512,128]{1,0:T(8,128)(2,1)S(1)} %get-tuple-element.67), channel_id=1, source_target_pairs={{0,16},{16,0},{1,17},{17,1},{2,18},{18,2},{3,19},{19,3},{4,20},{20... | collective-permute-start | bytes 393224 | tf_op jit(solution)/shard_map/ppermute | solution.py:366
  43.2 2.8 %collective-permute-done.7.refs_3_ = bf16[120,512]{1,0:T(8,128)(2,1)S(1)} collective-permute-done((bf16[120,512]{1,0:T(8,128)(2,1)S(1)}, bf16[120,512]{1,0:T(8,128)(2,1)S(1)}, u32[]{:S(2)}, u32[]{:S(2)}) %collective-permute-start.7) | collective-permute-done | bytes 122912 | tf_op jit(solution)/shard_map/ppermute | solution.py:334
  46.2 0.3 shard_map.67
  46.5 0.3 shard_map.68
  47.1 2.5 %collective-permute-start.29 = (bf16[256,256]{1,0:T(8,128)(2,1)S(1)}, bf16[256,256]{1,0:T(8,128)(2,1)S(1)}, u32[]{:S(2)}, u32[]{:S(2)}) collective-permute-start(bf16[256,256]{1,0:T(8,128)(2,1)S(1)} %get-tuple-element.76), channel_id=1, source_target_pairs={{0,12},{4,8},{8,4},{12,0},{1,13},{5,9},{9,5},{13,1},{2,14},{6,10},... | collective-permute-start | bytes 393224 | tf_op jit(solution)/shard_map/ppermute | solution.py:399
  49.7 0.7 collective-permute-start.30
  50.4 0.5 shard_map.65
  50.9 2.7 %collective-permute-start.24 = (bf16[256,128]{1,0:T(8,128)(2,1)S(1)}, bf16[256,128]{1,0:T(8,128)(2,1)S(1)}, u32[]{:S(2)}, u32[]{:S(2)}) collective-permute-start(bf16[256,128]{1,0:T(8,128)(2,1)S(1)} %get-tuple-element.69), channel_id=1, source_target_pairs={{0,12},{4,8},{8,4},{12,0},{1,13},{5,9},{9,5},{13,1},{2,14},{6,10},... | collective-permute-start | bytes 196616 | tf_op jit(solution)/shard_map/ppermute | solution.py:399
  53.6 0.5 shard_map.63
  54.1 4.9 %collective-permute-done.31.refs_3_ = bf16[256,256]{1,0:T(8,128)(2,1)S(1)} collective-permute-done((bf16[256,256]{1,0:T(8,128)(2,1)S(1)}, bf16[256,256]{1,0:T(8,128)(2,1)S(1)}, u32[]{:S(2)}, u32[]{:S(2)}) %collective-permute-start.31) | collective-permute-done | bytes 131104 | tf_op jit(solution)/shard_map/ppermute | solution.py:399
  59.0 2.0 %collective-permute-start.19 = (bf16[256,128]{1,0:T(8,128)(2,1)S(1)}, bf16[256,128]{1,0:T(8,128)(2,1)S(1)}, u32[]{:S(2)}, u32[]{:S(2)}) collective-permute-start(bf16[256,128]{1,0:T(8,128)(2,1)S(1)} %get-tuple-element.63), channel_id=1, source_target_pairs={{0,12},{4,8},{8,4},{12,0},{1,13},{5,9},{9,5},{13,1},{2,14},{6,10},... | collective-permute-start | bytes 196616 | tf_op jit(solution)/shard_map/ppermute | solution.py:399
  61.0 2.5 %collective-permute-start.20 = (bf16[256,128]{1,0:T(8,128)(2,1)S(1)}, bf16[256,128]{1,0:T(8,128)(2,1)S(1)}, u32[]{:S(2)}, u32[]{:S(2)}) collective-permute-start(bf16[256,128]{1,0:T(8,128)(2,1)S(1)} %get-tuple-element.64), channel_id=1, source_target_pairs={{0,4},{4,0},{8,12},{12,8},{1,5},{5,1},{9,13},{13,9},{2,6},{6,2},{1... | collective-permute-start | bytes 196616 | tf_op jit(solution)/shard_map/ppermute | solution.py:399
  63.6 2.9 %collective-permute-start.21 = (bf16[256,128]{1,0:T(8,128)(2,1)S(1)}, bf16[256,128]{1,0:T(8,128)(2,1)S(1)}, u32[]{:S(2)}, u32[]{:S(2)}) collective-permute-start(bf16[256,128]{1,0:T(8,128)(2,1)S(1)} %get-tuple-element.65), channel_id=1, source_target_pairs={{0,8},{4,12},{8,0},{12,4},{1,9},{5,13},{9,1},{13,5},{2,10},{6,14},... | collective-permute-start | bytes 196616 | tf_op jit(solution)/shard_map/ppermute | solution.py:399
  66.4 1.5 %collective-permute-start.32 = (bf16[256,256]{1,0:T(8,128)(2,1)S(1)}, bf16[256,256]{1,0:T(8,128)(2,1)S(1)}, u32[]{:S(2)}, u32[]{:S(2)}) collective-permute-start(bf16[256,256]{1,0:T(8,128)(2,1)S(1)} %shard_map.69.refs_0_), channel_id=1, source_target_pairs={{0,16},{16,0},{1,17},{17,1},{2,18},{18,2},{3,19},{19,3},{4,20},{20... | collective-permute-start | bytes 393224 | tf_op jit(solution)/shard_map/ppermute | solution.py:414
  68.0 0.6 collective-permute-start.27
  68.8 2.4 %collective-permute-start.22 = (bf16[256,128]{1,0:T(8,128)(2,1)S(1)}, bf16[256,128]{1,0:T(8,128)(2,1)S(1)}, u32[]{:S(2)}, u32[]{:S(2)}) collective-permute-start(bf16[256,128]{1,0:T(8,128)(2,1)S(1)} %shard_map.64.refs_2_), channel_id=1, source_target_pairs={{0,16},{16,0},{1,17},{17,1},{2,18},{18,2},{3,19},{19,3},{4,20},{20... | collective-permute-start | bytes 196616 | tf_op jit(solution)/shard_map/ppermute | solution.py:414
  71.4 0.8 %shard_map.70.refs_2_ = bf16[512,512]{1,0:T(8,128)(2,1)} custom-call(bf16[256,256]{1,0:T(8,128)(2,1)S(1)} %shard_map.69.refs_0_, bf16[256,256]{1,0:T(8,128)(2,1)S(1)} %collective-permute-done.32.refs_1_, bf16[256,128]{1,0:T(8,128)(2,1)S(1)} %shard_map.64.refs_2_, bf16[256,128]{1,0:T(8,128)(2,1)S(1)} %shard_map.66.refs_3_), custom_call_target="tpu_custom_call" | custom-call | bytes 917504 | tf_op jit(solution)/shard_map/pallas_call | solution.py:38
  72.3 1.2 %collective-permute-done.22.refs_0_ = bf16[256,128]{1,0:T(8,128)(2,1)S(1)} collective-permute-done((bf16[256,128]{1,0:T(8,128)(2,1)S(1)}, bf16[256,128]{1,0:T(8,128)(2,1)S(1)}, u32[]{:S(2)}, u32[]{:S(2)}) %collective-permute-start.22) | collective-permute-done | bytes 65568 | tf_op jit(solution)/shard_map/ppermute | solution.py:414
  73.5 0.7 shard_map.71
  (39 shorter events, 2.1 us)
Async XLA Ops:
  0.0 8.9 %collective-permute-start.8 = (bf16[192,2048]{1,0:T(8,128)(2,1)}, bf16[192,2048]{1,0:T(8,128)(2,1)S(1)}, u32[]{:S(2)}, u32[]{:S(2)}) collective-permute-start(bf16[192,2048]{1,0:T(8,128)(2,1)} %refs_0_.1), channel_id=1, source_target_pairs={{0,1},{1,0},{2,3},{3,2},{4,5},{5,4},{6,7},{7,6},{8,9},{9,8},{10,11... | collective-permute-start | bytes 2359304 | tf_op jit(solution)/shard_map/ppermute | solution.py:282
  0.5 27.1 %collective-permute-start.1 = (bf16[192,2048]{1,0:T(8,128)(2,1)}, bf16[192,2048]{1,0:T(8,128)(2,1)S(1)}, u32[]{:S(2)}, u32[]{:S(2)}) collective-permute-start(bf16[192,2048]{1,0:T(8,128)(2,1)} %refs_2_.1), channel_id=1, source_target_pairs={{0,1},{1,0},{2,3},{3,2},{4,5},{5,4},{6,7},{7,6},{8,9},{9,8},{10,11... | collective-permute-start | bytes 2359304 | tf_op jit(solution)/shard_map/ppermute | solution.py:284
  1.8 5.7 %copy-start.1 = (s32[192,1]{0,1:T(1,128)S(1)}, s32[192,1]{0,1:T(1,128)}, u32[]{:S(2)}) copy-start(s32[192,1]{0,1:T(1,128)} %param.7) | copy-start | bytes 2308
  1.8 10.9 %collective-permute-start.12 = (bf16[256,256]{1,0:T(8,128)(2,1)S(1)}, bf16[256,256]{1,0:T(8,128)(2,1)S(1)}, u32[]{:S(2)}, u32[]{:S(2)}) collective-permute-start(bf16[256,256]{1,0:T(8,128)(2,1)S(1)} %get-tuple-element.57.refs_4_), channel_id=1, source_target_pairs={{0,4},{4,0},{8,12},{12,8},{1,5},{5,1},{9,13},{13,9},{2,6},{6,2},{1... | collective-permute-start | bytes 393224 | tf_op jit(solution)/shard_map/ppermute | solution.py:309
  4.9 8.9 %collective-permute-start.13 = (bf16[256,256]{1,0:T(8,128)(2,1)S(1)}, bf16[256,256]{1,0:T(8,128)(2,1)S(1)}, u32[]{:S(2)}, u32[]{:S(2)}) collective-permute-start(bf16[256,256]{1,0:T(8,128)(2,1)S(1)} %get-tuple-element.57.refs_4_), channel_id=1, source_target_pairs={{0,8},{4,12},{8,0},{12,4},{1,9},{5,13},{9,1},{13,5},{2,10},{6,14},... | collective-permute-start | bytes 393224 | tf_op jit(solution)/shard_map/ppermute | solution.py:309
  7.5 1.2 %collective-permute-start = (s32[1,192]{1,0:T(1,128)S(1)}, s32[1,192]{1,0:T(1,128)S(1)}, u32[]{:S(2)}, u32[]{:S(2)}) collective-permute-start(s32[1,192]{1,0:T(1,128)S(1)} %bitcast.4), channel_id=1, source_target_pairs={{0,1},{1,0},{2,3},{3,2},{4,5},{5,4},{6,7},{7,6},{8,9},{9,8},{10,11... | collective-permute-start | bytes 2312 | tf_op jit(solution)/shard_map/ppermute | solution.py:283
  9.7 17.9 %copy-start = (bf16[192,2048]{1,0:T(8,128)(2,1)S(1)}, bf16[192,2048]{1,0:T(8,128)(2,1)}, u32[]{:S(2)}) copy-start(bf16[192,2048]{1,0:T(8,128)(2,1)} %refs_2_.1) | copy-start | bytes 2359300
  9.7 12.1 %collective-permute-start.10 = (bf16[120,1024]{1,0:T(8,128)(2,1)S(1)}, bf16[120,1024]{1,0:T(8,128)(2,1)S(1)}, u32[]{:S(2)}, u32[]{:S(2)}) collective-permute-start(bf16[120,1024]{1,0:T(8,128)(2,1)S(1)} %get-tuple-element.55), channel_id=1, source_target_pairs={{0,16},{1,17},{2,18},{3,19},{16,0},{17,1},{18,2},{19,3},{4,20},{5,... | collective-permute-start | bytes 737288 | tf_op jit(solution)/shard_map/ppermute | solution.py:334
  11.2 12.9 %collective-permute-start.11 = (bf16[120,1024]{1,0:T(8,128)(2,1)S(1)}, bf16[120,1024]{1,0:T(8,128)(2,1)S(1)}, u32[]{:S(2)}, u32[]{:S(2)}) collective-permute-start(bf16[120,1024]{1,0:T(8,128)(2,1)S(1)} %get-tuple-element.56), channel_id=1, source_target_pairs={{0,18},{1,19},{2,16},{3,17},{16,2},{17,3},{18,0},{19,1},{4,22},{5,... | collective-permute-start | bytes 737288 | tf_op jit(solution)/shard_map/ppermute | solution.py:334
  12.7 12.7 %collective-permute-start.9 = (bf16[120,1024]{1,0:T(8,128)(2,1)S(1)}, bf16[120,1024]{1,0:T(8,128)(2,1)S(1)}, u32[]{:S(2)}, u32[]{:S(2)}) collective-permute-start(bf16[120,1024]{1,0:T(8,128)(2,1)S(1)} %get-tuple-element.54), channel_id=1, source_target_pairs={{0,2},{1,3},{2,0},{3,1},{16,18},{17,19},{18,16},{19,17},{4,6},{5,7... | collective-permute-start | bytes 737288 | tf_op jit(solution)/shard_map/ppermute | solution.py:334
  13.8 6.9 %collective-permute-start.14 = (bf16[256,256]{1,0:T(8,128)(2,1)S(1)}, bf16[256,256]{1,0:T(8,128)(2,1)S(1)}, u32[]{:S(2)}, u32[]{:S(2)}) collective-permute-start(bf16[256,256]{1,0:T(8,128)(2,1)S(1)} %get-tuple-element.57.refs_4_), channel_id=1, source_target_pairs={{0,12},{4,8},{8,4},{12,0},{1,13},{5,9},{9,5},{13,1},{2,14},{6,10},... | collective-permute-start | bytes 393224 | tf_op jit(solution)/shard_map/ppermute | solution.py:309
  20.7 8.8 %collective-permute-start.15 = (bf16[256,256]{1,0:T(8,128)(2,1)S(1)}, bf16[256,256]{1,0:T(8,128)(2,1)S(1)}, u32[]{:S(2)}, u32[]{:S(2)}) collective-permute-start(bf16[256,256]{1,0:T(8,128)(2,1)S(1)} %get-tuple-element.59.refs_1_), channel_id=1, source_target_pairs={{0,4},{4,0},{8,12},{12,8},{1,5},{5,1},{9,13},{13,9},{2,6},{6,2},{1... | collective-permute-start | bytes 393224 | tf_op jit(solution)/shard_map/ppermute | solution.py:309
  21.7 11.1 %collective-permute-start.16 = (bf16[256,256]{1,0:T(8,128)(2,1)S(1)}, bf16[256,256]{1,0:T(8,128)(2,1)S(1)}, u32[]{:S(2)}, u32[]{:S(2)}) collective-permute-start(bf16[256,256]{1,0:T(8,128)(2,1)S(1)} %get-tuple-element.59.refs_1_), channel_id=1, source_target_pairs={{0,8},{4,12},{8,0},{12,4},{1,9},{5,13},{9,1},{13,5},{2,10},{6,14},... | collective-permute-start | bytes 393224 | tf_op jit(solution)/shard_map/ppermute | solution.py:309
  24.1 10.4 %collective-permute-start.17 = (bf16[256,256]{1,0:T(8,128)(2,1)S(1)}, bf16[256,256]{1,0:T(8,128)(2,1)S(1)}, u32[]{:S(2)}, u32[]{:S(2)}) collective-permute-start(bf16[256,256]{1,0:T(8,128)(2,1)S(1)} %get-tuple-element.59.refs_1_), channel_id=1, source_target_pairs={{0,12},{4,8},{8,4},{12,0},{1,13},{5,9},{9,5},{13,1},{2,14},{6,10},... | collective-permute-start | bytes 393224 | tf_op jit(solution)/shard_map/ppermute | solution.py:309
  26.0 20.2 %collective-permute-start.28 = (bf16[512,256]{1,0:T(8,128)(2,1)S(1)}, bf16[512,256]{1,0:T(8,128)(2,1)S(1)}, u32[]{:S(2)}, u32[]{:S(2)}) collective-permute-start(bf16[512,256]{1,0:T(8,128)(2,1)S(1)} %get-tuple-element.73), channel_id=1, source_target_pairs={{0,16},{16,0},{1,17},{17,1},{2,18},{18,2},{3,19},{19,3},{4,20},{20... | collective-permute-start | bytes 786440 | tf_op jit(solution)/shard_map/ppermute | solution.py:366
  28.3 7.5 %collective-permute-start.2 = (bf16[120,512]{1,0:T(8,128)(2,1)S(1)}, bf16[120,512]{1,0:T(8,128)(2,1)S(1)}, u32[]{:S(2)}, u32[]{:S(2)}) collective-permute-start(bf16[120,512]{1,0:T(8,128)(2,1)S(1)} %get-tuple-element.45), channel_id=1, source_target_pairs={{0,2},{1,3},{2,0},{3,1},{16,18},{17,19},{18,16},{19,17},{4,6},{5,7... | collective-permute-start | bytes 368648 | tf_op jit(solution)/shard_map/ppermute | solution.py:334
  29.5 8.4 %collective-permute-start.3 = (bf16[120,512]{1,0:T(8,128)(2,1)S(1)}, bf16[120,512]{1,0:T(8,128)(2,1)S(1)}, u32[]{:S(2)}, u32[]{:S(2)}) collective-permute-start(bf16[120,512]{1,0:T(8,128)(2,1)S(1)} %get-tuple-element.46), channel_id=1, source_target_pairs={{0,16},{1,17},{2,18},{3,19},{16,0},{17,1},{18,2},{19,3},{4,20},{5,... | collective-permute-start | bytes 368648 | tf_op jit(solution)/shard_map/ppermute | solution.py:334
  32.8 7.9 %collective-permute-start.4 = (bf16[120,512]{1,0:T(8,128)(2,1)S(1)}, bf16[120,512]{1,0:T(8,128)(2,1)S(1)}, u32[]{:S(2)}, u32[]{:S(2)}) collective-permute-start(bf16[120,512]{1,0:T(8,128)(2,1)S(1)} %get-tuple-element.47), channel_id=1, source_target_pairs={{0,18},{1,19},{2,16},{3,17},{16,2},{17,3},{18,0},{19,1},{4,22},{5,... | collective-permute-start | bytes 368648 | tf_op jit(solution)/shard_map/ppermute | solution.py:334
  34.5 8.1 %collective-permute-start.5 = (bf16[120,512]{1,0:T(8,128)(2,1)S(1)}, bf16[120,512]{1,0:T(8,128)(2,1)S(1)}, u32[]{:S(2)}, u32[]{:S(2)}) collective-permute-start(bf16[120,512]{1,0:T(8,128)(2,1)S(1)} %get-tuple-element.49), channel_id=1, source_target_pairs={{0,2},{1,3},{2,0},{3,1},{16,18},{17,19},{18,16},{19,17},{4,6},{5,7... | collective-permute-start | bytes 368648 | tf_op jit(solution)/shard_map/ppermute | solution.py:334
  35.8 7.4 %collective-permute-start.6 = (bf16[120,512]{1,0:T(8,128)(2,1)S(1)}, bf16[120,512]{1,0:T(8,128)(2,1)S(1)}, u32[]{:S(2)}, u32[]{:S(2)}) collective-permute-start(bf16[120,512]{1,0:T(8,128)(2,1)S(1)} %get-tuple-element.50), channel_id=1, source_target_pairs={{0,16},{1,17},{2,18},{3,19},{16,0},{17,1},{18,2},{19,3},{4,20},{5,... | collective-permute-start | bytes 368648 | tf_op jit(solution)/shard_map/ppermute | solution.py:334
  37.9 8.1 %collective-permute-start.7 = (bf16[120,512]{1,0:T(8,128)(2,1)S(1)}, bf16[120,512]{1,0:T(8,128)(2,1)S(1)}, u32[]{:S(2)}, u32[]{:S(2)}) collective-permute-start(bf16[120,512]{1,0:T(8,128)(2,1)S(1)} %get-tuple-element.51), channel_id=1, source_target_pairs={{0,18},{1,19},{2,16},{3,17},{16,2},{17,3},{18,0},{19,1},{4,22},{5,... | collective-permute-start | bytes 368648 | tf_op jit(solution)/shard_map/ppermute | solution.py:334
  40.7 9.7 %collective-permute-start.23 = (bf16[512,128]{1,0:T(8,128)(2,1)S(1)}, bf16[512,128]{1,0:T(8,128)(2,1)S(1)}, u32[]{:S(2)}, u32[]{:S(2)}) collective-permute-start(bf16[512,128]{1,0:T(8,128)(2,1)S(1)} %get-tuple-element.67), channel_id=1, source_target_pairs={{0,16},{16,0},{1,17},{17,1},{2,18},{18,2},{3,19},{19,3},{4,20},{20... | collective-permute-start | bytes 393224 | tf_op jit(solution)/shard_map/ppermute | solution.py:366
  42.6 11.0 %collective-permute-start.18 = (bf16[512,128]{1,0:T(8,128)(2,1)S(1)}, bf16[512,128]{1,0:T(8,128)(2,1)S(1)}, u32[]{:S(2)}, u32[]{:S(2)}) collective-permute-start(bf16[512,128]{1,0:T(8,128)(2,1)S(1)} %get-tuple-element.61), channel_id=1, source_target_pairs={{0,16},{16,0},{1,17},{17,1},{2,18},{18,2},{3,19},{19,3},{4,20},{20... | collective-permute-start | bytes 393224 | tf_op jit(solution)/shard_map/ppermute | solution.py:366
  46.8 12.2 %collective-permute-start.31 = (bf16[256,256]{1,0:T(8,128)(2,1)S(1)}, bf16[256,256]{1,0:T(8,128)(2,1)S(1)}, u32[]{:S(2)}, u32[]{:S(2)}) collective-permute-start(bf16[256,256]{1,0:T(8,128)(2,1)S(1)} %get-tuple-element.78), channel_id=1, source_target_pairs={{0,8},{4,12},{8,0},{12,4},{1,9},{5,13},{9,1},{13,5},{2,10},{6,14},... | collective-permute-start | bytes 393224 | tf_op jit(solution)/shard_map/ppermute | solution.py:399
  47.1 11.9 %collective-permute-start.29 = (bf16[256,256]{1,0:T(8,128)(2,1)S(1)}, bf16[256,256]{1,0:T(8,128)(2,1)S(1)}, u32[]{:S(2)}, u32[]{:S(2)}) collective-permute-start(bf16[256,256]{1,0:T(8,128)(2,1)S(1)} %get-tuple-element.76), channel_id=1, source_target_pairs={{0,12},{4,8},{8,4},{12,0},{1,13},{5,9},{9,5},{13,1},{2,14},{6,10},... | collective-permute-start | bytes 393224 | tf_op jit(solution)/shard_map/ppermute | solution.py:399
  49.7 11.4 %collective-permute-start.30 = (bf16[256,256]{1,0:T(8,128)(2,1)S(1)}, bf16[256,256]{1,0:T(8,128)(2,1)S(1)}, u32[]{:S(2)}, u32[]{:S(2)}) collective-permute-start(bf16[256,256]{1,0:T(8,128)(2,1)S(1)} %get-tuple-element.77), channel_id=1, source_target_pairs={{0,4},{4,0},{8,12},{12,8},{1,5},{5,1},{9,13},{13,9},{2,6},{6,2},{1... | collective-permute-start | bytes 393224 | tf_op jit(solution)/shard_map/ppermute | solution.py:399
  50.9 12.7 %collective-permute-start.24 = (bf16[256,128]{1,0:T(8,128)(2,1)S(1)}, bf16[256,128]{1,0:T(8,128)(2,1)S(1)}, u32[]{:S(2)}, u32[]{:S(2)}) collective-permute-start(bf16[256,128]{1,0:T(8,128)(2,1)S(1)} %get-tuple-element.69), channel_id=1, source_target_pairs={{0,12},{4,8},{8,4},{12,0},{1,13},{5,9},{9,5},{13,1},{2,14},{6,10},... | collective-permute-start | bytes 196616 | tf_op jit(solution)/shard_map/ppermute | solution.py:399
  53.6 12.8 %collective-permute-start.25 = (bf16[256,128]{1,0:T(8,128)(2,1)S(1)}, bf16[256,128]{1,0:T(8,128)(2,1)S(1)}, u32[]{:S(2)}, u32[]{:S(2)}) collective-permute-start(bf16[256,128]{1,0:T(8,128)(2,1)S(1)} %get-tuple-element.70), channel_id=1, source_target_pairs={{0,4},{4,0},{8,12},{12,8},{1,5},{5,1},{9,13},{13,9},{2,6},{6,2},{1... | collective-permute-start | bytes 196616 | tf_op jit(solution)/shard_map/ppermute | solution.py:399
  59.0 9.0 %collective-permute-start.26 = (bf16[256,128]{1,0:T(8,128)(2,1)S(1)}, bf16[256,128]{1,0:T(8,128)(2,1)S(1)}, u32[]{:S(2)}, u32[]{:S(2)}) collective-permute-start(bf16[256,128]{1,0:T(8,128)(2,1)S(1)} %get-tuple-element.71), channel_id=1, source_target_pairs={{0,8},{4,12},{8,0},{12,4},{1,9},{5,13},{9,1},{13,5},{2,10},{6,14},... | collective-permute-start | bytes 196616 | tf_op jit(solution)/shard_map/ppermute | solution.py:399
  59.0 9.6 %collective-permute-start.19 = (bf16[256,128]{1,0:T(8,128)(2,1)S(1)}, bf16[256,128]{1,0:T(8,128)(2,1)S(1)}, u32[]{:S(2)}, u32[]{:S(2)}) collective-permute-start(bf16[256,128]{1,0:T(8,128)(2,1)S(1)} %get-tuple-element.63), channel_id=1, source_target_pairs={{0,12},{4,8},{8,4},{12,0},{1,13},{5,9},{9,5},{13,1},{2,14},{6,10},... | collective-permute-start | bytes 196616 | tf_op jit(solution)/shard_map/ppermute | solution.py:399
  61.0 7.5 %collective-permute-start.20 = (bf16[256,128]{1,0:T(8,128)(2,1)S(1)}, bf16[256,128]{1,0:T(8,128)(2,1)S(1)}, u32[]{:S(2)}, u32[]{:S(2)}) collective-permute-start(bf16[256,128]{1,0:T(8,128)(2,1)S(1)} %get-tuple-element.64), channel_id=1, source_target_pairs={{0,4},{4,0},{8,12},{12,8},{1,5},{5,1},{9,13},{13,9},{2,6},{6,2},{1... | collective-permute-start | bytes 196616 | tf_op jit(solution)/shard_map/ppermute | solution.py:399
  63.6 5.2 %collective-permute-start.21 = (bf16[256,128]{1,0:T(8,128)(2,1)S(1)}, bf16[256,128]{1,0:T(8,128)(2,1)S(1)}, u32[]{:S(2)}, u32[]{:S(2)}) collective-permute-start(bf16[256,128]{1,0:T(8,128)(2,1)S(1)} %get-tuple-element.65), channel_id=1, source_target_pairs={{0,8},{4,12},{8,0},{12,4},{1,9},{5,13},{9,1},{13,5},{2,10},{6,14},... | collective-permute-start | bytes 196616 | tf_op jit(solution)/shard_map/ppermute | solution.py:399
  66.4 5.0 %collective-permute-start.32 = (bf16[256,256]{1,0:T(8,128)(2,1)S(1)}, bf16[256,256]{1,0:T(8,128)(2,1)S(1)}, u32[]{:S(2)}, u32[]{:S(2)}) collective-permute-start(bf16[256,256]{1,0:T(8,128)(2,1)S(1)} %shard_map.69.refs_0_), channel_id=1, source_target_pairs={{0,16},{16,0},{1,17},{17,1},{2,18},{18,2},{3,19},{19,3},{4,20},{20... | collective-permute-start | bytes 393224 | tf_op jit(solution)/shard_map/ppermute | solution.py:414
  68.0 4.3 %collective-permute-start.27 = (bf16[256,128]{1,0:T(8,128)(2,1)S(1)}, bf16[256,128]{1,0:T(8,128)(2,1)S(1)}, u32[]{:S(2)}, u32[]{:S(2)}) collective-permute-start(bf16[256,128]{1,0:T(8,128)(2,1)S(1)} %shard_map.66.refs_3_), channel_id=1, source_target_pairs={{0,16},{16,0},{1,17},{17,1},{2,18},{18,2},{3,19},{19,3},{4,20},{20... | collective-permute-start | bytes 196616 | tf_op jit(solution)/shard_map/ppermute | solution.py:414
  68.8 4.7 %collective-permute-start.22 = (bf16[256,128]{1,0:T(8,128)(2,1)S(1)}, bf16[256,128]{1,0:T(8,128)(2,1)S(1)}, u32[]{:S(2)}, u32[]{:S(2)}) collective-permute-start(bf16[256,128]{1,0:T(8,128)(2,1)S(1)} %shard_map.64.refs_2_), channel_id=1, source_target_pairs={{0,16},{16,0},{1,17},{17,1},{2,18},{18,2},{3,19},{19,3},{4,20},{20... | collective-permute-start | bytes 196616 | tf_op jit(solution)/shard_map/ppermute | solution.py:414
